TPU v7x, 32 devices: a whole 2x2x4 slice. The times are simulated.
32 devices in a mesh: fsdp: 8 (over z, x), rep: 4 (over y, core).
Axes of the slice: x: 2, y: 2, z: 4, core: 2. Of those that a mesh axis runs over, the one named last changes fastest.
Arguments:
- tokens: bfloat16 [4096, 1024], P(('fsdp', 'rep')), may hold values from -6 to 6
- seq_lengths: int32 [32, 8], P(('fsdp', 'rep')), may hold values from 0 to 64, as said below
- cotangent: bfloat16 [4096, 1024], P(('fsdp', 'rep')), may hold values from -6 to 6
- attention_norm_gain: bfloat16 [1024], P(('fsdp', 'rep')), may hold values from 0.5 to 1.5
- w_qkv: bfloat16 [1024, 3072], P(('fsdp', 'rep')), may hold values from -0.1875 to 0.1875
- w_attn_out: bfloat16 [1024, 1024], P(('fsdp', 'rep')), may hold values from -0.75 to 0.75
- feedforward_norm_gain: bfloat16 [1024], P(('fsdp', 'rep')), may hold values from 0.5 to 1.5
- w_in: bfloat16 [1024, 5248], P(('fsdp', 'rep')), may hold values from -0.1875 to 0.1875
- w_out: bfloat16 [1024, 2624], P(('fsdp', 'rep')), may hold values from -0.125 to 0.125
Outputs:
- output: bfloat16 [4096, 1024], P(('fsdp', 'rep'))
- block_input_gradient: float32 [4096, 1024], P(('fsdp', 'rep'))
- attention_gain_gradient: float32 [1024], P(('fsdp', 'rep'))
- grad_w_qkv: float32 [1024, 3072], P(('fsdp', 'rep'))
- grad_w_attn_out: float32 [1024, 1024], P(('fsdp', 'rep'))
- feedforward_gain_gradient: float32 [1024], P(('fsdp', 'rep'))
- grad_w_in: float32 [1024, 5248], P(('fsdp', 'rep'))
- grad_w_out: float32 [1024, 2624], P(('fsdp', 'rep'))
Inputs may be any that keep to these rules, and one draw needn't show every extreme that they name: `seq_lengths`: A row's nonzero lengths come first; a row's lengths sum to at most 128, and to exactly 128 on some device; some sequence has length 64.
All inputs are finite; a program needn't handle non-finite values.
Results may differ from a plain program's by a relative error of at most 0.013.
Values may be sent and summed in bfloat16 or wider, within the bound.
No kernel may reach another device: no remote copies, remote signals or barrier semaphores. Data moves between devices by JAX's collectives and lax.ppermute only.
A program may use at most 256 MiB of HBM per device.

v0:
```python
import jax
import jax.numpy as jnp
from jax import lax
from jax.sharding import PartitionSpec as P

HEAD_DIM = 64


norm_eps = 1e-05
rope_base = 160000.0


def matmul(left_side, right_side):
    return jnp.dot(left_side, right_side, preferred_element_type=jnp.float32)


def matmul_right_t(left_side, right_side):
    return lax.dot_general(
        left_side, right_side, (((1,), (1,)), ((), ())), preferred_element_type=jnp.float32
    )


def matmul_left_t(left_side, right_side):
    return lax.dot_general(
        left_side, right_side, (((0,), (0,)), ((), ())), preferred_element_type=jnp.float32
    )


def batched(form, left_side, right_side):
    return jnp.einsum(form, left_side, right_side, preferred_element_type=jnp.float32)


def layout(lengths, row_count):
    ends = jnp.cumsum(lengths)
    starts = ends - lengths
    places = lax.iota(jnp.int32, row_count)
    sequence_segment = jnp.sum((ends[None, :] <= places[:, None]).astype(jnp.int32), axis=1)
    slot_ids = lax.iota(jnp.int32, lengths.shape[0])
    first_row = jnp.sum(
        jnp.where(sequence_segment[:, None] == slot_ids[None, :], starts[None, :], 0), axis=1
    )
    return (sequence_segment, places - first_row, sequence_segment < lengths.shape[0])


def rotary(positions, head_size):
    half_size = head_size // 2
    frequency = rope_base ** (-(lax.iota(jnp.float32, half_size) * (2.0 / head_size)))
    angles = positions.astype(jnp.float32)[..., None] * frequency
    cosine_table = jnp.concatenate([jnp.cos(angles), jnp.cos(angles)], axis=-1)
    sine_table = jnp.concatenate([jnp.sin(angles), jnp.sin(angles)], axis=-1)
    return (cosine_table, sine_table)


def rotate_half(vector):
    half_size = vector.shape[-1] // 2
    return jnp.concatenate([-vector[..., half_size:], vector[..., :half_size]], axis=-1)


def rotate_back(vector):
    half_size = vector.shape[-1] // 2
    return jnp.concatenate([vector[..., half_size:], -vector[..., :half_size]], axis=-1)


def norm_statistics(values):
    average = jnp.mean(values, axis=-1, keepdims=True)
    centred = values - average
    inverse = lax.rsqrt(jnp.mean(centred * centred, axis=-1, keepdims=True) + norm_eps)
    return (centred * inverse, inverse)


def norm_backward_pass(grad_normed, gain_vec, normalized, inverse):
    scaled = grad_normed * gain_vec.astype(jnp.float32)
    return inverse * (
        scaled
        - jnp.mean(scaled, axis=-1, keepdims=True)
        - normalized * jnp.mean(scaled * normalized, axis=-1, keepdims=True)
    )


def attend(rotated_query, rotated_key, value_reduced_precision, sequence_segment):
    scores = batched("thd,shd->hts", rotated_query, rotated_key)
    allowed = sequence_segment[:, None] == sequence_segment[None, :]
    scores = jnp.where(allowed[None], scores, -jnp.inf)
    logarithm_totals = jax.nn.logsumexp(scores, axis=-1)
    weights = jnp.exp(scores - logarithm_totals[..., None]).astype(jnp.bfloat16)
    attended = batched("hts,shd->thd", weights, value_reduced_precision).astype(jnp.bfloat16)
    return (attended, logarithm_totals)


def attend_back(
    rotated_query,
    rotated_key,
    value_reduced_precision,
    sequence_segment,
    logarithm_totals,
    grad_attended,
):
    scores = batched("thd,shd->hts", rotated_query, rotated_key)
    allowed = sequence_segment[:, None] == sequence_segment[None, :]
    scores = jnp.where(allowed[None], scores, -jnp.inf)
    probs_full = jnp.exp(scores - logarithm_totals[..., None])
    weights = probs_full.astype(jnp.bfloat16)
    grad_value = batched("hts,thd->shd", weights, grad_attended)
    grad_probs = batched("thd,shd->hts", grad_attended, value_reduced_precision)
    row_delta = jnp.sum(probs_full * grad_probs, axis=-1, keepdims=True)
    grad_scores = (probs_full * (grad_probs - row_delta)).astype(jnp.bfloat16)
    grad_query = batched("hts,shd->thd", grad_scores, rotated_key)
    grad_key = batched("hts,thd->shd", grad_scores, rotated_query)
    return (grad_query, grad_key, grad_value)


def forward(
    tokens, lengths, attention_norm_gain, w_qkv, w_attn_out, feedforward_norm_gain, w_in, w_out
):
    groups, row_count, embedding_width = tokens.shape
    head_count = embedding_width // HEAD_DIM
    hidden_units = w_in.shape[1] // 2
    sequence_segment, positions, valid = jax.vmap(
        lambda row_lengths: layout(row_lengths, row_count)
    )(lengths)
    cosine_table, sine_table = rotary(positions, HEAD_DIM)
    cosine_table = cosine_table[:, :, None, :]
    sine_table = sine_table[:, :, None, :]
    residual_input = tokens.reshape(groups * row_count, embedding_width).astype(jnp.float32)
    attention_standardized, attention_inverse_norm = norm_statistics(residual_input)
    attention_normed_input = (
        attention_standardized * attention_norm_gain.astype(jnp.float32)
    ).astype(jnp.bfloat16)
    packed = matmul(attention_normed_input, w_qkv).reshape(
        groups, row_count, 3, head_count, HEAD_DIM
    )
    query_raw = packed[:, :, 0]
    key_raw = packed[:, :, 1]
    rotated_query = (
        (query_raw * cosine_table + rotate_half(query_raw) * sine_table) * HEAD_DIM ** (-0.5)
    ).astype(jnp.bfloat16)
    rotated_key = (key_raw * cosine_table + rotate_half(key_raw) * sine_table).astype(jnp.bfloat16)
    value_reduced_precision = packed[:, :, 2].astype(jnp.bfloat16)
    attended, logarithm_totals = jax.vmap(attend)(
        rotated_query, rotated_key, value_reduced_precision, sequence_segment
    )
    attention_rows_flat = attended.reshape(groups * row_count, embedding_width)
    hidden_residual = residual_input + matmul(attention_rows_flat, w_attn_out)
    feedforward_standardized, feedforward_inverse_norm = norm_statistics(hidden_residual)
    feedforward_normed_input = (
        feedforward_standardized * feedforward_norm_gain.astype(jnp.float32)
    ).astype(jnp.bfloat16)
    inner_proj = matmul(feedforward_normed_input, w_in)
    gate_projection = inner_proj[:, :hidden_units]
    up_projection = inner_proj[:, hidden_units:]
    activation_output = jax.nn.gelu(gate_projection, approximate=False)
    mixed_input = (activation_output * up_projection).astype(jnp.bfloat16)
    live_token_rows = valid.reshape(groups * row_count, 1)
    mlp_result = matmul_right_t(mixed_input, w_out)
    output = jnp.where(live_token_rows, hidden_residual + mlp_result, 0.0).astype(jnp.bfloat16)
    saved_residuals = (
        sequence_segment,
        live_token_rows,
        cosine_table,
        sine_table,
        attention_standardized,
        attention_inverse_norm,
        attention_normed_input,
        rotated_query,
        rotated_key,
        value_reduced_precision,
        logarithm_totals,
        attention_rows_flat,
        feedforward_standardized,
        feedforward_inverse_norm,
        feedforward_normed_input,
        gate_projection,
        up_projection,
        activation_output,
        mixed_input,
    )
    return (output, saved_residuals)


def backward(
    saved_residuals,
    cotangent,
    attention_norm_gain,
    w_qkv,
    w_attn_out,
    feedforward_norm_gain,
    w_in,
    w_out,
):
    (
        sequence_segment,
        live_token_rows,
        cosine_table,
        sine_table,
        attention_standardized,
        attention_inverse_norm,
        attention_normed_input,
        rotated_query,
        rotated_key,
        value_reduced_precision,
        logarithm_totals,
        attention_rows_flat,
        feedforward_standardized,
        feedforward_inverse_norm,
        feedforward_normed_input,
        gate_projection,
        up_projection,
        activation_output,
        mixed_input,
    ) = saved_residuals
    groups, row_count = sequence_segment.shape
    embedding_width = attention_standardized.shape[1]
    head_count = embedding_width // HEAD_DIM
    flat_cot = cotangent.reshape(groups * row_count, embedding_width)
    output_gradient = jnp.where(live_token_rows, flat_cot, jnp.zeros((), flat_cot.dtype))
    grad_mixed = matmul(output_gradient, w_out)
    slope = (
        0.5 * (1.0 + lax.erf(gate_projection * 0.7071067811865476))
        + gate_projection * jnp.exp(-0.5 * gate_projection * gate_projection) * 0.3989422804014327
    )
    grad_inner = jnp.concatenate(
        [grad_mixed * up_projection * slope, grad_mixed * activation_output], axis=1
    ).astype(jnp.bfloat16)
    feedforward_normed_gradient = matmul_right_t(grad_inner, w_in)
    hidden_gradient = output_gradient.astype(jnp.float32) + norm_backward_pass(
        feedforward_normed_gradient,
        feedforward_norm_gain,
        feedforward_standardized,
        feedforward_inverse_norm,
    )
    grad_hidden_low = hidden_gradient.astype(jnp.bfloat16)
    grad_attended = matmul_right_t(grad_hidden_low, w_attn_out).astype(jnp.bfloat16)
    grad_attended = grad_attended.reshape(groups, row_count, head_count, HEAD_DIM)
    grad_query, grad_key, grad_value = jax.vmap(attend_back)(
        rotated_query,
        rotated_key,
        value_reduced_precision,
        sequence_segment,
        logarithm_totals,
        grad_attended,
    )
    grad_query = grad_query * HEAD_DIM ** (-0.5)
    grad_query = grad_query * cosine_table + rotate_back(grad_query * sine_table)
    grad_key = grad_key * cosine_table + rotate_back(grad_key * sine_table)
    grad_packed = jnp.stack([grad_query, grad_key, grad_value], axis=2)
    grad_packed = grad_packed.reshape(groups * row_count, 3 * embedding_width).astype(jnp.bfloat16)
    attention_normed_gradient = matmul_right_t(grad_packed, w_qkv)
    block_input_gradient = hidden_gradient + norm_backward_pass(
        attention_normed_gradient,
        attention_norm_gain,
        attention_standardized,
        attention_inverse_norm,
    )
    factors = (
        attention_normed_input,
        grad_packed,
        attention_rows_flat,
        grad_hidden_low,
        feedforward_normed_input,
        grad_inner,
        output_gradient,
        mixed_input,
        attention_normed_gradient,
        attention_standardized,
        feedforward_normed_gradient,
        feedforward_standardized,
    )
    return (block_input_gradient, factors)


def local(
    tokens,
    seq_lengths,
    cotangent,
    attention_norm_gain,
    w_qkv,
    w_attn_out,
    feedforward_norm_gain,
    w_in,
    w_out,
):
    row_count, embedding_width = tokens.shape
    gathered = (
        lax.all_gather(attention_norm_gain, ("fsdp", "rep"), axis=0, tiled=True),
        lax.all_gather(w_qkv, ("fsdp", "rep"), axis=0, tiled=True),
        lax.all_gather(w_attn_out, ("fsdp", "rep"), axis=0, tiled=True),
        lax.all_gather(feedforward_norm_gain, ("fsdp", "rep"), axis=0, tiled=True),
        lax.all_gather(w_in, ("fsdp", "rep"), axis=0, tiled=True),
        lax.all_gather(w_out, ("fsdp", "rep"), axis=0, tiled=True),
    )
    output, saved_residuals = forward(
        tokens.reshape(1, row_count, embedding_width),
        seq_lengths,
        gathered[0],
        gathered[1],
        gathered[2],
        gathered[3],
        gathered[4],
        gathered[5],
    )
    second_copy = (
        lax.all_gather(attention_norm_gain, ("fsdp", "rep"), axis=0, tiled=True),
        lax.all_gather(w_qkv, ("fsdp", "rep"), axis=0, tiled=True),
        lax.all_gather(w_attn_out, ("fsdp", "rep"), axis=0, tiled=True),
        lax.all_gather(feedforward_norm_gain, ("fsdp", "rep"), axis=0, tiled=True),
        lax.all_gather(w_in, ("fsdp", "rep"), axis=0, tiled=True),
        lax.all_gather(w_out, ("fsdp", "rep"), axis=0, tiled=True),
    )
    block_input_gradient, factors = backward(
        saved_residuals,
        cotangent.reshape(1, row_count, embedding_width),
        second_copy[0],
        second_copy[1],
        second_copy[2],
        second_copy[3],
        second_copy[4],
        second_copy[5],
    )
    (
        normed_attn,
        grad_packed,
        attended_rows,
        grad_hidden_low,
        normed_mlp,
        grad_inner,
        grad_out,
        mixed_input,
        grad_normed_attn,
        standard_attn,
        grad_normed_mlp,
        standard_mlp,
    ) = factors
    qkv_width = w_qkv.shape[1]
    attn_width = w_attn_out.shape[1]
    inner_width = w_in.shape[1]
    outer_width = w_out.shape[1]
    qkv_term = matmul_left_t(normed_attn, grad_packed)
    attn_term = matmul_left_t(attended_rows, grad_hidden_low)
    inner_term = matmul_left_t(normed_mlp, grad_inner)
    outer_term = matmul_left_t(grad_out, mixed_input)
    attn_gain_term = jnp.sum(grad_normed_attn * standard_attn, axis=0)
    mlp_gain_term = jnp.sum(grad_normed_mlp * standard_mlp, axis=0)
    summed = lax.psum_scatter(
        jnp.concatenate(
            [
                qkv_term,
                attn_term,
                inner_term,
                outer_term,
                attn_gain_term[:, None],
                mlp_gain_term[:, None],
            ],
            axis=1,
        ),
        ("fsdp", "rep"),
        scatter_dimension=0,
        tiled=True,
    )
    edge_two = qkv_width + attn_width
    edge_three = edge_two + inner_width
    edge_four = edge_three + outer_width
    return (
        output,
        block_input_gradient,
        summed[:, edge_four],
        summed[:, :qkv_width],
        summed[:, qkv_width:edge_two],
        summed[:, edge_four + 1],
        summed[:, edge_two:edge_three],
        summed[:, edge_three:edge_four],
    )


def solution(mesh):
    return jax.shard_map(
        local,
        mesh=mesh,
        in_specs=(
            P(("fsdp", "rep"), None),
            P(("fsdp", "rep"), None),
            P(("fsdp", "rep"), None),
            P(("fsdp", "rep")),
            P(("fsdp", "rep"), None),
            P(("fsdp", "rep"), None),
            P(("fsdp", "rep")),
            P(("fsdp", "rep"), None),
            P(("fsdp", "rep"), None),
        ),
        out_specs=(
            P(("fsdp", "rep"), None),
            P(("fsdp", "rep"), None),
            P(("fsdp", "rep")),
            P(("fsdp", "rep"), None),
            P(("fsdp", "rep"), None),
            P(("fsdp", "rep")),
            P(("fsdp", "rep"), None),
            P(("fsdp", "rep"), None),
        ),
        check_vma=False,
    )
```

profile of v0, /device:TPU:0, one launch (start us, length us, event | category | flops | bytes accessed | tf_op | source)
XLA Modules:
  0.0 939.0 jit_solution(12498870982710090608)
XLA Ops:
  11.7 42.5 %all-reduce.2 = (bf16[1024]{0:T(1024)(128)(2,1)S(1)}, bf16[1024]{0:T(1024)(128)(2,1)S(1)}) all-reduce(bf16[1024]{0:T(1024)(128)(2,1)S(1)} %dynamic-update-slice, bf16[1024]{0:T(1024)(128)(2,1)S(1)} %dynamic-update-slice.1), channel_id=1, replica_groups=mesh['fsdp'=8,'rep'=4] {'fsdp','rep'}, use_global_device_ids=true, to_apply=%add | all-reduce | flops 2048 | bytes 8192
  56.1 1.1 convert_reduce_fusion
  58.7 24.6 %all-gather.5.cloned.1.call-done = bf16[1024,3072]{1,0:T(8,128)(2,1)} async-done(((bf16[32,3072]{1,0:T(8,128)(2,1)}), bf16[1024,3072]{1,0:T(8,128)(2,1)}) %all-gather.5.cloned.1.call-update) | async-done | bytes 6291472 | tf_op jit(solution)/shard_map/all_gather | solution.py:285
  83.3 5.4 fusion.60
  91.2 49.9 %all-gather.7.cloned.1.call-done = bf16[1024,1024]{1,0:T(8,128)(2,1)} async-done(((bf16[32,1024]{1,0:T(8,128)(2,1)}), bf16[1024,1024]{1,0:T(8,128)(2,1)}) %all-gather.7.cloned.1.call-update) | async-done | bytes 2097168 | tf_op jit(solution)/shard_map/all_gather | solution.py:286
  141.1 2.2 fusion.67
  144.6 86.0 %all-gather.9.cloned.1.call-done = bf16[1024,5248]{1,0:T(8,128)(2,1)} async-done(((bf16[32,5248]{1,0:T(8,128)(2,1)}), bf16[1024,5248]{1,0:T(8,128)(2,1)}) %all-gather.9.cloned.1.call-update) | async-done | bytes 10747920 | tf_op jit(solution)/shard_map/all_gather | solution.py:288
  230.6 7.3 fusion.62
  237.9 60.2 %all-gather.11.cloned.1.call-done = bf16[1024,2624]{1,0:T(8,128)(2,1)} async-done(((bf16[32,2624]{1,0:T(8,128)(2,1)}), bf16[1024,2624]{1,0:T(8,128)(2,1)}) %all-gather.11.cloned.1.call-update) | async-done | bytes 5373968 | tf_op jit(solution)/shard_map/all_gather | solution.py:289
  298.1 9.0 multiply_convert_fusion
  307.1 4.2 multiply_reduce_fusion.1
  312.4 1.5 convolution_convert_fusion.1
  313.9 1.8 copy.46
  315.7 2.9 multiply_reduce_fusion
  318.7 1.2 fusion.17
  319.9 2.6 fusion.48
  322.5 8.9 fusion.18
  331.5 1.3 multiply_convert_fusion.1
  332.7 1.0 copy.53
  333.8 1.5 multiply_convert_fusion.2
  337.6 6.5 fusion.58
  344.1 3.1 fusion.32
  347.5 5.8 fusion.56
  353.3 57.1 %concatenate.52 = f32[1024,11970]{1,0:T(8,128)} concatenate(f32[1024,3072]{1,0:T(8,128)} %fusion.58, f32[1024,1024]{1,0:T(8,128)} %fusion.48, f32[1024,5248]{1,0:T(8,128)} %fusion.18, f32[1024,2624]{1,0:T(8,128)} %fusion.56, f32[1024,1]{1,0:T(8,128)S(1)} %copy.52, f32[1024,1]{1,0:T(8,128)S(1)} %copy-done.13), dimensions={1} | concatenate | bytes 98058240 | tf_op jit(solution)/shard_map/concatenate | solution.py:344
  411.5 1.0 fusion.31
  412.5 5.2 fusion.16
  417.7 506.3 %reduce-scatter.2.cloned.1.call-done = f32[32,11970]{1,0:T(8,128)} async-done(((f32[1024,11970]{1,0:T(8,128)}), f32[32,11970]{1,0:T(8,128)}) %reduce-scatter.2.cloned.1.call-update) | async-done | bytes 1532176 | tf_op jit(solution)/shard_map/reduce_scatter | solution.py:343
  923.9 1.5 slice_reduce_fusion
  925.4 1.6 slice.92
  927.0 1.7 slice.95
  928.7 1.8 slice.91
  930.5 2.0 slice.94
  (134 shorter events, 16.1 us)
Async XLA Ops:
  7.2 50.0 %copy-start.1 = (bf16[128,1024]{1,0:T(8,128)(2,1)S(1)}, bf16[128,1024]{1,0:T(8,128)(2,1)}, u32[]{:S(2)}) copy-start(bf16[128,1024]{1,0:T(8,128)(2,1)} %param.9) | copy-start | bytes 786436
  7.2 76.2 %all-gather.5.cloned.1.call-start = ((), (), s32[]{:S(2)}) async-start(), calls=%async_computation.1 | async-start | bytes 6488064 | tf_op jit(solution)/shard_map/all_gather | solution.py:285
  7.9 133.2 %all-gather.7.cloned.1.call-start = ((), (), s32[]{:S(2)}) async-start(), calls=%async_computation.2 | async-start | bytes 2162688 | tf_op jit(solution)/shard_map/all_gather | solution.py:286
  8.7 221.9 %all-gather.9.cloned.1.call-start = ((), (), s32[]{:S(2)}) async-start(), calls=%async_computation.3 | async-start | bytes 11083776 | tf_op jit(solution)/shard_map/all_gather | solution.py:288
  9.4 288.7 %all-gather.11.cloned.1.call-start = ((), (), s32[]{:S(2)}) async-start(), calls=%async_computation.4 | async-start | bytes 5677056 | tf_op jit(solution)/shard_map/all_gather | solution.py:289
  10.0 914.0 %reduce-scatter.2.cloned.1.call-start = ((), (), s32[]{:S(2)}) async-start(), calls=%async_computation.5 | async-start | bytes 50823168 | tf_op jit(solution)/shard_map/reduce_scatter | solution.py:343
  57.2 31.5 %copy-start.28 = (f32[128]{0:T(128)}, f32[128]{0:T(128)S(1)}, u32[]{:S(2)}) copy-start(f32[128]{0:T(128)S(1)} %broadcast_multiply_fusion.9) | copy-start | bytes 1540
  58.0 30.7 %copy-start.32 = (f32[128]{0:T(128)}, f32[128]{0:T(128)S(1)}, u32[]{:S(2)}) copy-start(f32[128]{0:T(128)S(1)} %add_rsqrt_fusion.1) | copy-start | bytes 1540
  89.2 2.0 copy-start.7
  89.2 2.0 copy-start.9
  298.1 9.0 copy-start
  298.1 9.0 copy-start.26
  298.1 9.0 copy-start.30
  307.0 4.3 copy-start.19
  307.0 4.3 copy-start.21
  307.1 4.3 copy-start.16
  307.1 4.3 copy-start.34
  307.1 5.3 copy-start.2
  315.7 2.9 copy-start.12
  319.8 2.7 copy-start.20
  319.9 2.7 copy-start.22
  319.9 2.7 copy-start.27
  319.9 2.6 copy-start.31
  322.5 8.9 copy-start.6
  322.5 8.9 copy-start.15
  331.5 2.3 copy-start.24
  336.7 7.5 slice-start
  337.6 6.5 slice-start.1
  344.1 3.3 copy-start.5
  344.1 3.3 copy-start.17
  344.1 3.3 copy-start.35
  347.5 5.8 copy-start.13
  (12 other events, 12.1 us)
Sparse Core Ops, SparseCore 0:
  10.9 72.3 all-gather.4
  86.2 54.8 all-gather.6
  144.0 86.5 all-gather.8
  233.4 64.6 all-gather.10
  410.6 513.3 reduce-scatter.1
where the time goes:
time: 948 us; the launch traced here: 939 us
  waiting for transfers between devices  730 us (77%)
  local copies, waits for them, and re-layouts  74.5 us (8%)
  matrix products  67.9 us (7%)
  blocking collectives  42.5 us (4%)
  between operations  14.3 us (2%)
  other arithmetic  10 us (1%)
    reduce_scatter x1, waiting for transfers between devices, local(): lax.psum_scatter(jnp.concatenate([qkv_term, attn_term, inner_term, outer_...  506 us
    all_gather x1, waiting for transfers between devices, local(): lax.all_gather(w_in, ('fsdp', 'rep'), axis=0, tiled=True)  86 us
    all_gather x1, waiting for transfers between devices, local(): lax.all_gather(w_out, ('fsdp', 'rep'), axis=0, tiled=True)  60.2 us
    concatenate x1, local copies, waits for them, and re-layouts, local(): jnp.concatenate([qkv_term, attn_term, inner_term, outer_term, attn_gain_t...  57.1 us
    all_gather x1, waiting for transfers between devices, local(): lax.all_gather(w_attn_out, ('fsdp', 'rep'), axis=0, tiled=True)  49.9 us
    unnamed x1, blocking collectives  42.5 us
    all_gather x1, waiting for transfers between devices, local(): lax.all_gather(w_qkv, ('fsdp', 'rep'), axis=0, tiled=True)  24.6 us
    dot_general x4, matrix products, matmul(): return jnp.dot(left_side, right_side, preferred_element_type=jnp.float32)  23.9 us
  transfers between devices with their start and end apart: 5, of which 5 were waited for; matrix products, arithmetic and copies ran while one was open for 3% of the time, Pallas kernels for 0%

commit v1 on v0

v1 whole, which is shorter than its diff:
```python
import jax
import jax.numpy as jnp
from jax import lax
from jax.sharding import PartitionSpec as P

HEAD_DIM = 64

norm_eps = 1e-05
rope_base = 160000.0
AXES = ("fsdp", "rep")


def matmul(left_side, right_side):
    return jnp.dot(left_side, right_side, preferred_element_type=jnp.float32)


def matmul_right_t(left_side, right_side):
    return lax.dot_general(
        left_side, right_side, (((1,), (1,)), ((), ())), preferred_element_type=jnp.float32
    )


def matmul_left_t(left_side, right_side):
    return lax.dot_general(
        left_side, right_side, (((0,), (0,)), ((), ())), preferred_element_type=jnp.float32
    )


def batched(form, left_side, right_side):
    return jnp.einsum(form, left_side, right_side, preferred_element_type=jnp.float32)


def layout(lengths, row_count):
    slot_ids = lax.iota(jnp.int32, lengths.shape[0])
    before = (slot_ids[:, None] <= slot_ids[None, :]).astype(jnp.int32)
    ends = jnp.sum(lengths[:, None] * before, axis=0)
    starts = ends - lengths
    places = lax.iota(jnp.int32, row_count)
    sequence_segment = jnp.sum((ends[None, :] <= places[:, None]).astype(jnp.int32), axis=1)
    first_row = jnp.sum(
        jnp.where(sequence_segment[:, None] == slot_ids[None, :], starts[None, :], 0), axis=1
    )
    return (sequence_segment, places - first_row, sequence_segment < lengths.shape[0])


def rotary(positions, head_size):
    half_size = head_size // 2
    frequency = rope_base ** (-(lax.iota(jnp.float32, half_size) * (2.0 / head_size)))
    angles = positions.astype(jnp.float32)[..., None] * frequency
    cosine, sine = jnp.cos(angles), jnp.sin(angles)
    return (
        jnp.concatenate([cosine, cosine], axis=-1),
        jnp.concatenate([sine, sine], axis=-1),
    )


def rotate_half(vector):
    half_size = vector.shape[-1] // 2
    return jnp.concatenate([-vector[..., half_size:], vector[..., :half_size]], axis=-1)


def rotate_back(vector):
    half_size = vector.shape[-1] // 2
    return jnp.concatenate([vector[..., half_size:], -vector[..., :half_size]], axis=-1)


def norm_statistics(values):
    average = jnp.mean(values, axis=-1, keepdims=True)
    centred = values - average
    inverse = lax.rsqrt(jnp.mean(centred * centred, axis=-1, keepdims=True) + norm_eps)
    return (centred * inverse, inverse)


def norm_backward_pass(scaled, normalized, inverse):
    return inverse * (
        scaled
        - jnp.mean(scaled, axis=-1, keepdims=True)
        - normalized * jnp.mean(scaled * normalized, axis=-1, keepdims=True)
    )


def attend(rotated_query, rotated_key, value_reduced_precision, sequence_segment):
    scores = batched("thd,shd->hts", rotated_query, rotated_key)
    allowed = sequence_segment[:, None] == sequence_segment[None, :]
    scores = jnp.where(allowed[None], scores, -jnp.inf)
    logarithm_totals = jax.nn.logsumexp(scores, axis=-1)
    weights = jnp.exp(scores - logarithm_totals[..., None]).astype(jnp.bfloat16)
    attended = batched("hts,shd->thd", weights, value_reduced_precision).astype(jnp.bfloat16)
    return (attended, logarithm_totals)


def attend_back(
    rotated_query,
    rotated_key,
    value_reduced_precision,
    sequence_segment,
    logarithm_totals,
    grad_attended,
):
    scores = batched("thd,shd->hts", rotated_query, rotated_key)
    allowed = sequence_segment[:, None] == sequence_segment[None, :]
    scores = jnp.where(allowed[None], scores, -jnp.inf)
    probs_full = jnp.exp(scores - logarithm_totals[..., None])
    weights = probs_full.astype(jnp.bfloat16)
    grad_value = batched("hts,thd->shd", weights, grad_attended)
    grad_probs = batched("thd,shd->hts", grad_attended, value_reduced_precision)
    row_delta = jnp.sum(probs_full * grad_probs, axis=-1, keepdims=True)
    grad_scores = (probs_full * (grad_probs - row_delta)).astype(jnp.bfloat16)
    grad_query = batched("hts,shd->thd", grad_scores, rotated_key)
    grad_key = batched("hts,thd->shd", grad_scores, rotated_query)
    return (grad_query, grad_key, grad_value)


def xor_order(items, index):
    bit = 1
    while bit < len(items):
        flip = (index & bit) != 0
        items = [jnp.where(flip, items[k ^ bit], items[k]) for k in range(len(items))]
        bit *= 2
    return items


def swap(value, distance):
    count = lax.axis_size("rep")
    return lax.ppermute(value, "rep", [(k, k ^ distance) for k in range(count)])


def rep_gather(block):
    across = swap(block, 2)
    beside = swap(jnp.stack([block, across]), 1)
    return jnp.concatenate([block, beside[0], across, beside[1]], axis=0)


def rep_scatter(partial):
    low = partial.astype(jnp.bfloat16)
    rows = partial.shape[0] // 4
    blocks = [low[k * rows : (k + 1) * rows] for k in range(4)]
    beside = swap(jnp.stack([blocks[1], blocks[3]]), 1).astype(jnp.float32)
    kept = blocks[0].astype(jnp.float32) + beside[0]
    sent = (blocks[2].astype(jnp.float32) + beside[1]).astype(jnp.bfloat16)
    return kept + swap(sent, 2).astype(jnp.float32)


def rep_exchange(pieces, rep):
    placed = xor_order(pieces, rep)
    received = [placed[0]] + [swap(placed[k], k) for k in range(1, len(placed))]
    return xor_order(received, rep)


class Ring:
    def __init__(self):
        self.index = lax.axis_index("fsdp")
        self.z, self.x = self.index // 2, self.index % 2

    def up(self, value):
        return lax.ppermute(value, "fsdp", [(k, (k + 2) % 8) for k in range(8)])

    def over(self, value):
        return lax.ppermute(value, "fsdp", [(k, k ^ 1) for k in range(8)])

    def relative(self, blocks):
        flip = self.x == 1
        blocks = [jnp.where(flip, blocks[k ^ 1], blocks[k]) for k in range(8)]
        for bit in (1, 2):
            turn = (self.z & bit) != 0
            blocks = [jnp.where(turn, blocks[(k + 2 * bit) % 8], blocks[k]) for k in range(8)]
        return blocks

    def absolute(self, blocks):
        flip = self.x == 1
        blocks = [jnp.where(flip, blocks[k ^ 1], blocks[k]) for k in range(8)]
        for bit in (1, 2):
            turn = (self.z & bit) != 0
            blocks = [jnp.where(turn, blocks[(k - 2 * bit) % 8], blocks[k]) for k in range(8)]
        return blocks

    def gather(self, own, more_z):
        first = self.up(own)
        second = self.up(first)
        third = self.up(second)
        over_own, over_first, over_second = self.over(own), self.over(first), self.over(second)
        over_third = self.up(over_second) if more_z else self.over(third)
        return [own, over_own, third, over_third, second, over_second, first, over_first]

    def scatter(self, blocks, more_z):
        wide = lambda value: value.astype(jnp.float32)
        low = lambda value: value.astype(jnp.bfloat16)
        blocks = [low(block) for block in blocks]
        total = wide(blocks[6])
        if more_z:
            blocks[5] = low(wide(blocks[5]) + wide(self.up(blocks[7])))
        else:
            total = total + wide(self.over(blocks[7]))
        for step in (2, 1, 0):
            here = wide(blocks[2 * step]) + wide(self.over(blocks[2 * step + 1]))
            total = here + wide(self.up(low(total)))
        return total


class Plain:
    def __init__(self):
        self.count = lax.axis_size("fsdp")

    def relative(self, blocks):
        return blocks

    absolute = relative

    def gather(self, own, more_z):
        whole = lax.all_gather(own, "fsdp", axis=0)
        return [whole[k] for k in range(self.count)]

    def scatter(self, blocks, more_z):
        return lax.psum_scatter(jnp.stack(blocks), "fsdp", scatter_dimension=0, tiled=False)


def split_columns(value, count):
    width = value.shape[1] // count
    return [value[:, k * width : (k + 1) * width] for k in range(count)]


def split_rows(value, count):
    width = value.shape[0] // count
    return [value[k * width : (k + 1) * width] for k in range(count)]


def columns(blocks):
    return jnp.concatenate(blocks, axis=1)


def rows(blocks):
    return jnp.concatenate(blocks, axis=0)


def local(
    tokens,
    seq_lengths,
    cotangent,
    attention_norm_gain,
    w_qkv,
    w_attn_out,
    feedforward_norm_gain,
    w_in,
    w_out,
):
    row_count, width = tokens.shape
    fsdp_count, rep_count = lax.axis_size("fsdp"), lax.axis_size("rep")
    rep = lax.axis_index("rep")
    ring = Ring() if fsdp_count == 8 else Plain()
    hidden = w_in.shape[1] // 2
    head_count = width // HEAD_DIM // rep_count
    own_width = head_count * HEAD_DIM
    low, wide = jnp.bfloat16, jnp.float32

    def relative(value):
        return columns(ring.relative(split_columns(value, fsdp_count)))

    def absolute(value):
        return columns(ring.absolute(split_columns(value, fsdp_count)))

    gain_attn = attention_norm_gain.astype(wide)[:, None]
    gain_mlp = feedforward_norm_gain.astype(wide)[:, None]
    qkv_parts = split_columns((w_qkv.astype(wide) * gain_attn).astype(low), 3 * rep_count)
    in_parts = split_columns((w_in.astype(wide) * gain_mlp).astype(low), 2 * rep_count)
    qkv_own = rows(
        rep_exchange([columns(qkv_parts[k::rep_count]) for k in range(rep_count)], rep)
    )
    order = [
        (k, (k % fsdp_count) * rep_count + k // fsdp_count) for k in range(fsdp_count * rep_count)
    ]
    attn_own = lax.ppermute(w_attn_out, AXES, order)
    in_own = rows(rep_exchange([columns(in_parts[k::rep_count]) for k in range(rep_count)], rep))
    out_own = rows(rep_exchange(split_columns(w_out, rep_count), rep))

    x_own = relative(tokens)
    x_low = rep_gather(x_own)
    cot = rep_gather(relative(cotangent))
    lengths = rep_gather(seq_lengths)

    qkv = rows(ring.gather(qkv_own, True))
    attn = relative(rows(ring.absolute(ring.gather(attn_own, True))))
    w_up = rows(ring.gather(in_own, False))
    w_down = rows(ring.gather(out_own, True))

    sequence_segment, positions, valid = jax.vmap(
        lambda row_lengths: layout(row_lengths, row_count)
    )(lengths)
    cosine, sine = rotary(positions, HEAD_DIM)
    cosine, sine = cosine[:, :, None, :], sine[:, :, None, :]
    live = valid.reshape(rep_count * row_count, 1)

    standard, inverse = norm_statistics(x_low.astype(wide))
    normed = standard.astype(low)
    packed = matmul(normed, qkv).reshape(rep_count, row_count, 3, head_count, HEAD_DIM)
    query, key = packed[:, :, 0], packed[:, :, 1]
    query = ((query * cosine + rotate_half(query) * sine) * HEAD_DIM ** (-0.5)).astype(low)
    key = (key * cosine + rotate_half(key) * sine).astype(low)
    value = packed[:, :, 2].astype(low)
    attended, totals = jax.vmap(attend)(query, key, value, sequence_segment)
    attended = attended.reshape(rep_count * row_count, own_width)
    hidden_own = x_own.astype(wide) + rep_scatter(matmul(attended, attn))
    standard_mlp, inverse_mlp = norm_statistics(hidden_own)
    normed_mlp = rep_gather(standard_mlp.astype(low))
    inner = matmul(normed_mlp, w_up)
    gate, up = inner[:, : hidden // rep_count], inner[:, hidden // rep_count :]
    phi = 0.5 * (1.0 + lax.erf(gate * 0.7071067811865476))
    activation = gate * phi
    mixed = (activation * up).astype(low)
    grad_out = jnp.where(live, cot, jnp.zeros((), low))

    term_out = matmul_left_t(grad_out, mixed)
    sum_out = ring.scatter(split_rows(term_out, fsdp_count), True)

    slope = phi + gate * jnp.exp(-0.5 * gate * gate) * 0.3989422804014327
    grad_mixed = matmul(grad_out, w_down)
    grad_inner = columns([grad_mixed * up * slope, grad_mixed * activation]).astype(low)
    scaled_mlp = rep_scatter(matmul_right_t(grad_inner, w_up))
    term_in = matmul_left_t(normed_mlp, grad_inner)
    sum_in = ring.scatter(split_rows(term_in, fsdp_count), False)
    grad_hidden = grad_out[:row_count].astype(wide) + norm_backward_pass(
        scaled_mlp, standard_mlp, inverse_mlp
    )
    grad_low = rep_gather(grad_hidden.astype(low))
    mlp_result = rep_scatter(matmul_right_t(mixed, w_down))
    output = jnp.where(live[:row_count], hidden_own + mlp_result, 0.0).astype(low)

    grad_attended = matmul_right_t(grad_low, attn).astype(low)
    grad_query, grad_key, grad_value = jax.vmap(attend_back)(
        query,
        key,
        value,
        sequence_segment,
        totals,
        grad_attended.reshape(rep_count, row_count, head_count, HEAD_DIM),
    )
    grad_query = grad_query * HEAD_DIM ** (-0.5)
    grad_query = grad_query * cosine + rotate_back(grad_query * sine)
    grad_key = grad_key * cosine + rotate_back(grad_key * sine)
    grad_packed = jnp.stack([grad_query, grad_key, grad_value], axis=2)
    grad_packed = grad_packed.reshape(rep_count * row_count, 3 * own_width).astype(low)
    term_qkv = matmul_left_t(normed, grad_packed)
    sum_qkv = ring.scatter(split_rows(term_qkv, fsdp_count), True)
    term_attn = absolute(matmul_left_t(attended, grad_low).astype(low))
    sum_attn = ring.scatter(ring.relative(split_rows(term_attn, fsdp_count)), True)
    scaled_attn = rep_scatter(matmul_right_t(grad_packed, qkv))
    block_input_gradient = grad_hidden + norm_backward_pass(
        scaled_attn, standard[:row_count], inverse[:row_count]
    )

    back_qkv = rep_exchange(split_rows(sum_qkv.astype(low), rep_count), rep)
    back_in = rep_exchange(split_rows(sum_in.astype(low), rep_count), rep)
    back_out = rep_exchange(split_rows(sum_out.astype(low), rep_count), rep)
    unit_qkv = columns(
        [split_columns(piece, 3)[part] for part in range(3) for piece in back_qkv]
    ).astype(wide)
    unit_in = columns(
        [split_columns(piece, 2)[part] for part in range(2) for piece in back_in]
    ).astype(wide)
    grad_w_attn_out = lax.ppermute(
        sum_attn.astype(low), AXES, [(there, here) for here, there in order]
    ).astype(wide)
    return (
        absolute(output),
        absolute(block_input_gradient),
        jnp.sum(unit_qkv * w_qkv.astype(wide), axis=1),
        unit_qkv * gain_attn,
        grad_w_attn_out,
        jnp.sum(unit_in * w_in.astype(wide), axis=1),
        unit_in * gain_mlp,
        columns(back_out).astype(wide),
    )


def solution(mesh):
    return jax.shard_map(
        local,
        mesh=mesh,
        in_specs=(
            P(AXES, None),
            P(AXES, None),
            P(AXES, None),
            P(AXES),
            P(AXES, None),
            P(AXES, None),
            P(AXES),
            P(AXES, None),
            P(AXES, None),
        ),
        out_specs=(
            P(AXES, None),
            P(AXES, None),
            P(AXES),
            P(AXES, None),
            P(AXES, None),
            P(AXES),
            P(AXES, None),
            P(AXES, None),
        ),
        check_vma=False,
    )
```

time: 948 us -> 372 us (0.39)
  waiting for transfers between devices: 730 us -> 169 us
  starting transfers between devices: 0.19 us -> 75.3 us
  matrix products: 67.9 us -> 19.8 us
  other arithmetic: 10 us -> 53.7 us
  blocking collectives: 42.5 us -> 0 us
  local copies, waits for them, and re-layouts: 74.5 us -> 44 us
  between operations: 14.3 us -> 3.25 us
    reduce_scatter x1 -> x0, waiting for transfers between devices: 506 us -> none  [local(): lax.psum_scatter(jnp.concatenate([qkv_term, attn_term, inner_term, outer_...]
    all_gather x4 -> x0, waiting for transfers between devices: 221 us -> none  [the longest x1 86 us: local(): lax.all_gather(w_in, ('fsdp', 'rep'), axis=0, tiled=True)]
    ppermute x0 -> x94, waiting for transfers between devices: none -> 169 us  [the longest x30 105 us: up(): return lax.ppermute(value, 'fsdp', [(k, (k + 2) % 8) for k in range(8)])]
    ppermute x0 -> x94, starting transfers between devices: none -> 75.3 us  [the longest x30 25.6 us: up(): return lax.ppermute(value, 'fsdp', [(k, (k + 2) % 8) for k in range(8)])]
    concatenate x1 -> x10, local copies, waits for them, and re-layouts: 57.1 us -> 13.4 us  [the longest x3 9.75 us: rows(): return jnp.concatenate(blocks, axis=0)]
    unnamed x1 -> x0, blocking collectives: 42.5 us -> none
    dot_general x4, matrix products: 23.8 us -> 4.13 us  [matmul_left_t(): lax.dot_general(left_side, right_side, (((0,), (0,)), ((), ())), preferre...]
    dot_general x4, matrix products: 23.9 us -> 7.94 us  [matmul(): return jnp.dot(left_side, right_side, preferred_element_type=jnp.float32)]
  transfers between devices with their start and end apart: 5 -> 94, of which waited for: 5 -> 37; matrix products, arithmetic and copies ran while one was open for 3% -> 23% of each run, Pallas kernels for 0% -> 0%
where the time goes in v1:
time: 372 us; the launch traced here: 365 us
  waiting for transfers between devices  169 us (45%)
  starting transfers between devices  75.3 us (20%)
  other arithmetic  53.7 us (14%)
  local copies, waits for them, and re-layouts  44 us (12%)
  matrix products  19.8 us (5%)
    ppermute x30, waiting for transfers between devices, up(): return lax.ppermute(value, 'fsdp', [(k, (k + 2) % 8) for k in range(8)])  105 us
    ppermute x26, waiting for transfers between devices, over(): return lax.ppermute(value, 'fsdp', [(k, k ^ 1) for k in range(8)])  45.6 us
    ppermute x30, starting transfers between devices, up(): return lax.ppermute(value, 'fsdp', [(k, (k + 2) % 8) for k in range(8)])  25.6 us
    ppermute x36, starting transfers between devices, swap(): return lax.ppermute(value, 'rep', [(k, k ^ distance) for k in range(count)])  24.6 us
    ppermute x26, starting transfers between devices, over(): return lax.ppermute(value, 'fsdp', [(k, k ^ 1) for k in range(8)])  23.7 us
    ppermute x36, waiting for transfers between devices, swap(): return lax.ppermute(value, 'rep', [(k, k ^ distance) for k in range(count)])  18.3 us
    unnamed x207, local copies, waits for them, and re-layouts  11.7 us
    concatenate x3, local copies, waits for them, and re-layouts, rows(): return jnp.concatenate(blocks, axis=0)  9.75 us
  transfers between devices with their start and end apart: 94, of which 37 were waited for; matrix products, arithmetic and copies ran while one was open for 23% of the time, Pallas kernels for 0%

profile of v1, /device:TPU:0, one launch (start us, length us, event | category | flops | bytes accessed | tf_op | source)
XLA Modules:
  0.0 364.8 jit_solution(18374988264480931238)
XLA Ops:
  5.4 3.0 collective-permute-start.27
  36.4 4.6 %collective-permute-start.2 = (bf16[128,1024]{1,0:T(8,128)(2,1)S(1)}, bf16[128,1024]{1,0:T(8,128)(2,1)S(1)}, u32[]{:S(2)}, u32[]{:S(2)}) collective-permute-start(bf16[128,1024]{1,0:T(8,128)(2,1)S(1)} %constant_dynamic-update-slice_fusion), channel_id=1, source_target_pairs={{0,2},{1,3},{2,0},{3,1},{4,6},{5,7},{6,4},{7,5},{8,10},{9,11},{10,... | collective-permute-start | bytes 786440 | tf_op jit(solution)/shard_map/ppermute | solution.py:125
  41.2 3.8 %collective-permute-start.15 = (bf16[32,1024]{1,0:T(8,128)(2,1)S(1)}, bf16[32,1024]{1,0:T(8,128)(2,1)S(1)}, u32[]{:S(2)}, u32[]{:S(2)}) collective-permute-start(bf16[32,1024]{1,0:T(8,128)(2,1)S(1)} %collective-permute-done.14), channel_id=1, source_target_pairs={{0,8},{4,12},{8,16},{12,20},{16,24},{20,28},{24,0},{28,4},{1,9},{5... | collective-permute-start | bytes 196616 | tf_op jit(solution)/shard_map/ppermute | solution.py:156
  54.3 4.3 %collective-permute-done.16 = bf16[32,1024]{1,0:T(8,128)(2,1)S(1)} collective-permute-done((bf16[32,1024]{1,0:T(8,128)(2,1)S(1)}, bf16[32,1024]{1,0:T(8,128)(2,1)S(1)}, u32[]{:S(2)}, u32[]{:S(2)}) %collective-permute-start.16) | collective-permute-done | bytes 65568 | tf_op jit(solution)/shard_map/ppermute | solution.py:156
  67.1 4.2 %collective-permute-start.9 = (bf16[128,768]{1,0:T(8,128)(2,1)S(1)}, bf16[128,768]{1,0:T(8,128)(2,1)S(1)}, u32[]{:S(2)}, u32[]{:S(2)}) collective-permute-start(bf16[128,768]{1,0:T(8,128)(2,1)S(1)} %collective-permute-done.8), channel_id=1, source_target_pairs={{0,8},{4,12},{8,16},{12,20},{16,24},{20,28},{24,0},{28,4},{1,9},{5... | collective-permute-start | bytes 589832 | tf_op jit(solution)/shard_map/ppermute | solution.py:156
  72.8 3.3 collective-permute-done.9
  78.6 5.0 %collective-permute-done.10 = bf16[128,768]{1,0:T(8,128)(2,1)S(1)} collective-permute-done((bf16[128,768]{1,0:T(8,128)(2,1)S(1)}, bf16[128,768]{1,0:T(8,128)(2,1)S(1)}, u32[]{:S(2)}, u32[]{:S(2)}) %collective-permute-start.10) | collective-permute-done | bytes 196640 | tf_op jit(solution)/shard_map/ppermute | solution.py:156
  87.6 6.1 %collective-permute-done.12 = bf16[128,768]{1,0:T(8,128)(2,1)S(1)} collective-permute-done((bf16[128,768]{1,0:T(8,128)(2,1)S(1)}, bf16[128,768]{1,0:T(8,128)(2,1)S(1)}, u32[]{:S(2)}, u32[]{:S(2)}) %collective-permute-start.12) | collective-permute-done | bytes 196640 | tf_op jit(solution)/shard_map/ppermute | solution.py:156
  107.2 12.5 %collective-permute-done.41 = bf16[128,656]{0,1:T(8,128)(2,1)S(1)} collective-permute-done((bf16[128,656]{0,1:T(8,128)(2,1)}, bf16[128,656]{0,1:T(8,128)(2,1)S(1)}, u32[]{:S(2)}, u32[]{:S(2)}) %collective-permute-start.41) | collective-permute-done | bytes 167968 | tf_op jit(solution)/shard_map/ppermute | solution.py:156
  123.7 4.7 %collective-permute-done.43 = bf16[128,656]{0,1:T(8,128)(2,1)S(1)} collective-permute-done((bf16[128,656]{0,1:T(8,128)(2,1)S(1)}, bf16[128,656]{0,1:T(8,128)(2,1)S(1)}, u32[]{:S(2)}, u32[]{:S(2)}) %collective-permute-start.43) | collective-permute-done | bytes 167968 | tf_op jit(solution)/shard_map/ppermute | solution.py:159
  132.7 8.0 %collective-permute-done.44 = bf16[128,656]{0,1:T(8,128)(2,1)S(1)} collective-permute-done((bf16[128,656]{0,1:T(8,128)(2,1)S(1)}, bf16[128,656]{0,1:T(8,128)(2,1)S(1)}, u32[]{:S(2)}, u32[]{:S(2)}) %collective-permute-start.44) | collective-permute-done | bytes 167968 | tf_op jit(solution)/shard_map/ppermute | solution.py:156
  141.7 3.7 %concatenate.139 = bf16[1024,656]{0,1:T(8,128)(2,1)} concatenate(bf16[32,656]{0,1:T(8,128)(2,1)} %copy-done.29, bf16[32,656]{0,1:T(8,128)(2,1)} %copy-done.28, bf16[32,656]{0,1:T(8,128)(2,1)} %copy-done.27, bf16[32,656]{0,1:T(8,128)(2,1)S(1)} %copy-done.26, bf16[128,656]{0,1:T(8,128)(2,1)} %copy-done.69, bf16[128,656]{0,1:T(8,128)(2,1)} %copy-done.72, ...), dimensions={0} | concatenate | bytes 2686976 | tf_op jit(solution)/shard_map/concatenate | solution.py:232
  151.3 3.6 collective-permute-done.32
  163.3 6.0 %concatenate.137 = bf16[1024,1312]{0,1:T(8,128)(2,1)} concatenate(bf16[32,1312]{0,1:T(8,128)(2,1)S(1)} %copy-done.10, bf16[32,1312]{0,1:T(8,128)(2,1)S(1)} %copy-done.8, bf16[32,1312]{0,1:T(8,128)(2,1)} %get-tuple-element.147, bf16[32,1312]{0,1:T(8,128)(2,1)S(1)} %copy-done.12, bf16[128,1312]{0,1:T(8,128)(2,1)} %collective-permute-done.29, bf16[128,1312]{0,1:T(8,128)(2,1)} %copy-done.53, ...), dimensions={0} | concatenate | bytes 5373952 | tf_op jit(solution)/shard_map/concatenate | solution.py:232
  170.4 3.7 %fusion.58 = f32[512,1312]{0,1:T(8,128)S(1)} fusion(bf16[1024,1312]{0,1:T(8,128)(2,1)} %concatenate.137, bf16[128,1024]{1,0:T(8,128)(2,1)S(1)} %get-tuple-element.200, bf16[128,1024]{1,0:T(8,128)(2,1)} %copy-done.60, bf16[128,1024]{1,0:T(8,128)(2,1)S(1)} %get-tuple-element.199, bf16[128,1024]{1,0:T(8,128)(2,1)} %copy-done.56), kind=kOutput, calls=%fused_computation.192 | convolution fusion | flops 1379926016 | bytes 6422528 | tf_op jit(solution)/shard_map/dot_general | solution.py:14
  184.1 9.8 %collective-permute-done.86 = bf16[128,656]{0,1:T(8,128)(2,1)S(1)} collective-permute-done((bf16[128,656]{0,1:T(8,128)(2,1)S(1)}, bf16[128,656]{0,1:T(8,128)(2,1)S(1)}, u32[]{:S(2)}, u32[]{:S(2)}) %collective-permute-start.86) | collective-permute-done | bytes 167968 | tf_op jit(solution)/shard_map/ppermute | solution.py:156
  197.0 4.3 %collective-permute-done.87 = bf16[128,656]{0,1:T(8,128)(2,1)S(1)} collective-permute-done((bf16[128,656]{0,1:T(8,128)(2,1)S(1)}, bf16[128,656]{0,1:T(8,128)(2,1)S(1)}, u32[]{:S(2)}, u32[]{:S(2)}) %collective-permute-start.87) | collective-permute-done | bytes 167968 | tf_op jit(solution)/shard_map/ppermute | solution.py:159
  202.0 6.5 %collective-permute-done.77 = bf16[128,1312]{0,1:T(8,128)(2,1)S(1)} collective-permute-done((bf16[128,1312]{0,1:T(8,128)(2,1)S(1)}, bf16[128,1312]{0,1:T(8,128)(2,1)S(1)}, u32[]{:S(2)}, u32[]{:S(2)}) %collective-permute-start.77) | collective-permute-done | bytes 335904 | tf_op jit(solution)/shard_map/ppermute | solution.py:159
  208.6 8.0 %collective-permute-done.85 = bf16[128,656]{0,1:T(8,128)(2,1)S(1)} collective-permute-done((bf16[128,656]{0,1:T(8,128)(2,1)S(1)}, bf16[128,656]{0,1:T(8,128)(2,1)S(1)}, u32[]{:S(2)}, u32[]{:S(2)}) %collective-permute-start.85) | collective-permute-done | bytes 167968 | tf_op jit(solution)/shard_map/ppermute | solution.py:159
  221.3 13.5 %collective-permute-done.84 = bf16[128,656]{0,1:T(8,128)(2,1)S(1)} collective-permute-done((bf16[128,656]{0,1:T(8,128)(2,1)S(1)}, bf16[128,656]{0,1:T(8,128)(2,1)S(1)}, u32[]{:S(2)}, u32[]{:S(2)}) %collective-permute-start.84) | collective-permute-done | bytes 167968 | tf_op jit(solution)/shard_map/ppermute | solution.py:159
  235.5 9.0 %collective-permute-done.78 = bf16[128,1312]{0,1:T(8,128)(2,1)S(1)} collective-permute-done((bf16[128,1312]{0,1:T(8,128)(2,1)S(1)}, bf16[128,1312]{0,1:T(8,128)(2,1)S(1)}, u32[]{:S(2)}, u32[]{:S(2)}) %collective-permute-start.78) | collective-permute-done | bytes 335904 | tf_op jit(solution)/shard_map/ppermute | solution.py:156
  265.5 10.1 %collective-permute-done.80 = bf16[128,1312]{0,1:T(8,128)(2,1)S(1)} collective-permute-done((bf16[128,1312]{0,1:T(8,128)(2,1)S(1)}, bf16[128,1312]{0,1:T(8,128)(2,1)S(1)}, u32[]{:S(2)}, u32[]{:S(2)}) %collective-permute-start.80) | collective-permute-done | bytes 335904 | tf_op jit(solution)/shard_map/ppermute | solution.py:156
  280.3 7.8 %collective-permute-done.82 = bf16[32,1312]{0,1:T(8,128)(2,1)S(1)} collective-permute-done((bf16[32,1312]{0,1:T(8,128)(2,1)S(1)}, bf16[32,1312]{0,1:T(8,128)(2,1)S(1)}, u32[]{:S(2)}, u32[]{:S(2)}) %collective-permute-start.82) | collective-permute-done | bytes 84000 | tf_op jit(solution)/shard_map/ppermute | solution.py:125
  288.1 3.1 collective-permute-done.81
  309.5 3.6 collective-permute-done.68
  320.5 4.2 %collective-permute-done.71 = bf16[32,1024]{1,0:T(8,128)(2,1)S(1)} collective-permute-done((bf16[32,1024]{1,0:T(8,128)(2,1)S(1)}, bf16[32,1024]{1,0:T(8,128)(2,1)S(1)}, u32[]{:S(2)}, u32[]{:S(2)}) %collective-permute-start.71) | collective-permute-done | bytes 65568 | tf_op jit(solution)/shard_map/ppermute | solution.py:156
  325.1 6.9 %collective-permute-done.58 = bf16[128,768]{1,0:T(8,128)(2,1)S(1)} collective-permute-done((bf16[128,768]{1,0:T(8,128)(2,1)S(1)}, bf16[128,768]{1,0:T(8,128)(2,1)S(1)}, u32[]{:S(2)}, u32[]{:S(2)}) %collective-permute-start.58) | collective-permute-done | bytes 196640 | tf_op jit(solution)/shard_map/ppermute | solution.py:156
  332.4 5.6 %collective-permute-done.72 = bf16[32,1024]{1,0:T(8,128)(2,1)S(1)} collective-permute-done((bf16[32,1024]{1,0:T(8,128)(2,1)S(1)}, bf16[32,1024]{1,0:T(8,128)(2,1)S(1)}, u32[]{:S(2)}, u32[]{:S(2)}) %collective-permute-start.72) | collective-permute-done | bytes 65568 | tf_op jit(solution)/shard_map/ppermute | solution.py:156
  338.9 3.4 collective-permute-start.61
  344.9 3.2 collective-permute-done.61
  350.3 5.4 %collective-permute-done.62 = bf16[128,768]{1,0:T(8,128)(2,1)S(1)} collective-permute-done((bf16[128,768]{1,0:T(8,128)(2,1)S(1)}, bf16[128,768]{1,0:T(8,128)(2,1)S(1)}, u32[]{:S(2)}, u32[]{:S(2)}) %collective-permute-start.62) | collective-permute-done | bytes 196640 | tf_op jit(solution)/shard_map/ppermute | solution.py:156
  355.8 3.4 collective-permute-start.64
  (601 shorter events, 177.2 us)
Async XLA Ops:
  5.4 39.6 %collective-permute-start.27 = (bf16[32,1312]{0,1:T(8,128)(2,1)}, bf16[32,1312]{0,1:T(8,128)(2,1)S(1)}, u32[]{:S(2)}, u32[]{:S(2)}) collective-permute-start(bf16[32,1312]{0,1:T(8,128)(2,1)} %get-tuple-element.164), channel_id=1, source_target_pairs={{0,2},{1,3},{2,0},{3,1},{4,6},{5,7},{6,4},{7,5},{8,10},{9,11},{10,... | collective-permute-start | bytes 251912 | tf_op jit(solution)/shard_map/ppermute | solution.py:125
  8.4 38.6 %collective-permute-start.26 = (bf16[32,1312]{0,1:T(8,128)(2,1)}, bf16[32,1312]{0,1:T(8,128)(2,1)S(1)}, u32[]{:S(2)}, u32[]{:S(2)}) collective-permute-start(bf16[32,1312]{0,1:T(8,128)(2,1)} %get-tuple-element.165), channel_id=1, source_target_pairs={{0,3},{1,2},{2,1},{3,0},{4,7},{5,6},{6,5},{7,4},{8,11},{9,10},{10,... | collective-permute-start | bytes 251912 | tf_op jit(solution)/shard_map/ppermute | solution.py:125
  8.4 16.1 %collective-permute-start = (s32[1,8]{1,0:T(1,128)S(1)}, s32[1,8]{1,0:T(1,128)S(1)}, u32[]{:S(2)}, u32[]{:S(2)}) collective-permute-start(s32[1,8]{1,0:T(1,128)S(1)} %copy-done.82), channel_id=1, source_target_pairs={{0,2},{1,3},{2,0},{3,1},{4,6},{5,7},{6,4},{7,5},{8,10},{9,11},{10,... | collective-permute-start | bytes 104 | tf_op jit(solution)/shard_map/ppermute | solution.py:125
  11.2 17.3 %collective-permute-start.37 = (bf16[32,656]{0,1:T(8,128)(2,1)}, bf16[32,656]{0,1:T(8,128)(2,1)}, u32[]{:S(2)}, u32[]{:S(2)}) collective-permute-start(bf16[32,656]{0,1:T(8,128)(2,1)} %get-tuple-element.181), channel_id=1, source_target_pairs={{0,2},{1,3},{2,0},{3,1},{4,6},{5,7},{6,4},{7,5},{8,10},{9,11},{10,... | collective-permute-start | bytes 125960 | tf_op jit(solution)/shard_map/ppermute | solution.py:125
  12.1 18.2 %collective-permute-start.36 = (bf16[32,656]{0,1:T(8,128)(2,1)}, bf16[32,656]{0,1:T(8,128)(2,1)}, u32[]{:S(2)}, u32[]{:S(2)}) collective-permute-start(bf16[32,656]{0,1:T(8,128)(2,1)} %get-tuple-element.182), channel_id=1, source_target_pairs={{0,3},{1,2},{2,1},{3,0},{4,7},{5,6},{6,5},{7,4},{8,11},{9,10},{10,... | collective-permute-start | bytes 125960 | tf_op jit(solution)/shard_map/ppermute | solution.py:125
  36.4 27.2 %collective-permute-start.2 = (bf16[128,1024]{1,0:T(8,128)(2,1)S(1)}, bf16[128,1024]{1,0:T(8,128)(2,1)S(1)}, u32[]{:S(2)}, u32[]{:S(2)}) collective-permute-start(bf16[128,1024]{1,0:T(8,128)(2,1)S(1)} %constant_dynamic-update-slice_fusion), channel_id=1, source_target_pairs={{0,2},{1,3},{2,0},{3,1},{4,6},{5,7},{6,4},{7,5},{8,10},{9,11},{10,... | collective-permute-start | bytes 786440 | tf_op jit(solution)/shard_map/ppermute | solution.py:125
  47.0 20.2 %collective-permute-start.8 = (bf16[128,768]{1,0:T(8,128)(2,1)S(1)}, bf16[128,768]{1,0:T(8,128)(2,1)S(1)}, u32[]{:S(2)}, u32[]{:S(2)}) collective-permute-start(bf16[128,768]{1,0:T(8,128)(2,1)S(1)} %pad_maximum_fusion.16), channel_id=1, source_target_pairs={{0,8},{4,12},{8,16},{12,20},{16,24},{20,28},{24,0},{28,4},{1,9},{5... | collective-permute-start | bytes 589832 | tf_op jit(solution)/shard_map/ppermute | solution.py:156
  48.0 17.3 %collective-permute-start.21 = (bf16[32,1024]{1,0:T(8,128)(2,1)S(1)}, bf16[32,1024]{1,0:T(8,128)(2,1)S(1)}, u32[]{:S(2)}, u32[]{:S(2)}) collective-permute-start(bf16[32,1024]{1,0:T(8,128)(2,1)S(1)} %collective-permute-done.14), channel_id=1, source_target_pairs={{0,4},{4,0},{8,12},{12,8},{16,20},{20,16},{24,28},{28,24},{1,5},{5... | collective-permute-start | bytes 196616 | tf_op jit(solution)/shard_map/ppermute | solution.py:159
  65.3 63.2 %collective-permute-start.48 = (bf16[128,1024]{1,0:T(8,128)(2,1)}, bf16[128,1024]{1,0:T(8,128)(2,1)}, u32[]{:S(2)}, u32[]{:S(2)}) collective-permute-start(bf16[128,1024]{1,0:T(8,128)(2,1)} %constant_dynamic-update-slice_fusion.43), channel_id=1, source_target_pairs={{0,2},{1,3},{2,0},{3,1},{4,6},{5,7},{6,4},{7,5},{8,10},{9,11},{10,... | collective-permute-start | bytes 786440 | tf_op jit(solution)/shard_map/ppermute | solution.py:125
  66.4 38.3 %collective-permute-start.40 = (bf16[128,656]{0,1:T(8,128)(2,1)}, bf16[128,656]{0,1:T(8,128)(2,1)}, u32[]{:S(2)}, u32[]{:S(2)}) collective-permute-start(bf16[128,656]{0,1:T(8,128)(2,1)} %pad_maximum_fusion.21), channel_id=1, source_target_pairs={{0,8},{4,12},{8,16},{12,20},{16,24},{20,28},{24,0},{28,4},{1,9},{5... | collective-permute-start | bytes 503816 | tf_op jit(solution)/shard_map/ppermute | solution.py:156
  71.3 15.5 %collective-permute-start.3 = (bf16[2,128,1024]{2,1,0:T(8,128)(2,1)S(1)}, bf16[2,128,1024]{2,1,0:T(8,128)(2,1)S(1)}, u32[]{:S(2)}, u32[]{:S(2)}) collective-permute-start(bf16[2,128,1024]{2,1,0:T(8,128)(2,1)S(1)} %pad_maximum_fusion.7), channel_id=1, source_target_pairs={{0,1},{1,0},{2,3},{3,2},{4,5},{5,4},{6,7},{7,6},{8,9},{9,8},{10,11... | collective-permute-start | bytes 1572872 | tf_op jit(solution)/shard_map/ppermute | solution.py:125
  102.4 17.3 %collective-permute-start.22 = (bf16[2,128,1024]{2,1,0:T(8,128)(2,1)S(1)}, bf16[2,128,1024]{2,1,0:T(8,128)(2,1)S(1)}, u32[]{:S(2)}, u32[]{:S(2)}) collective-permute-start(bf16[2,128,1024]{2,1,0:T(8,128)(2,1)S(1)} %pad_maximum_fusion.8), channel_id=1, source_target_pairs={{0,1},{1,0},{2,3},{3,2},{4,5},{5,4},{6,7},{7,6},{8,9},{9,8},{10,11... | collective-permute-start | bytes 1572872 | tf_op jit(solution)/shard_map/ppermute | solution.py:125
  104.6 19.1 %collective-permute-start.30 = (bf16[128,1312]{0,1:T(8,128)(2,1)}, bf16[128,1312]{0,1:T(8,128)(2,1)}, u32[]{:S(2)}, u32[]{:S(2)}) collective-permute-start(bf16[128,1312]{0,1:T(8,128)(2,1)} %pad_maximum_fusion.15), channel_id=1, source_target_pairs={{0,8},{4,12},{8,16},{12,20},{16,24},{20,28},{24,0},{28,4},{1,9},{5... | collective-permute-start | bytes 1007624 | tf_op jit(solution)/shard_map/ppermute | solution.py:156
  105.1 18.5 %collective-permute-start.39 = (bf16[128,656]{0,1:T(8,128)(2,1)}, bf16[128,656]{0,1:T(8,128)(2,1)S(1)}, u32[]{:S(2)}, u32[]{:S(2)}) collective-permute-start(bf16[128,656]{0,1:T(8,128)(2,1)} %pad_maximum_fusion.21), channel_id=1, source_target_pairs={{0,4},{4,0},{8,12},{12,8},{16,20},{20,16},{24,28},{28,24},{1,5},{5... | collective-permute-start | bytes 503816 | tf_op jit(solution)/shard_map/ppermute | solution.py:159
  123.7 21.7 %collective-permute-start.31 = (bf16[128,1312]{0,1:T(8,128)(2,1)}, bf16[128,1312]{0,1:T(8,128)(2,1)}, u32[]{:S(2)}, u32[]{:S(2)}) collective-permute-start(bf16[128,1312]{0,1:T(8,128)(2,1)} %collective-permute-done.30), channel_id=1, source_target_pairs={{0,8},{4,12},{8,16},{12,20},{16,24},{20,28},{24,0},{28,4},{1,9},{5... | collective-permute-start | bytes 1007624 | tf_op jit(solution)/shard_map/ppermute | solution.py:156
  128.5 17.2 %collective-permute-start.23 = (bf16[128,1024]{1,0:T(8,128)(2,1)}, bf16[128,1024]{1,0:T(8,128)(2,1)S(1)}, u32[]{:S(2)}, u32[]{:S(2)}) collective-permute-start(bf16[128,1024]{1,0:T(8,128)(2,1)} %fusion.34), channel_id=1, source_target_pairs={{0,2},{1,3},{2,0},{3,1},{4,6},{5,7},{6,4},{7,5},{8,10},{9,11},{10,... | collective-permute-start | bytes 786440 | tf_op jit(solution)/shard_map/ppermute | solution.py:125
  131.3 30.2 %collective-permute-start.29 = (bf16[128,1312]{0,1:T(8,128)(2,1)}, bf16[128,1312]{0,1:T(8,128)(2,1)}, u32[]{:S(2)}, u32[]{:S(2)}) collective-permute-start(bf16[128,1312]{0,1:T(8,128)(2,1)} %pad_maximum_fusion.15), channel_id=1, source_target_pairs={{0,4},{4,0},{8,12},{12,8},{16,20},{20,16},{24,28},{28,24},{1,5},{5... | collective-permute-start | bytes 1007624 | tf_op jit(solution)/shard_map/ppermute | solution.py:159
  132.7 17.1 %collective-permute-start.49 = (bf16[2,128,1024]{2,1,0:T(8,128)(2,1)}, bf16[2,128,1024]{2,1,0:T(8,128)(2,1)}, u32[]{:S(2)}, u32[]{:S(2)}) collective-permute-start(bf16[2,128,1024]{2,1,0:T(8,128)(2,1)} %pad_maximum_fusion.11), channel_id=1, source_target_pairs={{0,1},{1,0},{2,3},{3,2},{4,5},{5,4},{6,7},{7,6},{8,9},{9,8},{10,11... | collective-permute-start | bytes 1572872 | tf_op jit(solution)/shard_map/ppermute | solution.py:125
  141.3 20.2 %collective-permute-start.35 = (bf16[128,1312]{0,1:T(8,128)(2,1)}, bf16[128,1312]{0,1:T(8,128)(2,1)}, u32[]{:S(2)}, u32[]{:S(2)}) collective-permute-start(bf16[128,1312]{0,1:T(8,128)(2,1)} %collective-permute-done.30), channel_id=1, source_target_pairs={{0,4},{4,0},{8,12},{12,8},{16,20},{20,16},{24,28},{28,24},{1,5},{5... | collective-permute-start | bytes 1007624 | tf_op jit(solution)/shard_map/ppermute | solution.py:159
  146.4 15.1 %collective-permute-start.34 = (bf16[128,1312]{0,1:T(8,128)(2,1)}, bf16[128,1312]{0,1:T(8,128)(2,1)}, u32[]{:S(2)}, u32[]{:S(2)}) collective-permute-start(bf16[128,1312]{0,1:T(8,128)(2,1)} %collective-permute-done.31), channel_id=1, source_target_pairs={{0,4},{4,0},{8,12},{12,8},{16,20},{20,16},{24,28},{28,24},{1,5},{5... | collective-permute-start | bytes 1007624 | tf_op jit(solution)/shard_map/ppermute | solution.py:159
  177.8 40.9 %collective-permute-start.50 = (bf16[2,128,1024]{2,1,0:T(8,128)(2,1)S(1)}, bf16[2,128,1024]{2,1,0:T(8,128)(2,1)S(1)}, u32[]{:S(2)}, u32[]{:S(2)}) collective-permute-start(bf16[2,128,1024]{2,1,0:T(8,128)(2,1)S(1)} %pad_maximum_fusion.12), channel_id=1, source_target_pairs={{0,1},{1,0},{2,3},{3,2},{4,5},{5,4},{6,7},{7,6},{8,9},{9,8},{10,11... | collective-permute-start | bytes 1572872 | tf_op jit(solution)/shard_map/ppermute | solution.py:125
  196.2 24.1 %collective-permute-start.46 = (bf16[2,128,1024]{2,1,0:T(8,128)(2,1)S(1)}, bf16[2,128,1024]{2,1,0:T(8,128)(2,1)S(1)}, u32[]{:S(2)}, u32[]{:S(2)}) collective-permute-start(bf16[2,128,1024]{2,1,0:T(8,128)(2,1)S(1)} %pad_maximum_fusion.10), channel_id=1, source_target_pairs={{0,1},{1,0},{2,3},{3,2},{4,5},{5,4},{6,7},{7,6},{8,9},{9,8},{10,11... | collective-permute-start | bytes 1572872 | tf_op jit(solution)/shard_map/ppermute | solution.py:125
  196.3 39.2 %collective-permute-start.76 = (bf16[128,1312]{0,1:T(8,128)(2,1)S(1)}, bf16[128,1312]{0,1:T(8,128)(2,1)S(1)}, u32[]{:S(2)}, u32[]{:S(2)}) collective-permute-start(bf16[128,1312]{0,1:T(8,128)(2,1)S(1)} %get-tuple-element.144), channel_id=1, source_target_pairs={{0,4},{4,0},{8,12},{12,8},{16,20},{20,16},{24,28},{28,24},{1,5},{5... | collective-permute-start | bytes 1007624 | tf_op jit(solution)/shard_map/ppermute | solution.py:159
  201.2 15.3 %collective-permute-start.85 = (bf16[128,656]{0,1:T(8,128)(2,1)S(1)}, bf16[128,656]{0,1:T(8,128)(2,1)S(1)}, u32[]{:S(2)}, u32[]{:S(2)}) collective-permute-start(bf16[128,656]{0,1:T(8,128)(2,1)S(1)} %get-tuple-element.162), channel_id=1, source_target_pairs={{0,4},{4,0},{8,12},{12,8},{16,20},{20,16},{24,28},{28,24},{1,5},{5... | collective-permute-start | bytes 503816 | tf_op jit(solution)/shard_map/ppermute | solution.py:159
  216.6 46.2 %collective-permute-start.75 = (bf16[128,1312]{0,1:T(8,128)(2,1)}, bf16[128,1312]{0,1:T(8,128)(2,1)}, u32[]{:S(2)}, u32[]{:S(2)}) collective-permute-start(bf16[128,1312]{0,1:T(8,128)(2,1)} %get-tuple-element.145), channel_id=1, source_target_pairs={{0,4},{4,0},{8,12},{12,8},{16,20},{20,16},{24,28},{28,24},{1,5},{5... | collective-permute-start | bytes 1007624 | tf_op jit(solution)/shard_map/ppermute | solution.py:159
  217.2 48.3 %collective-permute-start.74 = (bf16[128,1312]{0,1:T(8,128)(2,1)}, bf16[128,1312]{0,1:T(8,128)(2,1)}, u32[]{:S(2)}, u32[]{:S(2)}) collective-permute-start(bf16[128,1312]{0,1:T(8,128)(2,1)} %get-tuple-element.142), channel_id=1, source_target_pairs={{0,4},{4,0},{8,12},{12,8},{16,20},{20,16},{24,28},{28,24},{1,5},{5... | collective-permute-start | bytes 1007624 | tf_op jit(solution)/shard_map/ppermute | solution.py:159
  218.7 16.1 %collective-permute-start.84 = (bf16[128,656]{0,1:T(8,128)(2,1)S(1)}, bf16[128,656]{0,1:T(8,128)(2,1)S(1)}, u32[]{:S(2)}, u32[]{:S(2)}) collective-permute-start(bf16[128,656]{0,1:T(8,128)(2,1)S(1)} %get-tuple-element.159), channel_id=1, source_target_pairs={{0,4},{4,0},{8,12},{12,8},{16,20},{20,16},{24,28},{28,24},{1,5},{5... | collective-permute-start | bytes 503816 | tf_op jit(solution)/shard_map/ppermute | solution.py:159
  247.5 15.3 %collective-permute-start.79 = (bf16[128,1312]{0,1:T(8,128)(2,1)}, bf16[128,1312]{0,1:T(8,128)(2,1)}, u32[]{:S(2)}, u32[]{:S(2)}) collective-permute-start(bf16[128,1312]{0,1:T(8,128)(2,1)} %add_convert_fusion.2), channel_id=1, source_target_pairs={{0,8},{4,12},{8,16},{12,20},{16,24},{20,28},{24,0},{28,4},{1,9},{5... | collective-permute-start | bytes 1007624 | tf_op jit(solution)/shard_map/ppermute | solution.py:156
  280.3 15.5 %collective-permute-start.53 = (bf16[2,128,1024]{2,1,0:T(8,128)(2,1)}, bf16[2,128,1024]{2,1,0:T(8,128)(2,1)}, u32[]{:S(2)}, u32[]{:S(2)}) collective-permute-start(bf16[2,128,1024]{2,1,0:T(8,128)(2,1)} %pad_maximum_fusion.13), channel_id=1, source_target_pairs={{0,1},{1,0},{2,3},{3,2},{4,5},{5,4},{6,7},{7,6},{8,9},{9,8},{10,11... | collective-permute-start | bytes 1572872 | tf_op jit(solution)/shard_map/ppermute | solution.py:125
  308.2 34.1 %collective-permute-start.54 = (bf16[2,128,1024]{2,1,0:T(8,128)(2,1)S(1)}, bf16[2,128,1024]{2,1,0:T(8,128)(2,1)S(1)}, u32[]{:S(2)}, u32[]{:S(2)}) collective-permute-start(bf16[2,128,1024]{2,1,0:T(8,128)(2,1)S(1)} %pad_maximum_fusion.14), channel_id=1, source_target_pairs={{0,1},{1,0},{2,3},{3,2},{4,5},{5,4},{6,7},{7,6},{8,9},{9,8},{10,11... | collective-permute-start | bytes 1572872 | tf_op jit(solution)/shard_map/ppermute | solution.py:125
  318.0 20.8 %collective-permute-start.60 = (bf16[128,768]{1,0:T(8,128)(2,1)S(1)}, bf16[128,768]{1,0:T(8,128)(2,1)S(1)}, u32[]{:S(2)}, u32[]{:S(2)}) collective-permute-start(bf16[128,768]{1,0:T(8,128)(2,1)S(1)} %get-tuple-element.154), channel_id=1, source_target_pairs={{0,8},{4,12},{8,16},{12,20},{16,24},{20,28},{24,0},{28,4},{1,9},{5... | collective-permute-start | bytes 589832 | tf_op jit(solution)/shard_map/ppermute | solution.py:156
  319.8 25.1 %collective-permute-start.57 = (bf16[128,768]{1,0:T(8,128)(2,1)S(1)}, bf16[128,768]{1,0:T(8,128)(2,1)S(1)}, u32[]{:S(2)}, u32[]{:S(2)}) collective-permute-start(bf16[128,768]{1,0:T(8,128)(2,1)S(1)} %get-tuple-element.156), channel_id=1, source_target_pairs={{0,4},{4,0},{8,12},{12,8},{16,20},{20,16},{24,28},{28,24},{1,5},{5... | collective-permute-start | bytes 589832 | tf_op jit(solution)/shard_map/ppermute | solution.py:159
  (156 other events, 1258.6 us)

commit v2 on v1

--- a/solution.py
+++ b/solution.py
@@ -111,13 +111,8 @@
     return (grad_query, grad_key, grad_value)
 
 
-def xor_order(items, index):
-    bit = 1
-    while bit < len(items):
-        flip = (index & bit) != 0
-        items = [jnp.where(flip, items[k ^ bit], items[k]) for k in range(len(items))]
-        bit *= 2
-    return items
+def after(value, *others):
+    return lax.optimization_barrier((value, *others))[0]
 
 
 def swap(value, distance):
@@ -141,10 +136,8 @@
     return kept + swap(sent, 2).astype(jnp.float32)
 
 
-def rep_exchange(pieces, rep):
-    placed = xor_order(pieces, rep)
-    received = [placed[0]] + [swap(placed[k], k) for k in range(1, len(placed))]
-    return xor_order(received, rep)
+def rep_exchange(pieces):
+    return lax.all_to_all(jnp.stack(pieces), "rep", 0, 0, tiled=True)
 
 
 class Ring:
@@ -154,6 +147,9 @@
 
     def up(self, value):
         return lax.ppermute(value, "fsdp", [(k, (k + 2) % 8) for k in range(8)])
+
+    def down(self, value):
+        return lax.ppermute(value, "fsdp", [(k, (k - 2) % 8) for k in range(8)])
 
     def over(self, value):
         return lax.ppermute(value, "fsdp", [(k, k ^ 1) for k in range(8)])
@@ -164,9 +160,10 @@
         for bit in (1, 2):
             turn = (self.z & bit) != 0
             blocks = [jnp.where(turn, blocks[(k + 2 * bit) % 8], blocks[k]) for k in range(8)]
-        return blocks
+        return [blocks[2 * ((p + 1) % 4) + i] for i in range(2) for p in range(4)]
 
     def absolute(self, blocks):
+        blocks = [blocks[4 * i + (j - 1) % 4] for j in range(4) for i in range(2)]
         flip = self.x == 1
         blocks = [jnp.where(flip, blocks[k ^ 1], blocks[k]) for k in range(8)]
         for bit in (1, 2):
@@ -174,27 +171,31 @@
             blocks = [jnp.where(turn, blocks[(k - 2 * bit) % 8], blocks[k]) for k in range(8)]
         return blocks
 
-    def gather(self, own, more_z):
-        first = self.up(own)
-        second = self.up(first)
-        third = self.up(second)
-        over_own, over_first, over_second = self.over(own), self.over(first), self.over(second)
-        over_third = self.up(over_second) if more_z else self.over(third)
-        return [own, over_own, third, over_third, second, over_second, first, over_first]
-
-    def scatter(self, blocks, more_z):
+    def gather(self, own, *others):
+        own = after(own, *others) if others else own
+        third, first, own_x = self.up(own), self.down(own), self.over(own)
+        second = self.up(third)
+        first_x, third_x, second_x = self.over(first), self.over(third), self.over(second)
+        return [first, second, third, own, first_x, second_x, third_x, own_x], (first, third)
+
+    def scatter(self, term, parts, middle=(), end=()):
         wide = lambda value: value.astype(jnp.float32)
         low = lambda value: value.astype(jnp.bfloat16)
-        blocks = [low(block) for block in blocks]
-        total = wide(blocks[6])
-        if more_z:
-            blocks[5] = low(wide(blocks[5]) + wide(self.up(blocks[7])))
-        else:
-            total = total + wide(self.over(blocks[7]))
-        for step in (2, 1, 0):
-            here = wide(blocks[2 * step]) + wide(self.over(blocks[2 * step + 1]))
-            total = here + wide(self.up(low(total)))
-        return total
+        term = low(term)
+        size = term.shape[0] // 8
+        received = [self.over(piece) for piece in split_rows(term[4 * size :], parts)]
+        received = lax.optimization_barrier((*received, *middle))[:parts]
+        sums = [
+            wide(mine) + wide(its)
+            for mine, its in zip(
+                split_rows(term[: 4 * size], 4),
+                [piece for whole in received for piece in split_rows(whole, 4 // parts)],
+            )
+        ]
+        second, third = self.up(low(sums[1])), self.down(low(sums[2]))
+        first = self.up(low(sums[0] + wide(second)))
+        first, third = lax.optimization_barrier((first, third, *end))[:2]
+        return sums[3] + wide(first) + wide(third)
 
 
 class Plain:
@@ -206,12 +207,12 @@
 
     absolute = relative
 
-    def gather(self, own, more_z):
+    def gather(self, own, *others):
         whole = lax.all_gather(own, "fsdp", axis=0)
-        return [whole[k] for k in range(self.count)]
-
-    def scatter(self, blocks, more_z):
-        return lax.psum_scatter(jnp.stack(blocks), "fsdp", scatter_dimension=0, tiled=False)
+        return [whole[k] for k in range(self.count)], ()
+
+    def scatter(self, term, parts, middle=(), end=()):
+        return lax.psum_scatter(term, "fsdp", scatter_dimension=0, tiled=True)
 
 
 def split_columns(value, count):
@@ -245,7 +246,6 @@
 ):
     row_count, width = tokens.shape
     fsdp_count, rep_count = lax.axis_size("fsdp"), lax.axis_size("rep")
-    rep = lax.axis_index("rep")
     ring = Ring() if fsdp_count == 8 else Plain()
     hidden = w_in.shape[1] // 2
     head_count = width // HEAD_DIM // rep_count
@@ -262,25 +262,35 @@
     gain_mlp = feedforward_norm_gain.astype(wide)[:, None]
     qkv_parts = split_columns((w_qkv.astype(wide) * gain_attn).astype(low), 3 * rep_count)
     in_parts = split_columns((w_in.astype(wide) * gain_mlp).astype(low), 2 * rep_count)
-    qkv_own = rows(
-        rep_exchange([columns(qkv_parts[k::rep_count]) for k in range(rep_count)], rep)
-    )
     order = [
         (k, (k % fsdp_count) * rep_count + k // fsdp_count) for k in range(fsdp_count * rep_count)
     ]
     attn_own = lax.ppermute(w_attn_out, AXES, order)
-    in_own = rows(rep_exchange([columns(in_parts[k::rep_count]) for k in range(rep_count)], rep))
-    out_own = rows(rep_exchange(split_columns(w_out, rep_count), rep))
+    qkv_own = rep_exchange([columns(qkv_parts[k::rep_count]) for k in range(rep_count)])
+    block = rep_count * w_qkv.shape[0]
+    first_own = columns(
+        [qkv_own.reshape(block, 3 * own_width), rows(split_columns(attn_own, rep_count))]
+    )
+    in_own = rep_exchange([columns(in_parts[k::rep_count]) for k in range(rep_count)])
+    out_own = rep_exchange(split_columns(w_out, rep_count))
 
     x_own = relative(tokens)
     x_low = rep_gather(x_own)
     cot = rep_gather(relative(cotangent))
     lengths = rep_gather(seq_lengths)
 
-    qkv = rows(ring.gather(qkv_own, True))
-    attn = relative(rows(ring.absolute(ring.gather(attn_own, True))))
-    w_up = rows(ring.gather(in_own, False))
-    w_down = rows(ring.gather(out_own, True))
+    first_blocks, first_in = ring.gather(first_own)
+    in_blocks, in_in = ring.gather(in_own.reshape(block, -1), *first_in)
+    out_blocks, _ = ring.gather(out_own.reshape(block, -1), *in_in)
+    qkv = rows([piece[:, : 3 * own_width] for piece in first_blocks])
+    attn = relative(
+        rows(
+            ring.absolute(
+                [columns(split_rows(piece[:, 3 * own_width :], rep_count)) for piece in first_blocks]
+            )
+        )
+    )
+    w_up, w_down = rows(in_blocks), rows(out_blocks)
 
     sequence_segment, positions, valid = jax.vmap(
         lambda row_lengths: layout(row_lengths, row_count)
@@ -309,14 +319,12 @@
     grad_out = jnp.where(live, cot, jnp.zeros((), low))
 
     term_out = matmul_left_t(grad_out, mixed)
-    sum_out = ring.scatter(split_rows(term_out, fsdp_count), True)
-
     slope = phi + gate * jnp.exp(-0.5 * gate * gate) * 0.3989422804014327
     grad_mixed = matmul(grad_out, w_down)
     grad_inner = columns([grad_mixed * up * slope, grad_mixed * activation]).astype(low)
-    scaled_mlp = rep_scatter(matmul_right_t(grad_inner, w_up))
+    partial_mlp = matmul_right_t(grad_inner, w_up)
+    scaled_mlp = rep_scatter(partial_mlp)
     term_in = matmul_left_t(normed_mlp, grad_inner)
-    sum_in = ring.scatter(split_rows(term_in, fsdp_count), False)
     grad_hidden = grad_out[:row_count].astype(wide) + norm_backward_pass(
         scaled_mlp, standard_mlp, inverse_mlp
     )
@@ -339,22 +347,25 @@
     grad_packed = jnp.stack([grad_query, grad_key, grad_value], axis=2)
     grad_packed = grad_packed.reshape(rep_count * row_count, 3 * own_width).astype(low)
     term_qkv = matmul_left_t(normed, grad_packed)
-    sum_qkv = ring.scatter(split_rows(term_qkv, fsdp_count), True)
     term_attn = absolute(matmul_left_t(attended, grad_low).astype(low))
-    sum_attn = ring.scatter(ring.relative(split_rows(term_attn, fsdp_count)), True)
+    term_attn = rows(ring.relative(split_rows(term_attn, fsdp_count)))
+    sum_out = ring.scatter(term_out, 1, (partial_mlp,), (grad_low,))
+    sum_in = ring.scatter(term_in, 2, (grad_low,), (grad_packed,))
+    sum_attn = ring.scatter(term_attn, 1, (grad_packed,))
+    sum_qkv = ring.scatter(term_qkv, 2)
     scaled_attn = rep_scatter(matmul_right_t(grad_packed, qkv))
     block_input_gradient = grad_hidden + norm_backward_pass(
         scaled_attn, standard[:row_count], inverse[:row_count]
     )
 
-    back_qkv = rep_exchange(split_rows(sum_qkv.astype(low), rep_count), rep)
-    back_in = rep_exchange(split_rows(sum_in.astype(low), rep_count), rep)
-    back_out = rep_exchange(split_rows(sum_out.astype(low), rep_count), rep)
+    back_out = rep_exchange(split_rows(sum_out.astype(low), rep_count))
+    back_in = rep_exchange(split_rows(sum_in.astype(low), rep_count))
+    back_qkv = rep_exchange(split_rows(sum_qkv.astype(low), rep_count))
     unit_qkv = columns(
-        [split_columns(piece, 3)[part] for part in range(3) for piece in back_qkv]
+        [split_columns(piece, 3)[part] for part in range(3) for piece in list(back_qkv)]
     ).astype(wide)
     unit_in = columns(
-        [split_columns(piece, 2)[part] for part in range(2) for piece in back_in]
+        [split_columns(piece, 2)[part] for part in range(2) for piece in list(back_in)]
     ).astype(wide)
     grad_w_attn_out = lax.ppermute(
         sum_attn.astype(low), AXES, [(there, here) for here, there in order]
@@ -367,7 +378,7 @@
         grad_w_attn_out,
         jnp.sum(unit_in * w_in.astype(wide), axis=1),
         unit_in * gain_mlp,
-        columns(back_out).astype(wide),
+        columns(list(back_out)).astype(wide),
     )
 
 

time: 372 us -> 311 us (0.84); the launches traced: 365 us -> 308 us
  waiting for transfers between devices: 169 us -> 101 us
  starting transfers between devices: 75.3 us -> 99 us
  other arithmetic: 53.7 us -> 48.4 us
    ppermute x30 -> x14, waiting for transfers between devices: 105 us -> 35.1 us  [up(): return lax.ppermute(value, 'fsdp', [(k, (k + 2) % 8) for k in range(8)])]
    all_to_all x0 -> x6, starting transfers between devices: none -> 25.3 us  [rep_exchange(): return lax.all_to_all(jnp.stack(pieces), 'rep', 0, 0, tiled=True)]
    ppermute x0 -> x7, starting transfers between devices: none -> 20.8 us  [down(): return lax.ppermute(value, 'fsdp', [(k, (k - 2) % 8) for k in range(8)])]
    ppermute x30 -> x14, starting transfers between devices: 25.6 us -> 11.9 us  [up(): return lax.ppermute(value, 'fsdp', [(k, (k + 2) % 8) for k in range(8)])]
    ppermute x36 -> x18, starting transfers between devices: 24.6 us -> 14.7 us  [swap(): return lax.ppermute(value, 'rep', [(k, k ^ distance) for k in range(count)])]
    select_n x15 -> x0, other arithmetic: 9.27 us -> none  [xor_order(): jnp.where(flip, items[k ^ bit], items[k])]
    convert_element_type x12 -> x9, other arithmetic: 2.88 us -> 11.3 us  [scatter(): low = lambda value: value.astype(jnp.bfloat16)]
    another operation x0 -> x15, local copies, waits for them, and re-layouts: none -> 8.33 us  [the longest x12 8.27 us: rep_exchange(): return lax.all_to_all(jnp.stack(pieces), 'rep', 0, 0, tiled=True)]
  transfers between devices with their start and end apart: 94 -> 65, of which waited for: 37 -> 19; matrix products, arithmetic and copies ran while one was open for 23% -> 29% of each run, Pallas kernels for 0% -> 0%
where the time goes in v2:
time: 311 us; the launch traced here: 308 us
  waiting for transfers between devices  101 us (32%)
  starting transfers between devices  99 us (32%)
  other arithmetic  48.4 us (16%)
  local copies, waits for them, and re-layouts  40.6 us (13%)
  matrix products  16.6 us (5%)
    ppermute x18, waiting for transfers between devices, over(): return lax.ppermute(value, 'fsdp', [(k, k ^ 1) for k in range(8)])  45.4 us
    ppermute x14, waiting for transfers between devices, up(): return lax.ppermute(value, 'fsdp', [(k, (k + 2) % 8) for k in range(8)])  35.1 us
    all_to_all x6, starting transfers between devices, rep_exchange(): return lax.all_to_all(jnp.stack(pieces), 'rep', 0, 0, tiled=True)  25.3 us
    ppermute x18, starting transfers between devices, over(): return lax.ppermute(value, 'fsdp', [(k, k ^ 1) for k in range(8)])  24 us
    ppermute x7, starting transfers between devices, down(): return lax.ppermute(value, 'fsdp', [(k, (k - 2) % 8) for k in range(8)])  20.8 us
    unnamed x156, local copies, waits for them, and re-layouts  18.7 us
    ppermute x18, waiting for transfers between devices, swap(): return lax.ppermute(value, 'rep', [(k, k ^ distance) for k in range(count)])  15.8 us
    ppermute x18, starting transfers between devices, swap(): return lax.ppermute(value, 'rep', [(k, k ^ distance) for k in range(count)])  14.7 us
  transfers between devices with their start and end apart: 65, of which 19 were waited for; matrix products, arithmetic and copies ran while one was open for 29% of the time, Pallas kernels for 0%

profile of v2, /device:TPU:0, one launch (start us, length us, event | category | flops | bytes accessed | tf_op | source)
XLA Modules:
  0.0 307.9 jit_solution(12069537380923323444)
XLA Ops:
  4.8 7.0 %all-to-all-start = ((bf16[4,32,768]{2,1,0:T(8,128)(2,1)}), bf16[4,32,768]{2,1,0:T(8,128)(2,1)S(1)}, u32[]{:S(2)}, u32[]{:S(2)}) async-start(bf16[4,32,768]{2,1,0:T(8,128)(2,1)} %pad_maximum_fusion.18), calls=%async_computation | async-start | bytes 393216 | tf_op jit(solution)/shard_map/all_to_all | solution.py:140
  12.1 2.1 collective-permute-start.2
  14.6 2.0 collective-permute-start.32
  18.8 4.5 %collective-permute-done = s32[1,8]{1,0:T(1,128)S(1)} collective-permute-done((s32[1,8]{1,0:T(1,128)S(1)}, s32[1,8]{1,0:T(1,128)S(1)}, u32[]{:S(2)}, u32[]{:S(2)}) %collective-permute-start) | collective-permute-done | bytes 64 | tf_op jit(solution)/shard_map/ppermute | solution.py:120
  26.9 4.1 %all-to-all-start.1 = ((bf16[4,32,1312]{2,1,0:T(8,128)(2,1)}), bf16[4,32,1312]{2,1,0:T(8,128)(2,1)}, u32[]{:S(2)}, u32[]{:S(2)}) async-start(bf16[4,32,1312]{2,1,0:T(8,128)(2,1)} %pad_maximum_fusion.15), calls=%async_computation.1 | async-start | bytes 720896 | tf_op jit(solution)/shard_map/all_to_all | solution.py:140
  31.7 2.5 collective-permute-start.5
  35.0 2.3 collective-permute-start.11
  38.8 4.0 %all-to-all-start.2 = ((bf16[4,32,656]{2,1,0:T(8,128)(2,1)}), bf16[4,32,656]{2,1,0:T(8,128)(2,1)}, u32[]{:S(2)}, u32[]{:S(2)}) async-start(bf16[4,32,656]{2,1,0:T(8,128)(2,1)} %pad_maximum_fusion.19), calls=%async_computation.2 | async-start | bytes 393216 | tf_op jit(solution)/shard_map/all_to_all | solution.py:140
  42.8 5.0 %collective-permute-done.6 = bf16[128,1024]{1,0:T(8,128)(2,1)S(1)} collective-permute-done((bf16[128,1024]{1,0:T(8,128)(2,1)}, bf16[128,1024]{1,0:T(8,128)(2,1)S(1)}, u32[]{:S(2)}, u32[]{:S(2)}) %collective-permute-start.6) | collective-permute-done | bytes 262176 | tf_op jit(solution)/shard_map/ppermute | solution.py:149
  53.3 18.5 %collective-permute-done.7 = bf16[128,1024]{1,0:T(8,128)(2,1)} collective-permute-done((bf16[128,1024]{1,0:T(8,128)(2,1)S(1)}, bf16[128,1024]{1,0:T(8,128)(2,1)}, u32[]{:S(2)}, u32[]{:S(2)}) %collective-permute-start.7) | collective-permute-done | bytes 262176 | tf_op jit(solution)/shard_map/ppermute | solution.py:149
  74.7 4.4 %collective-permute-done.8 = bf16[128,1024]{1,0:T(8,128)(2,1)S(1)} collective-permute-done((bf16[128,1024]{1,0:T(8,128)(2,1)}, bf16[128,1024]{1,0:T(8,128)(2,1)S(1)}, u32[]{:S(2)}, u32[]{:S(2)}) %collective-permute-start.8) | collective-permute-done | bytes 262176 | tf_op jit(solution)/shard_map/ppermute | solution.py:155
  81.8 3.9 %collective-permute-done.10 = bf16[128,1024]{1,0:T(8,128)(2,1)S(1)} collective-permute-done((bf16[128,1024]{1,0:T(8,128)(2,1)S(1)}, bf16[128,1024]{1,0:T(8,128)(2,1)S(1)}, u32[]{:S(2)}, u32[]{:S(2)}) %collective-permute-start.10) | collective-permute-done | bytes 262176 | tf_op jit(solution)/shard_map/ppermute | solution.py:155
  102.0 2.5 collective-permute-start.19
  106.7 2.3 fusion.43
  119.2 4.6 %collective-permute-done.25 = bf16[128,656]{1,0:T(8,128)(2,1)S(1)} collective-permute-done((bf16[128,656]{1,0:T(8,128)(2,1)}, bf16[128,656]{1,0:T(8,128)(2,1)S(1)}, u32[]{:S(2)}, u32[]{:S(2)}) %collective-permute-start.25) | collective-permute-done | bytes 167968 | tf_op jit(solution)/shard_map/ppermute | solution.py:149
  126.8 2.1 collective-permute-start.28
  132.2 6.7 %collective-permute-done.27 = bf16[128,656]{1,0:T(8,128)(2,1)S(1)} collective-permute-done((bf16[128,656]{1,0:T(8,128)(2,1)S(1)}, bf16[128,656]{1,0:T(8,128)(2,1)S(1)}, u32[]{:S(2)}, u32[]{:S(2)}) %collective-permute-start.27) | collective-permute-done | bytes 167968 | tf_op jit(solution)/shard_map/ppermute | solution.py:155
  144.7 4.8 %collective-permute-done.14 = bf16[128,1024]{1,0:T(8,128)(2,1)S(1)} collective-permute-done((bf16[128,1024]{1,0:T(8,128)(2,1)S(1)}, bf16[128,1024]{1,0:T(8,128)(2,1)S(1)}, u32[]{:S(2)}, u32[]{:S(2)}) %collective-permute-start.14) | collective-permute-done | bytes 262176 | tf_op jit(solution)/shard_map/ppermute | solution.py:120
  149.6 7.5 %collective-permute-done.20 = bf16[128,1312]{1,0:T(8,128)(2,1)S(1)} collective-permute-done((bf16[128,1312]{1,0:T(8,128)(2,1)}, bf16[128,1312]{1,0:T(8,128)(2,1)S(1)}, u32[]{:S(2)}, u32[]{:S(2)}) %collective-permute-start.20) | collective-permute-done | bytes 335904 | tf_op jit(solution)/shard_map/ppermute | solution.py:155
  175.0 9.0 %collective-permute-done.55 = bf16[512,656]{0,1:T(8,128)(2,1)S(1)} collective-permute-done((bf16[512,656]{0,1:T(8,128)(2,1)S(1)}, bf16[512,656]{0,1:T(8,128)(2,1)S(1)}, u32[]{:S(2)}, u32[]{:S(2)}) %collective-permute-start.55) | collective-permute-done | bytes 671776 | tf_op jit(solution)/shard_map/ppermute | solution.py:155
  185.1 3.7 %collective-permute-start.58 = (bf16[128,656]{0,1:T(8,128)(2,1)}, bf16[128,656]{0,1:T(8,128)(2,1)}, u32[]{:S(2)}, u32[]{:S(2)}) collective-permute-start(bf16[128,656]{0,1:T(8,128)(2,1)} %get-tuple-element.151), channel_id=1, source_target_pairs={{0,24},{4,28},{8,0},{12,4},{16,8},{20,12},{24,16},{28,20},{1,25},{... | collective-permute-start | bytes 503816 | tf_op jit(solution)/shard_map/ppermute | solution.py:152
  192.4 4.3 %collective-permute-done.36 = bf16[128,1024]{1,0:T(8,128)(2,1)S(1)} collective-permute-done((bf16[128,1024]{1,0:T(8,128)(2,1)S(1)}, bf16[128,1024]{1,0:T(8,128)(2,1)S(1)}, u32[]{:S(2)}, u32[]{:S(2)}) %collective-permute-start.36) | collective-permute-done | bytes 262176 | tf_op jit(solution)/shard_map/ppermute | solution.py:120
  213.8 2.3 add_convert_fusion.1
  221.1 3.4 %all-to-all-start.5 = ((bf16[4,32,656]{2,1,0:T(8,128)(2,1)}), bf16[4,32,656]{2,1,0:T(8,128)(2,1)S(1)}, u32[]{:S(2)}, u32[]{:S(2)}) async-start(bf16[4,32,656]{2,1,0:T(8,128)(2,1)} %pad_maximum_fusion.21), calls=%async_computation.5 | async-start | bytes 393216 | tf_op jit(solution)/shard_map/all_to_all | solution.py:140
  224.5 12.8 %collective-permute-done.45 = bf16[128,1024]{1,0:T(8,128)(2,1)} collective-permute-done((bf16[128,1024]{1,0:T(8,128)(2,1)}, bf16[128,1024]{1,0:T(8,128)(2,1)}, u32[]{:S(2)}, u32[]{:S(2)}) %collective-permute-start.45) | collective-permute-done | bytes 262176 | tf_op jit(solution)/shard_map/ppermute | solution.py:155
  240.1 5.2 %collective-permute-done.46 = bf16[32,1024]{1,0:T(8,128)(2,1)S(1)} collective-permute-done((bf16[32,1024]{1,0:T(8,128)(2,1)S(1)}, bf16[32,1024]{1,0:T(8,128)(2,1)S(1)}, u32[]{:S(2)}, u32[]{:S(2)}) %collective-permute-start.46) | collective-permute-done | bytes 65568 | tf_op jit(solution)/shard_map/ppermute | solution.py:149
  249.5 2.8 collective-permute-start.54
  257.4 4.6 %collective-permute-start.42 = (bf16[128,768]{1,0:T(8,128)(2,1)S(1)}, bf16[128,768]{1,0:T(8,128)(2,1)S(1)}, u32[]{:S(2)}, u32[]{:S(2)}) collective-permute-start(bf16[128,768]{1,0:T(8,128)(2,1)S(1)} %get-tuple-element.154), channel_id=1, source_target_pairs={{0,8},{4,12},{8,16},{12,20},{16,24},{20,28},{24,0},{28,4},{1,9},{5... | collective-permute-start | bytes 589832 | tf_op jit(solution)/shard_map/ppermute | solution.py:149
  262.1 7.3 %collective-permute-start.44 = (bf16[128,768]{1,0:T(8,128)(2,1)}, bf16[128,768]{1,0:T(8,128)(2,1)}, u32[]{:S(2)}, u32[]{:S(2)}) collective-permute-start(bf16[128,768]{1,0:T(8,128)(2,1)} %get-tuple-element.153), channel_id=1, source_target_pairs={{0,24},{4,28},{8,0},{12,4},{16,8},{20,12},{24,16},{28,20},{1,25},{... | collective-permute-start | bytes 589832 | tf_op jit(solution)/shard_map/ppermute | solution.py:152
  287.1 3.5 %all-to-all-start.4 = ((bf16[4,32,1312]{2,1,0:T(8,128)(2,1)}), bf16[4,32,1312]{2,1,0:T(8,128)(2,1)S(1)}, u32[]{:S(2)}, u32[]{:S(2)}) async-start(bf16[4,32,1312]{2,1,0:T(8,128)(2,1)} %pad_maximum_fusion.16), calls=%async_computation.4 | async-start | bytes 720896 | tf_op jit(solution)/shard_map/all_to_all | solution.py:140
  297.6 3.4 %all-to-all-start.3 = ((bf16[4,32,768]{2,1,0:T(8,128)(2,1)}), bf16[4,32,768]{2,1,0:T(8,128)(2,1)S(1)}, u32[]{:S(2)}, u32[]{:S(2)}) async-start(bf16[4,32,768]{2,1,0:T(8,128)(2,1)} %pad_maximum_fusion.20), calls=%async_computation.3 | async-start | bytes 393216 | tf_op jit(solution)/shard_map/all_to_all | solution.py:140
  303.3 3.0 all-to-all-done.3
  (482 shorter events, 149.2 us)
Async XLA Ops:
  0.7 26.2 %collective-permute-start.4 = (bf16[32,1024]{1,0:T(8,128)(2,1)}, bf16[32,1024]{1,0:T(8,128)(2,1)S(1)}, u32[]{:S(2)}, u32[]{:S(2)}) collective-permute-start(bf16[32,1024]{1,0:T(8,128)(2,1)} %param.14), channel_id=1, source_target_pairs={{0,0},{1,4},{2,8},{3,12},{4,16},{5,20},{6,24},{7,28},{8,1},{9,5},{... | collective-permute-start | bytes 196616 | tf_op jit(solution)/shard_map/ppermute | solution.py:268
  4.8 22.1 %all-to-all-start = ((bf16[4,32,768]{2,1,0:T(8,128)(2,1)}), bf16[4,32,768]{2,1,0:T(8,128)(2,1)S(1)}, u32[]{:S(2)}, u32[]{:S(2)}) async-start(bf16[4,32,768]{2,1,0:T(8,128)(2,1)} %pad_maximum_fusion.18), calls=%async_computation | async-start | bytes 393216 | tf_op jit(solution)/shard_map/all_to_all | solution.py:140
  12.1 25.3 %collective-permute-start.2 = (bf16[128,1024]{1,0:T(8,128)(2,1)S(1)}, bf16[128,1024]{1,0:T(8,128)(2,1)S(1)}, u32[]{:S(2)}, u32[]{:S(2)}) collective-permute-start(bf16[128,1024]{1,0:T(8,128)(2,1)S(1)} %constant_dynamic-update-slice_fusion), channel_id=1, source_target_pairs={{0,2},{1,3},{2,0},{3,1},{4,6},{5,7},{6,4},{7,5},{8,10},{9,11},{10,... | collective-permute-start | bytes 786440 | tf_op jit(solution)/shard_map/ppermute | solution.py:120
  14.6 23.6 %collective-permute-start.32 = (bf16[128,1024]{1,0:T(8,128)(2,1)S(1)}, bf16[128,1024]{1,0:T(8,128)(2,1)S(1)}, u32[]{:S(2)}, u32[]{:S(2)}) collective-permute-start(bf16[128,1024]{1,0:T(8,128)(2,1)S(1)} %constant_dynamic-update-slice_fusion.49), channel_id=1, source_target_pairs={{0,2},{1,3},{2,0},{3,1},{4,6},{5,7},{6,4},{7,5},{8,10},{9,11},{10,... | collective-permute-start | bytes 786440 | tf_op jit(solution)/shard_map/ppermute | solution.py:120
  38.2 53.2 %collective-permute-start.3 = (bf16[2,128,1024]{2,1,0:T(8,128)(2,1)}, bf16[2,128,1024]{2,1,0:T(8,128)(2,1)}, u32[]{:S(2)}, u32[]{:S(2)}) collective-permute-start(bf16[2,128,1024]{2,1,0:T(8,128)(2,1)} %pad_maximum_fusion.7), channel_id=1, source_target_pairs={{0,1},{1,0},{2,3},{3,2},{4,5},{5,4},{6,7},{7,6},{8,9},{9,8},{10,11... | collective-permute-start | bytes 1572872 | tf_op jit(solution)/shard_map/ppermute | solution.py:120
  38.2 56.8 %collective-permute-start.33 = (bf16[2,128,1024]{2,1,0:T(8,128)(2,1)S(1)}, bf16[2,128,1024]{2,1,0:T(8,128)(2,1)S(1)}, u32[]{:S(2)}, u32[]{:S(2)}) collective-permute-start(bf16[2,128,1024]{2,1,0:T(8,128)(2,1)S(1)} %pad_maximum_fusion.11), channel_id=1, source_target_pairs={{0,1},{1,0},{2,3},{3,2},{4,5},{5,4},{6,7},{7,6},{8,9},{9,8},{10,11... | collective-permute-start | bytes 1572872 | tf_op jit(solution)/shard_map/ppermute | solution.py:120
  38.8 49.0 %all-to-all-start.2 = ((bf16[4,32,656]{2,1,0:T(8,128)(2,1)}), bf16[4,32,656]{2,1,0:T(8,128)(2,1)}, u32[]{:S(2)}, u32[]{:S(2)}) async-start(bf16[4,32,656]{2,1,0:T(8,128)(2,1)} %pad_maximum_fusion.19), calls=%async_computation.2 | async-start | bytes 393216 | tf_op jit(solution)/shard_map/all_to_all | solution.py:140
  47.9 39.8 %collective-permute-start.16 = (bf16[128,1312]{1,0:T(8,128)(2,1)}, bf16[128,1312]{1,0:T(8,128)(2,1)}, u32[]{:S(2)}, u32[]{:S(2)}) collective-permute-start(bf16[128,1312]{1,0:T(8,128)(2,1)} %bitcast.30), channel_id=1, source_target_pairs={{0,24},{4,28},{8,0},{12,4},{16,8},{20,12},{24,16},{28,20},{1,25},{... | collective-permute-start | bytes 1007624 | tf_op jit(solution)/shard_map/ppermute | solution.py:152
  49.6 38.2 %collective-permute-start.17 = (bf16[128,1312]{1,0:T(8,128)(2,1)}, bf16[128,1312]{1,0:T(8,128)(2,1)}, u32[]{:S(2)}, u32[]{:S(2)}) collective-permute-start(bf16[128,1312]{1,0:T(8,128)(2,1)} %bitcast.30), channel_id=1, source_target_pairs={{0,8},{4,12},{8,16},{12,20},{16,24},{20,28},{24,0},{28,4},{1,9},{5... | collective-permute-start | bytes 1007624 | tf_op jit(solution)/shard_map/ppermute | solution.py:149
  50.7 21.0 %collective-permute-start.7 = (bf16[128,1024]{1,0:T(8,128)(2,1)S(1)}, bf16[128,1024]{1,0:T(8,128)(2,1)}, u32[]{:S(2)}, u32[]{:S(2)}) collective-permute-start(bf16[128,1024]{1,0:T(8,128)(2,1)S(1)} %collective-permute-done.6), channel_id=1, source_target_pairs={{0,8},{4,12},{8,16},{12,20},{16,24},{20,28},{24,0},{28,4},{1,9},{5... | collective-permute-start | bytes 786440 | tf_op jit(solution)/shard_map/ppermute | solution.py:149
  85.7 71.5 %collective-permute-start.22 = (bf16[128,1312]{1,0:T(8,128)(2,1)}, bf16[128,1312]{1,0:T(8,128)(2,1)}, u32[]{:S(2)}, u32[]{:S(2)}) collective-permute-start(bf16[128,1312]{1,0:T(8,128)(2,1)} %bitcast.30), channel_id=1, source_target_pairs={{0,4},{4,0},{8,12},{12,8},{16,20},{20,16},{24,28},{28,24},{1,5},{5... | collective-permute-start | bytes 1007624 | tf_op jit(solution)/shard_map/ppermute | solution.py:155
  91.3 24.4 %collective-permute-start.24 = (bf16[128,656]{1,0:T(8,128)(2,1)}, bf16[128,656]{1,0:T(8,128)(2,1)}, u32[]{:S(2)}, u32[]{:S(2)}) collective-permute-start(bf16[128,656]{1,0:T(8,128)(2,1)} %bitcast.35), channel_id=1, source_target_pairs={{0,8},{4,12},{8,16},{12,20},{16,24},{20,28},{24,0},{28,4},{1,9},{5... | collective-permute-start | bytes 503816 | tf_op jit(solution)/shard_map/ppermute | solution.py:149
  95.1 48.5 %collective-permute-start.29 = (bf16[128,656]{1,0:T(8,128)(2,1)}, bf16[128,656]{1,0:T(8,128)(2,1)}, u32[]{:S(2)}, u32[]{:S(2)}) collective-permute-start(bf16[128,656]{1,0:T(8,128)(2,1)} %bitcast.35), channel_id=1, source_target_pairs={{0,4},{4,0},{8,12},{12,8},{16,20},{20,16},{24,28},{28,24},{1,5},{5... | collective-permute-start | bytes 503816 | tf_op jit(solution)/shard_map/ppermute | solution.py:155
  98.3 17.9 %collective-permute-start.18 = (bf16[128,1312]{1,0:T(8,128)(2,1)}, bf16[128,1312]{1,0:T(8,128)(2,1)}, u32[]{:S(2)}, u32[]{:S(2)}) collective-permute-start(bf16[128,1312]{1,0:T(8,128)(2,1)} %collective-permute-done.17), channel_id=1, source_target_pairs={{0,8},{4,12},{8,16},{12,20},{16,24},{20,28},{24,0},{28,4},{1,9},{5... | collective-permute-start | bytes 1007624 | tf_op jit(solution)/shard_map/ppermute | solution.py:149
  102.0 24.9 %collective-permute-start.19 = (bf16[128,1312]{1,0:T(8,128)(2,1)}, bf16[128,1312]{1,0:T(8,128)(2,1)}, u32[]{:S(2)}, u32[]{:S(2)}) collective-permute-start(bf16[128,1312]{1,0:T(8,128)(2,1)} %collective-permute-done.16), channel_id=1, source_target_pairs={{0,4},{4,0},{8,12},{12,8},{16,20},{20,16},{24,28},{28,24},{1,5},{5... | collective-permute-start | bytes 1007624 | tf_op jit(solution)/shard_map/ppermute | solution.py:155
  138.9 18.2 %collective-permute-start.21 = (bf16[128,1312]{1,0:T(8,128)(2,1)}, bf16[128,1312]{1,0:T(8,128)(2,1)S(1)}, u32[]{:S(2)}, u32[]{:S(2)}) collective-permute-start(bf16[128,1312]{1,0:T(8,128)(2,1)} %collective-permute-done.17), channel_id=1, source_target_pairs={{0,4},{4,0},{8,12},{12,8},{16,20},{20,16},{24,28},{28,24},{1,5},{5... | collective-permute-start | bytes 1007624 | tf_op jit(solution)/shard_map/ppermute | solution.py:155
  166.0 18.0 %collective-permute-start.55 = (bf16[512,656]{0,1:T(8,128)(2,1)S(1)}, bf16[512,656]{0,1:T(8,128)(2,1)S(1)}, u32[]{:S(2)}, u32[]{:S(2)}) collective-permute-start(bf16[512,656]{0,1:T(8,128)(2,1)S(1)} %slice.1198), channel_id=1, source_target_pairs={{0,4},{4,0},{8,12},{12,8},{16,20},{20,16},{24,28},{28,24},{1,5},{5... | collective-permute-start | bytes 2015240 | tf_op jit(solution)/shard_map/ppermute | solution.py:155
  170.5 41.3 %collective-permute-start.50 = (bf16[256,1312]{0,1:T(8,128)(2,1)}, bf16[256,1312]{0,1:T(8,128)(2,1)}, u32[]{:S(2)}, u32[]{:S(2)}) collective-permute-start(bf16[256,1312]{0,1:T(8,128)(2,1)} %get-tuple-element.149), channel_id=1, source_target_pairs={{0,4},{4,0},{8,12},{12,8},{16,20},{20,16},{24,28},{28,24},{1,5},{5... | collective-permute-start | bytes 2015240 | tf_op jit(solution)/shard_map/ppermute | solution.py:155
  171.0 42.4 %collective-permute-start.51 = (bf16[256,1312]{0,1:T(8,128)(2,1)}, bf16[256,1312]{0,1:T(8,128)(2,1)}, u32[]{:S(2)}, u32[]{:S(2)}) collective-permute-start(bf16[256,1312]{0,1:T(8,128)(2,1)} %get-tuple-element.148), channel_id=1, source_target_pairs={{0,4},{4,0},{8,12},{12,8},{16,20},{20,16},{24,28},{28,24},{1,5},{5... | collective-permute-start | bytes 2015240 | tf_op jit(solution)/shard_map/ppermute | solution.py:155
  185.1 31.8 %collective-permute-start.58 = (bf16[128,656]{0,1:T(8,128)(2,1)}, bf16[128,656]{0,1:T(8,128)(2,1)}, u32[]{:S(2)}, u32[]{:S(2)}) collective-permute-start(bf16[128,656]{0,1:T(8,128)(2,1)} %get-tuple-element.151), channel_id=1, source_target_pairs={{0,24},{4,28},{8,0},{12,4},{16,8},{20,12},{24,16},{28,20},{1,25},{... | collective-permute-start | bytes 503816 | tf_op jit(solution)/shard_map/ppermute | solution.py:152
  197.7 20.7 %collective-permute-start.57 = (bf16[128,656]{0,1:T(8,128)(2,1)}, bf16[128,656]{0,1:T(8,128)(2,1)}, u32[]{:S(2)}, u32[]{:S(2)}) collective-permute-start(bf16[128,656]{0,1:T(8,128)(2,1)} %add_convert_fusion.10), channel_id=1, source_target_pairs={{0,8},{4,12},{8,16},{12,20},{16,24},{20,28},{24,0},{28,4},{1,9},{5... | collective-permute-start | bytes 503816 | tf_op jit(solution)/shard_map/ppermute | solution.py:149
  207.2 62.8 %collective-permute-start.38 = (bf16[2,128,1024]{2,1,0:T(8,128)(2,1)}, bf16[2,128,1024]{2,1,0:T(8,128)(2,1)}, u32[]{:S(2)}, u32[]{:S(2)}) collective-permute-start(bf16[2,128,1024]{2,1,0:T(8,128)(2,1)} %pad_maximum_fusion.14), channel_id=1, source_target_pairs={{0,1},{1,0},{2,3},{3,2},{4,5},{5,4},{6,7},{7,6},{8,9},{9,8},{10,11... | collective-permute-start | bytes 1572872 | tf_op jit(solution)/shard_map/ppermute | solution.py:120
  211.8 37.7 %collective-permute-start.40 = (bf16[256,768]{1,0:T(8,128)(2,1)}, bf16[256,768]{1,0:T(8,128)(2,1)S(1)}, u32[]{:S(2)}, u32[]{:S(2)}) collective-permute-start(bf16[256,768]{1,0:T(8,128)(2,1)} %get-tuple-element.156), channel_id=1, source_target_pairs={{0,4},{4,0},{8,12},{12,8},{16,20},{20,16},{24,28},{28,24},{1,5},{5... | collective-permute-start | bytes 1179656 | tf_op jit(solution)/shard_map/ppermute | solution.py:155
  213.4 39.0 %collective-permute-start.41 = (bf16[256,768]{1,0:T(8,128)(2,1)}, bf16[256,768]{1,0:T(8,128)(2,1)S(1)}, u32[]{:S(2)}, u32[]{:S(2)}) collective-permute-start(bf16[256,768]{1,0:T(8,128)(2,1)} %get-tuple-element.155), channel_id=1, source_target_pairs={{0,4},{4,0},{8,12},{12,8},{16,20},{20,16},{24,28},{28,24},{1,5},{5... | collective-permute-start | bytes 1179656 | tf_op jit(solution)/shard_map/ppermute | solution.py:155
  216.9 20.4 %collective-permute-start.45 = (bf16[128,1024]{1,0:T(8,128)(2,1)}, bf16[128,1024]{1,0:T(8,128)(2,1)}, u32[]{:S(2)}, u32[]{:S(2)}) collective-permute-start(bf16[128,1024]{1,0:T(8,128)(2,1)} %pad_maximum_fusion.17), channel_id=1, source_target_pairs={{0,4},{4,0},{8,12},{12,8},{16,20},{20,16},{24,28},{28,24},{1,5},{5... | collective-permute-start | bytes 786440 | tf_op jit(solution)/shard_map/ppermute | solution.py:155
  218.5 28.7 %collective-permute-start.52 = (bf16[128,1312]{0,1:T(8,128)(2,1)}, bf16[128,1312]{0,1:T(8,128)(2,1)S(1)}, u32[]{:S(2)}, u32[]{:S(2)}) collective-permute-start(bf16[128,1312]{0,1:T(8,128)(2,1)} %get-tuple-element.147), channel_id=1, source_target_pairs={{0,8},{4,12},{8,16},{12,20},{16,24},{20,28},{24,0},{28,4},{1,9},{5... | collective-permute-start | bytes 1007624 | tf_op jit(solution)/shard_map/ppermute | solution.py:149
  221.1 18.0 %all-to-all-start.5 = ((bf16[4,32,656]{2,1,0:T(8,128)(2,1)}), bf16[4,32,656]{2,1,0:T(8,128)(2,1)S(1)}, u32[]{:S(2)}, u32[]{:S(2)}) async-start(bf16[4,32,656]{2,1,0:T(8,128)(2,1)} %pad_maximum_fusion.21), calls=%async_computation.5 | async-start | bytes 393216 | tf_op jit(solution)/shard_map/all_to_all | solution.py:140
  249.5 27.0 %collective-permute-start.54 = (bf16[128,1312]{0,1:T(8,128)(2,1)}, bf16[128,1312]{0,1:T(8,128)(2,1)S(1)}, u32[]{:S(2)}, u32[]{:S(2)}) collective-permute-start(bf16[128,1312]{0,1:T(8,128)(2,1)} %get-tuple-element.146), channel_id=1, source_target_pairs={{0,24},{4,28},{8,0},{12,4},{16,8},{20,12},{24,16},{28,20},{1,25},{... | collective-permute-start | bytes 1007624 | tf_op jit(solution)/shard_map/ppermute | solution.py:152
  252.4 24.2 %collective-permute-start.53 = (bf16[128,1312]{0,1:T(8,128)(2,1)S(1)}, bf16[128,1312]{0,1:T(8,128)(2,1)S(1)}, u32[]{:S(2)}, u32[]{:S(2)}) collective-permute-start(bf16[128,1312]{0,1:T(8,128)(2,1)S(1)} %add_convert_fusion.2), channel_id=1, source_target_pairs={{0,8},{4,12},{8,16},{12,20},{16,24},{20,28},{24,0},{28,4},{1,9},{5... | collective-permute-start | bytes 1007624 | tf_op jit(solution)/shard_map/ppermute | solution.py:149
  262.1 31.4 %collective-permute-start.44 = (bf16[128,768]{1,0:T(8,128)(2,1)}, bf16[128,768]{1,0:T(8,128)(2,1)}, u32[]{:S(2)}, u32[]{:S(2)}) collective-permute-start(bf16[128,768]{1,0:T(8,128)(2,1)} %get-tuple-element.153), channel_id=1, source_target_pairs={{0,24},{4,28},{8,0},{12,4},{16,8},{20,12},{24,16},{28,20},{1,25},{... | collective-permute-start | bytes 589832 | tf_op jit(solution)/shard_map/ppermute | solution.py:152
  271.9 18.6 %collective-permute-start.39 = (bf16[128,1024]{1,0:T(8,128)(2,1)}, bf16[128,1024]{1,0:T(8,128)(2,1)}, u32[]{:S(2)}, u32[]{:S(2)}) collective-permute-start(bf16[128,1024]{1,0:T(8,128)(2,1)} %fusion.16), channel_id=1, source_target_pairs={{0,2},{1,3},{2,0},{3,1},{4,6},{5,7},{6,4},{7,5},{8,10},{9,11},{10,... | collective-permute-start | bytes 786440 | tf_op jit(solution)/shard_map/ppermute | solution.py:120
  274.6 18.9 %collective-permute-start.43 = (bf16[128,768]{1,0:T(8,128)(2,1)}, bf16[128,768]{1,0:T(8,128)(2,1)}, u32[]{:S(2)}, u32[]{:S(2)}) collective-permute-start(bf16[128,768]{1,0:T(8,128)(2,1)} %add_convert_fusion.6), channel_id=1, source_target_pairs={{0,8},{4,12},{8,16},{12,20},{16,24},{20,28},{24,0},{28,4},{1,9},{5... | collective-permute-start | bytes 589832 | tf_op jit(solution)/shard_map/ppermute | solution.py:149
  (95 other events, 820.7 us)

commit v3 on v0

--- a/solution.py
+++ b/solution.py
@@ -1,6 +1,8 @@
 import jax
 import jax.numpy as jnp
 from jax import lax
+from jax.experimental import pallas as pl
+from jax.experimental.pallas import tpu as pltpu
 from jax.sharding import PartitionSpec as P
 
 HEAD_DIM = 64
@@ -31,11 +33,12 @@
 
 
 def layout(lengths, row_count):
-    ends = jnp.cumsum(lengths)
+    slot_ids = lax.iota(jnp.int32, lengths.shape[0])
+    before = (slot_ids[:, None] <= slot_ids[None, :]).astype(jnp.int32)
+    ends = jnp.sum(lengths[:, None] * before, axis=0)
     starts = ends - lengths
     places = lax.iota(jnp.int32, row_count)
     sequence_segment = jnp.sum((ends[None, :] <= places[:, None]).astype(jnp.int32), axis=1)
-    slot_ids = lax.iota(jnp.int32, lengths.shape[0])
     first_row = jnp.sum(
         jnp.where(sequence_segment[:, None] == slot_ids[None, :], starts[None, :], 0), axis=1
     )
@@ -268,7 +271,7 @@
     return (block_input_gradient, factors)
 
 
-def local(
+def local_plain(
     tokens,
     seq_lengths,
     cotangent,
@@ -371,30 +374,586 @@
     )
 
 
+AXES = ("fsdp", "rep")
+LANES = 128
+HALF = HEAD_DIM // 2
+
+
+def tie(*values):
+    return lax.optimization_barrier(values)
+
+
+def wide(value):
+    return value.astype(jnp.float32)
+
+
+def low(value):
+    return value.astype(jnp.bfloat16)
+
+
+def split_columns(value, count):
+    width = value.shape[1] // count
+    return [value[:, k * width : (k + 1) * width] for k in range(count)]
+
+
+def split_rows(value, count):
+    width = value.shape[0] // count
+    return [value[k * width : (k + 1) * width] for k in range(count)]
+
+
+def columns(blocks):
+    return jnp.concatenate(blocks, axis=1)
+
+
+def rows(blocks):
+    return jnp.concatenate(blocks, axis=0)
+
+
+def swap(value, distance):
+    return lax.ppermute(value, "rep", [(k, k ^ distance) for k in range(4)])
+
+
+def rep_exchange(value):
+    blocks = value.reshape(4, value.shape[0] // 4, value.shape[1])
+    return lax.all_to_all(blocks, "rep", 0, 0, tiled=True).reshape(value.shape)
+
+
+def up(value):
+    return lax.ppermute(value, "fsdp", [(k, (k + 2) % 8) for k in range(8)])
+
+
+def down(value):
+    return lax.ppermute(value, "fsdp", [(k, (k - 2) % 8) for k in range(8)])
+
+
+def over(value):
+    return lax.ppermute(value, "fsdp", [(k, k ^ 1) for k in range(8)])
+
+
+def relative(value, z, x):
+    blocks = split_columns(value, 8)
+    blocks = [jnp.where(x == 1, blocks[k ^ 1], blocks[k]) for k in range(8)]
+    for bit in (1, 2):
+        turn = (z & bit) != 0
+        blocks = [jnp.where(turn, blocks[(k + 2 * bit) % 8], blocks[k]) for k in range(8)]
+    return columns([blocks[2 * ((p + 1) % 4) + i] for i in range(2) for p in range(4)])
+
+
+def absolute(value, z, x):
+    blocks = split_columns(value, 8)
+    blocks = [blocks[4 * i + (j - 1) % 4] for j in range(4) for i in range(2)]
+    blocks = [jnp.where(x == 1, blocks[k ^ 1], blocks[k]) for k in range(8)]
+    for bit in (1, 2):
+        turn = (z & bit) != 0
+        blocks = [jnp.where(turn, blocks[(k - 2 * bit) % 8], blocks[k]) for k in range(8)]
+    return columns(blocks)
+
+
+def place_of(place, step, side):
+    z, x = place[0], place[1]
+    return 2 * lax.rem(z + step + 1, 4) + (x if side == 0 else 1 - x)
+
+
+def block_of(place, z_at, side):
+    z, x = place[0], place[1]
+    return 4 * (x if side == 0 else 1 - x) + lax.rem(z_at - z + 7, 4)
+
+
+def turned(value):
+    width = value.shape[1]
+    lane = lax.broadcasted_iota(jnp.int32, value.shape, 1)
+    return jnp.where(
+        lane % HEAD_DIM < HALF,
+        pltpu.roll(value, width - HALF, 1),
+        pltpu.roll(value, HALF, 1),
+    )
+
+
+def head_masks(row_count):
+    lane = lax.broadcasted_iota(jnp.int32, (row_count, LANES), 1)
+    return [low(wide(lane < HEAD_DIM)), low(wide(lane >= HEAD_DIM))], lane < HEAD_DIM
+
+
+def token_rows(mine, across, beside, first, step):
+    count = 128
+    return [
+        mine[first : first + count],
+        beside[first : first + count],
+        across[first : first + count],
+        beside[step + first : step + first + count],
+    ]
+
+
+def attention_forward(
+    place, seg_col, seg_row, cosine, sine, mine, across, beside,
+    first, second, third, own, others, other_second, other,
+    normed, qkv, attn, query, key, value, probs, attended, send, keep,
+):
+    size = own.shape[0]
+    blocks = [
+        (first, 0), (second, 0), (third, 0), (own, 0),
+        (others, 0), (other_second, 0), (others, size), (other, 0),
+    ]
+    part = size // 4
+    for at, (ref, row) in enumerate(blocks):
+        qkv[size * at : size * (at + 1), :] = ref[row : row + size, :768]
+        target = pl.multiple_of(place_of(place, at % 4, at // 4) * part, part)
+        for z_at in range(4):
+            for side in range(2):
+                lanes = pl.multiple_of(block_of(place, z_at, side) * LANES, LANES)
+                attn[pl.ds(target, part), pl.ds(lanes, LANES)] = ref[
+                    row + part * z_at : row + part * (z_at + 1),
+                    768 + LANES * side : 768 + LANES * (side + 1),
+                ]
+    count = 128
+    for at, ref in enumerate(token_rows(mine, across, beside, 0, mine.shape[0])):
+        values = wide(ref)
+        centred = values - jnp.mean(values, axis=1, keepdims=True)
+        inverse = lax.rsqrt(jnp.mean(centred * centred, axis=1, keepdims=True) + norm_eps)
+        normed[count * at : count * (at + 1), :] = low(centred * inverse)
+    packed = matmul(normed[...], qkv[...])
+    cos_all, sin_all = columns([cosine[...]] * 2), columns([sine[...]] * 2)
+    raw = packed[:, :256]
+    query[...] = low((raw * cos_all + turned(raw) * sin_all) * HEAD_DIM ** (-0.5))
+    raw = packed[:, 256:512]
+    key[...] = low(raw * cos_all + turned(raw) * sin_all)
+    value[...] = low(packed[:, 512:])
+    masks, is_first = head_masks(count)
+    for at in range(4):
+        here = slice(count * at, count * (at + 1))
+        allowed = seg_col[here, :] == seg_row[at : at + 1, :]
+        for pair in range(2):
+            lanes = slice(LANES * pair, LANES * (pair + 1))
+            made = []
+            for head in range(2):
+                scores = matmul_right_t(query[here, lanes] * masks[head], key[here, lanes])
+                scores = jnp.where(allowed, scores, -jnp.inf)
+                powers = jnp.exp(scores - jnp.max(scores, axis=1, keepdims=True))
+                weights = powers / jnp.sum(powers, axis=1, keepdims=True)
+                slot = count * (4 * at + 2 * pair + head)
+                probs[slot : slot + count, :] = weights
+                made.append(matmul(low(weights), value[here, lanes]))
+            attended[here, lanes] = low(jnp.where(is_first, made[0], made[1]))
+    total = low(matmul(attended[...], attn[...]))
+    keep[:count, :], send[:count, :] = total[:count], total[count : 2 * count]
+    keep[count:, :], send[count:, :] = total[2 * count : 3 * count], total[3 * count :]
+
+
+def mlp(
+    seg_col, norm_own, norm_across, norm_beside, mine, across, beside,
+    first, second, third, own, others, other_second, other,
+    out_first, out_second, out_third, out_own,
+    normed, grad_out, mixed, grad_inner, send, keep,
+    w_up, w_down, inner, grad_mixed,
+):
+    size, count = own.shape[0], 128
+    blocks = [
+        (first, 0), (second, 0), (third, 0), (own, 0),
+        (others, 0), (other_second, 0), (others, size), (other, 0),
+    ]
+    for at, (ref, row) in enumerate(blocks):
+        w_up[size * at : size * (at + 1), :] = ref[row : row + size, :]
+    for at, ref in enumerate((out_first, out_second, out_third, out_own)):
+        w_down[size * at : size * (at + 1), :] = ref[:size, :]
+        w_down[size * (at + 4) : size * (at + 5), :] = ref[size:, :]
+    for at, ref in enumerate(
+        (norm_own[...], norm_beside[:count, :], norm_across[...], norm_beside[count:, :])
+    ):
+        normed[count * at : count * (at + 1), :] = ref
+    for at, ref in enumerate(token_rows(mine, across, beside, count, mine.shape[0])):
+        live = wide(seg_col[count * at : count * (at + 1), :] < 8)
+        grad_out[count * at : count * (at + 1), :] = low(wide(ref) * live)
+    inner[...] = matmul(normed[...], w_up[...])
+    grad_mixed[...] = matmul(grad_out[...], w_down[...])
+    main = (w_down.shape[1] // LANES - 1) * LANES
+    rest = 16
+
+    def parts(gate):
+        phi = 0.5 * (1.0 + lax.erf(gate * 0.7071067811865476))
+        slope = phi + gate * jnp.exp(-0.5 * gate * gate) * 0.3989422804014327
+        return gate * phi, slope
+
+    @pl.loop(0, 8)
+    def _(step):
+        here = pl.ds(pl.multiple_of(step * 64, 64), 64)
+        gate, up_part = inner[here, :main], inner[here, main : 2 * main]
+        grad = grad_mixed[here, :main]
+        activation, slope = parts(gate)
+        mixed[here, :main] = low(activation * up_part)
+        grad_inner[here, :main] = low(grad * up_part * slope)
+        grad_inner[here, main : 2 * main] = low(grad * activation)
+        tail = inner[here, 2 * main :]
+        grad = grad_mixed[here, main:]
+        activation, slope = parts(tail)
+        tail_up = pltpu.roll(tail, LANES - rest, 1)
+        mixed[here, main:] = low(activation * tail_up)
+        grad_inner[here, 2 * main :] = low(
+            grad * tail_up * slope + pltpu.roll(grad * activation, rest, 1)
+        )
+
+    total = low(matmul_right_t(grad_inner[...], w_up[...]))
+    keep[:count, :], send[:count, :] = total[:count], total[count : 2 * count]
+    keep[count:, :], send[count:, :] = total[2 * count : 3 * count], total[3 * count :]
+
+
+def mlp_terms(
+    normed, grad_inner, grad_out, mixed,
+    in_keep, in_early, in_late, out_first, out_second, out_third, out_own,
+):
+    term = low(matmul_left_t(normed[...], grad_inner[...]))
+    half, quarter = term.shape[0] // 2, term.shape[0] // 4
+    in_keep[...] = term[:half]
+    in_early[...] = term[half : half + quarter]
+    in_late[...] = term[half + quarter :]
+    term = low(matmul_left_t(grad_out[...], mixed[...]))
+    size = term.shape[0] // 8
+    for at, ref in enumerate((out_first, out_second, out_third, out_own)):
+        ref[:size, :] = term[size * at : size * (at + 1)]
+        ref[size:, :] = term[size * (at + 4) : size * (at + 5)]
+
+
+def attention_backward(
+    place, cosine, sine, low_own, low_across, low_beside, attn, query, key, value, probs,
+    attended, normed,
+    grad_packed, g_keep, g_early, g_late, grad_low, grad_attended, term_attn,
+):
+    count = 128
+    for at, ref in enumerate(
+        (low_own[...], low_beside[:count, :], low_across[...], low_beside[count:, :])
+    ):
+        grad_low[count * at : count * (at + 1), :] = ref
+    grad_attended[...] = low(matmul_right_t(grad_low[...], attn[...]))
+    masks, is_first = head_masks(count)
+    for at in range(4):
+        here = slice(count * at, count * (at + 1))
+        cos, sin = cosine[here, :], sine[here, :]
+        for pair in range(2):
+            lanes = slice(LANES * pair, LANES * (pair + 1))
+            q, k, v = query[here, lanes], key[here, lanes], value[here, lanes]
+            grad = grad_attended[here, lanes]
+            made = []
+            for head in range(2):
+                slot = count * (4 * at + 2 * pair + head)
+                weights = probs[slot : slot + count, :]
+                grad_value = matmul_left_t(low(weights), grad)
+                grad_probs = matmul_right_t(grad * masks[head], v)
+                delta = jnp.sum(weights * grad_probs, axis=1, keepdims=True)
+                grad_scores = low(weights * (grad_probs - delta))
+                made.append((matmul(grad_scores, k), matmul_left_t(grad_scores, q), grad_value))
+            grad_q, grad_k, grad_v = (jnp.where(is_first, *both) for both in zip(*made))
+            grad_q = grad_q * HEAD_DIM ** (-0.5)
+            grad_packed[here, lanes] = low(grad_q * cos - turned(grad_q) * sin)
+            lanes = slice(256 + LANES * pair, 256 + LANES * (pair + 1))
+            grad_packed[here, lanes] = low(grad_k * cos - turned(grad_k) * sin)
+            lanes = slice(512 + LANES * pair, 512 + LANES * (pair + 1))
+            grad_packed[here, lanes] = low(grad_v)
+    term = low(matmul_left_t(normed[...], grad_packed[...]))
+    half, quarter = term.shape[0] // 2, term.shape[0] // 4
+    g_keep[:, :768] = term[:half]
+    g_early[:, :768] = term[half : half + quarter]
+    g_late[:, :768] = term[half + quarter :]
+    term_attn[...] = low(matmul_left_t(attended[...], grad_low[...]))
+    size = term.shape[0] // 8
+    part = size // 4
+    targets = [(g_keep, size * p) for p in range(4)]
+    targets += [(g_early, 0), (g_early, size), (g_late, 0), (g_late, size)]
+    for at, (ref, row) in enumerate(targets):
+        source = pl.multiple_of(place_of(place, at % 4, at // 4) * part, part)
+        for z_at in range(4):
+            for side in range(2):
+                lanes = pl.multiple_of(block_of(place, z_at, side) * LANES, LANES)
+                ref[
+                    row + part * z_at : row + part * (z_at + 1),
+                    768 + LANES * side : 768 + LANES * (side + 1),
+                ] = term_attn[pl.ds(source, part), pl.ds(lanes, LANES)]
+
+
+def projections(
+    grad_packed, qkv, mixed, out_first, out_second, out_third, out_own, send, keep, w_down
+):
+    size, count = out_own.shape[0] // 2, 128
+    for at, ref in enumerate((out_first, out_second, out_third, out_own)):
+        w_down[size * at : size * (at + 1), :] = ref[:size, :]
+        w_down[size * (at + 4) : size * (at + 5), :] = ref[size:, :]
+    for row, total in (
+        (0, low(matmul_right_t(grad_packed[...], qkv[...]))),
+        (count, low(matmul_right_t(mixed[...], w_down[...]))),
+    ):
+        keep[row : row + count, :] = total[:count]
+        send[row : row + count, :] = total[count : 2 * count]
+        keep[2 * count + row : 3 * count + row, :] = total[2 * count : 3 * count]
+        send[2 * count + row : 3 * count + row, :] = total[3 * count :]
+
+
+def kernel(body, outs, cost, *args, scratch=(), scalars=0):
+    flops, transcendentals = cost
+    shapes = [jax.ShapeDtypeStruct(shape, kind) for shape, kind in outs]
+    moved = sum(arg.size * arg.dtype.itemsize for arg in (*args, *shapes))
+    return pl.pallas_call(
+        body,
+        out_shape=shapes,
+        in_specs=[
+            pl.BlockSpec(memory_space=pltpu.SMEM if k < scalars else pltpu.VMEM)
+            for k in range(len(args))
+        ],
+        out_specs=[pl.BlockSpec(memory_space=pltpu.VMEM)] * len(shapes),
+        scratch_shapes=[pltpu.VMEM(shape, kind) for shape, kind in scratch],
+        compiler_params=pltpu.CompilerParams(vmem_limit_bytes=48 * 2**20),
+        cost_estimate=pl.CostEstimate(
+            flops=flops, bytes_accessed=moved, transcendentals=transcendentals
+        ),
+        name=body.__name__,
+    )(*args)
+
+
+def scatter_last(send, keep):
+    beside = split_rows(swap(send, 1), 2)
+    kept = split_rows(keep, 2)
+    sent = low(wide(kept[1]) + wide(beside[1]))
+    return wide(kept[0]) + wide(beside[0]), sent
+
+
+def local_ring(
+    tokens,
+    seq_lengths,
+    cotangent,
+    attention_norm_gain,
+    w_qkv,
+    w_attn_out,
+    feedforward_norm_gain,
+    w_in,
+    w_out,
+):
+    count, width = tokens.shape
+    index = lax.axis_index("fsdp")
+    z, x = index // 2, index % 2
+    place = jnp.stack([z, x]).astype(jnp.int32)
+    hidden = w_in.shape[1] // 2
+    part = hidden // 4
+    main = part // LANES * LANES
+    in_width, out_width = 2 * main + LANES, main + LANES
+    f32, b16 = jnp.float32, jnp.bfloat16
+    group = 4 * count
+
+    gain_attn = wide(attention_norm_gain)[:, None]
+    gain_mlp = wide(feedforward_norm_gain)[:, None]
+    order = [(k, (k % 8) * 4 + k // 8) for k in range(32)]
+    attn_own = lax.ppermute(w_attn_out, AXES, order)
+    qkv_parts = split_columns(low(wide(w_qkv) * gain_attn), 12)
+    qkv_own = rep_exchange(rows([columns(qkv_parts[k::4]) for k in range(4)]))
+    first_own = columns([qkv_own, rows(split_columns(attn_own, 4))])
+
+    scaled_in = low(wide(w_in) * gain_mlp)
+    pieces = []
+    for k in range(4):
+        gate = scaled_in[:, part * k : part * (k + 1)]
+        up_part = scaled_in[:, hidden + part * k : hidden + part * (k + 1)]
+        out_part = w_out[:, part * k : part * (k + 1)]
+        fill = [jnp.zeros((w_in.shape[0], n), b16) for n in (in_width - 2 * part, out_width - part)]
+        pieces.append(
+            columns(
+                [gate[:, :main], up_part[:, :main], gate[:, main:], up_part[:, main:], fill[0]]
+                + [out_part, fill[1]]
+            )
+        )
+    lengths_row = jnp.pad(low(wide(seq_lengths)), ((0, 15), (0, width - seq_lengths.shape[1])))
+    mine = rows([relative(tokens, z, x), relative(cotangent, z, x), lengths_row])
+    first_own, rest, mine = tie(first_own, rows(pieces), mine)
+    rest = rep_exchange(rest)
+    in_own, out_own = rest[:, :in_width], rest[:, in_width:]
+    across = swap(mine, 2)
+
+    third, first, other = up(first_own), down(first_own), over(first_own)
+    third, first, other = tie(third, first, other)
+    second, others = up(third), over(rows([first, third]))
+    beside = swap(rows([mine, across]), 1)
+    second, in_own, out_own = tie(second, in_own, out_own)
+    other_second = over(second)
+    in_third, in_first = up(in_own), down(in_own)
+    out_pair = rows([out_own, over(tie(out_own, others)[0])])
+
+    step = mine.shape[0]
+    lengths = rows(
+        [mine[2 * count : 2 * count + 1], beside[2 * count : 2 * count + 1]]
+        + [across[2 * count : 2 * count + 1], beside[step + 2 * count : step + 2 * count + 1]]
+    )[:, : seq_lengths.shape[1]].astype(jnp.int32)
+    segment, positions, _ = jax.vmap(lambda row: layout(row, count))(lengths)
+    frequency = rope_base ** (-(lax.iota(f32, HALF) * (2.0 / HEAD_DIM)))
+    angles = positions.reshape(group, 1).astype(f32) * frequency
+    cosine, sine = jnp.cos(angles), jnp.sin(angles)
+    cosine, sine = columns([cosine] * 4), columns([-sine, sine] * 2)
+    seg_col = segment.reshape(group, 1)
+
+    normed, qkv, attn, query, key, value, probs, attended, send, keep = kernel(
+        attention_forward,
+        [((group, width), b16), ((width, 768), b16), ((256, width), b16)]
+        + [((group, 256), b16)] * 3
+        + [((16 * count, count), f32), ((group, 256), b16)]
+        + [((2 * count, width), b16)] * 2,
+        (2 * group * width * (768 + 256) + 4 * 16 * count * count * LANES, 16 * count * count),
+        place, seg_col, segment, cosine, sine, mine, across, beside,
+        first, second, third, first_own, others, other_second, other,
+        scalars=1,
+    )
+    in_third, in_first, _ = tie(in_third, in_first, send)
+    in_second, in_others = up(in_third), over(rows([in_first, in_third]))
+    in_other = over(tie(in_own, send)[0])
+    x_own = wide(mine[:count])
+    kept, sent = scatter_last(send, keep)
+    in_second, out_pair, _ = tie(in_second, out_pair, sent)
+    in_other_second = over(in_second)
+    out_third, out_first = up(out_pair), down(out_pair)
+    hidden_sum = x_own + kept + wide(swap(sent, 2))
+    standard_mlp, inverse_mlp = norm_statistics(hidden_sum)
+    norm_own = low(standard_mlp)
+    norm_across = swap(norm_own, 2)
+    out_third, out_first, _ = tie(out_third, out_first, norm_own)
+    out_second = up(out_third)
+    norm_beside = swap(rows([norm_own, norm_across]), 1)
+
+    normed_mlp, grad_out, mixed, grad_inner, send, keep = kernel(
+        mlp,
+        [((group, width), b16)] * 2
+        + [((group, out_width), b16), ((group, in_width), b16)]
+        + [((2 * count, width), b16)] * 2,
+        (2 * group * width * (2 * in_width + out_width), 3 * group * part),
+        seg_col, norm_own, norm_across, norm_beside, mine, across, beside,
+        in_first, in_second, in_third, in_own, in_others, in_other_second, in_other,
+        out_first, out_second, out_third, out_pair,
+        scratch=[
+            ((width, in_width), b16),
+            ((width, out_width), b16),
+            ((group, in_width), f32),
+            ((group, out_width), f32),
+        ],
+    )
+    in_keep, in_early, in_late, *out_terms = kernel(
+        mlp_terms,
+        [((width // 2, in_width), b16)]
+        + [((width // 4, in_width), b16)] * 2
+        + [((width // 4, out_width), b16)] * 4,
+        (2 * group * width * (in_width + out_width), 0),
+        normed_mlp, grad_inner, grad_out, mixed,
+    )
+    out_up, out_down = up(out_terms[1]), down(out_terms[2])
+    in_early, in_late = over(in_early), over(in_late)
+    kept, sent = scatter_last(send, keep)
+    scaled_mlp = kept + wide(swap(sent, 2))
+    grad_hidden = wide(grad_out[:count]) + norm_backward_pass(
+        scaled_mlp, jnp.ones((), f32), standard_mlp, inverse_mlp
+    )
+    low_own = low(grad_hidden)
+    low_across = swap(low_own, 2)
+    out_up, out_down, _ = tie(out_up, out_down, low_own)
+    out_turned = up(low(wide(out_terms[0]) + wide(out_up)))
+    low_beside = swap(rows([low_own, low_across]), 1)
+    in_early, out_turned, low_beside = tie(in_early, out_turned, low_beside)
+    in_kept, in_first_two = split_rows(in_keep, 4), split_rows(in_early, 2)
+    in_up = up(low(wide(in_kept[1]) + wide(in_first_two[1])))
+    out_sums = split_rows(wide(out_terms[3]) + wide(out_turned) + wide(out_down), 2)
+    out_over = over(low(out_sums[1]))
+
+    grad_packed, g_keep, g_early, g_late = kernel(
+        attention_backward,
+        [((group, 768), b16), ((width // 2, width), b16)] + [((width // 4, width), b16)] * 2,
+        (2 * group * width * (768 + 512) + 10 * 16 * count * count * LANES, 0),
+        place, cosine, sine, low_own, low_across, low_beside, attn, query, key, value, probs,
+        attended, normed,
+        scratch=[((group, width), b16), ((group, 256), b16), ((256, width), b16)],
+        scalars=1,
+    )
+    g_over_early, g_over_late = over(g_early), over(g_late)
+    in_late, in_up, _ = tie(in_late, in_up, g_keep)
+    in_last_two = split_rows(in_late, 2)
+    in_turned = up(low(wide(in_kept[0]) + wide(in_first_two[0]) + wide(in_up)))
+    in_down = down(low(wide(in_kept[2]) + wide(in_last_two[0])))
+    send, keep = kernel(
+        projections,
+        [((4 * count, width), b16)] * 2,
+        (2 * group * width * (768 + out_width), 0),
+        grad_packed, qkv, mixed, out_first, out_second, out_third, out_pair,
+        scratch=[((width, out_width), b16)],
+    )
+    g_over_early, in_turned, in_down = tie(g_over_early, in_turned, in_down)
+    g_kept, g_first_two = split_rows(g_keep, 4), split_rows(g_over_early, 2)
+    g_up = up(low(wide(g_kept[1]) + wide(g_first_two[1])))
+    sum_in = wide(in_kept[3]) + wide(in_last_two[1]) + wide(in_turned) + wide(in_down)
+    sum_out = out_sums[0] + wide(out_over)
+    back = rep_exchange(columns([low(sum_in), low(sum_out)]))
+    g_over_late, g_up = tie(g_over_late, g_up)
+    g_last_two = split_rows(g_over_late, 2)
+    g_turned = up(low(wide(g_kept[0]) + wide(g_first_two[0]) + wide(g_up)))
+    g_down = down(low(wide(g_kept[2]) + wide(g_last_two[0])))
+    kept, sent = scatter_last(send, keep)
+    last = kept + wide(swap(sent, 2))
+    sum_g = low(wide(g_kept[3]) + wide(g_last_two[1]) + wide(g_turned) + wide(g_down))
+    back_qkv = rep_exchange(sum_g[:, :768])
+    grad_w_attn_out = wide(
+        lax.ppermute(
+            columns(split_rows(sum_g[:, 768:], 4)), AXES, [(there, here) for here, there in order]
+        )
+    )
+
+    standard, inverse = norm_statistics(x_own)
+    block_input_gradient = grad_hidden + norm_backward_pass(
+        last[:count], jnp.ones((), f32), standard, inverse
+    )
+    output = low(jnp.where(seg_col[:count] < 8, hidden_sum + last[count:], 0.0))
+    back = split_rows(back, 4)
+    back_qkv = [split_columns(piece, 3) for piece in split_rows(back_qkv, 4)]
+    unit_qkv = wide(columns([piece[k] for k in range(3) for piece in back_qkv]))
+    rest_width = part - main
+    unit_in = wide(
+        columns(
+            [
+                value
+                for k in range(2)
+                for piece in back
+                for value in (
+                    piece[:, main * k : main * (k + 1)],
+                    piece[:, 2 * main + rest_width * k : 2 * main + rest_width * (k + 1)],
+                )
+            ]
+        )
+    )
+    grad_w_out = wide(columns([piece[:, in_width : in_width + part] for piece in back]))
+    return (
+        absolute(output, z, x),
+        absolute(block_input_gradient, z, x),
+        jnp.sum(unit_qkv * wide(w_qkv), axis=1),
+        unit_qkv * gain_attn,
+        grad_w_attn_out,
+        jnp.sum(unit_in * wide(w_in), axis=1),
+        unit_in * gain_mlp,
+        grad_w_out,
+    )
+
+
 def solution(mesh):
+    ringed = dict(mesh.shape) == {"fsdp": 8, "rep": 4}
     return jax.shard_map(
-        local,
+        local_ring if ringed else local_plain,
         mesh=mesh,
         in_specs=(
-            P(("fsdp", "rep"), None),
-            P(("fsdp", "rep"), None),
-            P(("fsdp", "rep"), None),
-            P(("fsdp", "rep")),
-            P(("fsdp", "rep"), None),
-            P(("fsdp", "rep"), None),
-            P(("fsdp", "rep")),
-            P(("fsdp", "rep"), None),
-            P(("fsdp", "rep"), None),
+            P(AXES, None),
+            P(AXES, None),
+            P(AXES, None),
+            P(AXES),
+            P(AXES, None),
+            P(AXES, None),
+            P(AXES),
+            P(AXES, None),
+            P(AXES, None),
         ),
         out_specs=(
-            P(("fsdp", "rep"), None),
-            P(("fsdp", "rep"), None),
-            P(("fsdp", "rep")),
-            P(("fsdp", "rep"), None),
-            P(("fsdp", "rep"), None),
-            P(("fsdp", "rep")),
-            P(("fsdp", "rep"), None),
-            P(("fsdp", "rep"), None),
+            P(AXES, None),
+            P(AXES, None),
+            P(AXES),
+            P(AXES, None),
+            P(AXES, None),
+            P(AXES),
+            P(AXES, None),
+            P(AXES, None),
         ),
         check_vma=False,
     )

time: 948 us -> 283 us (0.30)
  waiting for transfers between devices: 730 us -> 144 us
  matrix products: 67.9 us -> 0 us
  local copies, waits for them, and re-layouts: 74.5 us -> 13.1 us
  starting transfers between devices: 0.19 us -> 56.4 us
  blocking collectives: 42.5 us -> 0 us
  Pallas kernels: 0 us -> 34.1 us
  other arithmetic: 10 us -> 28.6 us
  between operations: 14.3 us -> 1.5 us
    reduce_scatter x1 -> x0, waiting for transfers between devices: 506 us -> none  [local(): lax.psum_scatter(jnp.concatenate([qkv_term, attn_term, inner_term, outer_...]
    all_gather x4 -> x0, waiting for transfers between devices: 221 us -> none  [the longest x1 86 us: local(): lax.all_gather(w_in, ('fsdp', 'rep'), axis=0, tiled=True)]
    ppermute x0 -> x44, waiting for transfers between devices: none -> 140 us  [the longest x12 52.7 us: up(): return lax.ppermute(value, 'fsdp', [(k, (k + 2) % 8) for k in range(8)])]
    dot_general x18 -> x0, matrix products: 67.9 us -> none  [the longest x4 23.9 us: matmul(): return jnp.dot(left_side, right_side, preferred_element_type=jnp.float32)]
    concatenate x1 -> x7, local copies, waits for them, and re-layouts: 57.1 us -> 0.82 us  [columns(): return jnp.concatenate(blocks, axis=1)]
    unnamed x1 -> x0, blocking collectives: 42.5 us -> none
    ppermute x0 -> x44, starting transfers between devices: none -> 38.5 us  [the longest x6 13.7 us: down(): return lax.ppermute(value, 'fsdp', [(k, (k - 2) % 8) for k in range(8)])]
    pallas_call x0 -> x5, Pallas kernels: none -> 34.1 us  [kernel(): pl.pallas_call(body, out_shape=shapes, in_specs=[pl.BlockSpec(memory_spac...]
  transfers between devices with their start and end apart: 5 -> 48, of which waited for: 5 -> 24; matrix products, arithmetic and copies ran while one was open for 3% -> 11% of each run, Pallas kernels for 0% -> 6%
where the time goes in v3:
time: 283 us; the launch traced here: 277 us
  waiting for transfers between devices  144 us (51%)
  starting transfers between devices  56.4 us (20%)
  Pallas kernels  34.1 us (12%)
  other arithmetic  28.6 us (10%)
  local copies, waits for them, and re-layouts  13.1 us (5%)
    ppermute x12, waiting for transfers between devices, up(): return lax.ppermute(value, 'fsdp', [(k, (k + 2) % 8) for k in range(8)])  52.7 us
    ppermute x12, waiting for transfers between devices, over(): return lax.ppermute(value, 'fsdp', [(k, k ^ 1) for k in range(8)])  36.5 us
    pallas_call x5, Pallas kernels, kernel(): pl.pallas_call(body, out_shape=shapes, in_specs=[pl.BlockSpec(memory_spac...  34.1 us
    ppermute x6, waiting for transfers between devices, down(): return lax.ppermute(value, 'fsdp', [(k, (k - 2) % 8) for k in range(8)])  28.7 us
    ppermute x12, waiting for transfers between devices, swap(): return lax.ppermute(value, 'rep', [(k, k ^ distance) for k in range(4)])  21.8 us
    all_to_all x4, starting transfers between devices, rep_exchange(): return lax.all_to_all(blocks, 'rep', 0, 0, tiled=True).reshape(value.shape)  17.9 us
    ppermute x6, starting transfers between devices, down(): return lax.ppermute(value, 'fsdp', [(k, (k - 2) % 8) for k in range(8)])  13.7 us
    convert_element_type x16, other arithmetic, low(): return value.astype(jnp.bfloat16)  9.34 us
  transfers between devices with their start and end apart: 48, of which 24 were waited for; matrix products, arithmetic and copies ran while one was open for 11% of the time, Pallas kernels for 6%

profile of v3, /device:TPU:0, one launch (start us, length us, event | category | flops | bytes accessed | tf_op | source)
XLA Modules:
  0.0 277.3 jit_solution(15904185388180945545)
XLA Ops:
  4.7 7.0 %all-to-all-start = ((bf16[4,32,768]{2,1,0:T(8,128)(2,1)}), bf16[4,32,768]{2,1,0:T(8,128)(2,1)S(1)}, u32[]{:S(2)}, u32[]{:S(2)}) async-start(bf16[4,32,768]{2,1,0:T(8,128)(2,1)} %bitcast), calls=%async_computation | async-start | bytes 393216 | tf_op jit(solution)/shard_map/all_to_all | solution.py:418
  14.7 2.6 all-to-all-done
  17.5 14.3 %collective-permute-done.1.across = bf16[272,1024]{1,0:T(8,128)(2,1)S(1)} collective-permute-done((bf16[272,1024]{1,0:T(8,128)(2,1)S(1)}, bf16[272,1024]{1,0:T(8,128)(2,1)S(1)}, u32[]{:S(2)}, u32[]{:S(2)}) %collective-permute-start.1) | collective-permute-done | bytes 557088 | tf_op jit(solution)/shard_map/ppermute | solution.py:413
  32.9 2.3 collective-permute-start.5
  37.3 3.5 %all-to-all-start.1 = ((bf16[4,32,2176]{2,1,0:T(8,128)(2,1)}), bf16[4,32,2176]{2,1,0:T(8,128)(2,1)S(1)}, u32[]{:S(2)}, u32[]{:S(2)}) async-start(bf16[4,32,2176]{2,1,0:T(8,128)(2,1)} %bitcast.7), calls=%async_computation.1 | async-start | bytes 1114112 | tf_op jit(solution)/shard_map/all_to_all | solution.py:418
  43.9 6.0 %collective-permute-done.3.third = bf16[128,1024]{1,0:T(8,128)(2,1)S(1)} collective-permute-done((bf16[128,1024]{1,0:T(8,128)(2,1)S(1)}, bf16[128,1024]{1,0:T(8,128)(2,1)S(1)}, u32[]{:S(2)}, u32[]{:S(2)}) %collective-permute-start.3) | collective-permute-done | bytes 262176 | tf_op jit(solution)/shard_map/ppermute | solution.py:422
  54.6 4.7 %collective-permute-done.6.second = bf16[128,1024]{1,0:T(8,128)(2,1)S(1)} collective-permute-done((bf16[128,1024]{1,0:T(8,128)(2,1)S(1)}, bf16[128,1024]{1,0:T(8,128)(2,1)S(1)}, u32[]{:S(2)}, u32[]{:S(2)}) %collective-permute-start.6) | collective-permute-done | bytes 262176 | tf_op jit(solution)/shard_map/ppermute | solution.py:422
  66.4 4.1 %collective-permute-done.8.other_second = bf16[128,1024]{1,0:T(8,128)(2,1)S(1)} collective-permute-done((bf16[128,1024]{1,0:T(8,128)(2,1)S(1)}, bf16[128,1024]{1,0:T(8,128)(2,1)S(1)}, u32[]{:S(2)}, u32[]{:S(2)}) %collective-permute-start.8) | collective-permute-done | bytes 262176 | tf_op jit(solution)/shard_map/ppermute | solution.py:430
  70.5 9.2 %attention_forward.1 = (bf16[512,1024]{1,0:T(8,128)(2,1)}, bf16[1024,768]{1,0:T(8,128)(2,1)}, bf16[256,1024]{1,0:T(8,128)(2,1)S(1)}, bf16[512,256]{1,0:T(8,128)(...) custom-call(s32[2]{0:T(128)S(1)} %pad_add_fusion.place, ...), custom_call_target="tpu_custom_call" | custom-call | flops 1207959552 | bytes 11145224 | tf_op jit(solution)/shard_map/attention_forward/pallas_call | solution.py:692
  79.8 2.9 %collective-permute-start.14 = (bf16[128,1408]{1,0:T(8,128)(2,1)S(1)}, bf16[128,1408]{1,0:T(8,128)(2,1)S(1)}, u32[]{:S(2)}, u32[]{:S(2)}) collective-permute-start(bf16[128,1408]{1,0:T(8,128)(2,1)S(1)} %slice.718.own), channel_id=1, source_target_pairs={{0,24},{4,28},{8,0},{12,4},{16,8},{20,12},{24,16},{28,20},{1,25},{... | collective-permute-start | bytes 1081352 | tf_op jit(solution)/shard_map/ppermute | solution.py:426
  83.2 8.2 %collective-permute-done.14.first = bf16[128,1408]{1,0:T(8,128)(2,1)S(1)} collective-permute-done((bf16[128,1408]{1,0:T(8,128)(2,1)S(1)}, bf16[128,1408]{1,0:T(8,128)(2,1)S(1)}, u32[]{:S(2)}, u32[]{:S(2)}) %collective-permute-start.14) | collective-permute-done | bytes 360480 | tf_op jit(solution)/shard_map/ppermute | solution.py:426
  91.4 8.0 %collective-permute-done.13.third = bf16[128,1408]{1,0:T(8,128)(2,1)S(1)} collective-permute-done((bf16[128,1408]{1,0:T(8,128)(2,1)S(1)}, bf16[128,1408]{1,0:T(8,128)(2,1)S(1)}, u32[]{:S(2)}, u32[]{:S(2)}) %collective-permute-start.13) | collective-permute-done | bytes 360480 | tf_op jit(solution)/shard_map/ppermute | solution.py:422
  102.0 9.4 %collective-permute-done.15.second = bf16[128,1408]{1,0:T(8,128)(2,1)S(1)} collective-permute-done((bf16[128,1408]{1,0:T(8,128)(2,1)S(1)}, bf16[128,1408]{1,0:T(8,128)(2,1)S(1)}, u32[]{:S(2)}, u32[]{:S(2)}) %collective-permute-start.15) | collective-permute-done | bytes 360480 | tf_op jit(solution)/shard_map/ppermute | solution.py:422
  115.4 5.5 %collective-permute-done.11.norm_across = bf16[128,1024]{1,0:T(8,128)(2,1)S(1)} collective-permute-done((bf16[128,1024]{1,0:T(8,128)(2,1)S(1)}, bf16[128,1024]{1,0:T(8,128)(2,1)S(1)}, u32[]{:S(2)}, u32[]{:S(2)}) %collective-permute-start.11) | collective-permute-done | bytes 262176 | tf_op jit(solution)/shard_map/ppermute | solution.py:413
  121.1 8.9 %collective-permute-done.21.out_first = bf16[256,768]{1,0:T(8,128)(2,1)S(1)} collective-permute-done((bf16[256,768]{1,0:T(8,128)(2,1)S(1)}, bf16[256,768]{1,0:T(8,128)(2,1)S(1)}, u32[]{:S(2)}, u32[]{:S(2)}) %collective-permute-start.21) | collective-permute-done | bytes 393248 | tf_op jit(solution)/shard_map/ppermute | solution.py:426
  132.4 9.3 %collective-permute-done.19.other = bf16[128,1408]{1,0:T(8,128)(2,1)S(1)} collective-permute-done((bf16[128,1408]{1,0:T(8,128)(2,1)S(1)}, bf16[128,1408]{1,0:T(8,128)(2,1)S(1)}, u32[]{:S(2)}, u32[]{:S(2)}) %collective-permute-start.19) | collective-permute-done | bytes 360480 | tf_op jit(solution)/shard_map/ppermute | solution.py:430
  141.7 5.4 %collective-permute-done.18.other_second = bf16[128,1408]{1,0:T(8,128)(2,1)S(1)} collective-permute-done((bf16[128,1408]{1,0:T(8,128)(2,1)S(1)}, bf16[128,1408]{1,0:T(8,128)(2,1)S(1)}, u32[]{:S(2)}, u32[]{:S(2)}) %collective-permute-start.18) | collective-permute-done | bytes 360480 | tf_op jit(solution)/shard_map/ppermute | solution.py:430
  147.1 7.7 %mlp.1 = (bf16[512,1024]{1,0:T(8,128)(2,1)}, bf16[512,1024]{1,0:T(8,128)(2,1)}, bf16[512,768]{1,0:T(8,128)(2,1)}, bf16[512,1408]{1,0:T(8,128)(2,1)}, bf16[256,10...) custom-call(s32[512,1]{1,0:T(8,128)S(1)} %copy.22.seg_col, bf16[128,1024]{1,0:T(8,128)(2,1)S(1)} %fusion.16.norm_own, ...), custom_call_target="tpu_custom_call" | custom-call | flops 3758096384 | bytes 13109248 | tf_op jit(solution)/shard_map/mlp/pallas_call | solution.py:692
  161.5 4.6 %mlp_terms.1 = (bf16[512,1408]{1,0:T(8,128)(2,1)}, bf16[256,1408]{1,0:T(8,128)(2,1)S(1)}, bf16[256,1408]{1,0:T(8,128)(2,1)S(1)}, bf16[256,768]{1,0:T(8,128)(2,1)...) custom-call(bf16[512,1024]{1,0:T(8,128)(2,1)S(1)} %copy-done.4, ...), custom_call_target="tpu_custom_call" | custom-call | flops 2281701376 | bytes 8781824 | tf_op jit(solution)/shard_map/mlp_terms/pallas_call | solution.py:692
  172.5 7.3 %collective-permute-done.27 = bf16[256,768]{1,0:T(8,128)(2,1)S(1)} collective-permute-done((bf16[256,768]{1,0:T(8,128)(2,1)S(1)}, bf16[256,768]{1,0:T(8,128)(2,1)S(1)}, u32[]{:S(2)}, u32[]{:S(2)}) %collective-permute-start.27) | collective-permute-done | bytes 393248 | tf_op jit(solution)/shard_map/ppermute | solution.py:422
  179.8 7.3 %collective-permute-done.28 = bf16[256,768]{1,0:T(8,128)(2,1)S(1)} collective-permute-done((bf16[256,768]{1,0:T(8,128)(2,1)S(1)}, bf16[256,768]{1,0:T(8,128)(2,1)S(1)}, u32[]{:S(2)}, u32[]{:S(2)}) %collective-permute-start.28) | collective-permute-done | bytes 393248 | tf_op jit(solution)/shard_map/ppermute | solution.py:426
  189.2 11.4 %collective-permute-done.29 = bf16[256,768]{1,0:T(8,128)(2,1)S(1)} collective-permute-done((bf16[256,768]{1,0:T(8,128)(2,1)S(1)}, bf16[256,768]{1,0:T(8,128)(2,1)S(1)}, u32[]{:S(2)}, u32[]{:S(2)}) %collective-permute-start.29) | collective-permute-done | bytes 393248 | tf_op jit(solution)/shard_map/ppermute | solution.py:422
  201.7 9.3 %attention_backward.1 = (bf16[512,768]{1,0:T(8,128)(2,1)S(1)}, bf16[512,1024]{1,0:T(8,128)(2,1)S(1)}, bf16[256,1024]{1,0:T(8,128)(2,1)S(1)}, bf16[256,1024]{1,0:T(8,128)(2,1)}) custom-call(s32[2]{0:T(128)S(1)} %pad_add_fusion.place, f32[512,128]{1,0:T(8,128)S(1)} %pad_maximum_fusion.8.cosine, f32[512,128]{1,0:T(8,128)S(1)} %pad_maximum_fusion.9.sine, ...), custom_call_target="tpu_custom_call" | custom-call | flops 1677721600 | bytes 8126472 | tf_op jit(solution)/shard_map/attention_backward/pallas_call | solution.py:692
  213.3 3.9 %collective-permute-start.38 = (bf16[128,1408]{1,0:T(8,128)(2,1)S(1)}, bf16[128,1408]{1,0:T(8,128)(2,1)S(1)}, u32[]{:S(2)}, u32[]{:S(2)}) collective-permute-start(bf16[128,1408]{1,0:T(8,128)(2,1)S(1)} %get-tuple-element.172), channel_id=1, source_target_pairs={{0,24},{4,28},{8,0},{12,4},{16,8},{20,12},{24,16},{28,20},{1,25},{... | collective-permute-start | bytes 1081352 | tf_op jit(solution)/shard_map/ppermute | solution.py:426
  217.2 3.2 %projections.1 = (bf16[512,1024]{1,0:T(8,128)(2,1)S(1)}, bf16[512,1024]{1,0:T(8,128)(2,1)S(1)}) custom-call(bf16[512,768]{1,0:T(8,128)(2,1)S(1)} %get-tuple-element.104.grad_packed, bf16[1024,768]{1,0:T(8,128)(2,1)} %get-tuple-element.105.qkv, bf16[512,768]{1,0:T(8,128)(2,1)S(1)} %copy-done.3, bf16[256,768]{1,0:T(8,128)(2,1)S(1)} %collective-permute-done.21.out_first, ...), custom_call_target="tpu_custom_call" | custom-call | flops 1610612736 | bytes 6815744 | tf_op jit(solution)/shard_map/projections/pallas_call | solution.py:692
  220.6 15.2 %collective-permute-done.34 = bf16[256,1024]{1,0:T(8,128)(2,1)S(1)} collective-permute-done((bf16[256,1024]{1,0:T(8,128)(2,1)S(1)}, bf16[256,1024]{1,0:T(8,128)(2,1)S(1)}, u32[]{:S(2)}, u32[]{:S(2)}) %collective-permute-start.34) | collective-permute-done | bytes 524320 | tf_op jit(solution)/shard_map/ppermute | solution.py:430
  237.7 4.2 %all-to-all-start.3 = ((bf16[4,32,2176]{2,1,0:T(8,128)(2,1)}), bf16[4,32,2176]{2,1,0:T(8,128)(2,1)}, u32[]{:S(2)}, u32[]{:S(2)}) async-start(bf16[4,32,2176]{2,1,0:T(8,128)(2,1)} %bitcast.30), calls=%async_computation.3 | async-start | bytes 1114112 | tf_op jit(solution)/shard_map/all_to_all | solution.py:418
  241.9 3.5 %collective-permute-done.39 = bf16[128,1024]{1,0:T(8,128)(2,1)S(1)} collective-permute-done((bf16[128,1024]{1,0:T(8,128)(2,1)}, bf16[128,1024]{1,0:T(8,128)(2,1)S(1)}, u32[]{:S(2)}, u32[]{:S(2)}) %collective-permute-start.39) | collective-permute-done | bytes 262176 | tf_op jit(solution)/shard_map/ppermute | solution.py:422
  247.4 3.8 %collective-permute-start.41 = (bf16[128,1024]{1,0:T(8,128)(2,1)}, bf16[128,1024]{1,0:T(8,128)(2,1)}, u32[]{:S(2)}, u32[]{:S(2)}) collective-permute-start(bf16[128,1024]{1,0:T(8,128)(2,1)} %get-tuple-element.177), channel_id=1, source_target_pairs={{0,24},{4,28},{8,0},{12,4},{16,8},{20,12},{24,16},{28,20},{1,25},{... | collective-permute-start | bytes 786440 | tf_op jit(solution)/shard_map/ppermute | solution.py:426
  256.0 2.3 collective-permute-done.40
  258.3 2.6 collective-permute-done.41
  262.9 3.4 %all-to-all-start.2 = ((bf16[4,32,768]{2,1,0:T(8,128)(2,1)}), bf16[4,32,768]{2,1,0:T(8,128)(2,1)S(1)}, u32[]{:S(2)}, u32[]{:S(2)}) async-start(bf16[4,32,768]{2,1,0:T(8,128)(2,1)} %bitcast.9), calls=%async_computation.2 | async-start | bytes 393216 | tf_op jit(solution)/shard_map/all_to_all | solution.py:418
  (259 shorter events, 74.7 us)
Async XLA Ops:
  0.7 14.1 %collective-permute-start = (bf16[32,1024]{1,0:T(8,128)(2,1)}, bf16[32,1024]{1,0:T(8,128)(2,1)S(1)}, u32[]{:S(2)}, u32[]{:S(2)}) collective-permute-start(bf16[32,1024]{1,0:T(8,128)(2,1)} %param.14), channel_id=1, source_target_pairs={{0,0},{1,4},{2,8},{3,12},{4,16},{5,20},{6,24},{7,28},{8,1},{9,5},{... | collective-permute-start | bytes 196616 | tf_op jit(solution)/shard_map/ppermute | solution.py:741
  17.3 14.5 %collective-permute-start.1 = (bf16[272,1024]{1,0:T(8,128)(2,1)S(1)}, bf16[272,1024]{1,0:T(8,128)(2,1)S(1)}, u32[]{:S(2)}, u32[]{:S(2)}) collective-permute-start(bf16[272,1024]{1,0:T(8,128)(2,1)S(1)} %fusion.7.mine), channel_id=1, source_target_pairs={{0,2},{1,3},{2,0},{3,1},{4,6},{5,7},{6,4},{7,5},{8,10},{9,11},{10,... | collective-permute-start | bytes 1671176 | tf_op jit(solution)/shard_map/ppermute | solution.py:413
  32.9 27.4 %collective-permute-start.2 = (bf16[544,1024]{1,0:T(8,128)(2,1)}, bf16[544,1024]{1,0:T(8,128)(2,1)}, u32[]{:S(2)}, u32[]{:S(2)}) collective-permute-start(bf16[544,1024]{1,0:T(8,128)(2,1)} %pad_maximum_fusion), channel_id=1, source_target_pairs={{0,1},{1,0},{2,3},{3,2},{4,5},{5,4},{6,7},{7,6},{8,9},{9,8},{10,11... | collective-permute-start | bytes 3342344 | tf_op jit(solution)/shard_map/ppermute | solution.py:413
  36.7 13.2 %collective-permute-start.3 = (bf16[128,1024]{1,0:T(8,128)(2,1)S(1)}, bf16[128,1024]{1,0:T(8,128)(2,1)S(1)}, u32[]{:S(2)}, u32[]{:S(2)}) collective-permute-start(bf16[128,1024]{1,0:T(8,128)(2,1)S(1)} %maximum_maximum_fusion.own), channel_id=1, source_target_pairs={{0,8},{4,12},{8,16},{12,20},{16,24},{20,28},{24,0},{28,4},{1,9},{5... | collective-permute-start | bytes 786440 | tf_op jit(solution)/shard_map/ppermute | solution.py:422
  37.3 14.8 %all-to-all-start.1 = ((bf16[4,32,2176]{2,1,0:T(8,128)(2,1)}), bf16[4,32,2176]{2,1,0:T(8,128)(2,1)S(1)}, u32[]{:S(2)}, u32[]{:S(2)}) async-start(bf16[4,32,2176]{2,1,0:T(8,128)(2,1)} %bitcast.7), calls=%async_computation.1 | async-start | bytes 1114112 | tf_op jit(solution)/shard_map/all_to_all | solution.py:418
  51.7 18.8 %collective-permute-start.7 = (bf16[256,1024]{1,0:T(8,128)(2,1)}, bf16[256,1024]{1,0:T(8,128)(2,1)S(1)}, u32[]{:S(2)}, u32[]{:S(2)}) collective-permute-start(bf16[256,1024]{1,0:T(8,128)(2,1)} %pad_maximum_fusion.4), channel_id=1, source_target_pairs={{0,4},{4,0},{8,12},{12,8},{16,20},{20,16},{24,28},{28,24},{1,5},{5... | collective-permute-start | bytes 1572872 | tf_op jit(solution)/shard_map/ppermute | solution.py:430
  79.8 21.5 %collective-permute-start.9 = (bf16[256,1024]{1,0:T(8,128)(2,1)S(1)}, bf16[256,1024]{1,0:T(8,128)(2,1)S(1)}, u32[]{:S(2)}, u32[]{:S(2)}) collective-permute-start(bf16[256,1024]{1,0:T(8,128)(2,1)S(1)} %get-tuple-element.74), channel_id=1, source_target_pairs={{0,1},{1,0},{2,3},{3,2},{4,5},{5,4},{6,7},{7,6},{8,9},{9,8},{10,11... | collective-permute-start | bytes 1572872 | tf_op jit(solution)/shard_map/ppermute | solution.py:413
  82.6 16.8 %collective-permute-start.13 = (bf16[128,1408]{1,0:T(8,128)(2,1)S(1)}, bf16[128,1408]{1,0:T(8,128)(2,1)S(1)}, u32[]{:S(2)}, u32[]{:S(2)}) collective-permute-start(bf16[128,1408]{1,0:T(8,128)(2,1)S(1)} %slice.718.own), channel_id=1, source_target_pairs={{0,8},{4,12},{8,16},{12,20},{16,24},{20,28},{24,0},{28,4},{1,9},{5... | collective-permute-start | bytes 1081352 | tf_op jit(solution)/shard_map/ppermute | solution.py:422
  82.8 19.2 %collective-permute-start.16 = (bf16[128,768]{1,0:T(8,128)(2,1)S(1)}, bf16[128,768]{1,0:T(8,128)(2,1)S(1)}, u32[]{:S(2)}, u32[]{:S(2)}) collective-permute-start(bf16[128,768]{1,0:T(8,128)(2,1)S(1)} %copy-done.16), channel_id=1, source_target_pairs={{0,4},{4,0},{8,12},{12,8},{16,20},{20,16},{24,28},{28,24},{1,5},{5... | collective-permute-start | bytes 589832 | tf_op jit(solution)/shard_map/ppermute | solution.py:430
  111.5 18.5 %collective-permute-start.21 = (bf16[256,768]{1,0:T(8,128)(2,1)S(1)}, bf16[256,768]{1,0:T(8,128)(2,1)S(1)}, u32[]{:S(2)}, u32[]{:S(2)}) collective-permute-start(bf16[256,768]{1,0:T(8,128)(2,1)S(1)} %pad_maximum_fusion.7.out_own), channel_id=1, source_target_pairs={{0,24},{4,28},{8,0},{12,4},{16,8},{20,12},{24,16},{28,20},{1,25},{... | collective-permute-start | bytes 1179656 | tf_op jit(solution)/shard_map/ppermute | solution.py:426
  111.5 18.5 %collective-permute-start.20 = (bf16[256,768]{1,0:T(8,128)(2,1)S(1)}, bf16[256,768]{1,0:T(8,128)(2,1)S(1)}, u32[]{:S(2)}, u32[]{:S(2)}) collective-permute-start(bf16[256,768]{1,0:T(8,128)(2,1)S(1)} %pad_maximum_fusion.7.out_own), channel_id=1, source_target_pairs={{0,8},{4,12},{8,16},{12,20},{16,24},{20,28},{24,0},{28,4},{1,9},{5... | collective-permute-start | bytes 1179656 | tf_op jit(solution)/shard_map/ppermute | solution.py:422
  114.9 26.8 %collective-permute-start.17 = (bf16[256,1408]{1,0:T(8,128)(2,1)S(1)}, bf16[256,1408]{1,0:T(8,128)(2,1)S(1)}, u32[]{:S(2)}, u32[]{:S(2)}) collective-permute-start(bf16[256,1408]{1,0:T(8,128)(2,1)S(1)} %pad_maximum_fusion.1), channel_id=1, source_target_pairs={{0,4},{4,0},{8,12},{12,8},{16,20},{20,16},{24,28},{28,24},{1,5},{5... | collective-permute-start | bytes 2162696 | tf_op jit(solution)/shard_map/ppermute | solution.py:430
  121.0 26.1 %collective-permute-start.12 = (bf16[256,1024]{1,0:T(8,128)(2,1)S(1)}, bf16[256,1024]{1,0:T(8,128)(2,1)S(1)}, u32[]{:S(2)}, u32[]{:S(2)}) collective-permute-start(bf16[256,1024]{1,0:T(8,128)(2,1)S(1)} %pad_maximum_fusion.5), channel_id=1, source_target_pairs={{0,1},{1,0},{2,3},{3,2},{4,5},{5,4},{6,7},{7,6},{8,9},{9,8},{10,11... | collective-permute-start | bytes 1572872 | tf_op jit(solution)/shard_map/ppermute | solution.py:413
  130.0 17.0 %collective-permute-start.22 = (bf16[256,768]{1,0:T(8,128)(2,1)S(1)}, bf16[256,768]{1,0:T(8,128)(2,1)S(1)}, u32[]{:S(2)}, u32[]{:S(2)}) collective-permute-start(bf16[256,768]{1,0:T(8,128)(2,1)S(1)} %collective-permute-done.20.out_third), channel_id=1, source_target_pairs={{0,8},{4,12},{8,16},{12,20},{16,24},{20,28},{24,0},{28,4},{1,9},{5... | collective-permute-start | bytes 1179656 | tf_op jit(solution)/shard_map/ppermute | solution.py:422
  130.7 16.4 %collective-permute-start.18 = (bf16[128,1408]{1,0:T(8,128)(2,1)S(1)}, bf16[128,1408]{1,0:T(8,128)(2,1)S(1)}, u32[]{:S(2)}, u32[]{:S(2)}) collective-permute-start(bf16[128,1408]{1,0:T(8,128)(2,1)S(1)} %collective-permute-done.15.second), channel_id=1, source_target_pairs={{0,4},{4,0},{8,12},{12,8},{16,20},{20,16},{24,28},{28,24},{1,5},{5... | collective-permute-start | bytes 1081352 | tf_op jit(solution)/shard_map/ppermute | solution.py:430
  156.7 13.1 %collective-permute-start.24 = (bf16[128,1024]{1,0:T(8,128)(2,1)S(1)}, bf16[128,1024]{1,0:T(8,128)(2,1)S(1)}, u32[]{:S(2)}, u32[]{:S(2)}) collective-permute-start(bf16[128,1024]{1,0:T(8,128)(2,1)S(1)} %add_convert_fusion.10), channel_id=1, source_target_pairs={{0,2},{1,3},{2,0},{3,1},{4,6},{5,7},{6,4},{7,5},{8,10},{9,11},{10,... | collective-permute-start | bytes 786440 | tf_op jit(solution)/shard_map/ppermute | solution.py:413
  166.0 13.8 %collective-permute-start.27 = (bf16[256,768]{1,0:T(8,128)(2,1)S(1)}, bf16[256,768]{1,0:T(8,128)(2,1)S(1)}, u32[]{:S(2)}, u32[]{:S(2)}) collective-permute-start(bf16[256,768]{1,0:T(8,128)(2,1)S(1)} %get-tuple-element.93), channel_id=1, source_target_pairs={{0,8},{4,12},{8,16},{12,20},{16,24},{20,28},{24,0},{28,4},{1,9},{5... | collective-permute-start | bytes 1179656 | tf_op jit(solution)/shard_map/ppermute | solution.py:422
  168.1 19.0 %collective-permute-start.28 = (bf16[256,768]{1,0:T(8,128)(2,1)S(1)}, bf16[256,768]{1,0:T(8,128)(2,1)S(1)}, u32[]{:S(2)}, u32[]{:S(2)}) collective-permute-start(bf16[256,768]{1,0:T(8,128)(2,1)S(1)} %get-tuple-element.94), channel_id=1, source_target_pairs={{0,24},{4,28},{8,0},{12,4},{16,8},{20,12},{24,16},{28,20},{1,25},{... | collective-permute-start | bytes 1179656 | tf_op jit(solution)/shard_map/ppermute | solution.py:426
  171.2 15.9 %collective-permute-start.25 = (bf16[128,1024]{1,0:T(8,128)(2,1)S(1)}, bf16[128,1024]{1,0:T(8,128)(2,1)S(1)}, u32[]{:S(2)}, u32[]{:S(2)}) collective-permute-start(bf16[128,1024]{1,0:T(8,128)(2,1)S(1)} %get-tuple-element.148.low_own), channel_id=1, source_target_pairs={{0,2},{1,3},{2,0},{3,1},{4,6},{5,7},{6,4},{7,5},{8,10},{9,11},{10,... | collective-permute-start | bytes 786440 | tf_op jit(solution)/shard_map/ppermute | solution.py:413
  172.2 17.1 %collective-permute-start.26 = (bf16[256,1408]{1,0:T(8,128)(2,1)S(1)}, bf16[256,1408]{1,0:T(8,128)(2,1)S(1)}, u32[]{:S(2)}, u32[]{:S(2)}) collective-permute-start(bf16[256,1408]{1,0:T(8,128)(2,1)S(1)} %get-tuple-element.91), channel_id=1, source_target_pairs={{0,4},{4,0},{8,12},{12,8},{16,20},{20,16},{24,28},{28,24},{1,5},{5... | collective-permute-start | bytes 2162696 | tf_op jit(solution)/shard_map/ppermute | solution.py:430
  187.1 13.5 %collective-permute-start.30 = (bf16[256,1024]{1,0:T(8,128)(2,1)S(1)}, bf16[256,1024]{1,0:T(8,128)(2,1)S(1)}, u32[]{:S(2)}, u32[]{:S(2)}) collective-permute-start(bf16[256,1024]{1,0:T(8,128)(2,1)S(1)} %pad_maximum_fusion.6), channel_id=1, source_target_pairs={{0,1},{1,0},{2,3},{3,2},{4,5},{5,4},{6,7},{7,6},{8,9},{9,8},{10,11... | collective-permute-start | bytes 1572872 | tf_op jit(solution)/shard_map/ppermute | solution.py:413
  187.3 13.4 %collective-permute-start.29 = (bf16[256,768]{1,0:T(8,128)(2,1)S(1)}, bf16[256,768]{1,0:T(8,128)(2,1)S(1)}, u32[]{:S(2)}, u32[]{:S(2)}) collective-permute-start(bf16[256,768]{1,0:T(8,128)(2,1)S(1)} %add_convert_fusion.1), channel_id=1, source_target_pairs={{0,8},{4,12},{8,16},{12,20},{16,24},{20,28},{24,0},{28,4},{1,9},{5... | collective-permute-start | bytes 1179656 | tf_op jit(solution)/shard_map/ppermute | solution.py:422
  187.7 25.4 %collective-permute-start.35 = (bf16[256,1408]{1,0:T(8,128)(2,1)S(1)}, bf16[256,1408]{1,0:T(8,128)(2,1)S(1)}, u32[]{:S(2)}, u32[]{:S(2)}) collective-permute-start(bf16[256,1408]{1,0:T(8,128)(2,1)S(1)} %get-tuple-element.113), channel_id=1, source_target_pairs={{0,4},{4,0},{8,12},{12,8},{16,20},{20,16},{24,28},{28,24},{1,5},{5... | collective-permute-start | bytes 2162696 | tf_op jit(solution)/shard_map/ppermute | solution.py:430
  201.2 19.2 %collective-permute-start.43 = (bf16[128,768]{1,0:T(8,128)(2,1)S(1)}, bf16[128,768]{1,0:T(8,128)(2,1)S(1)}, u32[]{:S(2)}, u32[]{:S(2)}) collective-permute-start(bf16[128,768]{1,0:T(8,128)(2,1)S(1)} %slice.934), channel_id=1, source_target_pairs={{0,4},{4,0},{8,12},{12,8},{16,20},{20,16},{24,28},{28,24},{1,5},{5... | collective-permute-start | bytes 589832 | tf_op jit(solution)/shard_map/ppermute | solution.py:430
  211.1 30.8 %collective-permute-start.33 = (bf16[256,1024]{1,0:T(8,128)(2,1)}, bf16[256,1024]{1,0:T(8,128)(2,1)}, u32[]{:S(2)}, u32[]{:S(2)}) collective-permute-start(bf16[256,1024]{1,0:T(8,128)(2,1)} %get-tuple-element.109), channel_id=1, source_target_pairs={{0,4},{4,0},{8,12},{12,8},{16,20},{20,16},{24,28},{28,24},{1,5},{5... | collective-permute-start | bytes 1572872 | tf_op jit(solution)/shard_map/ppermute | solution.py:430
  212.7 23.1 %collective-permute-start.34 = (bf16[256,1024]{1,0:T(8,128)(2,1)S(1)}, bf16[256,1024]{1,0:T(8,128)(2,1)S(1)}, u32[]{:S(2)}, u32[]{:S(2)}) collective-permute-start(bf16[256,1024]{1,0:T(8,128)(2,1)S(1)} %get-tuple-element.110), channel_id=1, source_target_pairs={{0,4},{4,0},{8,12},{12,8},{16,20},{20,16},{24,28},{28,24},{1,5},{5... | collective-permute-start | bytes 1572872 | tf_op jit(solution)/shard_map/ppermute | solution.py:430
  213.3 22.5 %collective-permute-start.38 = (bf16[128,1408]{1,0:T(8,128)(2,1)S(1)}, bf16[128,1408]{1,0:T(8,128)(2,1)S(1)}, u32[]{:S(2)}, u32[]{:S(2)}) collective-permute-start(bf16[128,1408]{1,0:T(8,128)(2,1)S(1)} %get-tuple-element.172), channel_id=1, source_target_pairs={{0,24},{4,28},{8,0},{12,4},{16,8},{20,12},{24,16},{28,20},{1,25},{... | collective-permute-start | bytes 1081352 | tf_op jit(solution)/shard_map/ppermute | solution.py:426
  217.2 18.6 %collective-permute-start.37 = (bf16[128,1408]{1,0:T(8,128)(2,1)S(1)}, bf16[128,1408]{1,0:T(8,128)(2,1)S(1)}, u32[]{:S(2)}, u32[]{:S(2)}) collective-permute-start(bf16[128,1408]{1,0:T(8,128)(2,1)S(1)} %get-tuple-element.173), channel_id=1, source_target_pairs={{0,8},{4,12},{8,16},{12,20},{16,24},{20,28},{24,0},{28,4},{1,9},{5... | collective-permute-start | bytes 1081352 | tf_op jit(solution)/shard_map/ppermute | solution.py:422
  220.4 30.8 %collective-permute-start.31 = (bf16[512,1024]{1,0:T(8,128)(2,1)S(1)}, bf16[512,1024]{1,0:T(8,128)(2,1)}, u32[]{:S(2)}, u32[]{:S(2)}) collective-permute-start(bf16[512,1024]{1,0:T(8,128)(2,1)S(1)} %get-tuple-element.107), channel_id=1, source_target_pairs={{0,1},{1,0},{2,3},{3,2},{4,5},{5,4},{6,7},{7,6},{8,9},{9,8},{10,11... | collective-permute-start | bytes 3145736 | tf_op jit(solution)/shard_map/ppermute | solution.py:413
  237.7 16.5 %all-to-all-start.3 = ((bf16[4,32,2176]{2,1,0:T(8,128)(2,1)}), bf16[4,32,2176]{2,1,0:T(8,128)(2,1)}, u32[]{:S(2)}, u32[]{:S(2)}) async-start(bf16[4,32,2176]{2,1,0:T(8,128)(2,1)} %bitcast.30), calls=%async_computation.3 | async-start | bytes 1114112 | tf_op jit(solution)/shard_map/all_to_all | solution.py:418
  247.4 13.5 %collective-permute-start.41 = (bf16[128,1024]{1,0:T(8,128)(2,1)}, bf16[128,1024]{1,0:T(8,128)(2,1)}, u32[]{:S(2)}, u32[]{:S(2)}) collective-permute-start(bf16[128,1024]{1,0:T(8,128)(2,1)} %get-tuple-element.177), channel_id=1, source_target_pairs={{0,24},{4,28},{8,0},{12,4},{16,8},{20,12},{24,16},{28,20},{1,25},{... | collective-permute-start | bytes 786440 | tf_op jit(solution)/shard_map/ppermute | solution.py:426
  253.3 20.0 %collective-permute-start.32 = (bf16[256,1024]{1,0:T(8,128)(2,1)}, bf16[256,1024]{1,0:T(8,128)(2,1)}, u32[]{:S(2)}, u32[]{:S(2)}) collective-permute-start(bf16[256,1024]{1,0:T(8,128)(2,1)} %add_convert_fusion), channel_id=1, source_target_pairs={{0,2},{1,3},{2,0},{3,1},{4,6},{5,7},{6,4},{7,5},{8,10},{9,11},{10,... | collective-permute-start | bytes 1572872 | tf_op jit(solution)/shard_map/ppermute | solution.py:413
  (40 other events, 435.0 us)

commit v4 on v3

--- a/solution.py
+++ b/solution.py
@@ -541,21 +541,15 @@
 
 def mlp(
     seg_col, norm_own, norm_across, norm_beside, mine, across, beside,
-    first, second, third, own, others, other_second, other,
-    out_first, out_second, out_third, out_own,
-    normed, grad_out, mixed, grad_inner, send, keep,
-    w_up, w_down, inner, grad_mixed,
+    first, second, third, own, other_first, other_second, other_third, other,
+    normed, grad_out, mixed, grad_inner, send, keep, w_down,
+    w_up, inner, grad_mixed,
 ):
-    size, count = own.shape[0], 128
-    blocks = [
-        (first, 0), (second, 0), (third, 0), (own, 0),
-        (others, 0), (other_second, 0), (others, size), (other, 0),
-    ]
-    for at, (ref, row) in enumerate(blocks):
-        w_up[size * at : size * (at + 1), :] = ref[row : row + size, :]
-    for at, ref in enumerate((out_first, out_second, out_third, out_own)):
-        w_down[size * at : size * (at + 1), :] = ref[:size, :]
-        w_down[size * (at + 4) : size * (at + 5), :] = ref[size:, :]
+    size, count, edge = own.shape[0], 128, w_up.shape[1]
+    blocks = (first, second, third, own, other_first, other_second, other_third, other)
+    for at, ref in enumerate(blocks):
+        w_up[size * at : size * (at + 1), :] = ref[:, :edge]
+        w_down[size * at : size * (at + 1), :] = ref[:, edge:]
     for at, ref in enumerate(
         (norm_own[...], norm_beside[:count, :], norm_across[...], norm_beside[count:, :])
     ):
@@ -668,13 +662,8 @@
                 ] = term_attn[pl.ds(source, part), pl.ds(lanes, LANES)]
 
 
-def projections(
-    grad_packed, qkv, mixed, out_first, out_second, out_third, out_own, send, keep, w_down
-):
-    size, count = out_own.shape[0] // 2, 128
-    for at, ref in enumerate((out_first, out_second, out_third, out_own)):
-        w_down[size * at : size * (at + 1), :] = ref[:size, :]
-        w_down[size * (at + 4) : size * (at + 5), :] = ref[size:, :]
+def projections(grad_packed, qkv, mixed, w_down, send, keep):
+    count = 128
     for row, total in (
         (0, low(matmul_right_t(grad_packed[...], qkv[...]))),
         (count, low(matmul_right_t(mixed[...], w_down[...]))),
@@ -740,8 +729,16 @@
     order = [(k, (k % 8) * 4 + k // 8) for k in range(32)]
     attn_own = lax.ppermute(w_attn_out, AXES, order)
     qkv_parts = split_columns(low(wide(w_qkv) * gain_attn), 12)
-    qkv_own = rep_exchange(rows([columns(qkv_parts[k::4]) for k in range(4)]))
-    first_own = columns([qkv_own, rows(split_columns(attn_own, 4))])
+    size = w_qkv.shape[0]
+    slots = seq_lengths.shape[1]
+    lengths_low = jnp.pad(low(wide(seq_lengths)), ((0, size - 1), (0, LANES - slots)))
+    exchanged = rep_exchange(rows([columns([*qkv_parts[k::4], lengths_low]) for k in range(4)]))
+    first_own = columns([exchanged[:, :768], rows(split_columns(attn_own, 4))])
+    lengths = rows([exchanged[size * k : size * k + 1, 768 : 768 + slots] for k in range(4)])
+    lengths = wide(lengths).astype(jnp.int32)
+    for bit in (1, 2):
+        turned_rows = rows([lengths[k ^ bit : (k ^ bit) + 1] for k in range(4)])
+        lengths = jnp.where((lax.axis_index("rep") & bit) != 0, turned_rows, lengths)
 
     scaled_in = low(wide(w_in) * gain_mlp)
     pieces = []
@@ -756,27 +753,21 @@
                 + [out_part, fill[1]]
             )
         )
-    lengths_row = jnp.pad(low(wide(seq_lengths)), ((0, 15), (0, width - seq_lengths.shape[1])))
-    mine = rows([relative(tokens, z, x), relative(cotangent, z, x), lengths_row])
+    mine = rows([relative(tokens, z, x), relative(cotangent, z, x)])
     first_own, rest, mine = tie(first_own, rows(pieces), mine)
     rest = rep_exchange(rest)
-    in_own, out_own = rest[:, :in_width], rest[:, in_width:]
+
+    third, first, other = up(first_own), down(first_own), over(first_own)
+    third, first, other, mine = tie(third, first, other, mine)
     across = swap(mine, 2)
-
-    third, first, other = up(first_own), down(first_own), over(first_own)
-    third, first, other = tie(third, first, other)
     second, others = up(third), over(rows([first, third]))
+    second, others, across, rest = tie(second, others, across, rest)
+    other_second = over(second)
+    rest_third, rest_first = up(rest), down(rest)
     beside = swap(rows([mine, across]), 1)
-    second, in_own, out_own = tie(second, in_own, out_own)
-    other_second = over(second)
-    in_third, in_first = up(in_own), down(in_own)
-    out_pair = rows([out_own, over(tie(out_own, others)[0])])
+    rest_other = over(tie(rest, other_second, beside)[0])
 
     step = mine.shape[0]
-    lengths = rows(
-        [mine[2 * count : 2 * count + 1], beside[2 * count : 2 * count + 1]]
-        + [across[2 * count : 2 * count + 1], beside[step + 2 * count : step + 2 * count + 1]]
-    )[:, : seq_lengths.shape[1]].astype(jnp.int32)
     segment, positions, _ = jax.vmap(lambda row: layout(row, count))(lengths)
     frequency = rope_base ** (-(lax.iota(f32, HALF) * (2.0 / HEAD_DIM)))
     angles = positions.reshape(group, 1).astype(f32) * frequency
@@ -795,34 +786,31 @@
         first, second, third, first_own, others, other_second, other,
         scalars=1,
     )
-    in_third, in_first, _ = tie(in_third, in_first, send)
-    in_second, in_others = up(in_third), over(rows([in_first, in_third]))
-    in_other = over(tie(in_own, send)[0])
+    rest_third, rest_first, rest_other, send = tie(rest_third, rest_first, rest_other, send)
+    rest_second, rest_other_third = up(rest_third), over(rest_third)
     x_own = wide(mine[:count])
     kept, sent = scatter_last(send, keep)
-    in_second, out_pair, _ = tie(in_second, out_pair, sent)
-    in_other_second = over(in_second)
-    out_third, out_first = up(out_pair), down(out_pair)
+    rest_other_first = over(tie(rest_first, rest_other_third)[0])
     hidden_sum = x_own + kept + wide(swap(sent, 2))
     standard_mlp, inverse_mlp = norm_statistics(hidden_sum)
     norm_own = low(standard_mlp)
     norm_across = swap(norm_own, 2)
-    out_third, out_first, _ = tie(out_third, out_first, norm_own)
-    out_second = up(out_third)
+    rest_second, rest_other_third, _ = tie(rest_second, rest_other_third, norm_own)
+    rest_other_second = up(rest_other_third)
     norm_beside = swap(rows([norm_own, norm_across]), 1)
 
-    normed_mlp, grad_out, mixed, grad_inner, send, keep = kernel(
+    normed_mlp, grad_out, mixed, grad_inner, send, keep, w_down = kernel(
         mlp,
         [((group, width), b16)] * 2
         + [((group, out_width), b16), ((group, in_width), b16)]
-        + [((2 * count, width), b16)] * 2,
+        + [((2 * count, width), b16)] * 2
+        + [((width, out_width), b16)],
         (2 * group * width * (2 * in_width + out_width), 3 * group * part),
         seg_col, norm_own, norm_across, norm_beside, mine, across, beside,
-        in_first, in_second, in_third, in_own, in_others, in_other_second, in_other,
-        out_first, out_second, out_third, out_pair,
+        rest_first, rest_second, rest_third, rest,
+        rest_other_first, rest_other_second, rest_other_third, rest_other,
         scratch=[
             ((width, in_width), b16),
-            ((width, out_width), b16),
             ((group, in_width), f32),
             ((group, out_width), f32),
         ],
@@ -836,7 +824,7 @@
         normed_mlp, grad_inner, grad_out, mixed,
     )
     out_up, out_down = up(out_terms[1]), down(out_terms[2])
-    in_early, in_late = over(in_early), over(in_late)
+    in_early = over(in_early)
     kept, sent = scatter_last(send, keep)
     scaled_mlp = kept + wide(swap(sent, 2))
     grad_hidden = wide(grad_out[:count]) + norm_backward_pass(
@@ -844,14 +832,12 @@
     )
     low_own = low(grad_hidden)
     low_across = swap(low_own, 2)
-    out_up, out_down, _ = tie(out_up, out_down, low_own)
-    out_turned = up(low(wide(out_terms[0]) + wide(out_up)))
+    in_early, low_across, out_up, out_down = tie(in_early, low_across, out_up, out_down)
+    in_late = over(tie(in_late, in_early)[0])
     low_beside = swap(rows([low_own, low_across]), 1)
-    in_early, out_turned, low_beside = tie(in_early, out_turned, low_beside)
     in_kept, in_first_two = split_rows(in_keep, 4), split_rows(in_early, 2)
     in_up = up(low(wide(in_kept[1]) + wide(in_first_two[1])))
-    out_sums = split_rows(wide(out_terms[3]) + wide(out_turned) + wide(out_down), 2)
-    out_over = over(low(out_sums[1]))
+    out_turned = up(low(wide(out_terms[0]) + wide(out_up)))
 
     grad_packed, g_keep, g_early, g_late = kernel(
         attention_backward,
@@ -862,19 +848,21 @@
         scratch=[((group, width), b16), ((group, 256), b16), ((256, width), b16)],
         scalars=1,
     )
-    g_over_early, g_over_late = over(g_early), over(g_late)
-    in_late, in_up, _ = tie(in_late, in_up, g_keep)
+    g_over_early = over(g_early)
+    in_late, in_up, out_turned, _ = tie(in_late, in_up, out_turned, g_keep)
     in_last_two = split_rows(in_late, 2)
     in_turned = up(low(wide(in_kept[0]) + wide(in_first_two[0]) + wide(in_up)))
     in_down = down(low(wide(in_kept[2]) + wide(in_last_two[0])))
+    out_sums = split_rows(wide(out_terms[3]) + wide(out_turned) + wide(out_down), 2)
     send, keep = kernel(
         projections,
         [((4 * count, width), b16)] * 2,
         (2 * group * width * (768 + out_width), 0),
-        grad_packed, qkv, mixed, out_first, out_second, out_third, out_pair,
-        scratch=[((width, out_width), b16)],
-    )
-    g_over_early, in_turned, in_down = tie(g_over_early, in_turned, in_down)
+        grad_packed, qkv, mixed, w_down,
+    )
+    g_over_early, _ = tie(g_over_early, send)
+    g_over_late = over(tie(g_late, g_over_early)[0])
+    out_over = over(low(out_sums[1]))
     g_kept, g_first_two = split_rows(g_keep, 4), split_rows(g_over_early, 2)
     g_up = up(low(wide(g_kept[1]) + wide(g_first_two[1])))
     sum_in = wide(in_kept[3]) + wide(in_last_two[1]) + wide(in_turned) + wide(in_down)

time: 283 us -> 277 us (0.979); the launches traced: 277 us -> 276 us
  waiting for transfers between devices: 144 us -> 126 us
  starting transfers between devices: 56.4 us -> 64.6 us
  local copies, waits for them, and re-layouts: 13.1 us -> 20.7 us
    ppermute x6 -> x5, waiting for transfers between devices: 28.7 us -> 15 us  [down(): return lax.ppermute(value, 'fsdp', [(k, (k - 2) % 8) for k in range(8)])]
    all_to_all x4, waiting for transfers between devices: 3.95 us -> 15.8 us  [rep_exchange(): return lax.all_to_all(blocks, 'rep', 0, 0, tiled=True).reshape(value.shape)]
    ppermute x12 -> x11, waiting for transfers between devices: 52.7 us -> 42.5 us  [up(): return lax.ppermute(value, 'fsdp', [(k, (k + 2) % 8) for k in range(8)])]
    ppermute x12, starting transfers between devices: 4.74 us -> 9.55 us  [swap(): return lax.ppermute(value, 'rep', [(k, k ^ distance) for k in range(4)])]
    ppermute x12 -> x11, starting transfers between devices: 9.33 us -> 13.2 us  [over(): return lax.ppermute(value, 'fsdp', [(k, k ^ 1) for k in range(8)])]
    ppermute x12 -> x11, waiting for transfers between devices: 36.5 us -> 33.1 us  [over(): return lax.ppermute(value, 'fsdp', [(k, k ^ 1) for k in range(8)])]
    unnamed x59 -> x71, local copies, waits for them, and re-layouts: 6.33 us -> 9.74 us
    slice x5 -> x4, local copies, waits for them, and re-layouts: 3.17 us -> 0.03 us  [the longest x1 0.01 us: local_ring(): first_own = columns([exchanged[:, :768], rows(split_columns(attn_own, 4))])]
  transfers between devices with their start and end apart: 48 -> 45, of which waited for: 24 -> 25; matrix products, arithmetic and copies ran while one was open for 11% -> 12% of each run, Pallas kernels for 6% -> 10%
where the time goes in v4:
time: 277 us; the launch traced here: 276 us
  waiting for transfers between devices  126 us (45%)
  starting transfers between devices  64.6 us (23%)
  Pallas kernels  35.7 us (13%)
  other arithmetic  27 us (10%)
  local copies, waits for them, and re-layouts  20.7 us (7%)
    ppermute x11, waiting for transfers between devices, up(): return lax.ppermute(value, 'fsdp', [(k, (k + 2) % 8) for k in range(8)])  42.5 us
    pallas_call x5, Pallas kernels, kernel(): pl.pallas_call(body, out_shape=shapes, in_specs=[pl.BlockSpec(memory_spac...  35.7 us
    ppermute x11, waiting for transfers between devices, over(): return lax.ppermute(value, 'fsdp', [(k, k ^ 1) for k in range(8)])  33.1 us
    ppermute x12, waiting for transfers between devices, swap(): return lax.ppermute(value, 'rep', [(k, k ^ distance) for k in range(4)])  19.8 us
    all_to_all x4, starting transfers between devices, rep_exchange(): return lax.all_to_all(blocks, 'rep', 0, 0, tiled=True).reshape(value.shape)  18 us
    all_to_all x4, waiting for transfers between devices, rep_exchange(): return lax.all_to_all(blocks, 'rep', 0, 0, tiled=True).reshape(value.shape)  15.8 us
    ppermute x5, waiting for transfers between devices, down(): return lax.ppermute(value, 'fsdp', [(k, (k - 2) % 8) for k in range(8)])  15 us
    ppermute x5, starting transfers between devices, down(): return lax.ppermute(value, 'fsdp', [(k, (k - 2) % 8) for k in range(8)])  13.7 us
  transfers between devices with their start and end apart: 45, of which 25 were waited for; matrix products, arithmetic and copies ran while one was open for 12% of the time, Pallas kernels for 10%

profile of v4, /device:TPU:0, one launch (start us, length us, event | category | flops | bytes accessed | tf_op | source)
XLA Modules:
  0.0 275.6 jit_solution(14817028381628044062)
XLA Ops:
  5.4 6.8 %all-to-all-start = ((bf16[4,32,896]{2,1,0:T(8,128)(2,1)}), bf16[4,32,896]{2,1,0:T(8,128)(2,1)S(1)}, u32[]{:S(2)}, u32[]{:S(2)}) async-start(bf16[4,32,896]{2,1,0:T(8,128)(2,1)} %bitcast), calls=%async_computation | async-start | bytes 458752 | tf_op jit(solution)/shard_map/all_to_all | solution.py:418
  15.0 3.2 %all-to-all-done = bf16[4,32,896]{2,1,0:T(8,128)(2,1)S(1)} async-done(((bf16[4,32,896]{2,1,0:T(8,128)(2,1)}), bf16[4,32,896]{2,1,0:T(8,128)(2,1)S(1)}, u32[]{:S(2)}, u32[]{:S(2)}) %all-to-all-start) | async-done | bytes 229408 | tf_op jit(solution)/shard_map/all_to_all | solution.py:418
  18.3 2.7 collective-permute-start.3
  23.0 4.1 %collective-permute-done.3.other = bf16[128,1024]{1,0:T(8,128)(2,1)S(1)} collective-permute-done((bf16[128,1024]{1,0:T(8,128)(2,1)S(1)}, bf16[128,1024]{1,0:T(8,128)(2,1)S(1)}, u32[]{:S(2)}, u32[]{:S(2)}) %collective-permute-start.3) | collective-permute-done | bytes 262176 | tf_op jit(solution)/shard_map/ppermute | solution.py:430
  27.0 2.6 collective-permute-done.2.first
  29.6 5.0 %collective-permute-done.1.third = bf16[128,1024]{1,0:T(8,128)(2,1)S(1)} collective-permute-done((bf16[128,1024]{1,0:T(8,128)(2,1)S(1)}, bf16[128,1024]{1,0:T(8,128)(2,1)S(1)}, u32[]{:S(2)}, u32[]{:S(2)}) %collective-permute-start.1) | collective-permute-done | bytes 262176 | tf_op jit(solution)/shard_map/ppermute | solution.py:422
  36.6 3.5 %all-to-all-start.1 = ((bf16[4,32,2176]{2,1,0:T(8,128)(2,1)}), bf16[4,32,2176]{2,1,0:T(8,128)(2,1)S(1)}, u32[]{:S(2)}, u32[]{:S(2)}) async-start(bf16[4,32,2176]{2,1,0:T(8,128)(2,1)} %bitcast.7), calls=%async_computation.1 | async-start | bytes 1114112 | tf_op jit(solution)/shard_map/all_to_all | solution.py:418
  41.1 12.6 %all-to-all-done.1 = bf16[4,32,2176]{2,1,0:T(8,128)(2,1)S(1)} async-done(((bf16[4,32,2176]{2,1,0:T(8,128)(2,1)}), bf16[4,32,2176]{2,1,0:T(8,128)(2,1)S(1)}, u32[]{:S(2)}, u32[]{:S(2)}) %all-to-all-start.1) | async-done | bytes 557088 | tf_op jit(solution)/shard_map/all_to_all | solution.py:418
  58.3 4.5 %collective-permute-done.8.other_second = bf16[128,1024]{1,0:T(8,128)(2,1)S(1)} collective-permute-done((bf16[128,1024]{1,0:T(8,128)(2,1)S(1)}, bf16[128,1024]{1,0:T(8,128)(2,1)S(1)}, u32[]{:S(2)}, u32[]{:S(2)}) %collective-permute-start.8) | collective-permute-done | bytes 262176 | tf_op jit(solution)/shard_map/ppermute | solution.py:430
  66.1 9.2 %attention_forward.1 = (bf16[512,1024]{1,0:T(8,128)(2,1)}, bf16[1024,768]{1,0:T(8,128)(2,1)}, bf16[256,1024]{1,0:T(8,128)(2,1)S(1)}, bf16[512,256]{1,0:T(8,128)(...) custom-call(s32[2]{0:T(128)S(1)} %pad_add_fusion.place, ...), custom_call_target="tpu_custom_call" | custom-call | flops 1207959552 | bytes 11014152 | tf_op jit(solution)/shard_map/attention_forward/pallas_call | solution.py:681
  75.3 8.5 %collective-permute-done.9.third = bf16[128,2176]{1,0:T(8,128)(2,1)} collective-permute-done((bf16[128,2176]{1,0:T(8,128)(2,1)S(1)}, bf16[128,2176]{1,0:T(8,128)(2,1)}, u32[]{:S(2)}, u32[]{:S(2)}) %collective-permute-start.9) | collective-permute-done | bytes 557088 | tf_op jit(solution)/shard_map/ppermute | solution.py:422
  88.5 5.8 %collective-permute-done.13 = bf16[128,1024]{1,0:T(8,128)(2,1)S(1)} collective-permute-done((bf16[128,1024]{1,0:T(8,128)(2,1)S(1)}, bf16[128,1024]{1,0:T(8,128)(2,1)S(1)}, u32[]{:S(2)}, u32[]{:S(2)}) %collective-permute-start.13) | collective-permute-done | bytes 262176 | tf_op jit(solution)/shard_map/ppermute | solution.py:413
  95.6 5.7 %collective-permute-done.17.other_third = bf16[128,2176]{1,0:T(8,128)(2,1)S(1)} collective-permute-done((bf16[128,2176]{1,0:T(8,128)(2,1)}, bf16[128,2176]{1,0:T(8,128)(2,1)S(1)}, u32[]{:S(2)}, u32[]{:S(2)}) %collective-permute-start.17) | collective-permute-done | bytes 557088 | tf_op jit(solution)/shard_map/ppermute | solution.py:430
  103.4 11.6 %collective-permute-done.18.other_first = bf16[128,2176]{1,0:T(8,128)(2,1)S(1)} collective-permute-done((bf16[128,2176]{1,0:T(8,128)(2,1)}, bf16[128,2176]{1,0:T(8,128)(2,1)S(1)}, u32[]{:S(2)}, u32[]{:S(2)}) %collective-permute-start.18) | collective-permute-done | bytes 557088 | tf_op jit(solution)/shard_map/ppermute | solution.py:430
  115.0 3.2 %collective-permute-done.19.other_second = bf16[128,2176]{1,0:T(8,128)(2,1)S(1)} collective-permute-done((bf16[128,2176]{1,0:T(8,128)(2,1)S(1)}, bf16[128,2176]{1,0:T(8,128)(2,1)S(1)}, u32[]{:S(2)}, u32[]{:S(2)}) %collective-permute-start.19) | collective-permute-done | bytes 557088 | tf_op jit(solution)/shard_map/ppermute | solution.py:422
  119.1 8.4 %mlp.1 = (bf16[512,1024]{1,0:T(8,128)(2,1)}, bf16[512,1024]{1,0:T(8,128)(2,1)}, bf16[512,768]{1,0:T(8,128)(2,1)}, bf16[512,1408]{1,0:T(8,128)(2,1)}, bf16[256,10...) custom-call(s32[512,1]{1,0:T(8,128)S(1)} %copy.22.seg_col, ...), custom_call_target="tpu_custom_call" | custom-call | flops 3758096384 | bytes 14551040 | tf_op jit(solution)/shard_map/mlp/pallas_call | solution.py:681
  134.4 4.5 %mlp_terms.1 = (bf16[512,1408]{1,0:T(8,128)(2,1)}, bf16[256,1408]{1,0:T(8,128)(2,1)S(1)}, bf16[256,1408]{1,0:T(8,128)(2,1)S(1)}, bf16[256,768]{1,0:T(8,128)(2,1)...) custom-call(bf16[512,1024]{1,0:T(8,128)(2,1)S(1)} %copy-done.6, ...), custom_call_target="tpu_custom_call" | custom-call | flops 2281701376 | bytes 8781824 | tf_op jit(solution)/shard_map/mlp_terms/pallas_call | solution.py:681
  139.0 3.8 %collective-permute-start.25 = (bf16[256,768]{1,0:T(8,128)(2,1)S(1)}, bf16[256,768]{1,0:T(8,128)(2,1)S(1)}, u32[]{:S(2)}, u32[]{:S(2)}) collective-permute-start(bf16[256,768]{1,0:T(8,128)(2,1)S(1)} %get-tuple-element.98), channel_id=1, source_target_pairs={{0,24},{4,28},{8,0},{12,4},{16,8},{20,12},{24,16},{28,20},{1,25},{... | collective-permute-start | bytes 1179656 | tf_op jit(solution)/shard_map/ppermute | solution.py:426
  146.4 6.3 %collective-permute-done.24 = bf16[256,768]{1,0:T(8,128)(2,1)S(1)} collective-permute-done((bf16[256,768]{1,0:T(8,128)(2,1)S(1)}, bf16[256,768]{1,0:T(8,128)(2,1)S(1)}, u32[]{:S(2)}, u32[]{:S(2)}) %collective-permute-start.24) | collective-permute-done | bytes 393248 | tf_op jit(solution)/shard_map/ppermute | solution.py:422
  152.8 5.5 %collective-permute-done.25 = bf16[256,768]{1,0:T(8,128)(2,1)S(1)} collective-permute-done((bf16[256,768]{1,0:T(8,128)(2,1)S(1)}, bf16[256,768]{1,0:T(8,128)(2,1)S(1)}, u32[]{:S(2)}, u32[]{:S(2)}) %collective-permute-start.25) | collective-permute-done | bytes 393248 | tf_op jit(solution)/shard_map/ppermute | solution.py:426
  163.6 9.3 %attention_backward.1 = (bf16[512,768]{1,0:T(8,128)(2,1)S(1)}, bf16[512,1024]{1,0:T(8,128)(2,1)S(1)}, bf16[256,1024]{1,0:T(8,128)(2,1)}, bf16[256,1024]{1,0:T(8,128)(2,1)S(1)}) custom-call(s32[2]{0:T(128)S(1)} %pad_add_fusion.place, f32[512,128]{1,0:T(8,128)S(1)} %get-tuple-element.268.cosine, f32[512,128]{1,0:T(8,128)S(1)} %get-tuple-element.269.sine, ...), custom_call_target="tpu_custom_call" | custom-call | flops 1677721600 | bytes 8126472 | tf_op jit(solution)/shard_map/attention_backward/pallas_call | solution.py:681
  173.0 6.2 %collective-permute-done.36 = bf16[128,1408]{1,0:T(8,128)(2,1)S(1)} collective-permute-done((bf16[128,1408]{1,0:T(8,128)(2,1)S(1)}, bf16[128,1408]{1,0:T(8,128)(2,1)S(1)}, u32[]{:S(2)}, u32[]{:S(2)}) %collective-permute-start.36) | collective-permute-done | bytes 360480 | tf_op jit(solution)/shard_map/ppermute | solution.py:422
  182.3 3.0 %collective-permute-start.39 = (bf16[128,1408]{1,0:T(8,128)(2,1)S(1)}, bf16[128,1408]{1,0:T(8,128)(2,1)S(1)}, u32[]{:S(2)}, u32[]{:S(2)}) collective-permute-start(bf16[128,1408]{1,0:T(8,128)(2,1)S(1)} %get-tuple-element.179), channel_id=1, source_target_pairs={{0,24},{4,28},{8,0},{12,4},{16,8},{20,12},{24,16},{28,20},{1,25},{... | collective-permute-start | bytes 1081352 | tf_op jit(solution)/shard_map/ppermute | solution.py:426
  186.2 8.4 %collective-permute-done.38 = bf16[128,1408]{1,0:T(8,128)(2,1)S(1)} collective-permute-done((bf16[128,1408]{1,0:T(8,128)(2,1)S(1)}, bf16[128,1408]{1,0:T(8,128)(2,1)S(1)}, u32[]{:S(2)}, u32[]{:S(2)}) %collective-permute-start.38) | collective-permute-done | bytes 360480 | tf_op jit(solution)/shard_map/ppermute | solution.py:422
  194.6 4.8 %collective-permute-done.39 = bf16[128,1408]{1,0:T(8,128)(2,1)S(1)} collective-permute-done((bf16[128,1408]{1,0:T(8,128)(2,1)S(1)}, bf16[128,1408]{1,0:T(8,128)(2,1)S(1)}, u32[]{:S(2)}, u32[]{:S(2)}) %collective-permute-start.39) | collective-permute-done | bytes 360480 | tf_op jit(solution)/shard_map/ppermute | solution.py:426
  200.5 4.2 %all-to-all-start.3 = ((bf16[4,32,2176]{2,1,0:T(8,128)(2,1)}), bf16[4,32,2176]{2,1,0:T(8,128)(2,1)}, u32[]{:S(2)}, u32[]{:S(2)}) async-start(bf16[4,32,2176]{2,1,0:T(8,128)(2,1)} %bitcast.14), calls=%async_computation.3 | async-start | bytes 1114112 | tf_op jit(solution)/shard_map/all_to_all | solution.py:418
  208.8 4.2 %projections.1 = (bf16[512,1024]{1,0:T(8,128)(2,1)}, bf16[512,1024]{1,0:T(8,128)(2,1)S(1)}) custom-call(bf16[512,768]{1,0:T(8,128)(2,1)S(1)} %copy-done.3, bf16[1024,768]{1,0:T(8,128)(2,1)S(1)} %copy-done.1, bf16[512,768]{1,0:T(8,128)(2,1)S(1)} %copy-done.5, bf16[1024,768]{1,0:T(8,128)(2,1)} %get-tuple-element.109.w_down), custom_call_target="tpu_custom_call" | custom-call | flops 1610612736 | bytes 6815744 | tf_op jit(solution)/shard_map/projections/pallas_call | solution.py:681
  225.5 5.2 %collective-permute-done.30 = bf16[256,1024]{1,0:T(8,128)(2,1)} collective-permute-done((bf16[256,1024]{1,0:T(8,128)(2,1)S(1)}, bf16[256,1024]{1,0:T(8,128)(2,1)}, u32[]{:S(2)}, u32[]{:S(2)}) %collective-permute-start.30) | collective-permute-done | bytes 524320 | tf_op jit(solution)/shard_map/ppermute | solution.py:430
  233.4 3.2 %collective-permute-start.33 = (bf16[128,1024]{1,0:T(8,128)(2,1)}, bf16[128,1024]{1,0:T(8,128)(2,1)}, u32[]{:S(2)}, u32[]{:S(2)}) collective-permute-start(bf16[128,1024]{1,0:T(8,128)(2,1)} %get-tuple-element.181), channel_id=1, source_target_pairs={{0,24},{4,28},{8,0},{12,4},{16,8},{20,12},{24,16},{28,20},{1,25},{... | collective-permute-start | bytes 786440 | tf_op jit(solution)/shard_map/ppermute | solution.py:426
  248.1 3.6 %all-to-all-start.2 = ((bf16[4,32,768]{2,1,0:T(8,128)(2,1)}), bf16[4,32,768]{2,1,0:T(8,128)(2,1)S(1)}, u32[]{:S(2)}, u32[]{:S(2)}) async-start(bf16[4,32,768]{2,1,0:T(8,128)(2,1)} %bitcast.9), calls=%async_computation.2 | async-start | bytes 393216 | tf_op jit(solution)/shard_map/all_to_all | solution.py:418
  254.5 4.8 %collective-permute-start.28 = (bf16[256,1024]{1,0:T(8,128)(2,1)}, bf16[256,1024]{1,0:T(8,128)(2,1)S(1)}, u32[]{:S(2)}, u32[]{:S(2)}) collective-permute-start(bf16[256,1024]{1,0:T(8,128)(2,1)} %add_convert_fusion), channel_id=1, source_target_pairs={{0,2},{1,3},{2,0},{3,1},{4,6},{5,7},{6,4},{7,5},{8,10},{9,11},{10,... | collective-permute-start | bytes 1572872 | tf_op jit(solution)/shard_map/ppermute | solution.py:413
  261.6 10.2 %collective-permute-done.28 = bf16[256,1024]{1,0:T(8,128)(2,1)S(1)} collective-permute-done((bf16[256,1024]{1,0:T(8,128)(2,1)}, bf16[256,1024]{1,0:T(8,128)(2,1)S(1)}, u32[]{:S(2)}, u32[]{:S(2)}) %collective-permute-start.28) | collective-permute-done | bytes 524320 | tf_op jit(solution)/shard_map/ppermute | solution.py:413
  (264 shorter events, 89.3 us)
Async XLA Ops:
  0.7 14.4 %collective-permute-start = (bf16[32,1024]{1,0:T(8,128)(2,1)}, bf16[32,1024]{1,0:T(8,128)(2,1)S(1)}, u32[]{:S(2)}, u32[]{:S(2)}) collective-permute-start(bf16[32,1024]{1,0:T(8,128)(2,1)} %param.14), channel_id=1, source_target_pairs={{0,0},{1,4},{2,8},{3,12},{4,16},{5,20},{6,24},{7,28},{8,1},{9,5},{... | collective-permute-start | bytes 196616 | tf_op jit(solution)/shard_map/ppermute | solution.py:730
  5.4 12.8 %all-to-all-start = ((bf16[4,32,896]{2,1,0:T(8,128)(2,1)}), bf16[4,32,896]{2,1,0:T(8,128)(2,1)S(1)}, u32[]{:S(2)}, u32[]{:S(2)}) async-start(bf16[4,32,896]{2,1,0:T(8,128)(2,1)} %bitcast), calls=%async_computation | async-start | bytes 458752 | tf_op jit(solution)/shard_map/all_to_all | solution.py:418
  22.4 12.3 %collective-permute-start.1 = (bf16[128,1024]{1,0:T(8,128)(2,1)S(1)}, bf16[128,1024]{1,0:T(8,128)(2,1)S(1)}, u32[]{:S(2)}, u32[]{:S(2)}) collective-permute-start(bf16[128,1024]{1,0:T(8,128)(2,1)S(1)} %maximum_maximum_fusion.own), channel_id=1, source_target_pairs={{0,8},{4,12},{8,16},{12,20},{16,24},{20,28},{24,0},{28,4},{1,9},{5... | collective-permute-start | bytes 786440 | tf_op jit(solution)/shard_map/ppermute | solution.py:422
  35.5 18.3 %collective-permute-start.5 = (bf16[256,1024]{1,0:T(8,128)(2,1)}, bf16[256,1024]{1,0:T(8,128)(2,1)}, u32[]{:S(2)}, u32[]{:S(2)}) collective-permute-start(bf16[256,1024]{1,0:T(8,128)(2,1)} %pad_maximum_fusion.4), channel_id=1, source_target_pairs={{0,4},{4,0},{8,12},{12,8},{16,20},{20,16},{24,28},{28,24},{1,5},{5... | collective-permute-start | bytes 1572872 | tf_op jit(solution)/shard_map/ppermute | solution.py:430
  35.8 18.0 %collective-permute-start.6 = (bf16[256,1024]{1,0:T(8,128)(2,1)S(1)}, bf16[256,1024]{1,0:T(8,128)(2,1)S(1)}, u32[]{:S(2)}, u32[]{:S(2)}) collective-permute-start(bf16[256,1024]{1,0:T(8,128)(2,1)S(1)} %pad_maximum_fusion.3.mine), channel_id=1, source_target_pairs={{0,2},{1,3},{2,0},{3,1},{4,6},{5,7},{6,4},{7,5},{8,10},{9,11},{10,... | collective-permute-start | bytes 1572872 | tf_op jit(solution)/shard_map/ppermute | solution.py:413
  36.6 17.2 %all-to-all-start.1 = ((bf16[4,32,2176]{2,1,0:T(8,128)(2,1)}), bf16[4,32,2176]{2,1,0:T(8,128)(2,1)S(1)}, u32[]{:S(2)}, u32[]{:S(2)}) async-start(bf16[4,32,2176]{2,1,0:T(8,128)(2,1)} %bitcast.7), calls=%async_computation.1 | async-start | bytes 1114112 | tf_op jit(solution)/shard_map/all_to_all | solution.py:418
  40.0 13.7 %collective-permute-start.4 = (bf16[128,1024]{1,0:T(8,128)(2,1)S(1)}, bf16[128,1024]{1,0:T(8,128)(2,1)S(1)}, u32[]{:S(2)}, u32[]{:S(2)}) collective-permute-start(bf16[128,1024]{1,0:T(8,128)(2,1)S(1)} %collective-permute-done.1.third), channel_id=1, source_target_pairs={{0,8},{4,12},{8,16},{12,20},{16,24},{20,28},{24,0},{28,4},{1,9},{5... | collective-permute-start | bytes 786440 | tf_op jit(solution)/shard_map/ppermute | solution.py:422
  56.0 19.3 %collective-permute-start.10 = (bf16[128,2176]{1,0:T(8,128)(2,1)S(1)}, bf16[128,2176]{1,0:T(8,128)(2,1)}, u32[]{:S(2)}, u32[]{:S(2)}) collective-permute-start(bf16[128,2176]{1,0:T(8,128)(2,1)S(1)} %bitcast.29), channel_id=1, source_target_pairs={{0,24},{4,28},{8,0},{12,4},{16,8},{20,12},{24,16},{28,20},{1,25},{... | collective-permute-start | bytes 1671176 | tf_op jit(solution)/shard_map/ppermute | solution.py:426
  58.3 25.6 %collective-permute-start.9 = (bf16[128,2176]{1,0:T(8,128)(2,1)S(1)}, bf16[128,2176]{1,0:T(8,128)(2,1)}, u32[]{:S(2)}, u32[]{:S(2)}) collective-permute-start(bf16[128,2176]{1,0:T(8,128)(2,1)S(1)} %bitcast.30), channel_id=1, source_target_pairs={{0,8},{4,12},{8,16},{12,20},{16,24},{20,28},{24,0},{28,4},{1,9},{5... | collective-permute-start | bytes 1671176 | tf_op jit(solution)/shard_map/ppermute | solution.py:422
  62.8 21.1 %collective-permute-start.11 = (bf16[128,2176]{1,0:T(8,128)(2,1)S(1)}, bf16[128,2176]{1,0:T(8,128)(2,1)}, u32[]{:S(2)}, u32[]{:S(2)}) collective-permute-start(bf16[128,2176]{1,0:T(8,128)(2,1)S(1)} %bitcast.31), channel_id=1, source_target_pairs={{0,4},{4,0},{8,12},{12,8},{16,20},{20,16},{24,28},{28,24},{1,5},{5... | collective-permute-start | bytes 1671176 | tf_op jit(solution)/shard_map/ppermute | solution.py:430
  86.6 14.7 %collective-permute-start.17 = (bf16[128,2176]{1,0:T(8,128)(2,1)}, bf16[128,2176]{1,0:T(8,128)(2,1)S(1)}, u32[]{:S(2)}, u32[]{:S(2)}) collective-permute-start(bf16[128,2176]{1,0:T(8,128)(2,1)} %collective-permute-done.9.third), channel_id=1, source_target_pairs={{0,4},{4,0},{8,12},{12,8},{16,20},{20,16},{24,28},{28,24},{1,5},{5... | collective-permute-start | bytes 1671176 | tf_op jit(solution)/shard_map/ppermute | solution.py:430
  87.2 16.1 %collective-permute-start.16 = (bf16[128,2176]{1,0:T(8,128)(2,1)}, bf16[128,2176]{1,0:T(8,128)(2,1)S(1)}, u32[]{:S(2)}, u32[]{:S(2)}) collective-permute-start(bf16[128,2176]{1,0:T(8,128)(2,1)} %collective-permute-done.9.third), channel_id=1, source_target_pairs={{0,8},{4,12},{8,16},{12,20},{16,24},{20,28},{24,0},{28,4},{1,9},{5... | collective-permute-start | bytes 1671176 | tf_op jit(solution)/shard_map/ppermute | solution.py:422
  101.3 13.7 %collective-permute-start.18 = (bf16[128,2176]{1,0:T(8,128)(2,1)}, bf16[128,2176]{1,0:T(8,128)(2,1)S(1)}, u32[]{:S(2)}, u32[]{:S(2)}) collective-permute-start(bf16[128,2176]{1,0:T(8,128)(2,1)} %collective-permute-done.10.first), channel_id=1, source_target_pairs={{0,4},{4,0},{8,12},{12,8},{16,20},{20,16},{24,28},{28,24},{1,5},{5... | collective-permute-start | bytes 1671176 | tf_op jit(solution)/shard_map/ppermute | solution.py:430
  103.3 15.0 %collective-permute-start.19 = (bf16[128,2176]{1,0:T(8,128)(2,1)S(1)}, bf16[128,2176]{1,0:T(8,128)(2,1)S(1)}, u32[]{:S(2)}, u32[]{:S(2)}) collective-permute-start(bf16[128,2176]{1,0:T(8,128)(2,1)S(1)} %collective-permute-done.17.other_third), channel_id=1, source_target_pairs={{0,8},{4,12},{8,16},{12,20},{16,24},{20,28},{24,0},{28,4},{1,9},{5... | collective-permute-start | bytes 1671176 | tf_op jit(solution)/shard_map/ppermute | solution.py:422
  103.3 14.9 %collective-permute-start.15 = (bf16[256,1024]{1,0:T(8,128)(2,1)S(1)}, bf16[256,1024]{1,0:T(8,128)(2,1)S(1)}, u32[]{:S(2)}, u32[]{:S(2)}) collective-permute-start(bf16[256,1024]{1,0:T(8,128)(2,1)S(1)} %pad_maximum_fusion.5), channel_id=1, source_target_pairs={{0,1},{1,0},{2,3},{3,2},{4,5},{5,4},{6,7},{7,6},{8,9},{9,8},{10,11... | collective-permute-start | bytes 1572872 | tf_op jit(solution)/shard_map/ppermute | solution.py:413
  129.5 15.0 %collective-permute-start.21 = (bf16[128,1024]{1,0:T(8,128)(2,1)S(1)}, bf16[128,1024]{1,0:T(8,128)(2,1)S(1)}, u32[]{:S(2)}, u32[]{:S(2)}) collective-permute-start(bf16[128,1024]{1,0:T(8,128)(2,1)S(1)} %add_convert_fusion.10), channel_id=1, source_target_pairs={{0,2},{1,3},{2,0},{3,1},{4,6},{5,7},{6,4},{7,5},{8,10},{9,11},{10,... | collective-permute-start | bytes 786440 | tf_op jit(solution)/shard_map/ppermute | solution.py:413
  139.0 13.8 %collective-permute-start.24 = (bf16[256,768]{1,0:T(8,128)(2,1)S(1)}, bf16[256,768]{1,0:T(8,128)(2,1)S(1)}, u32[]{:S(2)}, u32[]{:S(2)}) collective-permute-start(bf16[256,768]{1,0:T(8,128)(2,1)S(1)} %get-tuple-element.97), channel_id=1, source_target_pairs={{0,8},{4,12},{8,16},{12,20},{16,24},{20,28},{24,0},{28,4},{1,9},{5... | collective-permute-start | bytes 1179656 | tf_op jit(solution)/shard_map/ppermute | solution.py:422
  139.0 19.3 %collective-permute-start.25 = (bf16[256,768]{1,0:T(8,128)(2,1)S(1)}, bf16[256,768]{1,0:T(8,128)(2,1)S(1)}, u32[]{:S(2)}, u32[]{:S(2)}) collective-permute-start(bf16[256,768]{1,0:T(8,128)(2,1)S(1)} %get-tuple-element.98), channel_id=1, source_target_pairs={{0,24},{4,28},{8,0},{12,4},{16,8},{20,12},{24,16},{28,20},{1,25},{... | collective-permute-start | bytes 1179656 | tf_op jit(solution)/shard_map/ppermute | solution.py:426
  142.8 17.3 %collective-permute-start.22 = (bf16[256,1408]{1,0:T(8,128)(2,1)S(1)}, bf16[256,1408]{1,0:T(8,128)(2,1)S(1)}, u32[]{:S(2)}, u32[]{:S(2)}) collective-permute-start(bf16[256,1408]{1,0:T(8,128)(2,1)S(1)} %get-tuple-element.96), channel_id=1, source_target_pairs={{0,4},{4,0},{8,12},{12,8},{16,20},{20,16},{24,28},{28,24},{1,5},{5... | collective-permute-start | bytes 2162696 | tf_op jit(solution)/shard_map/ppermute | solution.py:430
  145.8 14.3 %collective-permute-start.23 = (bf16[128,1024]{1,0:T(8,128)(2,1)S(1)}, bf16[128,1024]{1,0:T(8,128)(2,1)S(1)}, u32[]{:S(2)}, u32[]{:S(2)}) collective-permute-start(bf16[128,1024]{1,0:T(8,128)(2,1)S(1)} %get-tuple-element.154.low_own), channel_id=1, source_target_pairs={{0,2},{1,3},{2,0},{3,1},{4,6},{5,7},{6,4},{7,5},{8,10},{9,11},{10,... | collective-permute-start | bytes 786440 | tf_op jit(solution)/shard_map/ppermute | solution.py:413
  160.2 19.0 %collective-permute-start.37 = (bf16[256,768]{1,0:T(8,128)(2,1)S(1)}, bf16[256,768]{1,0:T(8,128)(2,1)S(1)}, u32[]{:S(2)}, u32[]{:S(2)}) collective-permute-start(bf16[256,768]{1,0:T(8,128)(2,1)S(1)} %add_convert_fusion.1), channel_id=1, source_target_pairs={{0,8},{4,12},{8,16},{12,20},{16,24},{20,28},{24,0},{28,4},{1,9},{5... | collective-permute-start | bytes 1179656 | tf_op jit(solution)/shard_map/ppermute | solution.py:422
  160.4 18.8 %collective-permute-start.35 = (bf16[256,1408]{1,0:T(8,128)(2,1)S(1)}, bf16[256,1408]{1,0:T(8,128)(2,1)S(1)}, u32[]{:S(2)}, u32[]{:S(2)}) collective-permute-start(bf16[256,1408]{1,0:T(8,128)(2,1)S(1)} %get-tuple-element.122), channel_id=1, source_target_pairs={{0,4},{4,0},{8,12},{12,8},{16,20},{20,16},{24,28},{28,24},{1,5},{5... | collective-permute-start | bytes 2162696 | tf_op jit(solution)/shard_map/ppermute | solution.py:430
  162.3 16.9 %collective-permute-start.36 = (bf16[128,1408]{1,0:T(8,128)(2,1)S(1)}, bf16[128,1408]{1,0:T(8,128)(2,1)S(1)}, u32[]{:S(2)}, u32[]{:S(2)}) collective-permute-start(bf16[128,1408]{1,0:T(8,128)(2,1)S(1)} %add_convert_fusion.5), channel_id=1, source_target_pairs={{0,8},{4,12},{8,16},{12,20},{16,24},{20,28},{24,0},{28,4},{1,9},{5... | collective-permute-start | bytes 1081352 | tf_op jit(solution)/shard_map/ppermute | solution.py:422
  181.4 13.2 %collective-permute-start.38 = (bf16[128,1408]{1,0:T(8,128)(2,1)S(1)}, bf16[128,1408]{1,0:T(8,128)(2,1)S(1)}, u32[]{:S(2)}, u32[]{:S(2)}) collective-permute-start(bf16[128,1408]{1,0:T(8,128)(2,1)S(1)} %get-tuple-element.178), channel_id=1, source_target_pairs={{0,8},{4,12},{8,16},{12,20},{16,24},{20,28},{24,0},{28,4},{1,9},{5... | collective-permute-start | bytes 1081352 | tf_op jit(solution)/shard_map/ppermute | solution.py:422
  182.3 17.1 %collective-permute-start.39 = (bf16[128,1408]{1,0:T(8,128)(2,1)S(1)}, bf16[128,1408]{1,0:T(8,128)(2,1)S(1)}, u32[]{:S(2)}, u32[]{:S(2)}) collective-permute-start(bf16[128,1408]{1,0:T(8,128)(2,1)S(1)} %get-tuple-element.179), channel_id=1, source_target_pairs={{0,24},{4,28},{8,0},{12,4},{16,8},{20,12},{24,16},{28,20},{1,25},{... | collective-permute-start | bytes 1081352 | tf_op jit(solution)/shard_map/ppermute | solution.py:426
  185.8 27.7 %collective-permute-start.29 = (bf16[256,1024]{1,0:T(8,128)(2,1)}, bf16[256,1024]{1,0:T(8,128)(2,1)}, u32[]{:S(2)}, u32[]{:S(2)}) collective-permute-start(bf16[256,1024]{1,0:T(8,128)(2,1)} %get-tuple-element.114), channel_id=1, source_target_pairs={{0,4},{4,0},{8,12},{12,8},{16,20},{20,16},{24,28},{28,24},{1,5},{5... | collective-permute-start | bytes 1572872 | tf_op jit(solution)/shard_map/ppermute | solution.py:430
  200.5 16.9 %all-to-all-start.3 = ((bf16[4,32,2176]{2,1,0:T(8,128)(2,1)}), bf16[4,32,2176]{2,1,0:T(8,128)(2,1)}, u32[]{:S(2)}, u32[]{:S(2)}) async-start(bf16[4,32,2176]{2,1,0:T(8,128)(2,1)} %bitcast.14), calls=%async_computation.3 | async-start | bytes 1114112 | tf_op jit(solution)/shard_map/all_to_all | solution.py:418
  213.0 39.4 %collective-permute-start.27 = (bf16[512,1024]{1,0:T(8,128)(2,1)}, bf16[512,1024]{1,0:T(8,128)(2,1)}, u32[]{:S(2)}, u32[]{:S(2)}) collective-permute-start(bf16[512,1024]{1,0:T(8,128)(2,1)} %get-tuple-element.111), channel_id=1, source_target_pairs={{0,1},{1,0},{2,3},{3,2},{4,5},{5,4},{6,7},{7,6},{8,9},{9,8},{10,11... | collective-permute-start | bytes 3145736 | tf_op jit(solution)/shard_map/ppermute | solution.py:413
  217.0 13.7 %collective-permute-start.30 = (bf16[256,1024]{1,0:T(8,128)(2,1)S(1)}, bf16[256,1024]{1,0:T(8,128)(2,1)}, u32[]{:S(2)}, u32[]{:S(2)}) collective-permute-start(bf16[256,1024]{1,0:T(8,128)(2,1)S(1)} %get-tuple-element.116), channel_id=1, source_target_pairs={{0,4},{4,0},{8,12},{12,8},{16,20},{20,16},{24,28},{28,24},{1,5},{5... | collective-permute-start | bytes 1572872 | tf_op jit(solution)/shard_map/ppermute | solution.py:430
  233.4 12.8 %collective-permute-start.33 = (bf16[128,1024]{1,0:T(8,128)(2,1)}, bf16[128,1024]{1,0:T(8,128)(2,1)}, u32[]{:S(2)}, u32[]{:S(2)}) collective-permute-start(bf16[128,1024]{1,0:T(8,128)(2,1)} %get-tuple-element.181), channel_id=1, source_target_pairs={{0,24},{4,28},{8,0},{12,4},{16,8},{20,12},{24,16},{28,20},{1,25},{... | collective-permute-start | bytes 786440 | tf_op jit(solution)/shard_map/ppermute | solution.py:426
  248.1 11.9 %all-to-all-start.2 = ((bf16[4,32,768]{2,1,0:T(8,128)(2,1)}), bf16[4,32,768]{2,1,0:T(8,128)(2,1)S(1)}, u32[]{:S(2)}, u32[]{:S(2)}) async-start(bf16[4,32,768]{2,1,0:T(8,128)(2,1)} %bitcast.9), calls=%async_computation.2 | async-start | bytes 393216 | tf_op jit(solution)/shard_map/all_to_all | solution.py:418
  254.5 17.3 %collective-permute-start.28 = (bf16[256,1024]{1,0:T(8,128)(2,1)}, bf16[256,1024]{1,0:T(8,128)(2,1)S(1)}, u32[]{:S(2)}, u32[]{:S(2)}) collective-permute-start(bf16[256,1024]{1,0:T(8,128)(2,1)} %add_convert_fusion), channel_id=1, source_target_pairs={{0,2},{1,3},{2,0},{3,1},{4,6},{5,7},{6,4},{7,5},{8,10},{9,11},{10,... | collective-permute-start | bytes 1572872 | tf_op jit(solution)/shard_map/ppermute | solution.py:413
  (43 other events, 332.8 us)

commit v5 on v4

--- a/solution.py
+++ b/solution.py
@@ -609,7 +609,7 @@
 def attention_backward(
     place, cosine, sine, low_own, low_across, low_beside, attn, query, key, value, probs,
     attended, normed,
-    grad_packed, g_keep, g_early, g_late, grad_low, grad_attended, term_attn,
+    grad_packed, g_keep, g_send, grad_low, grad_attended, term_attn,
 ):
     count = 128
     for at, ref in enumerate(
@@ -642,15 +642,13 @@
             lanes = slice(512 + LANES * pair, 512 + LANES * (pair + 1))
             grad_packed[here, lanes] = low(grad_v)
     term = low(matmul_left_t(normed[...], grad_packed[...]))
-    half, quarter = term.shape[0] // 2, term.shape[0] // 4
+    half = term.shape[0] // 2
     g_keep[:, :768] = term[:half]
-    g_early[:, :768] = term[half : half + quarter]
-    g_late[:, :768] = term[half + quarter :]
+    g_send[:, :768] = term[half:]
     term_attn[...] = low(matmul_left_t(attended[...], grad_low[...]))
     size = term.shape[0] // 8
     part = size // 4
-    targets = [(g_keep, size * p) for p in range(4)]
-    targets += [(g_early, 0), (g_early, size), (g_late, 0), (g_late, size)]
+    targets = [(ref, size * p) for ref in (g_keep, g_send) for p in range(4)]
     for at, (ref, row) in enumerate(targets):
         source = pl.multiple_of(place_of(place, at % 4, at // 4) * part, part)
         for z_at in range(4):
@@ -758,7 +756,7 @@
     rest = rep_exchange(rest)
 
     third, first, other = up(first_own), down(first_own), over(first_own)
-    third, first, other, mine = tie(third, first, other, mine)
+    third, first, other, mine, rest = tie(third, first, other, mine, rest)
     across = swap(mine, 2)
     second, others = up(third), over(rows([first, third]))
     second, others, across, rest = tie(second, others, across, rest)
@@ -832,24 +830,24 @@
     )
     low_own = low(grad_hidden)
     low_across = swap(low_own, 2)
-    in_early, low_across, out_up, out_down = tie(in_early, low_across, out_up, out_down)
+    in_early, low_across, out_up = tie(in_early, low_across, out_up)
     in_late = over(tie(in_late, in_early)[0])
     low_beside = swap(rows([low_own, low_across]), 1)
     in_kept, in_first_two = split_rows(in_keep, 4), split_rows(in_early, 2)
     in_up = up(low(wide(in_kept[1]) + wide(in_first_two[1])))
     out_turned = up(low(wide(out_terms[0]) + wide(out_up)))
 
-    grad_packed, g_keep, g_early, g_late = kernel(
+    grad_packed, g_keep, g_send = kernel(
         attention_backward,
-        [((group, 768), b16), ((width // 2, width), b16)] + [((width // 4, width), b16)] * 2,
+        [((group, 768), b16)] + [((width // 2, width), b16)] * 2,
         (2 * group * width * (768 + 512) + 10 * 16 * count * count * LANES, 0),
         place, cosine, sine, low_own, low_across, low_beside, attn, query, key, value, probs,
         attended, normed,
         scratch=[((group, width), b16), ((group, 256), b16), ((256, width), b16)],
         scalars=1,
     )
-    g_over_early = over(g_early)
-    in_late, in_up, out_turned, _ = tie(in_late, in_up, out_turned, g_keep)
+    g_over = over(g_send)
+    in_late, in_up, out_turned, out_down, _ = tie(in_late, in_up, out_turned, out_down, g_keep)
     in_last_two = split_rows(in_late, 2)
     in_turned = up(low(wide(in_kept[0]) + wide(in_first_two[0]) + wide(in_up)))
     in_down = down(low(wide(in_kept[2]) + wide(in_last_two[0])))
@@ -860,21 +858,21 @@
         (2 * group * width * (768 + out_width), 0),
         grad_packed, qkv, mixed, w_down,
     )
-    g_over_early, _ = tie(g_over_early, send)
-    g_over_late = over(tie(g_late, g_over_early)[0])
-    out_over = over(low(out_sums[1]))
-    g_kept, g_first_two = split_rows(g_keep, 4), split_rows(g_over_early, 2)
-    g_up = up(low(wide(g_kept[1]) + wide(g_first_two[1])))
+    g_over, send, in_turned, in_down = tie(g_over, send, in_turned, in_down)
+    g_sums = [wide(a) + wide(b) for a, b in zip(split_rows(g_keep, 4), split_rows(g_over, 4))]
+    g_up, g_down = up(low(g_sums[1])), down(low(g_sums[2]))
+    kept, sent = scatter_last(send, keep)
+    out_over = over(tie(low(out_sums[1]), g_over)[0])
+    g_up, g_down, sent = tie(g_up, g_down, sent)
+    last_across = swap(sent, 2)
+    g_turned = up(low(g_sums[0] + wide(g_up)))
+    out_over, _ = tie(out_over, g_up)
     sum_in = wide(in_kept[3]) + wide(in_last_two[1]) + wide(in_turned) + wide(in_down)
     sum_out = out_sums[0] + wide(out_over)
     back = rep_exchange(columns([low(sum_in), low(sum_out)]))
-    g_over_late, g_up = tie(g_over_late, g_up)
-    g_last_two = split_rows(g_over_late, 2)
-    g_turned = up(low(wide(g_kept[0]) + wide(g_first_two[0]) + wide(g_up)))
-    g_down = down(low(wide(g_kept[2]) + wide(g_last_two[0])))
-    kept, sent = scatter_last(send, keep)
-    last = kept + wide(swap(sent, 2))
-    sum_g = low(wide(g_kept[3]) + wide(g_last_two[1]) + wide(g_turned) + wide(g_down))
+    g_turned, g_down, last_across = tie(g_turned, g_down, last_across)
+    last = kept + wide(last_across)
+    sum_g = low(g_sums[3] + wide(g_turned) + wide(g_down))
     back_qkv = rep_exchange(sum_g[:, :768])
     grad_w_attn_out = wide(
         lax.ppermute(

time: 277 us -> 260 us (0.939)
  local copies, waits for them, and re-layouts: 20.7 us -> 11.1 us
  starting transfers between devices: 64.6 us -> 59.7 us
    ppermute x11, waiting for transfers between devices: 42.5 us -> 54.4 us  [up(): return lax.ppermute(value, 'fsdp', [(k, (k + 2) % 8) for k in range(8)])]
    ppermute x12, waiting for transfers between devices: 19.8 us -> 11.8 us  [swap(): return lax.ppermute(value, 'rep', [(k, k ^ distance) for k in range(4)])]
    unnamed x71 -> x73, local copies, waits for them, and re-layouts: 9.74 us -> 4.78 us
    all_to_all x4, waiting for transfers between devices: 15.8 us -> 11.2 us  [rep_exchange(): return lax.all_to_all(blocks, 'rep', 0, 0, tiled=True).reshape(value.shape)]
    ppermute x11, starting transfers between devices: 7.72 us -> 4.42 us  [up(): return lax.ppermute(value, 'fsdp', [(k, (k + 2) % 8) for k in range(8)])]
    ppermute x11 -> x10, waiting for transfers between devices: 33.1 us -> 35 us  [over(): return lax.ppermute(value, 'fsdp', [(k, k ^ 1) for k in range(8)])]
    ppermute x11 -> x10, starting transfers between devices: 13.2 us -> 12.8 us  [over(): return lax.ppermute(value, 'fsdp', [(k, k ^ 1) for k in range(8)])]
  transfers between devices with their start and end apart: 45 -> 44, of which waited for: 25 -> 26; matrix products, arithmetic and copies ran while one was open for 12% -> 9% of each run, Pallas kernels for 10% -> 10%
where the time goes in v5:
time: 260 us; the launch traced here: 256 us
  waiting for transfers between devices  125 us (48%)
  starting transfers between devices  59.7 us (23%)
  Pallas kernels  33.9 us (13%)
  other arithmetic  24.5 us (9%)
  local copies, waits for them, and re-layouts  11.1 us (4%)
    ppermute x11, waiting for transfers between devices, up(): return lax.ppermute(value, 'fsdp', [(k, (k + 2) % 8) for k in range(8)])  54.4 us
    ppermute x10, waiting for transfers between devices, over(): return lax.ppermute(value, 'fsdp', [(k, k ^ 1) for k in range(8)])  35 us
    pallas_call x5, Pallas kernels, kernel(): pl.pallas_call(body, out_shape=shapes, in_specs=[pl.BlockSpec(memory_spac...  33.9 us
    all_to_all x4, starting transfers between devices, rep_exchange(): return lax.all_to_all(blocks, 'rep', 0, 0, tiled=True).reshape(value.shape)  17.2 us
    ppermute x5, starting transfers between devices, down(): return lax.ppermute(value, 'fsdp', [(k, (k - 2) % 8) for k in range(8)])  14 us
    ppermute x5, waiting for transfers between devices, down(): return lax.ppermute(value, 'fsdp', [(k, (k - 2) % 8) for k in range(8)])  12.8 us
    ppermute x10, starting transfers between devices, over(): return lax.ppermute(value, 'fsdp', [(k, k ^ 1) for k in range(8)])  12.8 us
    ppermute x12, waiting for transfers between devices, swap(): return lax.ppermute(value, 'rep', [(k, k ^ distance) for k in range(4)])  11.8 us
  transfers between devices with their start and end apart: 44, of which 26 were waited for; matrix products, arithmetic and copies ran while one was open for 9% of the time, Pallas kernels for 10%

profile of v5, /device:TPU:0, one launch (start us, length us, event | category | flops | bytes accessed | tf_op | source)
XLA Modules:
  0.0 255.9 jit_solution(18169085639686148774)
XLA Ops:
  5.4 6.8 %all-to-all-start = ((bf16[4,32,896]{2,1,0:T(8,128)(2,1)}), bf16[4,32,896]{2,1,0:T(8,128)(2,1)S(1)}, u32[]{:S(2)}, u32[]{:S(2)}) async-start(bf16[4,32,896]{2,1,0:T(8,128)(2,1)} %bitcast), calls=%async_computation | async-start | bytes 458752 | tf_op jit(solution)/shard_map/all_to_all | solution.py:418
  15.0 3.2 %all-to-all-done = bf16[4,32,896]{2,1,0:T(8,128)(2,1)S(1)} async-done(((bf16[4,32,896]{2,1,0:T(8,128)(2,1)}), bf16[4,32,896]{2,1,0:T(8,128)(2,1)S(1)}, u32[]{:S(2)}, u32[]{:S(2)}) %all-to-all-start) | async-done | bytes 229408 | tf_op jit(solution)/shard_map/all_to_all | solution.py:418
  18.3 3.5 %all-to-all-start.1 = ((bf16[4,32,2176]{2,1,0:T(8,128)(2,1)}), bf16[4,32,2176]{2,1,0:T(8,128)(2,1)S(1)}, u32[]{:S(2)}, u32[]{:S(2)}) async-start(bf16[4,32,2176]{2,1,0:T(8,128)(2,1)} %bitcast.3), calls=%async_computation.1 | async-start | bytes 1114112 | tf_op jit(solution)/shard_map/all_to_all | solution.py:418
  26.5 4.8 %collective-permute-done.3.other = bf16[128,1024]{1,0:T(8,128)(2,1)S(1)} collective-permute-done((bf16[128,1024]{1,0:T(8,128)(2,1)S(1)}, bf16[128,1024]{1,0:T(8,128)(2,1)S(1)}, u32[]{:S(2)}, u32[]{:S(2)}) %collective-permute-start.3) | collective-permute-done | bytes 262176 | tf_op jit(solution)/shard_map/ppermute | solution.py:430
  33.1 5.8 %collective-permute-done.1.third = bf16[128,1024]{1,0:T(8,128)(2,1)S(1)} collective-permute-done((bf16[128,1024]{1,0:T(8,128)(2,1)S(1)}, bf16[128,1024]{1,0:T(8,128)(2,1)S(1)}, u32[]{:S(2)}, u32[]{:S(2)}) %collective-permute-start.1) | collective-permute-done | bytes 262176 | tf_op jit(solution)/shard_map/ppermute | solution.py:422
  42.8 7.4 %collective-permute-done.4.second = bf16[128,1024]{1,0:T(8,128)(2,1)S(1)} collective-permute-done((bf16[128,1024]{1,0:T(8,128)(2,1)S(1)}, bf16[128,1024]{1,0:T(8,128)(2,1)S(1)}, u32[]{:S(2)}, u32[]{:S(2)}) %collective-permute-start.4) | collective-permute-done | bytes 262176 | tf_op jit(solution)/shard_map/ppermute | solution.py:422
  50.2 3.0 %collective-permute-done.5.others = bf16[256,1024]{1,0:T(8,128)(2,1)} collective-permute-done((bf16[256,1024]{1,0:T(8,128)(2,1)}, bf16[256,1024]{1,0:T(8,128)(2,1)}, u32[]{:S(2)}, u32[]{:S(2)}) %collective-permute-start.5) | collective-permute-done | bytes 524320 | tf_op jit(solution)/shard_map/ppermute | solution.py:430
  57.2 5.0 %collective-permute-done.8.other_second = bf16[128,1024]{1,0:T(8,128)(2,1)S(1)} collective-permute-done((bf16[128,1024]{1,0:T(8,128)(2,1)S(1)}, bf16[128,1024]{1,0:T(8,128)(2,1)S(1)}, u32[]{:S(2)}, u32[]{:S(2)}) %collective-permute-start.8) | collective-permute-done | bytes 262176 | tf_op jit(solution)/shard_map/ppermute | solution.py:430
  65.3 9.2 %attention_forward.1 = (bf16[512,1024]{1,0:T(8,128)(2,1)}, bf16[1024,768]{1,0:T(8,128)(2,1)}, bf16[256,1024]{1,0:T(8,128)(2,1)S(1)}, bf16[512,256]{1,0:T(8,128)(...) custom-call(s32[2]{0:T(128)S(1)} %pad_add_fusion.place, ...), custom_call_target="tpu_custom_call" | custom-call | flops 1207959552 | bytes 11014152 | tf_op jit(solution)/shard_map/attention_forward/pallas_call | solution.py:679
  74.5 7.9 %collective-permute-done.9.third = bf16[128,2176]{1,0:T(8,128)(2,1)} collective-permute-done((bf16[128,2176]{1,0:T(8,128)(2,1)S(1)}, bf16[128,2176]{1,0:T(8,128)(2,1)}, u32[]{:S(2)}, u32[]{:S(2)}) %collective-permute-start.9) | collective-permute-done | bytes 557088 | tf_op jit(solution)/shard_map/ppermute | solution.py:422
  87.9 4.8 %collective-permute-done.13 = bf16[128,1024]{1,0:T(8,128)(2,1)S(1)} collective-permute-done((bf16[128,1024]{1,0:T(8,128)(2,1)S(1)}, bf16[128,1024]{1,0:T(8,128)(2,1)S(1)}, u32[]{:S(2)}, u32[]{:S(2)}) %collective-permute-start.13) | collective-permute-done | bytes 262176 | tf_op jit(solution)/shard_map/ppermute | solution.py:413
  95.0 5.7 %collective-permute-done.17.other_third = bf16[128,2176]{1,0:T(8,128)(2,1)S(1)} collective-permute-done((bf16[128,2176]{1,0:T(8,128)(2,1)}, bf16[128,2176]{1,0:T(8,128)(2,1)S(1)}, u32[]{:S(2)}, u32[]{:S(2)}) %collective-permute-start.17) | collective-permute-done | bytes 557088 | tf_op jit(solution)/shard_map/ppermute | solution.py:430
  103.0 11.5 %collective-permute-done.18.other_first = bf16[128,2176]{1,0:T(8,128)(2,1)S(1)} collective-permute-done((bf16[128,2176]{1,0:T(8,128)(2,1)}, bf16[128,2176]{1,0:T(8,128)(2,1)S(1)}, u32[]{:S(2)}, u32[]{:S(2)}) %collective-permute-start.18) | collective-permute-done | bytes 557088 | tf_op jit(solution)/shard_map/ppermute | solution.py:430
  114.5 3.4 %collective-permute-done.19.other_second = bf16[128,2176]{1,0:T(8,128)(2,1)S(1)} collective-permute-done((bf16[128,2176]{1,0:T(8,128)(2,1)S(1)}, bf16[128,2176]{1,0:T(8,128)(2,1)S(1)}, u32[]{:S(2)}, u32[]{:S(2)}) %collective-permute-start.19) | collective-permute-done | bytes 557088 | tf_op jit(solution)/shard_map/ppermute | solution.py:422
  118.6 8.5 %mlp.1 = (bf16[512,1024]{1,0:T(8,128)(2,1)}, bf16[512,1024]{1,0:T(8,128)(2,1)}, bf16[512,768]{1,0:T(8,128)(2,1)}, bf16[512,1408]{1,0:T(8,128)(2,1)}, bf16[256,10...) custom-call(s32[512,1]{1,0:T(8,128)S(1)} %copy.22.seg_col, ...), custom_call_target="tpu_custom_call" | custom-call | flops 3758096384 | bytes 14551040 | tf_op jit(solution)/shard_map/mlp/pallas_call | solution.py:679
  133.3 4.5 %mlp_terms.1 = (bf16[512,1408]{1,0:T(8,128)(2,1)}, bf16[256,1408]{1,0:T(8,128)(2,1)S(1)}, bf16[256,1408]{1,0:T(8,128)(2,1)S(1)}, bf16[256,768]{1,0:T(8,128)(2,1)...) custom-call(bf16[512,1024]{1,0:T(8,128)(2,1)S(1)} %copy-done.4, ...), custom_call_target="tpu_custom_call" | custom-call | flops 2281701376 | bytes 8781824 | tf_op jit(solution)/shard_map/mlp_terms/pallas_call | solution.py:679
  142.1 3.8 %collective-permute-start.30 = (bf16[256,768]{1,0:T(8,128)(2,1)S(1)}, bf16[256,768]{1,0:T(8,128)(2,1)S(1)}, u32[]{:S(2)}, u32[]{:S(2)}) collective-permute-start(bf16[256,768]{1,0:T(8,128)(2,1)S(1)} %get-tuple-element.127), channel_id=1, source_target_pairs={{0,24},{4,28},{8,0},{12,4},{16,8},{20,12},{24,16},{28,20},{1,25},{... | collective-permute-start | bytes 1179656 | tf_op jit(solution)/shard_map/ppermute | solution.py:426
  145.9 5.7 %collective-permute-done.24 = bf16[256,768]{1,0:T(8,128)(2,1)S(1)} collective-permute-done((bf16[256,768]{1,0:T(8,128)(2,1)S(1)}, bf16[256,768]{1,0:T(8,128)(2,1)S(1)}, u32[]{:S(2)}, u32[]{:S(2)}) %collective-permute-start.24) | collective-permute-done | bytes 393248 | tf_op jit(solution)/shard_map/ppermute | solution.py:422
  151.7 4.0 %collective-permute-done.22 = bf16[256,1408]{1,0:T(8,128)(2,1)S(1)} collective-permute-done((bf16[256,1408]{1,0:T(8,128)(2,1)S(1)}, bf16[256,1408]{1,0:T(8,128)(2,1)S(1)}, u32[]{:S(2)}, u32[]{:S(2)}) %collective-permute-start.22) | collective-permute-done | bytes 720928 | tf_op jit(solution)/shard_map/ppermute | solution.py:430
  158.2 8.5 %attention_backward.1 = (bf16[512,768]{1,0:T(8,128)(2,1)S(1)}, bf16[512,1024]{1,0:T(8,128)(2,1)S(1)}, bf16[512,1024]{1,0:T(8,128)(2,1)S(1)}) custom-call(s32[2]{0:T(128)S(1)} %pad_add_fusion.place, f32[512,128]{1,0:T(8,128)S(1)} %get-tuple-element.284.cosine, f32[512,128]{1,0:T(8,128)S(1)} %get-tuple-element.285.sine, ...), custom_call_target="tpu_custom_call" | custom-call | flops 1677721600 | bytes 8126472 | tf_op jit(solution)/shard_map/attention_backward/pallas_call | solution.py:679
  168.0 7.4 %collective-permute-done.28 = bf16[128,1408]{1,0:T(8,128)(2,1)S(1)} collective-permute-done((bf16[128,1408]{1,0:T(8,128)(2,1)S(1)}, bf16[128,1408]{1,0:T(8,128)(2,1)S(1)}, u32[]{:S(2)}, u32[]{:S(2)}) %collective-permute-start.28) | collective-permute-done | bytes 360480 | tf_op jit(solution)/shard_map/ppermute | solution.py:422
  175.6 3.5 %collective-permute-start.32 = (bf16[128,1408]{1,0:T(8,128)(2,1)S(1)}, bf16[128,1408]{1,0:T(8,128)(2,1)S(1)}, u32[]{:S(2)}, u32[]{:S(2)}) collective-permute-start(bf16[128,1408]{1,0:T(8,128)(2,1)S(1)} %get-tuple-element.196), channel_id=1, source_target_pairs={{0,24},{4,28},{8,0},{12,4},{16,8},{20,12},{24,16},{28,20},{1,25},{... | collective-permute-start | bytes 1081352 | tf_op jit(solution)/shard_map/ppermute | solution.py:426
  179.1 3.2 %projections.1 = (bf16[512,1024]{1,0:T(8,128)(2,1)S(1)}, bf16[512,1024]{1,0:T(8,128)(2,1)S(1)}) custom-call(bf16[512,768]{1,0:T(8,128)(2,1)S(1)} %get-tuple-element.115.grad_packed, bf16[1024,768]{1,0:T(8,128)(2,1)S(1)} %copy-done.1, bf16[512,768]{1,0:T(8,128)(2,1)S(1)} %copy-done.3, bf16[1024,768]{1,0:T(8,128)(2,1)} %get-tuple-element.117.w_down), custom_call_target="tpu_custom_call" | custom-call | flops 1610612736 | bytes 6815744 | tf_op jit(solution)/shard_map/projections/pallas_call | solution.py:679
  182.3 5.6 %collective-permute-done.32 = bf16[128,1408]{1,0:T(8,128)(2,1)S(1)} collective-permute-done((bf16[128,1408]{1,0:T(8,128)(2,1)S(1)}, bf16[128,1408]{1,0:T(8,128)(2,1)S(1)}, u32[]{:S(2)}, u32[]{:S(2)}) %collective-permute-start.32) | collective-permute-done | bytes 360480 | tf_op jit(solution)/shard_map/ppermute | solution.py:426
  187.9 8.1 %collective-permute-done.31 = bf16[128,1408]{1,0:T(8,128)(2,1)S(1)} collective-permute-done((bf16[128,1408]{1,0:T(8,128)(2,1)S(1)}, bf16[128,1408]{1,0:T(8,128)(2,1)S(1)}, u32[]{:S(2)}, u32[]{:S(2)}) %collective-permute-start.31) | collective-permute-done | bytes 360480 | tf_op jit(solution)/shard_map/ppermute | solution.py:422
  199.5 3.9 %collective-permute-start.35 = (bf16[128,1024]{1,0:T(8,128)(2,1)S(1)}, bf16[128,1024]{1,0:T(8,128)(2,1)}, u32[]{:S(2)}, u32[]{:S(2)}) collective-permute-start(bf16[128,1024]{1,0:T(8,128)(2,1)S(1)} %get-tuple-element.194), channel_id=1, source_target_pairs={{0,24},{4,28},{8,0},{12,4},{16,8},{20,12},{24,16},{28,20},{1,25},{... | collective-permute-start | bytes 786440 | tf_op jit(solution)/shard_map/ppermute | solution.py:426
  204.6 5.4 %collective-permute-done.35 = bf16[128,1024]{1,0:T(8,128)(2,1)} collective-permute-done((bf16[128,1024]{1,0:T(8,128)(2,1)S(1)}, bf16[128,1024]{1,0:T(8,128)(2,1)}, u32[]{:S(2)}, u32[]{:S(2)}) %collective-permute-start.35) | collective-permute-done | bytes 262176 | tf_op jit(solution)/shard_map/ppermute | solution.py:426
  210.0 7.0 %collective-permute-done.34 = bf16[128,1024]{1,0:T(8,128)(2,1)S(1)} collective-permute-done((bf16[128,1024]{1,0:T(8,128)(2,1)S(1)}, bf16[128,1024]{1,0:T(8,128)(2,1)S(1)}, u32[]{:S(2)}, u32[]{:S(2)}) %collective-permute-start.34) | collective-permute-done | bytes 262176 | tf_op jit(solution)/shard_map/ppermute | solution.py:422
  217.9 3.5 %all-to-all-start.3 = ((bf16[4,32,2176]{2,1,0:T(8,128)(2,1)}), bf16[4,32,2176]{2,1,0:T(8,128)(2,1)S(1)}, u32[]{:S(2)}, u32[]{:S(2)}) async-start(bf16[4,32,2176]{2,1,0:T(8,128)(2,1)} %bitcast.34), calls=%async_computation.3 | async-start | bytes 1114112 | tf_op jit(solution)/shard_map/all_to_all | solution.py:418
  226.0 5.0 %all-to-all-done.3 = bf16[4,32,2176]{2,1,0:T(8,128)(2,1)S(1)} async-done(((bf16[4,32,2176]{2,1,0:T(8,128)(2,1)}), bf16[4,32,2176]{2,1,0:T(8,128)(2,1)S(1)}, u32[]{:S(2)}, u32[]{:S(2)}) %all-to-all-start.3) | async-done | bytes 557088 | tf_op jit(solution)/shard_map/all_to_all | solution.py:418
  238.8 3.2 %collective-permute-done.37 = bf16[256,1024]{1,0:T(8,128)(2,1)} collective-permute-done((bf16[256,1024]{1,0:T(8,128)(2,1)}, bf16[256,1024]{1,0:T(8,128)(2,1)}, u32[]{:S(2)}, u32[]{:S(2)}) %collective-permute-start.37) | collective-permute-done | bytes 524320 | tf_op jit(solution)/shard_map/ppermute | solution.py:413
  245.6 3.4 %all-to-all-start.2 = ((bf16[4,32,768]{2,1,0:T(8,128)(2,1)}), bf16[4,32,768]{2,1,0:T(8,128)(2,1)S(1)}, u32[]{:S(2)}, u32[]{:S(2)}) async-start(bf16[4,32,768]{2,1,0:T(8,128)(2,1)} %bitcast.9), calls=%async_computation.2 | async-start | bytes 393216 | tf_op jit(solution)/shard_map/all_to_all | solution.py:418
  (264 shorter events, 78.0 us)
Async XLA Ops:
  0.7 14.4 %collective-permute-start = (bf16[32,1024]{1,0:T(8,128)(2,1)}, bf16[32,1024]{1,0:T(8,128)(2,1)S(1)}, u32[]{:S(2)}, u32[]{:S(2)}) collective-permute-start(bf16[32,1024]{1,0:T(8,128)(2,1)} %param.14), channel_id=1, source_target_pairs={{0,0},{1,4},{2,8},{3,12},{4,16},{5,20},{6,24},{7,28},{8,1},{9,5},{... | collective-permute-start | bytes 196616 | tf_op jit(solution)/shard_map/ppermute | solution.py:728
  5.4 12.8 %all-to-all-start = ((bf16[4,32,896]{2,1,0:T(8,128)(2,1)}), bf16[4,32,896]{2,1,0:T(8,128)(2,1)S(1)}, u32[]{:S(2)}, u32[]{:S(2)}) async-start(bf16[4,32,896]{2,1,0:T(8,128)(2,1)} %bitcast), calls=%async_computation | async-start | bytes 458752 | tf_op jit(solution)/shard_map/all_to_all | solution.py:418
  18.3 20.6 %all-to-all-start.1 = ((bf16[4,32,2176]{2,1,0:T(8,128)(2,1)}), bf16[4,32,2176]{2,1,0:T(8,128)(2,1)S(1)}, u32[]{:S(2)}, u32[]{:S(2)}) async-start(bf16[4,32,2176]{2,1,0:T(8,128)(2,1)} %bitcast.3), calls=%async_computation.1 | async-start | bytes 1114112 | tf_op jit(solution)/shard_map/all_to_all | solution.py:418
  21.8 9.5 %collective-permute-start.3 = (bf16[128,1024]{1,0:T(8,128)(2,1)S(1)}, bf16[128,1024]{1,0:T(8,128)(2,1)S(1)}, u32[]{:S(2)}, u32[]{:S(2)}) collective-permute-start(bf16[128,1024]{1,0:T(8,128)(2,1)S(1)} %maximum_maximum_fusion.own), channel_id=1, source_target_pairs={{0,4},{4,0},{8,12},{12,8},{16,20},{20,16},{24,28},{28,24},{1,5},{5... | collective-permute-start | bytes 786440 | tf_op jit(solution)/shard_map/ppermute | solution.py:430
  25.8 13.1 %collective-permute-start.1 = (bf16[128,1024]{1,0:T(8,128)(2,1)S(1)}, bf16[128,1024]{1,0:T(8,128)(2,1)S(1)}, u32[]{:S(2)}, u32[]{:S(2)}) collective-permute-start(bf16[128,1024]{1,0:T(8,128)(2,1)S(1)} %maximum_maximum_fusion.own), channel_id=1, source_target_pairs={{0,8},{4,12},{8,16},{12,20},{16,24},{20,28},{24,0},{28,4},{1,9},{5... | collective-permute-start | bytes 786440 | tf_op jit(solution)/shard_map/ppermute | solution.py:422
  39.7 13.5 %collective-permute-start.5 = (bf16[256,1024]{1,0:T(8,128)(2,1)}, bf16[256,1024]{1,0:T(8,128)(2,1)}, u32[]{:S(2)}, u32[]{:S(2)}) collective-permute-start(bf16[256,1024]{1,0:T(8,128)(2,1)} %pad_maximum_fusion.4), channel_id=1, source_target_pairs={{0,4},{4,0},{8,12},{12,8},{16,20},{20,16},{24,28},{28,24},{1,5},{5... | collective-permute-start | bytes 1572872 | tf_op jit(solution)/shard_map/ppermute | solution.py:430
  40.1 13.1 %collective-permute-start.6 = (bf16[256,1024]{1,0:T(8,128)(2,1)S(1)}, bf16[256,1024]{1,0:T(8,128)(2,1)S(1)}, u32[]{:S(2)}, u32[]{:S(2)}) collective-permute-start(bf16[256,1024]{1,0:T(8,128)(2,1)S(1)} %pad_maximum_fusion.3.mine), channel_id=1, source_target_pairs={{0,2},{1,3},{2,0},{3,1},{4,6},{5,7},{6,4},{7,5},{8,10},{9,11},{10,... | collective-permute-start | bytes 1572872 | tf_op jit(solution)/shard_map/ppermute | solution.py:413
  55.2 19.3 %collective-permute-start.10 = (bf16[128,2176]{1,0:T(8,128)(2,1)S(1)}, bf16[128,2176]{1,0:T(8,128)(2,1)}, u32[]{:S(2)}, u32[]{:S(2)}) collective-permute-start(bf16[128,2176]{1,0:T(8,128)(2,1)S(1)} %bitcast.29), channel_id=1, source_target_pairs={{0,24},{4,28},{8,0},{12,4},{16,8},{20,12},{24,16},{28,20},{1,25},{... | collective-permute-start | bytes 1671176 | tf_op jit(solution)/shard_map/ppermute | solution.py:426
  56.7 25.7 %collective-permute-start.9 = (bf16[128,2176]{1,0:T(8,128)(2,1)S(1)}, bf16[128,2176]{1,0:T(8,128)(2,1)}, u32[]{:S(2)}, u32[]{:S(2)}) collective-permute-start(bf16[128,2176]{1,0:T(8,128)(2,1)S(1)} %bitcast.30), channel_id=1, source_target_pairs={{0,8},{4,12},{8,16},{12,20},{16,24},{20,28},{24,0},{28,4},{1,9},{5... | collective-permute-start | bytes 1671176 | tf_op jit(solution)/shard_map/ppermute | solution.py:422
  62.2 20.2 %collective-permute-start.11 = (bf16[128,2176]{1,0:T(8,128)(2,1)S(1)}, bf16[128,2176]{1,0:T(8,128)(2,1)}, u32[]{:S(2)}, u32[]{:S(2)}) collective-permute-start(bf16[128,2176]{1,0:T(8,128)(2,1)S(1)} %bitcast.31), channel_id=1, source_target_pairs={{0,4},{4,0},{8,12},{12,8},{16,20},{20,16},{24,28},{28,24},{1,5},{5... | collective-permute-start | bytes 1671176 | tf_op jit(solution)/shard_map/ppermute | solution.py:430
  86.1 14.7 %collective-permute-start.17 = (bf16[128,2176]{1,0:T(8,128)(2,1)}, bf16[128,2176]{1,0:T(8,128)(2,1)S(1)}, u32[]{:S(2)}, u32[]{:S(2)}) collective-permute-start(bf16[128,2176]{1,0:T(8,128)(2,1)} %collective-permute-done.9.third), channel_id=1, source_target_pairs={{0,4},{4,0},{8,12},{12,8},{16,20},{20,16},{24,28},{28,24},{1,5},{5... | collective-permute-start | bytes 1671176 | tf_op jit(solution)/shard_map/ppermute | solution.py:430
  86.7 16.1 %collective-permute-start.16 = (bf16[128,2176]{1,0:T(8,128)(2,1)}, bf16[128,2176]{1,0:T(8,128)(2,1)S(1)}, u32[]{:S(2)}, u32[]{:S(2)}) collective-permute-start(bf16[128,2176]{1,0:T(8,128)(2,1)} %collective-permute-done.9.third), channel_id=1, source_target_pairs={{0,8},{4,12},{8,16},{12,20},{16,24},{20,28},{24,0},{28,4},{1,9},{5... | collective-permute-start | bytes 1671176 | tf_op jit(solution)/shard_map/ppermute | solution.py:422
  100.7 13.7 %collective-permute-start.18 = (bf16[128,2176]{1,0:T(8,128)(2,1)}, bf16[128,2176]{1,0:T(8,128)(2,1)S(1)}, u32[]{:S(2)}, u32[]{:S(2)}) collective-permute-start(bf16[128,2176]{1,0:T(8,128)(2,1)} %collective-permute-done.10.first), channel_id=1, source_target_pairs={{0,4},{4,0},{8,12},{12,8},{16,20},{20,16},{24,28},{28,24},{1,5},{5... | collective-permute-start | bytes 1671176 | tf_op jit(solution)/shard_map/ppermute | solution.py:430
  102.9 15.0 %collective-permute-start.19 = (bf16[128,2176]{1,0:T(8,128)(2,1)S(1)}, bf16[128,2176]{1,0:T(8,128)(2,1)S(1)}, u32[]{:S(2)}, u32[]{:S(2)}) collective-permute-start(bf16[128,2176]{1,0:T(8,128)(2,1)S(1)} %collective-permute-done.17.other_third), channel_id=1, source_target_pairs={{0,8},{4,12},{8,16},{12,20},{16,24},{20,28},{24,0},{28,4},{1,9},{5... | collective-permute-start | bytes 1671176 | tf_op jit(solution)/shard_map/ppermute | solution.py:422
  102.9 14.9 %collective-permute-start.15 = (bf16[256,1024]{1,0:T(8,128)(2,1)S(1)}, bf16[256,1024]{1,0:T(8,128)(2,1)S(1)}, u32[]{:S(2)}, u32[]{:S(2)}) collective-permute-start(bf16[256,1024]{1,0:T(8,128)(2,1)S(1)} %pad_maximum_fusion.5), channel_id=1, source_target_pairs={{0,1},{1,0},{2,3},{3,2},{4,5},{5,4},{6,7},{7,6},{8,9},{9,8},{10,11... | collective-permute-start | bytes 1572872 | tf_op jit(solution)/shard_map/ppermute | solution.py:413
  129.1 10.1 %collective-permute-start.21 = (bf16[128,1024]{1,0:T(8,128)(2,1)S(1)}, bf16[128,1024]{1,0:T(8,128)(2,1)S(1)}, u32[]{:S(2)}, u32[]{:S(2)}) collective-permute-start(bf16[128,1024]{1,0:T(8,128)(2,1)S(1)} %add_convert_fusion.10), channel_id=1, source_target_pairs={{0,2},{1,3},{2,0},{3,1},{4,6},{5,7},{6,4},{7,5},{8,10},{9,11},{10,... | collective-permute-start | bytes 786440 | tf_op jit(solution)/shard_map/ppermute | solution.py:413
  137.8 13.9 %collective-permute-start.24 = (bf16[256,768]{1,0:T(8,128)(2,1)S(1)}, bf16[256,768]{1,0:T(8,128)(2,1)S(1)}, u32[]{:S(2)}, u32[]{:S(2)}) collective-permute-start(bf16[256,768]{1,0:T(8,128)(2,1)S(1)} %get-tuple-element.106), channel_id=1, source_target_pairs={{0,8},{4,12},{8,16},{12,20},{16,24},{20,28},{24,0},{28,4},{1,9},{5... | collective-permute-start | bytes 1179656 | tf_op jit(solution)/shard_map/ppermute | solution.py:422
  137.8 17.9 %collective-permute-start.22 = (bf16[256,1408]{1,0:T(8,128)(2,1)S(1)}, bf16[256,1408]{1,0:T(8,128)(2,1)S(1)}, u32[]{:S(2)}, u32[]{:S(2)}) collective-permute-start(bf16[256,1408]{1,0:T(8,128)(2,1)S(1)} %get-tuple-element.105), channel_id=1, source_target_pairs={{0,4},{4,0},{8,12},{12,8},{16,20},{20,16},{24,28},{28,24},{1,5},{5... | collective-permute-start | bytes 2162696 | tf_op jit(solution)/shard_map/ppermute | solution.py:430
  140.6 15.1 %collective-permute-start.23 = (bf16[128,1024]{1,0:T(8,128)(2,1)S(1)}, bf16[128,1024]{1,0:T(8,128)(2,1)S(1)}, u32[]{:S(2)}, u32[]{:S(2)}) collective-permute-start(bf16[128,1024]{1,0:T(8,128)(2,1)S(1)} %get-tuple-element.170.low_own), channel_id=1, source_target_pairs={{0,2},{1,3},{2,0},{3,1},{4,6},{5,7},{6,4},{7,5},{8,10},{9,11},{10,... | collective-permute-start | bytes 786440 | tf_op jit(solution)/shard_map/ppermute | solution.py:413
  142.1 25.8 %collective-permute-start.30 = (bf16[256,768]{1,0:T(8,128)(2,1)S(1)}, bf16[256,768]{1,0:T(8,128)(2,1)S(1)}, u32[]{:S(2)}, u32[]{:S(2)}) collective-permute-start(bf16[256,768]{1,0:T(8,128)(2,1)S(1)} %get-tuple-element.127), channel_id=1, source_target_pairs={{0,24},{4,28},{8,0},{12,4},{16,8},{20,12},{24,16},{28,20},{1,25},{... | collective-permute-start | bytes 1179656 | tf_op jit(solution)/shard_map/ppermute | solution.py:426
  155.8 19.6 %collective-permute-start.29 = (bf16[256,768]{1,0:T(8,128)(2,1)S(1)}, bf16[256,768]{1,0:T(8,128)(2,1)S(1)}, u32[]{:S(2)}, u32[]{:S(2)}) collective-permute-start(bf16[256,768]{1,0:T(8,128)(2,1)S(1)} %add_convert_fusion.1), channel_id=1, source_target_pairs={{0,8},{4,12},{8,16},{12,20},{16,24},{20,28},{24,0},{28,4},{1,9},{5... | collective-permute-start | bytes 1179656 | tf_op jit(solution)/shard_map/ppermute | solution.py:422
  156.0 19.4 %collective-permute-start.27 = (bf16[256,1408]{1,0:T(8,128)(2,1)S(1)}, bf16[256,1408]{1,0:T(8,128)(2,1)S(1)}, u32[]{:S(2)}, u32[]{:S(2)}) collective-permute-start(bf16[256,1408]{1,0:T(8,128)(2,1)S(1)} %get-tuple-element.124), channel_id=1, source_target_pairs={{0,4},{4,0},{8,12},{12,8},{16,20},{20,16},{24,28},{28,24},{1,5},{5... | collective-permute-start | bytes 2162696 | tf_op jit(solution)/shard_map/ppermute | solution.py:430
  157.6 17.8 %collective-permute-start.28 = (bf16[128,1408]{1,0:T(8,128)(2,1)S(1)}, bf16[128,1408]{1,0:T(8,128)(2,1)S(1)}, u32[]{:S(2)}, u32[]{:S(2)}) collective-permute-start(bf16[128,1408]{1,0:T(8,128)(2,1)S(1)} %add_convert_fusion.5), channel_id=1, source_target_pairs={{0,8},{4,12},{8,16},{12,20},{16,24},{20,28},{24,0},{28,4},{1,9},{5... | collective-permute-start | bytes 1081352 | tf_op jit(solution)/shard_map/ppermute | solution.py:422
  166.8 30.2 %collective-permute-start.26 = (bf16[512,1024]{1,0:T(8,128)(2,1)S(1)}, bf16[512,1024]{1,0:T(8,128)(2,1)S(1)}, u32[]{:S(2)}, u32[]{:S(2)}) collective-permute-start(bf16[512,1024]{1,0:T(8,128)(2,1)S(1)} %get-tuple-element.119), channel_id=1, source_target_pairs={{0,4},{4,0},{8,12},{12,8},{16,20},{20,16},{24,28},{28,24},{1,5},{5... | collective-permute-start | bytes 3145736 | tf_op jit(solution)/shard_map/ppermute | solution.py:430
  175.6 12.3 %collective-permute-start.32 = (bf16[128,1408]{1,0:T(8,128)(2,1)S(1)}, bf16[128,1408]{1,0:T(8,128)(2,1)S(1)}, u32[]{:S(2)}, u32[]{:S(2)}) collective-permute-start(bf16[128,1408]{1,0:T(8,128)(2,1)S(1)} %get-tuple-element.196), channel_id=1, source_target_pairs={{0,24},{4,28},{8,0},{12,4},{16,8},{20,12},{24,16},{28,20},{1,25},{... | collective-permute-start | bytes 1081352 | tf_op jit(solution)/shard_map/ppermute | solution.py:426
  179.1 17.0 %collective-permute-start.31 = (bf16[128,1408]{1,0:T(8,128)(2,1)S(1)}, bf16[128,1408]{1,0:T(8,128)(2,1)S(1)}, u32[]{:S(2)}, u32[]{:S(2)}) collective-permute-start(bf16[128,1408]{1,0:T(8,128)(2,1)S(1)} %get-tuple-element.197), channel_id=1, source_target_pairs={{0,8},{4,12},{8,16},{12,20},{16,24},{20,28},{24,0},{28,4},{1,9},{5... | collective-permute-start | bytes 1081352 | tf_op jit(solution)/shard_map/ppermute | solution.py:422
  197.8 19.3 %collective-permute-start.39 = (bf16[128,768]{1,0:T(8,128)(2,1)S(1)}, bf16[128,768]{1,0:T(8,128)(2,1)S(1)}, u32[]{:S(2)}, u32[]{:S(2)}) collective-permute-start(bf16[128,768]{1,0:T(8,128)(2,1)S(1)} %slice.954), channel_id=1, source_target_pairs={{0,4},{4,0},{8,12},{12,8},{16,20},{20,16},{24,28},{28,24},{1,5},{5... | collective-permute-start | bytes 589832 | tf_op jit(solution)/shard_map/ppermute | solution.py:430
  199.5 10.6 %collective-permute-start.35 = (bf16[128,1024]{1,0:T(8,128)(2,1)S(1)}, bf16[128,1024]{1,0:T(8,128)(2,1)}, u32[]{:S(2)}, u32[]{:S(2)}) collective-permute-start(bf16[128,1024]{1,0:T(8,128)(2,1)S(1)} %get-tuple-element.194), channel_id=1, source_target_pairs={{0,24},{4,28},{8,0},{12,4},{16,8},{20,12},{24,16},{28,20},{1,25},{... | collective-permute-start | bytes 786440 | tf_op jit(solution)/shard_map/ppermute | solution.py:426
  203.3 13.7 %collective-permute-start.34 = (bf16[128,1024]{1,0:T(8,128)(2,1)S(1)}, bf16[128,1024]{1,0:T(8,128)(2,1)S(1)}, u32[]{:S(2)}, u32[]{:S(2)}) collective-permute-start(bf16[128,1024]{1,0:T(8,128)(2,1)S(1)} %get-tuple-element.195), channel_id=1, source_target_pairs={{0,8},{4,12},{8,16},{12,20},{16,24},{20,28},{24,0},{28,4},{1,9},{5... | collective-permute-start | bytes 786440 | tf_op jit(solution)/shard_map/ppermute | solution.py:422
  217.9 13.1 %all-to-all-start.3 = ((bf16[4,32,2176]{2,1,0:T(8,128)(2,1)}), bf16[4,32,2176]{2,1,0:T(8,128)(2,1)S(1)}, u32[]{:S(2)}, u32[]{:S(2)}) async-start(bf16[4,32,2176]{2,1,0:T(8,128)(2,1)} %bitcast.34), calls=%async_computation.3 | async-start | bytes 1114112 | tf_op jit(solution)/shard_map/all_to_all | solution.py:418
  223.7 15.0 %collective-permute-start.36 = (bf16[128,1024]{1,0:T(8,128)(2,1)}, bf16[128,1024]{1,0:T(8,128)(2,1)}, u32[]{:S(2)}, u32[]{:S(2)}) collective-permute-start(bf16[128,1024]{1,0:T(8,128)(2,1)} %add_convert_fusion.7), channel_id=1, source_target_pairs={{0,8},{4,12},{8,16},{12,20},{16,24},{20,28},{24,0},{28,4},{1,9},{5... | collective-permute-start | bytes 786440 | tf_op jit(solution)/shard_map/ppermute | solution.py:422
  224.0 17.9 %collective-permute-start.37 = (bf16[256,1024]{1,0:T(8,128)(2,1)}, bf16[256,1024]{1,0:T(8,128)(2,1)}, u32[]{:S(2)}, u32[]{:S(2)}) collective-permute-start(bf16[256,1024]{1,0:T(8,128)(2,1)} %add_convert_fusion), channel_id=1, source_target_pairs={{0,2},{1,3},{2,0},{3,1},{4,6},{5,7},{6,4},{7,5},{8,10},{9,11},{10,... | collective-permute-start | bytes 1572872 | tf_op jit(solution)/shard_map/ppermute | solution.py:413
  (43 other events, 304.0 us)

commit v6 on v5

--- a/solution.py
+++ b/solution.py
@@ -590,26 +590,26 @@
     keep[count:, :], send[count:, :] = total[2 * count : 3 * count], total[3 * count :]
 
 
-def mlp_terms(
-    normed, grad_inner, grad_out, mixed,
-    in_keep, in_early, in_late, out_first, out_second, out_third, out_own,
-):
+def place_term(term, keep, pair, near, far, lanes):
+    size = term.shape[0] // 8
+    for at, (ref, row) in enumerate(
+        [(keep, 0), (pair, 0), (keep, 1), (keep, 2), (near, 0), (pair, 1), (far, 0), (far, 1)]
+    ):
+        ref[size * row : size * (row + 1), lanes] = term[size * at : size * (at + 1)]
+
+
+def mlp_terms(normed, grad_inner, grad_out, mixed, keep, pair, near, far):
+    edge = grad_inner.shape[1]
     term = low(matmul_left_t(normed[...], grad_inner[...]))
-    half, quarter = term.shape[0] // 2, term.shape[0] // 4
-    in_keep[...] = term[:half]
-    in_early[...] = term[half : half + quarter]
-    in_late[...] = term[half + quarter :]
+    place_term(term, keep, pair, near, far, slice(0, edge))
     term = low(matmul_left_t(grad_out[...], mixed[...]))
-    size = term.shape[0] // 8
-    for at, ref in enumerate((out_first, out_second, out_third, out_own)):
-        ref[:size, :] = term[size * at : size * (at + 1)]
-        ref[size:, :] = term[size * (at + 4) : size * (at + 5)]
+    place_term(term, keep, pair, near, far, slice(edge, edge + mixed.shape[1]))
 
 
 def attention_backward(
     place, cosine, sine, low_own, low_across, low_beside, attn, query, key, value, probs,
     attended, normed,
-    grad_packed, g_keep, g_send, grad_low, grad_attended, term_attn,
+    grad_packed, keep, pair, near, far, grad_low, grad_attended, term_attn,
 ):
     count = 128
     for at, ref in enumerate(
@@ -621,13 +621,13 @@
     for at in range(4):
         here = slice(count * at, count * (at + 1))
         cos, sin = cosine[here, :], sine[here, :]
-        for pair in range(2):
-            lanes = slice(LANES * pair, LANES * (pair + 1))
+        for half in range(2):
+            lanes = slice(LANES * half, LANES * (half + 1))
             q, k, v = query[here, lanes], key[here, lanes], value[here, lanes]
             grad = grad_attended[here, lanes]
             made = []
             for head in range(2):
-                slot = count * (4 * at + 2 * pair + head)
+                slot = count * (4 * at + 2 * half + head)
                 weights = probs[slot : slot + count, :]
                 grad_value = matmul_left_t(low(weights), grad)
                 grad_probs = matmul_right_t(grad * masks[head], v)
@@ -637,18 +637,19 @@
             grad_q, grad_k, grad_v = (jnp.where(is_first, *both) for both in zip(*made))
             grad_q = grad_q * HEAD_DIM ** (-0.5)
             grad_packed[here, lanes] = low(grad_q * cos - turned(grad_q) * sin)
-            lanes = slice(256 + LANES * pair, 256 + LANES * (pair + 1))
+            lanes = slice(256 + LANES * half, 256 + LANES * (half + 1))
             grad_packed[here, lanes] = low(grad_k * cos - turned(grad_k) * sin)
-            lanes = slice(512 + LANES * pair, 512 + LANES * (pair + 1))
+            lanes = slice(512 + LANES * half, 512 + LANES * (half + 1))
             grad_packed[here, lanes] = low(grad_v)
     term = low(matmul_left_t(normed[...], grad_packed[...]))
-    half = term.shape[0] // 2
-    g_keep[:, :768] = term[:half]
-    g_send[:, :768] = term[half:]
+    place_term(term, keep, pair, near, far, slice(0, 768))
     term_attn[...] = low(matmul_left_t(attended[...], grad_low[...]))
     size = term.shape[0] // 8
     part = size // 4
-    targets = [(ref, size * p) for ref in (g_keep, g_send) for p in range(4)]
+    targets = [
+        (keep, 0), (pair, 0), (keep, size), (keep, 2 * size),
+        (near, 0), (pair, size), (far, 0), (far, size),
+    ]
     for at, (ref, row) in enumerate(targets):
         source = pl.multiple_of(place_of(place, at % 4, at // 4) * part, part)
         for z_at in range(4):
@@ -813,16 +814,15 @@
             ((group, out_width), f32),
         ],
     )
-    in_keep, in_early, in_late, *out_terms = kernel(
+    all_width = in_width + out_width
+    size = width // 8
+    io_keep, io_pair, io_near, io_far = kernel(
         mlp_terms,
-        [((width // 2, in_width), b16)]
-        + [((width // 4, in_width), b16)] * 2
-        + [((width // 4, out_width), b16)] * 4,
-        (2 * group * width * (in_width + out_width), 0),
+        [((size * n, all_width), b16) for n in (3, 2, 1, 2)],
+        (2 * group * width * all_width, 0),
         normed_mlp, grad_inner, grad_out, mixed,
     )
-    out_up, out_down = up(out_terms[1]), down(out_terms[2])
-    in_early = over(in_early)
+    io_pair, io_far = up(io_pair), over(io_far)
     kept, sent = scatter_last(send, keep)
     scaled_mlp = kept + wide(swap(sent, 2))
     grad_hidden = wide(grad_out[:count]) + norm_backward_pass(
@@ -830,49 +830,43 @@
     )
     low_own = low(grad_hidden)
     low_across = swap(low_own, 2)
-    in_early, low_across, out_up = tie(in_early, low_across, out_up)
-    in_late = over(tie(in_late, in_early)[0])
     low_beside = swap(rows([low_own, low_across]), 1)
-    in_kept, in_first_two = split_rows(in_keep, 4), split_rows(in_early, 2)
-    in_up = up(low(wide(in_kept[1]) + wide(in_first_two[1])))
-    out_turned = up(low(wide(out_terms[0]) + wide(out_up)))
-
-    grad_packed, g_keep, g_send = kernel(
+
+    grad_packed, g_keep, g_pair, g_near, g_far = kernel(
         attention_backward,
-        [((group, 768), b16)] + [((width // 2, width), b16)] * 2,
+        [((group, 768), b16)] + [((size * n, width), b16) for n in (3, 2, 1, 2)],
         (2 * group * width * (768 + 512) + 10 * 16 * count * count * LANES, 0),
         place, cosine, sine, low_own, low_across, low_beside, attn, query, key, value, probs,
         attended, normed,
         scratch=[((group, width), b16), ((group, 256), b16), ((256, width), b16)],
         scalars=1,
     )
-    g_over = over(g_send)
-    in_late, in_up, out_turned, out_down, _ = tie(in_late, in_up, out_turned, out_down, g_keep)
-    in_last_two = split_rows(in_late, 2)
-    in_turned = up(low(wide(in_kept[0]) + wide(in_first_two[0]) + wide(in_up)))
-    in_down = down(low(wide(in_kept[2]) + wide(in_last_two[0])))
-    out_sums = split_rows(wide(out_terms[3]) + wide(out_turned) + wide(out_down), 2)
+    g_pair, g_far = up(g_pair), over(g_far)
+    io_pair, io_far, _ = tie(io_pair, io_far, g_near)
+    io_kept, io_pair, io_far = split_rows(io_keep, 3), split_rows(io_pair, 2), split_rows(io_far, 2)
+    io_near = over(low(wide(io_near) + wide(io_pair[1])))
+    io_down = down(low(wide(io_kept[1]) + wide(io_far[0])))
     send, keep = kernel(
         projections,
         [((4 * count, width), b16)] * 2,
         (2 * group * width * (768 + out_width), 0),
         grad_packed, qkv, mixed, w_down,
     )
-    g_over, send, in_turned, in_down = tie(g_over, send, in_turned, in_down)
-    g_sums = [wide(a) + wide(b) for a, b in zip(split_rows(g_keep, 4), split_rows(g_over, 4))]
-    g_up, g_down = up(low(g_sums[1])), down(low(g_sums[2]))
+    io_near, io_down, g_pair, g_far, send = tie(io_near, io_down, g_pair, g_far, send)
+    g_kept, g_pair, g_far = split_rows(g_keep, 3), split_rows(g_pair, 2), split_rows(g_far, 2)
+    g_near = over(low(wide(g_near) + wide(g_pair[1])))
+    g_down = down(low(wide(g_kept[1]) + wide(g_far[0])))
     kept, sent = scatter_last(send, keep)
-    out_over = over(tie(low(out_sums[1]), g_over)[0])
-    g_up, g_down, sent = tie(g_up, g_down, sent)
+    io_up = up(low(wide(io_kept[0]) + wide(io_pair[0]) + wide(io_near)))
+    io_up, g_near, g_down, sent = tie(io_up, g_near, g_down, sent)
+    g_up = up(low(wide(g_kept[0]) + wide(g_pair[0]) + wide(g_near)))
     last_across = swap(sent, 2)
-    g_turned = up(low(g_sums[0] + wide(g_up)))
-    out_over, _ = tie(out_over, g_up)
-    sum_in = wide(in_kept[3]) + wide(in_last_two[1]) + wide(in_turned) + wide(in_down)
-    sum_out = out_sums[0] + wide(out_over)
-    back = rep_exchange(columns([low(sum_in), low(sum_out)]))
-    g_turned, g_down, last_across = tie(g_turned, g_down, last_across)
+    back = rep_exchange(
+        low(wide(io_kept[2]) + wide(io_far[1]) + wide(io_down) + wide(io_up))
+    )
+    g_up, g_down, last_across = tie(g_up, g_down, last_across)
     last = kept + wide(last_across)
-    sum_g = low(g_sums[3] + wide(g_turned) + wide(g_down))
+    sum_g = low(wide(g_kept[2]) + wide(g_far[1]) + wide(g_down) + wide(g_up))
     back_qkv = rep_exchange(sum_g[:, :768])
     grad_w_attn_out = wide(
         lax.ppermute(

time: 260 us -> 267 us (1.027)
  local copies, waits for them, and re-layouts: 11.1 us -> 17.2 us
  other arithmetic: 24.5 us -> 30.3 us
  starting transfers between devices: 59.7 us -> 54.2 us
    ppermute x5 -> x4, starting transfers between devices: 14 us -> 7.94 us  [down(): return lax.ppermute(value, 'fsdp', [(k, (k - 2) % 8) for k in range(8)])]
    ppermute x11 -> x9, waiting for transfers between devices: 54.4 us -> 48.4 us  [up(): return lax.ppermute(value, 'fsdp', [(k, (k + 2) % 8) for k in range(8)])]
    convert_element_type x16, other arithmetic: 8.16 us -> 13.6 us  [low(): return value.astype(jnp.bfloat16)]
    ppermute x12, waiting for transfers between devices: 11.8 us -> 16.9 us  [swap(): return lax.ppermute(value, 'rep', [(k, k ^ distance) for k in range(4)])]
    ppermute x5 -> x4, waiting for transfers between devices: 12.8 us -> 16.1 us  [down(): return lax.ppermute(value, 'fsdp', [(k, (k - 2) % 8) for k in range(8)])]
  transfers between devices with their start and end apart: 44 -> 41, of which waited for: 26 -> 23; matrix products, arithmetic and copies ran while one was open for 9% -> 13% of each run, Pallas kernels for 10% -> 10%
where the time goes in v6:
time: 267 us; the launch traced here: 262 us
  waiting for transfers between devices  124 us (46%)
  starting transfers between devices  54.2 us (20%)
  Pallas kernels  34.7 us (13%)
  other arithmetic  30.3 us (11%)
  local copies, waits for them, and re-layouts  17.2 us (6%)
    ppermute x9, waiting for transfers between devices, up(): return lax.ppermute(value, 'fsdp', [(k, (k + 2) % 8) for k in range(8)])  48.4 us
    pallas_call x5, Pallas kernels, kernel(): pl.pallas_call(body, out_shape=shapes, in_specs=[pl.BlockSpec(memory_spac...  34.7 us
    ppermute x10, waiting for transfers between devices, over(): return lax.ppermute(value, 'fsdp', [(k, k ^ 1) for k in range(8)])  32.7 us
    all_to_all x4, starting transfers between devices, rep_exchange(): return lax.all_to_all(blocks, 'rep', 0, 0, tiled=True).reshape(value.shape)  18 us
    ppermute x12, waiting for transfers between devices, swap(): return lax.ppermute(value, 'rep', [(k, k ^ distance) for k in range(4)])  16.9 us
    ppermute x4, waiting for transfers between devices, down(): return lax.ppermute(value, 'fsdp', [(k, (k - 2) % 8) for k in range(8)])  16.1 us
    convert_element_type x16, other arithmetic, low(): return value.astype(jnp.bfloat16)  13.6 us
    ppermute x10, starting transfers between devices, over(): return lax.ppermute(value, 'fsdp', [(k, k ^ 1) for k in range(8)])  12.2 us
  transfers between devices with their start and end apart: 41, of which 23 were waited for; matrix products, arithmetic and copies ran while one was open for 13% of the time, Pallas kernels for 10%

profile of v6, /device:TPU:0, one launch (start us, length us, event | category | flops | bytes accessed | tf_op | source)
XLA Modules:
  0.0 261.8 jit_solution(6711943420076433631)
XLA Ops:
  5.4 7.0 %all-to-all-start = ((bf16[4,32,896]{2,1,0:T(8,128)(2,1)}), bf16[4,32,896]{2,1,0:T(8,128)(2,1)S(1)}, u32[]{:S(2)}, u32[]{:S(2)}) async-start(bf16[4,32,896]{2,1,0:T(8,128)(2,1)} %bitcast), calls=%async_computation | async-start | bytes 458752 | tf_op jit(solution)/shard_map/all_to_all | solution.py:418
  15.4 3.0 %all-to-all-done = bf16[4,32,896]{2,1,0:T(8,128)(2,1)S(1)} async-done(((bf16[4,32,896]{2,1,0:T(8,128)(2,1)}), bf16[4,32,896]{2,1,0:T(8,128)(2,1)S(1)}, u32[]{:S(2)}, u32[]{:S(2)}) %all-to-all-start) | async-done | bytes 229408 | tf_op jit(solution)/shard_map/all_to_all | solution.py:418
  18.4 3.5 %all-to-all-start.1 = ((bf16[4,32,2176]{2,1,0:T(8,128)(2,1)}), bf16[4,32,2176]{2,1,0:T(8,128)(2,1)S(1)}, u32[]{:S(2)}, u32[]{:S(2)}) async-start(bf16[4,32,2176]{2,1,0:T(8,128)(2,1)} %bitcast.3), calls=%async_computation.1 | async-start | bytes 1114112 | tf_op jit(solution)/shard_map/all_to_all | solution.py:418
  21.9 2.7 %collective-permute-start.3 = (bf16[128,1024]{1,0:T(8,128)(2,1)S(1)}, bf16[128,1024]{1,0:T(8,128)(2,1)S(1)}, u32[]{:S(2)}, u32[]{:S(2)}) collective-permute-start(bf16[128,1024]{1,0:T(8,128)(2,1)S(1)} %maximum_maximum_fusion.own), channel_id=1, source_target_pairs={{0,4},{4,0},{8,12},{12,8},{16,20},{20,16},{24,28},{28,24},{1,5},{5... | collective-permute-start | bytes 786440 | tf_op jit(solution)/shard_map/ppermute | solution.py:430
  26.6 4.8 %collective-permute-done.3.other = bf16[128,1024]{1,0:T(8,128)(2,1)S(1)} collective-permute-done((bf16[128,1024]{1,0:T(8,128)(2,1)S(1)}, bf16[128,1024]{1,0:T(8,128)(2,1)S(1)}, u32[]{:S(2)}, u32[]{:S(2)}) %collective-permute-start.3) | collective-permute-done | bytes 262176 | tf_op jit(solution)/shard_map/ppermute | solution.py:430
  33.2 5.8 %collective-permute-done.1.third = bf16[128,1024]{1,0:T(8,128)(2,1)S(1)} collective-permute-done((bf16[128,1024]{1,0:T(8,128)(2,1)S(1)}, bf16[128,1024]{1,0:T(8,128)(2,1)S(1)}, u32[]{:S(2)}, u32[]{:S(2)}) %collective-permute-start.1) | collective-permute-done | bytes 262176 | tf_op jit(solution)/shard_map/ppermute | solution.py:422
  42.9 7.4 %collective-permute-done.4.second = bf16[128,1024]{1,0:T(8,128)(2,1)S(1)} collective-permute-done((bf16[128,1024]{1,0:T(8,128)(2,1)S(1)}, bf16[128,1024]{1,0:T(8,128)(2,1)S(1)}, u32[]{:S(2)}, u32[]{:S(2)}) %collective-permute-start.4) | collective-permute-done | bytes 262176 | tf_op jit(solution)/shard_map/ppermute | solution.py:422
  50.4 3.0 %collective-permute-done.5.others = bf16[256,1024]{1,0:T(8,128)(2,1)} collective-permute-done((bf16[256,1024]{1,0:T(8,128)(2,1)}, bf16[256,1024]{1,0:T(8,128)(2,1)}, u32[]{:S(2)}, u32[]{:S(2)}) %collective-permute-start.5) | collective-permute-done | bytes 524320 | tf_op jit(solution)/shard_map/ppermute | solution.py:430
  57.4 5.0 %collective-permute-done.8.other_second = bf16[128,1024]{1,0:T(8,128)(2,1)S(1)} collective-permute-done((bf16[128,1024]{1,0:T(8,128)(2,1)S(1)}, bf16[128,1024]{1,0:T(8,128)(2,1)S(1)}, u32[]{:S(2)}, u32[]{:S(2)}) %collective-permute-start.8) | collective-permute-done | bytes 262176 | tf_op jit(solution)/shard_map/ppermute | solution.py:430
  65.4 9.2 %attention_forward.1 = (bf16[512,1024]{1,0:T(8,128)(2,1)}, bf16[1024,768]{1,0:T(8,128)(2,1)}, bf16[256,1024]{1,0:T(8,128)(2,1)S(1)}, bf16[512,256]{1,0:T(8,128)(...) custom-call(s32[2]{0:T(128)S(1)} %pad_add_fusion.place, ...), custom_call_target="tpu_custom_call" | custom-call | flops 1207959552 | bytes 11014152 | tf_op jit(solution)/shard_map/attention_forward/pallas_call | solution.py:680
  74.7 7.9 %collective-permute-done.9.third = bf16[128,2176]{1,0:T(8,128)(2,1)} collective-permute-done((bf16[128,2176]{1,0:T(8,128)(2,1)S(1)}, bf16[128,2176]{1,0:T(8,128)(2,1)}, u32[]{:S(2)}, u32[]{:S(2)}) %collective-permute-start.9) | collective-permute-done | bytes 557088 | tf_op jit(solution)/shard_map/ppermute | solution.py:422
  88.1 4.8 %collective-permute-done.13 = bf16[128,1024]{1,0:T(8,128)(2,1)S(1)} collective-permute-done((bf16[128,1024]{1,0:T(8,128)(2,1)S(1)}, bf16[128,1024]{1,0:T(8,128)(2,1)S(1)}, u32[]{:S(2)}, u32[]{:S(2)}) %collective-permute-start.13) | collective-permute-done | bytes 262176 | tf_op jit(solution)/shard_map/ppermute | solution.py:413
  95.1 5.7 %collective-permute-done.17.other_third = bf16[128,2176]{1,0:T(8,128)(2,1)S(1)} collective-permute-done((bf16[128,2176]{1,0:T(8,128)(2,1)}, bf16[128,2176]{1,0:T(8,128)(2,1)S(1)}, u32[]{:S(2)}, u32[]{:S(2)}) %collective-permute-start.17) | collective-permute-done | bytes 557088 | tf_op jit(solution)/shard_map/ppermute | solution.py:430
  103.1 11.5 %collective-permute-done.18.other_first = bf16[128,2176]{1,0:T(8,128)(2,1)S(1)} collective-permute-done((bf16[128,2176]{1,0:T(8,128)(2,1)}, bf16[128,2176]{1,0:T(8,128)(2,1)S(1)}, u32[]{:S(2)}, u32[]{:S(2)}) %collective-permute-start.18) | collective-permute-done | bytes 557088 | tf_op jit(solution)/shard_map/ppermute | solution.py:430
  114.6 3.4 %collective-permute-done.19.other_second = bf16[128,2176]{1,0:T(8,128)(2,1)S(1)} collective-permute-done((bf16[128,2176]{1,0:T(8,128)(2,1)S(1)}, bf16[128,2176]{1,0:T(8,128)(2,1)S(1)}, u32[]{:S(2)}, u32[]{:S(2)}) %collective-permute-start.19) | collective-permute-done | bytes 557088 | tf_op jit(solution)/shard_map/ppermute | solution.py:422
  118.8 8.4 %mlp.1 = (bf16[512,1024]{1,0:T(8,128)(2,1)}, bf16[512,1024]{1,0:T(8,128)(2,1)}, bf16[512,768]{1,0:T(8,128)(2,1)}, bf16[512,1408]{1,0:T(8,128)(2,1)}, bf16[256,10...) custom-call(s32[512,1]{1,0:T(8,128)S(1)} %copy.22.seg_col, ...), custom_call_target="tpu_custom_call" | custom-call | flops 3758096384 | bytes 14551040 | tf_op jit(solution)/shard_map/mlp/pallas_call | solution.py:680
  133.4 5.1 %mlp_terms.1 = (bf16[384,2176]{1,0:T(8,128)(2,1)}, bf16[256,2176]{1,0:T(8,128)(2,1)S(1)}, bf16[128,2176]{1,0:T(8,128)(2,1)S(1)}, bf16[256,2176]{1,0:T(8,128)(2,1)S(1)}) custom-call(bf16[512,1024]{1,0:T(8,128)(2,1)S(1)} %copy-done.4, bf16[512,1408]{1,0:T(8,128)(2,1)} %get-tuple-element.108.grad_inner, bf16[512,1024]{1,0:T(8,128)(2,1)S(1)} %copy-done, ...), custom_call_target="tpu_custom_call" | custom-call | flops 2281701376 | bytes 8781824 | tf_op jit(solution)/shard_map/mlp_terms/pallas_call | solution.py:680
  142.8 6.3 %collective-permute-done.22.low_across = bf16[128,1024]{1,0:T(8,128)(2,1)S(1)} collective-permute-done((bf16[128,1024]{1,0:T(8,128)(2,1)S(1)}, bf16[128,1024]{1,0:T(8,128)(2,1)S(1)}, u32[]{:S(2)}, u32[]{:S(2)}) %collective-permute-start.22) | collective-permute-done | bytes 262176 | tf_op jit(solution)/shard_map/ppermute | solution.py:413
  151.1 8.7 %attention_backward.1 = (bf16[512,768]{1,0:T(8,128)(2,1)S(1)}, bf16[384,1024]{1,0:T(8,128)(2,1)S(1)}, bf16[256,1024]{1,0:T(8,128)(2,1)S(1)}, bf16[128,1024]{1,0:T(8,128)(2,1)S(1)}, bf16[256,1024]{1,0:T(8,128)(2,1)S(1)}) custom-call(s32[2]{0:T(128)S(1)} %pad_add_fusion.place, f32[512,128]{1,0:T(8,128)S(1)} %get-tuple-element.266.cosine, ...), custom_call_target="tpu_custom_call" | custom-call | flops 1677721600 | bytes 8126472 | tf_op jit(solution)/shard_map/attention_backward/pallas_call | solution.py:680
  159.8 7.0 %collective-permute-done.24 = bf16[256,2176]{1,0:T(8,128)(2,1)} collective-permute-done((bf16[256,2176]{1,0:T(8,128)(2,1)S(1)}, bf16[256,2176]{1,0:T(8,128)(2,1)}, u32[]{:S(2)}, u32[]{:S(2)}) %collective-permute-start.24) | collective-permute-done | bytes 1114144 | tf_op jit(solution)/shard_map/ppermute | solution.py:422
  173.9 3.2 %projections.1 = (bf16[512,1024]{1,0:T(8,128)(2,1)S(1)}, bf16[512,1024]{1,0:T(8,128)(2,1)S(1)}) custom-call(bf16[512,768]{1,0:T(8,128)(2,1)S(1)} %get-tuple-element.102.grad_packed, bf16[1024,768]{1,0:T(8,128)(2,1)S(1)} %copy-done.1, bf16[512,768]{1,0:T(8,128)(2,1)S(1)} %copy-done.3, bf16[1024,768]{1,0:T(8,128)(2,1)} %get-tuple-element.105.w_down), custom_call_target="tpu_custom_call" | custom-call | flops 1610612736 | bytes 6815744 | tf_op jit(solution)/shard_map/projections/pallas_call | solution.py:680
  177.1 15.4 %collective-permute-done.28 = bf16[256,1024]{1,0:T(8,128)(2,1)S(1)} collective-permute-done((bf16[256,1024]{1,0:T(8,128)(2,1)S(1)}, bf16[256,1024]{1,0:T(8,128)(2,1)S(1)}, u32[]{:S(2)}, u32[]{:S(2)}) %collective-permute-start.28) | collective-permute-done | bytes 524320 | tf_op jit(solution)/shard_map/ppermute | solution.py:422
  192.6 2.7 %collective-permute-done.29 = bf16[256,1024]{1,0:T(8,128)(2,1)S(1)} collective-permute-done((bf16[256,1024]{1,0:T(8,128)(2,1)S(1)}, bf16[256,1024]{1,0:T(8,128)(2,1)S(1)}, u32[]{:S(2)}, u32[]{:S(2)}) %collective-permute-start.29) | collective-permute-done | bytes 524320 | tf_op jit(solution)/shard_map/ppermute | solution.py:430
  197.5 3.3 %collective-permute-start.33 = (bf16[128,1024]{1,0:T(8,128)(2,1)S(1)}, bf16[128,1024]{1,0:T(8,128)(2,1)S(1)}, u32[]{:S(2)}, u32[]{:S(2)}) collective-permute-start(bf16[128,1024]{1,0:T(8,128)(2,1)S(1)} %add_convert_fusion.7), channel_id=1, source_target_pairs={{0,24},{4,28},{8,0},{12,4},{16,8},{20,12},{24,16},{28,20},{1,25},{... | collective-permute-start | bytes 786440 | tf_op jit(solution)/shard_map/ppermute | solution.py:426
  203.5 14.3 %collective-permute-done.33 = bf16[128,1024]{1,0:T(8,128)(2,1)S(1)} collective-permute-done((bf16[128,1024]{1,0:T(8,128)(2,1)S(1)}, bf16[128,1024]{1,0:T(8,128)(2,1)S(1)}, u32[]{:S(2)}, u32[]{:S(2)}) %collective-permute-start.33) | collective-permute-done | bytes 262176 | tf_op jit(solution)/shard_map/ppermute | solution.py:426
  217.8 2.3 add_convert_fusion
  220.0 4.1 %all-to-all-start.3 = ((bf16[4,32,2176]{2,1,0:T(8,128)(2,1)}), bf16[4,32,2176]{2,1,0:T(8,128)(2,1)}, u32[]{:S(2)}, u32[]{:S(2)}) async-start(bf16[4,32,2176]{2,1,0:T(8,128)(2,1)} %bitcast.34), calls=%async_computation.3 | async-start | bytes 1114112 | tf_op jit(solution)/shard_map/all_to_all | solution.py:418
  226.8 2.0 collective-permute-start.35
  228.8 5.1 %all-to-all-done.3 = bf16[4,32,2176]{2,1,0:T(8,128)(2,1)} async-done(((bf16[4,32,2176]{2,1,0:T(8,128)(2,1)}), bf16[4,32,2176]{2,1,0:T(8,128)(2,1)}, u32[]{:S(2)}, u32[]{:S(2)}) %all-to-all-start.3) | async-done | bytes 557088 | tf_op jit(solution)/shard_map/all_to_all | solution.py:418
  243.3 1.9 concatenate.143
  245.2 2.6 %convert_multiply_fusion = (f32[32,5248]{1,0:T(8,128)}, f32[32]{0:T(128)}) fusion(bf16[32,5248]{1,0:T(8,128)(2,1)} %concatenate.143, f32[32]{0:T(128)} %copy-done.25, bf16[32,5248]{1,0:T(8,128)(2,1)S(1)} %copy-done.7), kind=kLoop, calls=%fused_computation.7 | loop fusion | flops 839648 | bytes 1343744 | tf_op jit(solution)/shard_map/mul | solution.py:907
  251.5 3.4 %all-to-all-start.2 = ((bf16[4,32,768]{2,1,0:T(8,128)(2,1)}), bf16[4,32,768]{2,1,0:T(8,128)(2,1)S(1)}, u32[]{:S(2)}, u32[]{:S(2)}) async-start(bf16[4,32,768]{2,1,0:T(8,128)(2,1)} %bitcast.9), calls=%async_computation.2 | async-start | bytes 393216 | tf_op jit(solution)/shard_map/all_to_all | solution.py:418
  (255 shorter events, 79.9 us)
Async XLA Ops:
  0.7 14.7 %collective-permute-start = (bf16[32,1024]{1,0:T(8,128)(2,1)}, bf16[32,1024]{1,0:T(8,128)(2,1)S(1)}, u32[]{:S(2)}, u32[]{:S(2)}) collective-permute-start(bf16[32,1024]{1,0:T(8,128)(2,1)} %param.14), channel_id=1, source_target_pairs={{0,0},{1,4},{2,8},{3,12},{4,16},{5,20},{6,24},{7,28},{8,1},{9,5},{... | collective-permute-start | bytes 196616 | tf_op jit(solution)/shard_map/ppermute | solution.py:729
  5.4 13.0 %all-to-all-start = ((bf16[4,32,896]{2,1,0:T(8,128)(2,1)}), bf16[4,32,896]{2,1,0:T(8,128)(2,1)S(1)}, u32[]{:S(2)}, u32[]{:S(2)}) async-start(bf16[4,32,896]{2,1,0:T(8,128)(2,1)} %bitcast), calls=%async_computation | async-start | bytes 458752 | tf_op jit(solution)/shard_map/all_to_all | solution.py:418
  18.4 20.6 %all-to-all-start.1 = ((bf16[4,32,2176]{2,1,0:T(8,128)(2,1)}), bf16[4,32,2176]{2,1,0:T(8,128)(2,1)S(1)}, u32[]{:S(2)}, u32[]{:S(2)}) async-start(bf16[4,32,2176]{2,1,0:T(8,128)(2,1)} %bitcast.3), calls=%async_computation.1 | async-start | bytes 1114112 | tf_op jit(solution)/shard_map/all_to_all | solution.py:418
  21.9 9.5 %collective-permute-start.3 = (bf16[128,1024]{1,0:T(8,128)(2,1)S(1)}, bf16[128,1024]{1,0:T(8,128)(2,1)S(1)}, u32[]{:S(2)}, u32[]{:S(2)}) collective-permute-start(bf16[128,1024]{1,0:T(8,128)(2,1)S(1)} %maximum_maximum_fusion.own), channel_id=1, source_target_pairs={{0,4},{4,0},{8,12},{12,8},{16,20},{20,16},{24,28},{28,24},{1,5},{5... | collective-permute-start | bytes 786440 | tf_op jit(solution)/shard_map/ppermute | solution.py:430
  26.0 13.1 %collective-permute-start.1 = (bf16[128,1024]{1,0:T(8,128)(2,1)S(1)}, bf16[128,1024]{1,0:T(8,128)(2,1)S(1)}, u32[]{:S(2)}, u32[]{:S(2)}) collective-permute-start(bf16[128,1024]{1,0:T(8,128)(2,1)S(1)} %maximum_maximum_fusion.own), channel_id=1, source_target_pairs={{0,8},{4,12},{8,16},{12,20},{16,24},{20,28},{24,0},{28,4},{1,9},{5... | collective-permute-start | bytes 786440 | tf_op jit(solution)/shard_map/ppermute | solution.py:422
  39.9 13.5 %collective-permute-start.5 = (bf16[256,1024]{1,0:T(8,128)(2,1)}, bf16[256,1024]{1,0:T(8,128)(2,1)}, u32[]{:S(2)}, u32[]{:S(2)}) collective-permute-start(bf16[256,1024]{1,0:T(8,128)(2,1)} %pad_maximum_fusion.3), channel_id=1, source_target_pairs={{0,4},{4,0},{8,12},{12,8},{16,20},{20,16},{24,28},{28,24},{1,5},{5... | collective-permute-start | bytes 1572872 | tf_op jit(solution)/shard_map/ppermute | solution.py:430
  40.2 13.1 %collective-permute-start.6 = (bf16[256,1024]{1,0:T(8,128)(2,1)S(1)}, bf16[256,1024]{1,0:T(8,128)(2,1)S(1)}, u32[]{:S(2)}, u32[]{:S(2)}) collective-permute-start(bf16[256,1024]{1,0:T(8,128)(2,1)S(1)} %pad_maximum_fusion.2.mine), channel_id=1, source_target_pairs={{0,2},{1,3},{2,0},{3,1},{4,6},{5,7},{6,4},{7,5},{8,10},{9,11},{10,... | collective-permute-start | bytes 1572872 | tf_op jit(solution)/shard_map/ppermute | solution.py:413
  53.4 8.9 %collective-permute-start.7 = (bf16[512,1024]{1,0:T(8,128)(2,1)S(1)}, bf16[512,1024]{1,0:T(8,128)(2,1)S(1)}, u32[]{:S(2)}, u32[]{:S(2)}) collective-permute-start(bf16[512,1024]{1,0:T(8,128)(2,1)S(1)} %pad_maximum_fusion), channel_id=1, source_target_pairs={{0,1},{1,0},{2,3},{3,2},{4,5},{5,4},{6,7},{7,6},{8,9},{9,8},{10,11... | collective-permute-start | bytes 3145736 | tf_op jit(solution)/shard_map/ppermute | solution.py:413
  53.6 8.8 %collective-permute-start.8 = (bf16[128,1024]{1,0:T(8,128)(2,1)S(1)}, bf16[128,1024]{1,0:T(8,128)(2,1)S(1)}, u32[]{:S(2)}, u32[]{:S(2)}) collective-permute-start(bf16[128,1024]{1,0:T(8,128)(2,1)S(1)} %collective-permute-done.4.second), channel_id=1, source_target_pairs={{0,4},{4,0},{8,12},{12,8},{16,20},{20,16},{24,28},{28,24},{1,5},{5... | collective-permute-start | bytes 786440 | tf_op jit(solution)/shard_map/ppermute | solution.py:430
  55.3 19.3 %collective-permute-start.10 = (bf16[128,2176]{1,0:T(8,128)(2,1)S(1)}, bf16[128,2176]{1,0:T(8,128)(2,1)}, u32[]{:S(2)}, u32[]{:S(2)}) collective-permute-start(bf16[128,2176]{1,0:T(8,128)(2,1)S(1)} %bitcast.29), channel_id=1, source_target_pairs={{0,24},{4,28},{8,0},{12,4},{16,8},{20,12},{24,16},{28,20},{1,25},{... | collective-permute-start | bytes 1671176 | tf_op jit(solution)/shard_map/ppermute | solution.py:426
  56.8 25.7 %collective-permute-start.9 = (bf16[128,2176]{1,0:T(8,128)(2,1)S(1)}, bf16[128,2176]{1,0:T(8,128)(2,1)}, u32[]{:S(2)}, u32[]{:S(2)}) collective-permute-start(bf16[128,2176]{1,0:T(8,128)(2,1)S(1)} %bitcast.30), channel_id=1, source_target_pairs={{0,8},{4,12},{8,16},{12,20},{16,24},{20,28},{24,0},{28,4},{1,9},{5... | collective-permute-start | bytes 1671176 | tf_op jit(solution)/shard_map/ppermute | solution.py:422
  62.4 20.2 %collective-permute-start.11 = (bf16[128,2176]{1,0:T(8,128)(2,1)S(1)}, bf16[128,2176]{1,0:T(8,128)(2,1)}, u32[]{:S(2)}, u32[]{:S(2)}) collective-permute-start(bf16[128,2176]{1,0:T(8,128)(2,1)S(1)} %bitcast.31), channel_id=1, source_target_pairs={{0,4},{4,0},{8,12},{12,8},{16,20},{20,16},{24,28},{28,24},{1,5},{5... | collective-permute-start | bytes 1671176 | tf_op jit(solution)/shard_map/ppermute | solution.py:430
  86.2 14.7 %collective-permute-start.17 = (bf16[128,2176]{1,0:T(8,128)(2,1)}, bf16[128,2176]{1,0:T(8,128)(2,1)S(1)}, u32[]{:S(2)}, u32[]{:S(2)}) collective-permute-start(bf16[128,2176]{1,0:T(8,128)(2,1)} %collective-permute-done.9.third), channel_id=1, source_target_pairs={{0,4},{4,0},{8,12},{12,8},{16,20},{20,16},{24,28},{28,24},{1,5},{5... | collective-permute-start | bytes 1671176 | tf_op jit(solution)/shard_map/ppermute | solution.py:430
  86.9 16.1 %collective-permute-start.16 = (bf16[128,2176]{1,0:T(8,128)(2,1)}, bf16[128,2176]{1,0:T(8,128)(2,1)S(1)}, u32[]{:S(2)}, u32[]{:S(2)}) collective-permute-start(bf16[128,2176]{1,0:T(8,128)(2,1)} %collective-permute-done.9.third), channel_id=1, source_target_pairs={{0,8},{4,12},{8,16},{12,20},{16,24},{20,28},{24,0},{28,4},{1,9},{5... | collective-permute-start | bytes 1671176 | tf_op jit(solution)/shard_map/ppermute | solution.py:422
  93.6 9.4 %collective-permute-start.14 = (bf16[128,1024]{1,0:T(8,128)(2,1)S(1)}, bf16[128,1024]{1,0:T(8,128)(2,1)S(1)}, u32[]{:S(2)}, u32[]{:S(2)}) collective-permute-start(bf16[128,1024]{1,0:T(8,128)(2,1)S(1)} %fusion.14.norm_own), channel_id=1, source_target_pairs={{0,2},{1,3},{2,0},{3,1},{4,6},{5,7},{6,4},{7,5},{8,10},{9,11},{10,... | collective-permute-start | bytes 786440 | tf_op jit(solution)/shard_map/ppermute | solution.py:413
  100.9 13.7 %collective-permute-start.18 = (bf16[128,2176]{1,0:T(8,128)(2,1)}, bf16[128,2176]{1,0:T(8,128)(2,1)S(1)}, u32[]{:S(2)}, u32[]{:S(2)}) collective-permute-start(bf16[128,2176]{1,0:T(8,128)(2,1)} %collective-permute-done.10.first), channel_id=1, source_target_pairs={{0,4},{4,0},{8,12},{12,8},{16,20},{20,16},{24,28},{28,24},{1,5},{5... | collective-permute-start | bytes 1671176 | tf_op jit(solution)/shard_map/ppermute | solution.py:430
  103.0 15.0 %collective-permute-start.19 = (bf16[128,2176]{1,0:T(8,128)(2,1)S(1)}, bf16[128,2176]{1,0:T(8,128)(2,1)S(1)}, u32[]{:S(2)}, u32[]{:S(2)}) collective-permute-start(bf16[128,2176]{1,0:T(8,128)(2,1)S(1)} %collective-permute-done.17.other_third), channel_id=1, source_target_pairs={{0,8},{4,12},{8,16},{12,20},{16,24},{20,28},{24,0},{28,4},{1,9},{5... | collective-permute-start | bytes 1671176 | tf_op jit(solution)/shard_map/ppermute | solution.py:422
  103.0 14.9 %collective-permute-start.15 = (bf16[256,1024]{1,0:T(8,128)(2,1)S(1)}, bf16[256,1024]{1,0:T(8,128)(2,1)S(1)}, u32[]{:S(2)}, u32[]{:S(2)}) collective-permute-start(bf16[256,1024]{1,0:T(8,128)(2,1)S(1)} %pad_maximum_fusion.4), channel_id=1, source_target_pairs={{0,1},{1,0},{2,3},{3,2},{4,5},{5,4},{6,7},{7,6},{8,9},{9,8},{10,11... | collective-permute-start | bytes 1572872 | tf_op jit(solution)/shard_map/ppermute | solution.py:413
  129.2 10.8 %collective-permute-start.21 = (bf16[128,1024]{1,0:T(8,128)(2,1)S(1)}, bf16[128,1024]{1,0:T(8,128)(2,1)S(1)}, u32[]{:S(2)}, u32[]{:S(2)}) collective-permute-start(bf16[128,1024]{1,0:T(8,128)(2,1)S(1)} %add_convert_fusion.9), channel_id=1, source_target_pairs={{0,2},{1,3},{2,0},{3,1},{4,6},{5,7},{6,4},{7,5},{8,10},{9,11},{10,... | collective-permute-start | bytes 786440 | tf_op jit(solution)/shard_map/ppermute | solution.py:413
  138.5 28.2 %collective-permute-start.24 = (bf16[256,2176]{1,0:T(8,128)(2,1)S(1)}, bf16[256,2176]{1,0:T(8,128)(2,1)}, u32[]{:S(2)}, u32[]{:S(2)}) collective-permute-start(bf16[256,2176]{1,0:T(8,128)(2,1)S(1)} %get-tuple-element.110), channel_id=1, source_target_pairs={{0,8},{4,12},{8,16},{12,20},{16,24},{20,28},{24,0},{28,4},{1,9},{5... | collective-permute-start | bytes 3342344 | tf_op jit(solution)/shard_map/ppermute | solution.py:422
  138.5 28.2 %collective-permute-start.25 = (bf16[256,2176]{1,0:T(8,128)(2,1)S(1)}, bf16[256,2176]{1,0:T(8,128)(2,1)}, u32[]{:S(2)}, u32[]{:S(2)}) collective-permute-start(bf16[256,2176]{1,0:T(8,128)(2,1)S(1)} %get-tuple-element.111), channel_id=1, source_target_pairs={{0,4},{4,0},{8,12},{12,8},{16,20},{20,16},{24,28},{28,24},{1,5},{5... | collective-permute-start | bytes 3342344 | tf_op jit(solution)/shard_map/ppermute | solution.py:430
  168.0 27.2 %collective-permute-start.27 = (bf16[128,2176]{1,0:T(8,128)(2,1)S(1)}, bf16[128,2176]{1,0:T(8,128)(2,1)S(1)}, u32[]{:S(2)}, u32[]{:S(2)}) collective-permute-start(bf16[128,2176]{1,0:T(8,128)(2,1)S(1)} %add_convert_fusion.2), channel_id=1, source_target_pairs={{0,24},{4,28},{8,0},{12,4},{16,8},{20,12},{24,16},{28,20},{1,25},{... | collective-permute-start | bytes 1671176 | tf_op jit(solution)/shard_map/ppermute | solution.py:426
  171.0 24.2 %collective-permute-start.26 = (bf16[128,2176]{1,0:T(8,128)(2,1)S(1)}, bf16[128,2176]{1,0:T(8,128)(2,1)S(1)}, u32[]{:S(2)}, u32[]{:S(2)}) collective-permute-start(bf16[128,2176]{1,0:T(8,128)(2,1)S(1)} %add_convert_fusion.3), channel_id=1, source_target_pairs={{0,4},{4,0},{8,12},{12,8},{16,20},{20,16},{24,28},{28,24},{1,5},{5... | collective-permute-start | bytes 1671176 | tf_op jit(solution)/shard_map/ppermute | solution.py:430
  172.5 20.1 %collective-permute-start.28 = (bf16[256,1024]{1,0:T(8,128)(2,1)S(1)}, bf16[256,1024]{1,0:T(8,128)(2,1)S(1)}, u32[]{:S(2)}, u32[]{:S(2)}) collective-permute-start(bf16[256,1024]{1,0:T(8,128)(2,1)S(1)} %get-tuple-element.116), channel_id=1, source_target_pairs={{0,8},{4,12},{8,16},{12,20},{16,24},{20,28},{24,0},{28,4},{1,9},{5... | collective-permute-start | bytes 1572872 | tf_op jit(solution)/shard_map/ppermute | solution.py:422
  172.8 22.4 %collective-permute-start.29 = (bf16[256,1024]{1,0:T(8,128)(2,1)S(1)}, bf16[256,1024]{1,0:T(8,128)(2,1)S(1)}, u32[]{:S(2)}, u32[]{:S(2)}) collective-permute-start(bf16[256,1024]{1,0:T(8,128)(2,1)S(1)} %get-tuple-element.117), channel_id=1, source_target_pairs={{0,4},{4,0},{8,12},{12,8},{16,20},{20,16},{24,28},{28,24},{1,5},{5... | collective-permute-start | bytes 1572872 | tf_op jit(solution)/shard_map/ppermute | solution.py:430
  196.7 21.1 %collective-permute-start.31 = (bf16[128,2176]{1,0:T(8,128)(2,1)S(1)}, bf16[128,2176]{1,0:T(8,128)(2,1)S(1)}, u32[]{:S(2)}, u32[]{:S(2)}) collective-permute-start(bf16[128,2176]{1,0:T(8,128)(2,1)S(1)} %add_convert_fusion.1), channel_id=1, source_target_pairs={{0,8},{4,12},{8,16},{12,20},{16,24},{20,28},{24,0},{28,4},{1,9},{5... | collective-permute-start | bytes 1671176 | tf_op jit(solution)/shard_map/ppermute | solution.py:422
  197.5 20.3 %collective-permute-start.33 = (bf16[128,1024]{1,0:T(8,128)(2,1)S(1)}, bf16[128,1024]{1,0:T(8,128)(2,1)S(1)}, u32[]{:S(2)}, u32[]{:S(2)}) collective-permute-start(bf16[128,1024]{1,0:T(8,128)(2,1)S(1)} %add_convert_fusion.7), channel_id=1, source_target_pairs={{0,24},{4,28},{8,0},{12,4},{16,8},{20,12},{24,16},{28,20},{1,25},{... | collective-permute-start | bytes 786440 | tf_op jit(solution)/shard_map/ppermute | solution.py:426
  200.8 16.9 %collective-permute-start.32 = (bf16[128,1024]{1,0:T(8,128)(2,1)S(1)}, bf16[128,1024]{1,0:T(8,128)(2,1)S(1)}, u32[]{:S(2)}, u32[]{:S(2)}) collective-permute-start(bf16[128,1024]{1,0:T(8,128)(2,1)S(1)} %add_convert_fusion.8), channel_id=1, source_target_pairs={{0,4},{4,0},{8,12},{12,8},{16,20},{20,16},{24,28},{28,24},{1,5},{5... | collective-permute-start | bytes 786440 | tf_op jit(solution)/shard_map/ppermute | solution.py:430
  220.0 13.9 %all-to-all-start.3 = ((bf16[4,32,2176]{2,1,0:T(8,128)(2,1)}), bf16[4,32,2176]{2,1,0:T(8,128)(2,1)}, u32[]{:S(2)}, u32[]{:S(2)}) async-start(bf16[4,32,2176]{2,1,0:T(8,128)(2,1)} %bitcast.34), calls=%async_computation.3 | async-start | bytes 1114112 | tf_op jit(solution)/shard_map/all_to_all | solution.py:418
  226.5 21.4 %collective-permute-start.34 = (bf16[128,1024]{1,0:T(8,128)(2,1)}, bf16[128,1024]{1,0:T(8,128)(2,1)}, u32[]{:S(2)}, u32[]{:S(2)}) collective-permute-start(bf16[128,1024]{1,0:T(8,128)(2,1)} %add_convert_fusion.6), channel_id=1, source_target_pairs={{0,8},{4,12},{8,16},{12,20},{16,24},{20,28},{24,0},{28,4},{1,9},{5... | collective-permute-start | bytes 786440 | tf_op jit(solution)/shard_map/ppermute | solution.py:422
  226.8 21.1 %collective-permute-start.35 = (bf16[256,1024]{1,0:T(8,128)(2,1)}, bf16[256,1024]{1,0:T(8,128)(2,1)}, u32[]{:S(2)}, u32[]{:S(2)}) collective-permute-start(bf16[256,1024]{1,0:T(8,128)(2,1)} %add_convert_fusion.4), channel_id=1, source_target_pairs={{0,2},{1,3},{2,0},{3,1},{4,6},{5,7},{6,4},{7,5},{8,10},{9,11},{10,... | collective-permute-start | bytes 1572872 | tf_op jit(solution)/shard_map/ppermute | solution.py:413
  251.5 8.7 %all-to-all-start.2 = ((bf16[4,32,768]{2,1,0:T(8,128)(2,1)}), bf16[4,32,768]{2,1,0:T(8,128)(2,1)S(1)}, u32[]{:S(2)}, u32[]{:S(2)}) async-start(bf16[4,32,768]{2,1,0:T(8,128)(2,1)} %bitcast.9), calls=%async_computation.2 | async-start | bytes 393216 | tf_op jit(solution)/shard_map/all_to_all | solution.py:418
  (40 other events, 213.5 us)

commit v7 on v6

--- a/solution.py
+++ b/solution.py
@@ -673,6 +673,39 @@
         send[2 * count + row : 3 * count + row, :] = total[3 * count :]
 
 
+def unpack_rest(back, w_in, gain, grad_in, gain_grad, grad_out):
+    size, hidden, part = w_in.shape[0], w_in.shape[1] // 2, w_in.shape[1] // 8
+    main = part // LANES * LANES
+    rest, edge = part - main, 2 * main + LANES
+    total = jnp.zeros(gain_grad.shape, jnp.float32)
+    for k in range(4):
+        here = slice(size * k, size * (k + 1))
+        for half in range(2):
+            base = hidden * half + part * k
+            for source, target, count in (
+                (main * half, base, main),
+                (2 * main + rest * half, base + main, rest),
+            ):
+                piece = wide(back[here, source : source + count])
+                grad_in[:, target : target + count] = piece * gain[...]
+                weights = wide(w_in[:, target : target + count])
+                total += jnp.sum(piece * weights, axis=1, keepdims=True)
+        grad_out[:, part * k : part * (k + 1)] = wide(back[here, edge : edge + part])
+    gain_grad[...] = total
+
+
+def unpack_qkv(back, w_qkv, gain, grad, gain_grad):
+    size, part = w_qkv.shape[0], 256
+    total = jnp.zeros(gain_grad.shape, jnp.float32)
+    for k in range(4):
+        for third in range(3):
+            piece = wide(back[size * k : size * (k + 1), part * third : part * (third + 1)])
+            lanes = slice(part * (4 * third + k), part * (4 * third + k + 1))
+            grad[:, lanes] = piece * gain[...]
+            total += jnp.sum(piece * wide(w_qkv[:, lanes]), axis=1, keepdims=True)
+    gain_grad[...] = total
+
+
 def kernel(body, outs, cost, *args, scratch=(), scalars=0):
     flops, transcendentals = cost
     shapes = [jax.ShapeDtypeStruct(shape, kind) for shape, kind in outs]
@@ -686,7 +719,7 @@
         ],
         out_specs=[pl.BlockSpec(memory_space=pltpu.VMEM)] * len(shapes),
         scratch_shapes=[pltpu.VMEM(shape, kind) for shape, kind in scratch],
-        compiler_params=pltpu.CompilerParams(vmem_limit_bytes=48 * 2**20),
+        compiler_params=pltpu.CompilerParams(vmem_limit_bytes=28 * 2**20),
         cost_estimate=pl.CostEstimate(
             flops=flops, bytes_accessed=moved, transcendentals=transcendentals
         ),
@@ -864,8 +897,7 @@
     back = rep_exchange(
         low(wide(io_kept[2]) + wide(io_far[1]) + wide(io_down) + wide(io_up))
     )
-    g_up, g_down, last_across = tie(g_up, g_down, last_across)
-    last = kept + wide(last_across)
+    back, g_up = tie(back, g_up)
     sum_g = low(wide(g_kept[2]) + wide(g_far[1]) + wide(g_down) + wide(g_up))
     back_qkv = rep_exchange(sum_g[:, :768])
     grad_w_attn_out = wide(
@@ -873,38 +905,33 @@
             columns(split_rows(sum_g[:, 768:], 4)), AXES, [(there, here) for here, there in order]
         )
     )
+    grad_w_in, gain_in, grad_w_out = kernel(
+        unpack_rest,
+        [(w_in.shape, f32), (gain_mlp.shape, f32), (w_out.shape, f32)],
+        (4 * w_in.size, 0),
+        back, w_in, gain_mlp,
+    )
+    grad_w_qkv, gain_qkv = kernel(
+        unpack_qkv,
+        [(w_qkv.shape, f32), (gain_attn.shape, f32)],
+        (4 * w_qkv.size, 0),
+        back_qkv, w_qkv, gain_attn,
+    )
+    last = kept + wide(last_across)
 
     standard, inverse = norm_statistics(x_own)
     block_input_gradient = grad_hidden + norm_backward_pass(
         last[:count], jnp.ones((), f32), standard, inverse
     )
     output = low(jnp.where(seg_col[:count] < 8, hidden_sum + last[count:], 0.0))
-    back = split_rows(back, 4)
-    back_qkv = [split_columns(piece, 3) for piece in split_rows(back_qkv, 4)]
-    unit_qkv = wide(columns([piece[k] for k in range(3) for piece in back_qkv]))
-    rest_width = part - main
-    unit_in = wide(
-        columns(
-            [
-                value
-                for k in range(2)
-                for piece in back
-                for value in (
-                    piece[:, main * k : main * (k + 1)],
-                    piece[:, 2 * main + rest_width * k : 2 * main + rest_width * (k + 1)],
-                )
-            ]
-        )
-    )
-    grad_w_out = wide(columns([piece[:, in_width : in_width + part] for piece in back]))
     return (
         absolute(output, z, x),
         absolute(block_input_gradient, z, x),
-        jnp.sum(unit_qkv * wide(w_qkv), axis=1),
-        unit_qkv * gain_attn,
+        gain_qkv.reshape(-1),
+        grad_w_qkv,
         grad_w_attn_out,
-        jnp.sum(unit_in * wide(w_in), axis=1),
-        unit_in * gain_mlp,
+        gain_in.reshape(-1),
+        grad_w_in,
         grad_w_out,
     )
 

time: 267 us -> 245 us (0.918); the launches traced: 262 us -> 243 us
  local copies, waits for them, and re-layouts: 17.2 us -> 5.26 us
  other arithmetic: 30.3 us -> 22.9 us
  Pallas kernels: 34.7 us -> 31.1 us
  starting transfers between devices: 54.2 us -> 57.3 us
    ppermute x9, waiting for transfers between devices: 48.4 us -> 60.2 us  [up(): return lax.ppermute(value, 'fsdp', [(k, (k + 2) % 8) for k in range(8)])]
    all_to_all x4, waiting for transfers between devices: 10 us -> 1.32 us  [rep_exchange(): return lax.all_to_all(blocks, 'rep', 0, 0, tiled=True).reshape(value.shape)]
    ppermute x10, waiting for transfers between devices: 32.7 us -> 24.2 us  [over(): return lax.ppermute(value, 'fsdp', [(k, k ^ 1) for k in range(8)])]
    slice x12 -> x0, local copies, waits for them, and re-layouts: 6.48 us -> none  [the longest x4 2.52 us: local_ring(): piece[:, main * k:main * (k + 1)]]
    ppermute x4, starting transfers between devices: 7.94 us -> 13.6 us  [down(): return lax.ppermute(value, 'fsdp', [(k, (k - 2) % 8) for k in range(8)])]
    convert_element_type x16, other arithmetic: 13.6 us -> 9.01 us  [low(): return value.astype(jnp.bfloat16)]
    mul x2 -> x0, other arithmetic: 4.1 us -> none  [the longest x1 2.64 us: local_ring(): unit_in * gain_mlp]
    ppermute x12, waiting for transfers between devices: 16.9 us -> 21 us  [swap(): return lax.ppermute(value, 'rep', [(k, k ^ distance) for k in range(4)])]
  transfers between devices with their start and end apart: 41 -> 41, of which waited for: 23 -> 22; matrix products, arithmetic and copies ran while one was open for 13% -> 8% of each run, Pallas kernels for 10% -> 9%
where the time goes in v7:
time: 245 us; the launch traced here: 243 us
  waiting for transfers between devices  125 us (51%)
  starting transfers between devices  57.3 us (23%)
  Pallas kernels  31.1 us (13%)
  other arithmetic  22.9 us (9%)
  local copies, waits for them, and re-layouts  5.26 us (2%)
    ppermute x9, waiting for transfers between devices, up(): return lax.ppermute(value, 'fsdp', [(k, (k + 2) % 8) for k in range(8)])  60.2 us
    pallas_call x7, Pallas kernels, kernel(): pl.pallas_call(body, out_shape=shapes, in_specs=[pl.BlockSpec(memory_spac...  31.1 us
    ppermute x10, waiting for transfers between devices, over(): return lax.ppermute(value, 'fsdp', [(k, k ^ 1) for k in range(8)])  24.2 us
    ppermute x12, waiting for transfers between devices, swap(): return lax.ppermute(value, 'rep', [(k, k ^ distance) for k in range(4)])  21 us
    all_to_all x4, starting transfers between devices, rep_exchange(): return lax.all_to_all(blocks, 'rep', 0, 0, tiled=True).reshape(value.shape)  19.1 us
    ppermute x4, waiting for transfers between devices, down(): return lax.ppermute(value, 'fsdp', [(k, (k - 2) % 8) for k in range(8)])  18.3 us
    ppermute x4, starting transfers between devices, down(): return lax.ppermute(value, 'fsdp', [(k, (k - 2) % 8) for k in range(8)])  13.6 us
    convert_element_type x16, other arithmetic, low(): return value.astype(jnp.bfloat16)  9.01 us
  transfers between devices with their start and end apart: 41, of which 22 were waited for; matrix products, arithmetic and copies ran while one was open for 8% of the time, Pallas kernels for 9%

profile of v7, /device:TPU:0, one launch (start us, length us, event | category | flops | bytes accessed | tf_op | source)
XLA Modules:
  0.0 243.0 jit_solution(7113523366086957641)
XLA Ops:
  4.3 4.2 %all-to-all-start = ((bf16[4,32,896]{2,1,0:T(8,128)(2,1)}), bf16[4,32,896]{2,1,0:T(8,128)(2,1)S(1)}, u32[]{:S(2)}, u32[]{:S(2)}) async-start(bf16[4,32,896]{2,1,0:T(8,128)(2,1)} %bitcast), calls=%async_computation | async-start | bytes 458752 | tf_op jit(solution)/shard_map/all_to_all | solution.py:418
  14.3 7.2 %all-to-all-start.1 = ((bf16[4,32,2176]{2,1,0:T(8,128)(2,1)}), bf16[4,32,2176]{2,1,0:T(8,128)(2,1)}, u32[]{:S(2)}, u32[]{:S(2)}) async-start(bf16[4,32,2176]{2,1,0:T(8,128)(2,1)} %bitcast.3), calls=%async_computation.1 | async-start | bytes 1114112 | tf_op jit(solution)/shard_map/all_to_all | solution.py:418
  22.5 4.7 %collective-permute-start.2 = (bf16[128,1024]{1,0:T(8,128)(2,1)S(1)}, bf16[128,1024]{1,0:T(8,128)(2,1)S(1)}, u32[]{:S(2)}, u32[]{:S(2)}) collective-permute-start(bf16[128,1024]{1,0:T(8,128)(2,1)S(1)} %maximum_maximum_fusion.own), channel_id=1, source_target_pairs={{0,24},{4,28},{8,0},{12,4},{16,8},{20,12},{24,16},{28,20},{1,25},{... | collective-permute-start | bytes 786440 | tf_op jit(solution)/shard_map/ppermute | solution.py:426
  27.4 7.0 %collective-permute-done.1.third = bf16[128,1024]{1,0:T(8,128)(2,1)S(1)} collective-permute-done((bf16[128,1024]{1,0:T(8,128)(2,1)S(1)}, bf16[128,1024]{1,0:T(8,128)(2,1)S(1)}, u32[]{:S(2)}, u32[]{:S(2)}) %collective-permute-start.1) | collective-permute-done | bytes 262176 | tf_op jit(solution)/shard_map/ppermute | solution.py:422
  34.4 3.2 %collective-permute-done.2.first = bf16[128,1024]{1,0:T(8,128)(2,1)S(1)} collective-permute-done((bf16[128,1024]{1,0:T(8,128)(2,1)S(1)}, bf16[128,1024]{1,0:T(8,128)(2,1)S(1)}, u32[]{:S(2)}, u32[]{:S(2)}) %collective-permute-start.2) | collective-permute-done | bytes 262176 | tf_op jit(solution)/shard_map/ppermute | solution.py:426
  40.9 2.0 collective-permute-start.4
  43.0 6.5 %collective-permute-done.4.second = bf16[128,1024]{1,0:T(8,128)(2,1)S(1)} collective-permute-done((bf16[128,1024]{1,0:T(8,128)(2,1)S(1)}, bf16[128,1024]{1,0:T(8,128)(2,1)S(1)}, u32[]{:S(2)}, u32[]{:S(2)}) %collective-permute-start.4) | collective-permute-done | bytes 262176 | tf_op jit(solution)/shard_map/ppermute | solution.py:422
  49.6 2.6 %collective-permute-done.5.others = bf16[256,1024]{1,0:T(8,128)(2,1)S(1)} collective-permute-done((bf16[256,1024]{1,0:T(8,128)(2,1)}, bf16[256,1024]{1,0:T(8,128)(2,1)S(1)}, u32[]{:S(2)}, u32[]{:S(2)}) %collective-permute-start.5) | collective-permute-done | bytes 524320 | tf_op jit(solution)/shard_map/ppermute | solution.py:430
  54.3 3.9 %collective-permute-start.10 = (bf16[128,2176]{1,0:T(8,128)(2,1)}, bf16[128,2176]{1,0:T(8,128)(2,1)}, u32[]{:S(2)}, u32[]{:S(2)}) collective-permute-start(bf16[128,2176]{1,0:T(8,128)(2,1)} %bitcast.4.own), channel_id=1, source_target_pairs={{0,24},{4,28},{8,0},{12,4},{16,8},{20,12},{24,16},{28,20},{1,25},{... | collective-permute-start | bytes 1671176 | tf_op jit(solution)/shard_map/ppermute | solution.py:426
  58.1 4.0 %collective-permute-done.8.other_second = bf16[128,1024]{1,0:T(8,128)(2,1)S(1)} collective-permute-done((bf16[128,1024]{1,0:T(8,128)(2,1)}, bf16[128,1024]{1,0:T(8,128)(2,1)S(1)}, u32[]{:S(2)}, u32[]{:S(2)}) %collective-permute-start.8) | collective-permute-done | bytes 262176 | tf_op jit(solution)/shard_map/ppermute | solution.py:430
  65.3 7.0 %attention_forward.1 = (bf16[512,1024]{1,0:T(8,128)(2,1)S(1)}, bf16[1024,768]{1,0:T(8,128)(2,1)S(1)}, bf16[256,1024]{1,0:T(8,128)(2,1)S(1)}, bf16[512,256]{1,0:T...) custom-call(s32[2]{0:T(128)S(1)} %pad_add_fusion.place, ...), custom_call_target="tpu_custom_call" | custom-call | flops 1207959552 | bytes 11014152 | tf_op jit(solution)/shard_map/attention_forward/pallas_call | solution.py:713
  72.4 11.3 %collective-permute-done.9.third = bf16[128,2176]{1,0:T(8,128)(2,1)} collective-permute-done((bf16[128,2176]{1,0:T(8,128)(2,1)}, bf16[128,2176]{1,0:T(8,128)(2,1)}, u32[]{:S(2)}, u32[]{:S(2)}) %collective-permute-start.9) | collective-permute-done | bytes 557088 | tf_op jit(solution)/shard_map/ppermute | solution.py:422
  83.7 1.9 collective-permute-done.12
  90.0 4.1 %collective-permute-done.13 = bf16[128,1024]{1,0:T(8,128)(2,1)S(1)} collective-permute-done((bf16[128,1024]{1,0:T(8,128)(2,1)S(1)}, bf16[128,1024]{1,0:T(8,128)(2,1)S(1)}, u32[]{:S(2)}, u32[]{:S(2)}) %collective-permute-start.13) | collective-permute-done | bytes 262176 | tf_op jit(solution)/shard_map/ppermute | solution.py:413
  96.8 5.2 %collective-permute-done.17.other_third = bf16[128,2176]{1,0:T(8,128)(2,1)S(1)} collective-permute-done((bf16[128,2176]{1,0:T(8,128)(2,1)}, bf16[128,2176]{1,0:T(8,128)(2,1)S(1)}, u32[]{:S(2)}, u32[]{:S(2)}) %collective-permute-start.17) | collective-permute-done | bytes 557088 | tf_op jit(solution)/shard_map/ppermute | solution.py:430
  104.9 10.8 %collective-permute-done.18.other_first = bf16[128,2176]{1,0:T(8,128)(2,1)S(1)} collective-permute-done((bf16[128,2176]{1,0:T(8,128)(2,1)}, bf16[128,2176]{1,0:T(8,128)(2,1)S(1)}, u32[]{:S(2)}, u32[]{:S(2)}) %collective-permute-start.18) | collective-permute-done | bytes 557088 | tf_op jit(solution)/shard_map/ppermute | solution.py:430
  115.7 4.1 %collective-permute-done.19.other_second = bf16[128,2176]{1,0:T(8,128)(2,1)S(1)} collective-permute-done((bf16[128,2176]{1,0:T(8,128)(2,1)S(1)}, bf16[128,2176]{1,0:T(8,128)(2,1)S(1)}, u32[]{:S(2)}, u32[]{:S(2)}) %collective-permute-start.19) | collective-permute-done | bytes 557088 | tf_op jit(solution)/shard_map/ppermute | solution.py:422
  119.8 7.5 %mlp.1 = (bf16[512,1024]{1,0:T(8,128)(2,1)S(1)}, bf16[512,1024]{1,0:T(8,128)(2,1)S(1)}, bf16[512,768]{1,0:T(8,128)(2,1)S(1)}, bf16[512,1408]{1,0:T(8,128)(2,1)S(...) custom-call(s32[512,1]{1,0:T(8,128)S(1)} %copy.28.seg_col, ...), custom_call_target="tpu_custom_call" | custom-call | flops 3758096384 | bytes 14551040 | tf_op jit(solution)/shard_map/mlp/pallas_call | solution.py:713
  127.3 1.9 collective-permute-done.20
  129.9 2.7 %mlp_terms.1 = (bf16[384,2176]{1,0:T(8,128)(2,1)S(1)}, bf16[256,2176]{1,0:T(8,128)(2,1)S(1)}, bf16[128,2176]{1,0:T(8,128)(2,1)S(1)}, bf16[256,2176]{1,0:T(8,128)(2,1)S(1)}) custom-call(bf16[512,1024]{1,0:T(8,128)(2,1)S(1)} %get-tuple-element.111.normed, bf16[512,1408]{1,0:T(8,128)(2,1)S(1)} %get-tuple-element.112.grad_inner, ...), custom_call_target="tpu_custom_call" | custom-call | flops 2281701376 | bytes 8781824 | tf_op jit(solution)/shard_map/mlp_terms/pallas_call | solution.py:713
  133.5 4.2 %collective-permute-done.21 = bf16[128,1024]{1,0:T(8,128)(2,1)S(1)} collective-permute-done((bf16[128,1024]{1,0:T(8,128)(2,1)S(1)}, bf16[128,1024]{1,0:T(8,128)(2,1)S(1)}, u32[]{:S(2)}, u32[]{:S(2)}) %collective-permute-start.21) | collective-permute-done | bytes 262176 | tf_op jit(solution)/shard_map/ppermute | solution.py:413
  139.7 7.0 %collective-permute-done.22.low_across = bf16[128,1024]{1,0:T(8,128)(2,1)S(1)} collective-permute-done((bf16[128,1024]{1,0:T(8,128)(2,1)S(1)}, bf16[128,1024]{1,0:T(8,128)(2,1)S(1)}, u32[]{:S(2)}, u32[]{:S(2)}) %collective-permute-start.22) | collective-permute-done | bytes 262176 | tf_op jit(solution)/shard_map/ppermute | solution.py:413
  148.6 7.6 %attention_backward.1 = (bf16[512,768]{1,0:T(8,128)(2,1)S(1)}, bf16[384,1024]{1,0:T(8,128)(2,1)S(1)}, bf16[256,1024]{1,0:T(8,128)(2,1)S(1)}, bf16[128,1024]{1,0:T(8,128)(2,1)S(1)}, bf16[256,1024]{1,0:T(8,128)(2,1)S(1)}) custom-call(s32[2]{0:T(128)S(1)} %pad_add_fusion.place, f32[512,128]{1,0:T(8,128)S(1)} %get-tuple-element.250.cosine, ...), custom_call_target="tpu_custom_call" | custom-call | flops 1677721600 | bytes 8126472 | tf_op jit(solution)/shard_map/attention_backward/pallas_call | solution.py:713
  156.2 4.6 %collective-permute-done.24 = bf16[256,2176]{1,0:T(8,128)(2,1)S(1)} collective-permute-done((bf16[256,2176]{1,0:T(8,128)(2,1)S(1)}, bf16[256,2176]{1,0:T(8,128)(2,1)S(1)}, u32[]{:S(2)}, u32[]{:S(2)}) %collective-permute-start.24) | collective-permute-done | bytes 1114144 | tf_op jit(solution)/shard_map/ppermute | solution.py:422
  167.1 18.5 %collective-permute-done.28 = bf16[256,1024]{1,0:T(8,128)(2,1)S(1)} collective-permute-done((bf16[256,1024]{1,0:T(8,128)(2,1)S(1)}, bf16[256,1024]{1,0:T(8,128)(2,1)S(1)}, u32[]{:S(2)}, u32[]{:S(2)}) %collective-permute-start.28) | collective-permute-done | bytes 524320 | tf_op jit(solution)/shard_map/ppermute | solution.py:422
  188.1 3.3 %collective-permute-start.33 = (bf16[128,1024]{1,0:T(8,128)(2,1)S(1)}, bf16[128,1024]{1,0:T(8,128)(2,1)S(1)}, u32[]{:S(2)}, u32[]{:S(2)}) collective-permute-start(bf16[128,1024]{1,0:T(8,128)(2,1)S(1)} %add_convert_fusion.7), channel_id=1, source_target_pairs={{0,24},{4,28},{8,0},{12,4},{16,8},{20,12},{24,16},{28,20},{1,25},{... | collective-permute-start | bytes 786440 | tf_op jit(solution)/shard_map/ppermute | solution.py:426
  193.4 15.1 %collective-permute-done.33 = bf16[128,1024]{1,0:T(8,128)(2,1)S(1)} collective-permute-done((bf16[128,1024]{1,0:T(8,128)(2,1)S(1)}, bf16[128,1024]{1,0:T(8,128)(2,1)S(1)}, u32[]{:S(2)}, u32[]{:S(2)}) %collective-permute-start.33) | collective-permute-done | bytes 262176 | tf_op jit(solution)/shard_map/ppermute | solution.py:426
  209.7 3.5 %all-to-all-start.2 = ((bf16[4,32,2176]{2,1,0:T(8,128)(2,1)}), bf16[4,32,2176]{2,1,0:T(8,128)(2,1)S(1)}, u32[]{:S(2)}, u32[]{:S(2)}) async-start(bf16[4,32,2176]{2,1,0:T(8,128)(2,1)} %bitcast.22), calls=%async_computation.2 | async-start | bytes 1114112 | tf_op jit(solution)/shard_map/all_to_all | solution.py:418
  217.1 2.0 collective-permute-start.34
  219.1 6.7 %collective-permute-done.35 = bf16[128,1024]{1,0:T(8,128)(2,1)} collective-permute-done((bf16[128,1024]{1,0:T(8,128)(2,1)}, bf16[128,1024]{1,0:T(8,128)(2,1)}, u32[]{:S(2)}, u32[]{:S(2)}) %collective-permute-start.35) | collective-permute-done | bytes 262176 | tf_op jit(solution)/shard_map/ppermute | solution.py:422
  229.0 4.2 %all-to-all-start.3 = ((bf16[4,32,768]{2,1,0:T(8,128)(2,1)}), bf16[4,32,768]{2,1,0:T(8,128)(2,1)S(1)}, u32[]{:S(2)}, u32[]{:S(2)}) async-start(bf16[4,32,768]{2,1,0:T(8,128)(2,1)} %bitcast.11), calls=%async_computation.3 | async-start | bytes 393216 | tf_op jit(solution)/shard_map/all_to_all | solution.py:418
  233.2 3.6 %unpack_rest.1 = (f32[32,5248]{1,0:T(8,128)}, f32[32,1]{1,0:T(8,128)S(1)}, f32[32,2624]{1,0:T(8,128)}) custom-call(bf16[128,2176]{1,0:T(8,128)(2,1)S(1)} %bitcast.19, bf16[32,5248]{1,0:T(8,128)(2,1)S(1)} %copy-done, f32[32,1]{1,0:T(8,128)S(1)} %copy.31.gain), custom_call_target="tpu_custom_call" | custom-call | flops 671744 | bytes 1900800 | tf_op jit(solution)/shard_map/unpack_rest/pallas_call | solution.py:713
  (220 shorter events, 59.6 us)
Async XLA Ops:
  4.3 9.9 %all-to-all-start = ((bf16[4,32,896]{2,1,0:T(8,128)(2,1)}), bf16[4,32,896]{2,1,0:T(8,128)(2,1)S(1)}, u32[]{:S(2)}, u32[]{:S(2)}) async-start(bf16[4,32,896]{2,1,0:T(8,128)(2,1)} %bitcast), calls=%async_computation | async-start | bytes 458752 | tf_op jit(solution)/shard_map/all_to_all | solution.py:418
  14.3 23.3 %all-to-all-start.1 = ((bf16[4,32,2176]{2,1,0:T(8,128)(2,1)}), bf16[4,32,2176]{2,1,0:T(8,128)(2,1)}, u32[]{:S(2)}, u32[]{:S(2)}) async-start(bf16[4,32,2176]{2,1,0:T(8,128)(2,1)} %bitcast.3), calls=%async_computation.1 | async-start | bytes 1114112 | tf_op jit(solution)/shard_map/all_to_all | solution.py:418
  21.5 12.9 %collective-permute-start.1 = (bf16[128,1024]{1,0:T(8,128)(2,1)S(1)}, bf16[128,1024]{1,0:T(8,128)(2,1)S(1)}, u32[]{:S(2)}, u32[]{:S(2)}) collective-permute-start(bf16[128,1024]{1,0:T(8,128)(2,1)S(1)} %maximum_maximum_fusion.own), channel_id=1, source_target_pairs={{0,8},{4,12},{8,16},{12,20},{16,24},{20,28},{24,0},{28,4},{1,9},{5... | collective-permute-start | bytes 786440 | tf_op jit(solution)/shard_map/ppermute | solution.py:422
  22.5 15.0 %collective-permute-start.2 = (bf16[128,1024]{1,0:T(8,128)(2,1)S(1)}, bf16[128,1024]{1,0:T(8,128)(2,1)S(1)}, u32[]{:S(2)}, u32[]{:S(2)}) collective-permute-start(bf16[128,1024]{1,0:T(8,128)(2,1)S(1)} %maximum_maximum_fusion.own), channel_id=1, source_target_pairs={{0,24},{4,28},{8,0},{12,4},{16,8},{20,12},{24,16},{28,20},{1,25},{... | collective-permute-start | bytes 786440 | tf_op jit(solution)/shard_map/ppermute | solution.py:426
  27.2 10.3 %collective-permute-start.3 = (bf16[128,1024]{1,0:T(8,128)(2,1)S(1)}, bf16[128,1024]{1,0:T(8,128)(2,1)S(1)}, u32[]{:S(2)}, u32[]{:S(2)}) collective-permute-start(bf16[128,1024]{1,0:T(8,128)(2,1)S(1)} %maximum_maximum_fusion.own), channel_id=1, source_target_pairs={{0,4},{4,0},{8,12},{12,8},{16,20},{20,16},{24,28},{28,24},{1,5},{5... | collective-permute-start | bytes 786440 | tf_op jit(solution)/shard_map/ppermute | solution.py:430
  38.4 13.7 %collective-permute-start.5 = (bf16[256,1024]{1,0:T(8,128)(2,1)}, bf16[256,1024]{1,0:T(8,128)(2,1)S(1)}, u32[]{:S(2)}, u32[]{:S(2)}) collective-permute-start(bf16[256,1024]{1,0:T(8,128)(2,1)} %pad_maximum_fusion.3), channel_id=1, source_target_pairs={{0,4},{4,0},{8,12},{12,8},{16,20},{20,16},{24,28},{28,24},{1,5},{5... | collective-permute-start | bytes 1572872 | tf_op jit(solution)/shard_map/ppermute | solution.py:430
  39.2 13.7 %collective-permute-start.6 = (bf16[256,1024]{1,0:T(8,128)(2,1)S(1)}, bf16[256,1024]{1,0:T(8,128)(2,1)S(1)}, u32[]{:S(2)}, u32[]{:S(2)}) collective-permute-start(bf16[256,1024]{1,0:T(8,128)(2,1)S(1)} %pad_maximum_fusion.2.mine), channel_id=1, source_target_pairs={{0,2},{1,3},{2,0},{3,1},{4,6},{5,7},{6,4},{7,5},{8,10},{9,11},{10,... | collective-permute-start | bytes 1572872 | tf_op jit(solution)/shard_map/ppermute | solution.py:413
  53.0 9.9 %collective-permute-start.7 = (bf16[512,1024]{1,0:T(8,128)(2,1)S(1)}, bf16[512,1024]{1,0:T(8,128)(2,1)S(1)}, u32[]{:S(2)}, u32[]{:S(2)}) collective-permute-start(bf16[512,1024]{1,0:T(8,128)(2,1)S(1)} %pad_maximum_fusion), channel_id=1, source_target_pairs={{0,1},{1,0},{2,3},{3,2},{4,5},{5,4},{6,7},{7,6},{8,9},{9,8},{10,11... | collective-permute-start | bytes 3145736 | tf_op jit(solution)/shard_map/ppermute | solution.py:413
  53.2 9.0 %collective-permute-start.8 = (bf16[128,1024]{1,0:T(8,128)(2,1)}, bf16[128,1024]{1,0:T(8,128)(2,1)S(1)}, u32[]{:S(2)}, u32[]{:S(2)}) collective-permute-start(bf16[128,1024]{1,0:T(8,128)(2,1)} %copy-done.6), channel_id=1, source_target_pairs={{0,4},{4,0},{8,12},{12,8},{16,20},{20,16},{24,28},{28,24},{1,5},{5... | collective-permute-start | bytes 786440 | tf_op jit(solution)/shard_map/ppermute | solution.py:430
  54.3 18.1 %collective-permute-start.10 = (bf16[128,2176]{1,0:T(8,128)(2,1)}, bf16[128,2176]{1,0:T(8,128)(2,1)}, u32[]{:S(2)}, u32[]{:S(2)}) collective-permute-start(bf16[128,2176]{1,0:T(8,128)(2,1)} %bitcast.4.own), channel_id=1, source_target_pairs={{0,24},{4,28},{8,0},{12,4},{16,8},{20,12},{24,16},{28,20},{1,25},{... | collective-permute-start | bytes 1671176 | tf_op jit(solution)/shard_map/ppermute | solution.py:426
  58.1 25.6 %collective-permute-start.9 = (bf16[128,2176]{1,0:T(8,128)(2,1)}, bf16[128,2176]{1,0:T(8,128)(2,1)}, u32[]{:S(2)}, u32[]{:S(2)}) collective-permute-start(bf16[128,2176]{1,0:T(8,128)(2,1)} %bitcast.4.own), channel_id=1, source_target_pairs={{0,8},{4,12},{8,16},{12,20},{16,24},{20,28},{24,0},{28,4},{1,9},{5... | collective-permute-start | bytes 1671176 | tf_op jit(solution)/shard_map/ppermute | solution.py:422
  62.9 20.8 %collective-permute-start.11 = (bf16[128,2176]{1,0:T(8,128)(2,1)}, bf16[128,2176]{1,0:T(8,128)(2,1)}, u32[]{:S(2)}, u32[]{:S(2)}) collective-permute-start(bf16[128,2176]{1,0:T(8,128)(2,1)} %bitcast.4.own), channel_id=1, source_target_pairs={{0,4},{4,0},{8,12},{12,8},{16,20},{20,16},{24,28},{28,24},{1,5},{5... | collective-permute-start | bytes 1671176 | tf_op jit(solution)/shard_map/ppermute | solution.py:430
  87.3 14.7 %collective-permute-start.17 = (bf16[128,2176]{1,0:T(8,128)(2,1)}, bf16[128,2176]{1,0:T(8,128)(2,1)S(1)}, u32[]{:S(2)}, u32[]{:S(2)}) collective-permute-start(bf16[128,2176]{1,0:T(8,128)(2,1)} %collective-permute-done.9.third), channel_id=1, source_target_pairs={{0,4},{4,0},{8,12},{12,8},{16,20},{20,16},{24,28},{28,24},{1,5},{5... | collective-permute-start | bytes 1671176 | tf_op jit(solution)/shard_map/ppermute | solution.py:430
  88.7 16.1 %collective-permute-start.16 = (bf16[128,2176]{1,0:T(8,128)(2,1)}, bf16[128,2176]{1,0:T(8,128)(2,1)S(1)}, u32[]{:S(2)}, u32[]{:S(2)}) collective-permute-start(bf16[128,2176]{1,0:T(8,128)(2,1)} %collective-permute-done.9.third), channel_id=1, source_target_pairs={{0,8},{4,12},{8,16},{12,20},{16,24},{20,28},{24,0},{28,4},{1,9},{5... | collective-permute-start | bytes 1671176 | tf_op jit(solution)/shard_map/ppermute | solution.py:422
  95.2 9.6 %collective-permute-start.14 = (bf16[128,1024]{1,0:T(8,128)(2,1)S(1)}, bf16[128,1024]{1,0:T(8,128)(2,1)S(1)}, u32[]{:S(2)}, u32[]{:S(2)}) collective-permute-start(bf16[128,1024]{1,0:T(8,128)(2,1)S(1)} %fusion.12.norm_own), channel_id=1, source_target_pairs={{0,2},{1,3},{2,0},{3,1},{4,6},{5,7},{6,4},{7,5},{8,10},{9,11},{10,... | collective-permute-start | bytes 786440 | tf_op jit(solution)/shard_map/ppermute | solution.py:413
  102.0 13.7 %collective-permute-start.18 = (bf16[128,2176]{1,0:T(8,128)(2,1)}, bf16[128,2176]{1,0:T(8,128)(2,1)S(1)}, u32[]{:S(2)}, u32[]{:S(2)}) collective-permute-start(bf16[128,2176]{1,0:T(8,128)(2,1)} %collective-permute-done.10.first), channel_id=1, source_target_pairs={{0,4},{4,0},{8,12},{12,8},{16,20},{20,16},{24,28},{28,24},{1,5},{5... | collective-permute-start | bytes 1671176 | tf_op jit(solution)/shard_map/ppermute | solution.py:430
  104.8 15.0 %collective-permute-start.19 = (bf16[128,2176]{1,0:T(8,128)(2,1)S(1)}, bf16[128,2176]{1,0:T(8,128)(2,1)S(1)}, u32[]{:S(2)}, u32[]{:S(2)}) collective-permute-start(bf16[128,2176]{1,0:T(8,128)(2,1)S(1)} %collective-permute-done.17.other_third), channel_id=1, source_target_pairs={{0,8},{4,12},{8,16},{12,20},{16,24},{20,28},{24,0},{28,4},{1,9},{5... | collective-permute-start | bytes 1671176 | tf_op jit(solution)/shard_map/ppermute | solution.py:422
  104.9 14.9 %collective-permute-start.15 = (bf16[256,1024]{1,0:T(8,128)(2,1)S(1)}, bf16[256,1024]{1,0:T(8,128)(2,1)S(1)}, u32[]{:S(2)}, u32[]{:S(2)}) collective-permute-start(bf16[256,1024]{1,0:T(8,128)(2,1)S(1)} %pad_maximum_fusion.4), channel_id=1, source_target_pairs={{0,1},{1,0},{2,3},{3,2},{4,5},{5,4},{6,7},{7,6},{8,9},{9,8},{10,11... | collective-permute-start | bytes 1572872 | tf_op jit(solution)/shard_map/ppermute | solution.py:413
  132.6 28.2 %collective-permute-start.24 = (bf16[256,2176]{1,0:T(8,128)(2,1)S(1)}, bf16[256,2176]{1,0:T(8,128)(2,1)S(1)}, u32[]{:S(2)}, u32[]{:S(2)}) collective-permute-start(bf16[256,2176]{1,0:T(8,128)(2,1)S(1)} %get-tuple-element.114), channel_id=1, source_target_pairs={{0,8},{4,12},{8,16},{12,20},{16,24},{20,28},{24,0},{28,4},{1,9},{5... | collective-permute-start | bytes 3342344 | tf_op jit(solution)/shard_map/ppermute | solution.py:422
  132.7 28.1 %collective-permute-start.25 = (bf16[256,2176]{1,0:T(8,128)(2,1)S(1)}, bf16[256,2176]{1,0:T(8,128)(2,1)S(1)}, u32[]{:S(2)}, u32[]{:S(2)}) collective-permute-start(bf16[256,2176]{1,0:T(8,128)(2,1)S(1)} %get-tuple-element.115), channel_id=1, source_target_pairs={{0,4},{4,0},{8,12},{12,8},{16,20},{20,16},{24,28},{28,24},{1,5},{5... | collective-permute-start | bytes 3342344 | tf_op jit(solution)/shard_map/ppermute | solution.py:430
  161.0 26.1 %collective-permute-start.27 = (bf16[128,2176]{1,0:T(8,128)(2,1)S(1)}, bf16[128,2176]{1,0:T(8,128)(2,1)S(1)}, u32[]{:S(2)}, u32[]{:S(2)}) collective-permute-start(bf16[128,2176]{1,0:T(8,128)(2,1)S(1)} %add_convert_fusion.2), channel_id=1, source_target_pairs={{0,24},{4,28},{8,0},{12,4},{16,8},{20,12},{24,16},{28,20},{1,25},{... | collective-permute-start | bytes 1671176 | tf_op jit(solution)/shard_map/ppermute | solution.py:426
  162.9 24.2 %collective-permute-start.26 = (bf16[128,2176]{1,0:T(8,128)(2,1)S(1)}, bf16[128,2176]{1,0:T(8,128)(2,1)S(1)}, u32[]{:S(2)}, u32[]{:S(2)}) collective-permute-start(bf16[128,2176]{1,0:T(8,128)(2,1)S(1)} %add_convert_fusion.3), channel_id=1, source_target_pairs={{0,4},{4,0},{8,12},{12,8},{16,20},{20,16},{24,28},{28,24},{1,5},{5... | collective-permute-start | bytes 1671176 | tf_op jit(solution)/shard_map/ppermute | solution.py:430
  163.7 21.9 %collective-permute-start.28 = (bf16[256,1024]{1,0:T(8,128)(2,1)S(1)}, bf16[256,1024]{1,0:T(8,128)(2,1)S(1)}, u32[]{:S(2)}, u32[]{:S(2)}) collective-permute-start(bf16[256,1024]{1,0:T(8,128)(2,1)S(1)} %get-tuple-element.120), channel_id=1, source_target_pairs={{0,8},{4,12},{8,16},{12,20},{16,24},{20,28},{24,0},{28,4},{1,9},{5... | collective-permute-start | bytes 1572872 | tf_op jit(solution)/shard_map/ppermute | solution.py:422
  164.0 23.1 %collective-permute-start.29 = (bf16[256,1024]{1,0:T(8,128)(2,1)S(1)}, bf16[256,1024]{1,0:T(8,128)(2,1)S(1)}, u32[]{:S(2)}, u32[]{:S(2)}) collective-permute-start(bf16[256,1024]{1,0:T(8,128)(2,1)S(1)} %get-tuple-element.121), channel_id=1, source_target_pairs={{0,4},{4,0},{8,12},{12,8},{16,20},{20,16},{24,28},{28,24},{1,5},{5... | collective-permute-start | bytes 1572872 | tf_op jit(solution)/shard_map/ppermute | solution.py:430
  187.4 21.2 %collective-permute-start.31 = (bf16[128,2176]{1,0:T(8,128)(2,1)S(1)}, bf16[128,2176]{1,0:T(8,128)(2,1)S(1)}, u32[]{:S(2)}, u32[]{:S(2)}) collective-permute-start(bf16[128,2176]{1,0:T(8,128)(2,1)S(1)} %add_convert_fusion.1), channel_id=1, source_target_pairs={{0,8},{4,12},{8,16},{12,20},{16,24},{20,28},{24,0},{28,4},{1,9},{5... | collective-permute-start | bytes 1671176 | tf_op jit(solution)/shard_map/ppermute | solution.py:422
  188.1 20.4 %collective-permute-start.33 = (bf16[128,1024]{1,0:T(8,128)(2,1)S(1)}, bf16[128,1024]{1,0:T(8,128)(2,1)S(1)}, u32[]{:S(2)}, u32[]{:S(2)}) collective-permute-start(bf16[128,1024]{1,0:T(8,128)(2,1)S(1)} %add_convert_fusion.7), channel_id=1, source_target_pairs={{0,24},{4,28},{8,0},{12,4},{16,8},{20,12},{24,16},{28,20},{1,25},{... | collective-permute-start | bytes 786440 | tf_op jit(solution)/shard_map/ppermute | solution.py:426
  191.5 17.1 %collective-permute-start.32 = (bf16[128,1024]{1,0:T(8,128)(2,1)S(1)}, bf16[128,1024]{1,0:T(8,128)(2,1)S(1)}, u32[]{:S(2)}, u32[]{:S(2)}) collective-permute-start(bf16[128,1024]{1,0:T(8,128)(2,1)S(1)} %add_convert_fusion.8), channel_id=1, source_target_pairs={{0,4},{4,0},{8,12},{12,8},{16,20},{20,16},{24,28},{28,24},{1,5},{5... | collective-permute-start | bytes 786440 | tf_op jit(solution)/shard_map/ppermute | solution.py:430
  209.7 16.1 %all-to-all-start.2 = ((bf16[4,32,2176]{2,1,0:T(8,128)(2,1)}), bf16[4,32,2176]{2,1,0:T(8,128)(2,1)S(1)}, u32[]{:S(2)}, u32[]{:S(2)}) async-start(bf16[4,32,2176]{2,1,0:T(8,128)(2,1)} %bitcast.22), calls=%async_computation.2 | async-start | bytes 1114112 | tf_op jit(solution)/shard_map/all_to_all | solution.py:418
  215.0 10.8 %collective-permute-start.35 = (bf16[128,1024]{1,0:T(8,128)(2,1)}, bf16[128,1024]{1,0:T(8,128)(2,1)}, u32[]{:S(2)}, u32[]{:S(2)}) collective-permute-start(bf16[128,1024]{1,0:T(8,128)(2,1)} %add_convert_fusion.6), channel_id=1, source_target_pairs={{0,8},{4,12},{8,16},{12,20},{16,24},{20,28},{24,0},{28,4},{1,9},{5... | collective-permute-start | bytes 786440 | tf_op jit(solution)/shard_map/ppermute | solution.py:422
  217.1 21.0 %collective-permute-start.34 = (bf16[256,1024]{1,0:T(8,128)(2,1)}, bf16[256,1024]{1,0:T(8,128)(2,1)}, u32[]{:S(2)}, u32[]{:S(2)}) collective-permute-start(bf16[256,1024]{1,0:T(8,128)(2,1)} %add_convert_fusion.4), channel_id=1, source_target_pairs={{0,2},{1,3},{2,0},{3,1},{4,6},{5,7},{6,4},{7,5},{8,10},{9,11},{10,... | collective-permute-start | bytes 1572872 | tf_op jit(solution)/shard_map/ppermute | solution.py:413
  227.0 10.5 %collective-permute-start.36 = (bf16[32,1024]{1,0:T(8,128)(2,1)S(1)}, bf16[32,1024]{1,0:T(8,128)(2,1)S(1)}, u32[]{:S(2)}, u32[]{:S(2)}) collective-permute-start(bf16[32,1024]{1,0:T(8,128)(2,1)S(1)} %pad_maximum_fusion.8), channel_id=1, source_target_pairs={{0,0},{4,1},{8,2},{12,3},{16,4},{20,5},{24,6},{28,7},{1,8},{5,9},{... | collective-permute-start | bytes 196616 | tf_op jit(solution)/shard_map/ppermute | solution.py:904
  229.0 11.8 %all-to-all-start.3 = ((bf16[4,32,768]{2,1,0:T(8,128)(2,1)}), bf16[4,32,768]{2,1,0:T(8,128)(2,1)S(1)}, u32[]{:S(2)}, u32[]{:S(2)}) async-start(bf16[4,32,768]{2,1,0:T(8,128)(2,1)} %bitcast.11), calls=%async_computation.3 | async-start | bytes 393216 | tf_op jit(solution)/shard_map/all_to_all | solution.py:418
  (35 other events, 215.6 us)

commit v8 on v7

--- a/solution.py
+++ b/solution.py
@@ -792,10 +792,10 @@
     third, first, other = up(first_own), down(first_own), over(first_own)
     third, first, other, mine, rest = tie(third, first, other, mine, rest)
     across = swap(mine, 2)
-    second, others = up(third), over(rows([first, third]))
-    second, others, across, rest = tie(second, others, across, rest)
+    second, others, rest_third = up(third), over(rows([first, third])), up(rest)
+    second, others, across, rest_third, rest = tie(second, others, across, rest_third, rest)
     other_second = over(second)
-    rest_third, rest_first = up(rest), down(rest)
+    rest_first = down(rest)
     beside = swap(rows([mine, across]), 1)
     rest_other = over(tie(rest, other_second, beside)[0])
 
@@ -857,7 +857,7 @@
     )
     io_pair, io_far = up(io_pair), over(io_far)
     kept, sent = scatter_last(send, keep)
-    scaled_mlp = kept + wide(swap(sent, 2))
+    scaled_mlp = kept + wide(tie(swap(sent, 2), io_keep)[0])
     grad_hidden = wide(grad_out[:count]) + norm_backward_pass(
         scaled_mlp, jnp.ones((), f32), standard_mlp, inverse_mlp
     )
@@ -892,17 +892,21 @@
     kept, sent = scatter_last(send, keep)
     io_up = up(low(wide(io_kept[0]) + wide(io_pair[0]) + wide(io_near)))
     io_up, g_near, g_down, sent = tie(io_up, g_near, g_down, sent)
-    g_up = up(low(wide(g_kept[0]) + wide(g_pair[0]) + wide(g_near)))
+    sum_io, g_turned = tie(
+        low(wide(io_kept[2]) + wide(io_far[1]) + wide(io_down) + wide(io_up)),
+        low(wide(g_kept[0]) + wide(g_pair[0]) + wide(g_near)),
+    )
+    g_up = up(g_turned)
     last_across = swap(sent, 2)
-    back = rep_exchange(
-        low(wide(io_kept[2]) + wide(io_far[1]) + wide(io_down) + wide(io_up))
-    )
+    back = rep_exchange(sum_io)
     back, g_up = tie(back, g_up)
     sum_g = low(wide(g_kept[2]) + wide(g_far[1]) + wide(g_down) + wide(g_up))
     back_qkv = rep_exchange(sum_g[:, :768])
     grad_w_attn_out = wide(
         lax.ppermute(
-            columns(split_rows(sum_g[:, 768:], 4)), AXES, [(there, here) for here, there in order]
+            columns(split_rows(tie(sum_g, back)[0][:, 768:], 4)),
+            AXES,
+            [(there, here) for here, there in order],
         )
     )
     grad_w_in, gain_in, grad_w_out = kernel(

time: 245 us -> 245 us (level)
    ppermute x10, starting transfers between devices: 8.81 us -> 11.7 us  [over(): return lax.ppermute(value, 'fsdp', [(k, k ^ 1) for k in range(8)])]
  transfers between devices with their start and end apart: 41 -> 41, of which waited for: 22 -> 21; matrix products, arithmetic and copies ran while one was open for 8% -> 7% of each run, Pallas kernels for 9% -> 10%
where the time goes in v8:
time: 245 us; the launch traced here: 243 us
  waiting for transfers between devices  126 us (51%)
  starting transfers between devices  58.5 us (24%)
  Pallas kernels  31.4 us (13%)
  other arithmetic  22 us (9%)
  local copies, waits for them, and re-layouts  4.46 us (2%)
    ppermute x9, waiting for transfers between devices, up(): return lax.ppermute(value, 'fsdp', [(k, (k + 2) % 8) for k in range(8)])  58.8 us
    pallas_call x7, Pallas kernels, kernel(): pl.pallas_call(body, out_shape=shapes, in_specs=[pl.BlockSpec(memory_spac...  31.4 us
    ppermute x10, waiting for transfers between devices, over(): return lax.ppermute(value, 'fsdp', [(k, k ^ 1) for k in range(8)])  26.1 us
    ppermute x12, waiting for transfers between devices, swap(): return lax.ppermute(value, 'rep', [(k, k ^ distance) for k in range(4)])  20.9 us
    all_to_all x4, starting transfers between devices, rep_exchange(): return lax.all_to_all(blocks, 'rep', 0, 0, tiled=True).reshape(value.shape)  19.8 us
    ppermute x4, waiting for transfers between devices, down(): return lax.ppermute(value, 'fsdp', [(k, (k - 2) % 8) for k in range(8)])  18.6 us
    ppermute x10, starting transfers between devices, over(): return lax.ppermute(value, 'fsdp', [(k, k ^ 1) for k in range(8)])  11.7 us
    ppermute x4, starting transfers between devices, down(): return lax.ppermute(value, 'fsdp', [(k, (k - 2) % 8) for k in range(8)])  11.3 us
  transfers between devices with their start and end apart: 41, of which 21 were waited for; matrix products, arithmetic and copies ran while one was open for 7% of the time, Pallas kernels for 10%

profile of v8, /device:TPU:0, one launch (start us, length us, event | category | flops | bytes accessed | tf_op | source)
XLA Modules:
  0.0 243.4 jit_solution(13623440669499667271)
XLA Ops:
  4.3 4.2 %all-to-all-start = ((bf16[4,32,896]{2,1,0:T(8,128)(2,1)}), bf16[4,32,896]{2,1,0:T(8,128)(2,1)S(1)}, u32[]{:S(2)}, u32[]{:S(2)}) async-start(bf16[4,32,896]{2,1,0:T(8,128)(2,1)} %bitcast), calls=%async_computation | async-start | bytes 458752 | tf_op jit(solution)/shard_map/all_to_all | solution.py:418
  14.3 7.2 %all-to-all-start.1 = ((bf16[4,32,2176]{2,1,0:T(8,128)(2,1)}), bf16[4,32,2176]{2,1,0:T(8,128)(2,1)S(1)}, u32[]{:S(2)}, u32[]{:S(2)}) async-start(bf16[4,32,2176]{2,1,0:T(8,128)(2,1)} %bitcast.3), calls=%async_computation.1 | async-start | bytes 1114112 | tf_op jit(solution)/shard_map/all_to_all | solution.py:418
  22.1 4.5 %collective-permute-start.2 = (bf16[128,1024]{1,0:T(8,128)(2,1)S(1)}, bf16[128,1024]{1,0:T(8,128)(2,1)S(1)}, u32[]{:S(2)}, u32[]{:S(2)}) collective-permute-start(bf16[128,1024]{1,0:T(8,128)(2,1)S(1)} %maximum_maximum_fusion.own), channel_id=1, source_target_pairs={{0,24},{4,28},{8,0},{12,4},{16,8},{20,12},{24,16},{28,20},{1,25},{... | collective-permute-start | bytes 786440 | tf_op jit(solution)/shard_map/ppermute | solution.py:426
  27.4 6.3 %collective-permute-done.1.third = bf16[128,1024]{1,0:T(8,128)(2,1)S(1)} collective-permute-done((bf16[128,1024]{1,0:T(8,128)(2,1)S(1)}, bf16[128,1024]{1,0:T(8,128)(2,1)S(1)}, u32[]{:S(2)}, u32[]{:S(2)}) %collective-permute-start.1) | collective-permute-done | bytes 262176 | tf_op jit(solution)/shard_map/ppermute | solution.py:422
  33.7 3.2 %collective-permute-done.2.first = bf16[128,1024]{1,0:T(8,128)(2,1)S(1)} collective-permute-done((bf16[128,1024]{1,0:T(8,128)(2,1)S(1)}, bf16[128,1024]{1,0:T(8,128)(2,1)S(1)}, u32[]{:S(2)}, u32[]{:S(2)}) %collective-permute-start.2) | collective-permute-done | bytes 262176 | tf_op jit(solution)/shard_map/ppermute | solution.py:426
  38.8 2.0 collective-permute-start.7
  43.6 16.3 %collective-permute-done.4.second = bf16[128,1024]{1,0:T(8,128)(2,1)S(1)} collective-permute-done((bf16[128,1024]{1,0:T(8,128)(2,1)S(1)}, bf16[128,1024]{1,0:T(8,128)(2,1)S(1)}, u32[]{:S(2)}, u32[]{:S(2)}) %collective-permute-start.4) | collective-permute-done | bytes 262176 | tf_op jit(solution)/shard_map/ppermute | solution.py:422
  63.9 5.1 %collective-permute-done.9.other_second = bf16[128,1024]{1,0:T(8,128)(2,1)S(1)} collective-permute-done((bf16[128,1024]{1,0:T(8,128)(2,1)S(1)}, bf16[128,1024]{1,0:T(8,128)(2,1)S(1)}, u32[]{:S(2)}, u32[]{:S(2)}) %collective-permute-start.9) | collective-permute-done | bytes 262176 | tf_op jit(solution)/shard_map/ppermute | solution.py:430
  73.0 7.5 %attention_forward.1 = (bf16[512,1024]{1,0:T(8,128)(2,1)S(1)}, bf16[1024,768]{1,0:T(8,128)(2,1)S(1)}, bf16[256,1024]{1,0:T(8,128)(2,1)S(1)}, bf16[512,256]{1,0:T...) custom-call(s32[2]{0:T(128)S(1)} %pad_add_fusion.place, ...), custom_call_target="tpu_custom_call" | custom-call | flops 1207959552 | bytes 11014152 | tf_op jit(solution)/shard_map/attention_forward/pallas_call | solution.py:713
  80.5 3.9 %collective-permute-done.11.other = bf16[128,2176]{1,0:T(8,128)(2,1)} collective-permute-done((bf16[128,2176]{1,0:T(8,128)(2,1)}, bf16[128,2176]{1,0:T(8,128)(2,1)}, u32[]{:S(2)}, u32[]{:S(2)}) %collective-permute-start.11) | collective-permute-done | bytes 557088 | tf_op jit(solution)/shard_map/ppermute | solution.py:430
  84.4 1.9 collective-permute-done.12
  90.8 4.0 %collective-permute-done.13 = bf16[128,1024]{1,0:T(8,128)(2,1)S(1)} collective-permute-done((bf16[128,1024]{1,0:T(8,128)(2,1)S(1)}, bf16[128,1024]{1,0:T(8,128)(2,1)S(1)}, u32[]{:S(2)}, u32[]{:S(2)}) %collective-permute-start.13) | collective-permute-done | bytes 262176 | tf_op jit(solution)/shard_map/ppermute | solution.py:413
  97.2 5.2 %collective-permute-done.17.other_third = bf16[128,2176]{1,0:T(8,128)(2,1)S(1)} collective-permute-done((bf16[128,2176]{1,0:T(8,128)(2,1)}, bf16[128,2176]{1,0:T(8,128)(2,1)S(1)}, u32[]{:S(2)}, u32[]{:S(2)}) %collective-permute-start.17) | collective-permute-done | bytes 557088 | tf_op jit(solution)/shard_map/ppermute | solution.py:430
  105.7 10.3 %collective-permute-done.18.other_first = bf16[128,2176]{1,0:T(8,128)(2,1)S(1)} collective-permute-done((bf16[128,2176]{1,0:T(8,128)(2,1)}, bf16[128,2176]{1,0:T(8,128)(2,1)S(1)}, u32[]{:S(2)}, u32[]{:S(2)}) %collective-permute-start.18) | collective-permute-done | bytes 557088 | tf_op jit(solution)/shard_map/ppermute | solution.py:430
  116.1 4.5 %collective-permute-done.19.other_second = bf16[128,2176]{1,0:T(8,128)(2,1)S(1)} collective-permute-done((bf16[128,2176]{1,0:T(8,128)(2,1)S(1)}, bf16[128,2176]{1,0:T(8,128)(2,1)S(1)}, u32[]{:S(2)}, u32[]{:S(2)}) %collective-permute-start.19) | collective-permute-done | bytes 557088 | tf_op jit(solution)/shard_map/ppermute | solution.py:422
  120.6 7.3 %mlp.1 = (bf16[512,1024]{1,0:T(8,128)(2,1)S(1)}, bf16[512,1024]{1,0:T(8,128)(2,1)S(1)}, bf16[512,768]{1,0:T(8,128)(2,1)S(1)}, bf16[512,1408]{1,0:T(8,128)(2,1)S(...) custom-call(s32[512,1]{1,0:T(8,128)S(1)} %copy.28.seg_col, ...), custom_call_target="tpu_custom_call" | custom-call | flops 3758096384 | bytes 14551040 | tf_op jit(solution)/shard_map/mlp/pallas_call | solution.py:713
  128.0 1.9 collective-permute-done.20
  130.7 2.7 %mlp_terms.1 = (bf16[384,2176]{1,0:T(8,128)(2,1)S(1)}, bf16[256,2176]{1,0:T(8,128)(2,1)S(1)}, bf16[128,2176]{1,0:T(8,128)(2,1)S(1)}, bf16[256,2176]{1,0:T(8,128)(2,1)S(1)}) custom-call(bf16[512,1024]{1,0:T(8,128)(2,1)S(1)} %get-tuple-element.105.normed, bf16[512,1408]{1,0:T(8,128)(2,1)S(1)} %get-tuple-element.106.grad_inner, ...), custom_call_target="tpu_custom_call" | custom-call | flops 2281701376 | bytes 8781824 | tf_op jit(solution)/shard_map/mlp_terms/pallas_call | solution.py:713
  134.0 4.3 %collective-permute-done.21 = bf16[128,1024]{1,0:T(8,128)(2,1)S(1)} collective-permute-done((bf16[128,1024]{1,0:T(8,128)(2,1)S(1)}, bf16[128,1024]{1,0:T(8,128)(2,1)S(1)}, u32[]{:S(2)}, u32[]{:S(2)}) %collective-permute-start.21) | collective-permute-done | bytes 262176 | tf_op jit(solution)/shard_map/ppermute | solution.py:413
  140.4 6.8 %collective-permute-done.22.low_across = bf16[128,1024]{1,0:T(8,128)(2,1)S(1)} collective-permute-done((bf16[128,1024]{1,0:T(8,128)(2,1)S(1)}, bf16[128,1024]{1,0:T(8,128)(2,1)S(1)}, u32[]{:S(2)}, u32[]{:S(2)}) %collective-permute-start.22) | collective-permute-done | bytes 262176 | tf_op jit(solution)/shard_map/ppermute | solution.py:413
  147.4 1.9 collective-permute-done.23.low_beside
  149.3 7.6 %attention_backward.1 = (bf16[512,768]{1,0:T(8,128)(2,1)S(1)}, bf16[384,1024]{1,0:T(8,128)(2,1)S(1)}, bf16[256,1024]{1,0:T(8,128)(2,1)S(1)}, bf16[128,1024]{1,0:T(8,128)(2,1)S(1)}, bf16[256,1024]{1,0:T(8,128)(2,1)S(1)}) custom-call(s32[2]{0:T(128)S(1)} %pad_add_fusion.place, f32[512,128]{1,0:T(8,128)S(1)} %get-tuple-element.260.cosine, ...), custom_call_target="tpu_custom_call" | custom-call | flops 1677721600 | bytes 8126472 | tf_op jit(solution)/shard_map/attention_backward/pallas_call | solution.py:713
  156.9 4.7 %collective-permute-done.24 = bf16[256,2176]{1,0:T(8,128)(2,1)S(1)} collective-permute-done((bf16[256,2176]{1,0:T(8,128)(2,1)S(1)}, bf16[256,2176]{1,0:T(8,128)(2,1)S(1)}, u32[]{:S(2)}, u32[]{:S(2)}) %collective-permute-start.24) | collective-permute-done | bytes 1114144 | tf_op jit(solution)/shard_map/ppermute | solution.py:422
  166.0 1.8 projections.1
  167.9 18.5 %collective-permute-done.28 = bf16[256,1024]{1,0:T(8,128)(2,1)S(1)} collective-permute-done((bf16[256,1024]{1,0:T(8,128)(2,1)S(1)}, bf16[256,1024]{1,0:T(8,128)(2,1)S(1)}, u32[]{:S(2)}, u32[]{:S(2)}) %collective-permute-start.28) | collective-permute-done | bytes 524320 | tf_op jit(solution)/shard_map/ppermute | solution.py:422
  188.9 3.3 %collective-permute-start.33 = (bf16[128,1024]{1,0:T(8,128)(2,1)S(1)}, bf16[128,1024]{1,0:T(8,128)(2,1)S(1)}, u32[]{:S(2)}, u32[]{:S(2)}) collective-permute-start(bf16[128,1024]{1,0:T(8,128)(2,1)S(1)} %add_convert_fusion.7), channel_id=1, source_target_pairs={{0,24},{4,28},{8,0},{12,4},{16,8},{20,12},{24,16},{28,20},{1,25},{... | collective-permute-start | bytes 786440 | tf_op jit(solution)/shard_map/ppermute | solution.py:426
  193.9 15.4 %collective-permute-done.33 = bf16[128,1024]{1,0:T(8,128)(2,1)S(1)} collective-permute-done((bf16[128,1024]{1,0:T(8,128)(2,1)S(1)}, bf16[128,1024]{1,0:T(8,128)(2,1)S(1)}, u32[]{:S(2)}, u32[]{:S(2)}) %collective-permute-start.33) | collective-permute-done | bytes 262176 | tf_op jit(solution)/shard_map/ppermute | solution.py:426
  211.3 3.6 %all-to-all-start.2 = ((bf16[4,32,2176]{2,1,0:T(8,128)(2,1)}), bf16[4,32,2176]{2,1,0:T(8,128)(2,1)S(1)}, u32[]{:S(2)}, u32[]{:S(2)}) async-start(bf16[4,32,2176]{2,1,0:T(8,128)(2,1)} %bitcast.26), calls=%async_computation.2 | async-start | bytes 1114112 | tf_op jit(solution)/shard_map/all_to_all | solution.py:418
  216.8 1.9 collective-permute-start.34
  218.8 6.9 %collective-permute-done.35 = bf16[128,1024]{1,0:T(8,128)(2,1)} collective-permute-done((bf16[128,1024]{1,0:T(8,128)(2,1)}, bf16[128,1024]{1,0:T(8,128)(2,1)}, u32[]{:S(2)}, u32[]{:S(2)}) %collective-permute-start.35) | collective-permute-done | bytes 262176 | tf_op jit(solution)/shard_map/ppermute | solution.py:422
  228.9 4.8 %all-to-all-start.3 = ((bf16[4,32,768]{2,1,0:T(8,128)(2,1)}), bf16[4,32,768]{2,1,0:T(8,128)(2,1)S(1)}, u32[]{:S(2)}, u32[]{:S(2)}) async-start(bf16[4,32,768]{2,1,0:T(8,128)(2,1)} %bitcast.11), calls=%async_computation.3 | async-start | bytes 393216 | tf_op jit(solution)/shard_map/all_to_all | solution.py:418
  233.7 3.6 %unpack_rest.1 = (f32[32,5248]{1,0:T(8,128)}, f32[32,1]{1,0:T(8,128)S(1)}, f32[32,2624]{1,0:T(8,128)}) custom-call(bf16[128,2176]{1,0:T(8,128)(2,1)S(1)} %bitcast.19, bf16[32,5248]{1,0:T(8,128)(2,1)S(1)} %copy-done, f32[32,1]{1,0:T(8,128)S(1)} %copy.31.gain), custom_call_target="tpu_custom_call" | custom-call | flops 671744 | bytes 1900800 | tf_op jit(solution)/shard_map/unpack_rest/pallas_call | solution.py:713
  (216 shorter events, 58.8 us)
Async XLA Ops:
  4.3 9.9 %all-to-all-start = ((bf16[4,32,896]{2,1,0:T(8,128)(2,1)}), bf16[4,32,896]{2,1,0:T(8,128)(2,1)S(1)}, u32[]{:S(2)}, u32[]{:S(2)}) async-start(bf16[4,32,896]{2,1,0:T(8,128)(2,1)} %bitcast), calls=%async_computation | async-start | bytes 458752 | tf_op jit(solution)/shard_map/all_to_all | solution.py:418
  14.3 22.6 %all-to-all-start.1 = ((bf16[4,32,2176]{2,1,0:T(8,128)(2,1)}), bf16[4,32,2176]{2,1,0:T(8,128)(2,1)S(1)}, u32[]{:S(2)}, u32[]{:S(2)}) async-start(bf16[4,32,2176]{2,1,0:T(8,128)(2,1)} %bitcast.3), calls=%async_computation.1 | async-start | bytes 1114112 | tf_op jit(solution)/shard_map/all_to_all | solution.py:418
  21.5 12.2 %collective-permute-start.1 = (bf16[128,1024]{1,0:T(8,128)(2,1)S(1)}, bf16[128,1024]{1,0:T(8,128)(2,1)S(1)}, u32[]{:S(2)}, u32[]{:S(2)}) collective-permute-start(bf16[128,1024]{1,0:T(8,128)(2,1)S(1)} %maximum_maximum_fusion.own), channel_id=1, source_target_pairs={{0,8},{4,12},{8,16},{12,20},{16,24},{20,28},{24,0},{28,4},{1,9},{5... | collective-permute-start | bytes 786440 | tf_op jit(solution)/shard_map/ppermute | solution.py:422
  22.1 14.8 %collective-permute-start.2 = (bf16[128,1024]{1,0:T(8,128)(2,1)S(1)}, bf16[128,1024]{1,0:T(8,128)(2,1)S(1)}, u32[]{:S(2)}, u32[]{:S(2)}) collective-permute-start(bf16[128,1024]{1,0:T(8,128)(2,1)S(1)} %maximum_maximum_fusion.own), channel_id=1, source_target_pairs={{0,24},{4,28},{8,0},{12,4},{16,8},{20,12},{24,16},{28,20},{1,25},{... | collective-permute-start | bytes 786440 | tf_op jit(solution)/shard_map/ppermute | solution.py:426
  26.6 10.3 %collective-permute-start.3 = (bf16[128,1024]{1,0:T(8,128)(2,1)S(1)}, bf16[128,1024]{1,0:T(8,128)(2,1)S(1)}, u32[]{:S(2)}, u32[]{:S(2)}) collective-permute-start(bf16[128,1024]{1,0:T(8,128)(2,1)S(1)} %maximum_maximum_fusion.own), channel_id=1, source_target_pairs={{0,4},{4,0},{8,12},{12,8},{16,20},{20,16},{24,28},{28,24},{1,5},{5... | collective-permute-start | bytes 786440 | tf_op jit(solution)/shard_map/ppermute | solution.py:430
  37.8 22.1 %collective-permute-start.5 = (bf16[256,1024]{1,0:T(8,128)(2,1)}, bf16[256,1024]{1,0:T(8,128)(2,1)}, u32[]{:S(2)}, u32[]{:S(2)}) collective-permute-start(bf16[256,1024]{1,0:T(8,128)(2,1)} %pad_maximum_fusion.3), channel_id=1, source_target_pairs={{0,4},{4,0},{8,12},{12,8},{16,20},{20,16},{24,28},{28,24},{1,5},{5... | collective-permute-start | bytes 1572872 | tf_op jit(solution)/shard_map/ppermute | solution.py:430
  38.8 21.1 %collective-permute-start.7 = (bf16[128,2176]{1,0:T(8,128)(2,1)S(1)}, bf16[128,2176]{1,0:T(8,128)(2,1)}, u32[]{:S(2)}, u32[]{:S(2)}) collective-permute-start(bf16[128,2176]{1,0:T(8,128)(2,1)S(1)} %bitcast.21), channel_id=1, source_target_pairs={{0,8},{4,12},{8,16},{12,20},{16,24},{20,28},{24,0},{28,4},{1,9},{5... | collective-permute-start | bytes 1671176 | tf_op jit(solution)/shard_map/ppermute | solution.py:422
  40.9 19.1 %collective-permute-start.6 = (bf16[256,1024]{1,0:T(8,128)(2,1)S(1)}, bf16[256,1024]{1,0:T(8,128)(2,1)S(1)}, u32[]{:S(2)}, u32[]{:S(2)}) collective-permute-start(bf16[256,1024]{1,0:T(8,128)(2,1)S(1)} %pad_maximum_fusion.2.mine), channel_id=1, source_target_pairs={{0,2},{1,3},{2,0},{3,1},{4,6},{5,7},{6,4},{7,5},{8,10},{9,11},{10,... | collective-permute-start | bytes 1572872 | tf_op jit(solution)/shard_map/ppermute | solution.py:413
  42.5 17.4 %collective-permute-start.4 = (bf16[128,1024]{1,0:T(8,128)(2,1)S(1)}, bf16[128,1024]{1,0:T(8,128)(2,1)S(1)}, u32[]{:S(2)}, u32[]{:S(2)}) collective-permute-start(bf16[128,1024]{1,0:T(8,128)(2,1)S(1)} %collective-permute-done.1.third), channel_id=1, source_target_pairs={{0,8},{4,12},{8,16},{12,20},{16,24},{20,28},{24,0},{28,4},{1,9},{5... | collective-permute-start | bytes 786440 | tf_op jit(solution)/shard_map/ppermute | solution.py:422
  60.1 9.6 %collective-permute-start.8 = (bf16[512,1024]{1,0:T(8,128)(2,1)S(1)}, bf16[512,1024]{1,0:T(8,128)(2,1)S(1)}, u32[]{:S(2)}, u32[]{:S(2)}) collective-permute-start(bf16[512,1024]{1,0:T(8,128)(2,1)S(1)} %pad_maximum_fusion), channel_id=1, source_target_pairs={{0,1},{1,0},{2,3},{3,2},{4,5},{5,4},{6,7},{7,6},{8,9},{9,8},{10,11... | collective-permute-start | bytes 3145736 | tf_op jit(solution)/shard_map/ppermute | solution.py:413
  62.1 18.3 %collective-permute-start.10 = (bf16[128,2176]{1,0:T(8,128)(2,1)}, bf16[128,2176]{1,0:T(8,128)(2,1)}, u32[]{:S(2)}, u32[]{:S(2)}) collective-permute-start(bf16[128,2176]{1,0:T(8,128)(2,1)} %bitcast.22), channel_id=1, source_target_pairs={{0,24},{4,28},{8,0},{12,4},{16,8},{20,12},{24,16},{28,20},{1,25},{... | collective-permute-start | bytes 1671176 | tf_op jit(solution)/shard_map/ppermute | solution.py:426
  69.7 14.7 %collective-permute-start.11 = (bf16[128,2176]{1,0:T(8,128)(2,1)}, bf16[128,2176]{1,0:T(8,128)(2,1)}, u32[]{:S(2)}, u32[]{:S(2)}) collective-permute-start(bf16[128,2176]{1,0:T(8,128)(2,1)} %bitcast.23), channel_id=1, source_target_pairs={{0,4},{4,0},{8,12},{12,8},{16,20},{20,16},{24,28},{28,24},{1,5},{5... | collective-permute-start | bytes 1671176 | tf_op jit(solution)/shard_map/ppermute | solution.py:430
  87.7 14.7 %collective-permute-start.17 = (bf16[128,2176]{1,0:T(8,128)(2,1)}, bf16[128,2176]{1,0:T(8,128)(2,1)S(1)}, u32[]{:S(2)}, u32[]{:S(2)}) collective-permute-start(bf16[128,2176]{1,0:T(8,128)(2,1)} %collective-permute-done.7.third), channel_id=1, source_target_pairs={{0,4},{4,0},{8,12},{12,8},{16,20},{20,16},{24,28},{28,24},{1,5},{5... | collective-permute-start | bytes 1671176 | tf_op jit(solution)/shard_map/ppermute | solution.py:430
  89.5 16.1 %collective-permute-start.16 = (bf16[128,2176]{1,0:T(8,128)(2,1)}, bf16[128,2176]{1,0:T(8,128)(2,1)S(1)}, u32[]{:S(2)}, u32[]{:S(2)}) collective-permute-start(bf16[128,2176]{1,0:T(8,128)(2,1)} %collective-permute-done.7.third), channel_id=1, source_target_pairs={{0,8},{4,12},{8,16},{12,20},{16,24},{20,28},{24,0},{28,4},{1,9},{5... | collective-permute-start | bytes 1671176 | tf_op jit(solution)/shard_map/ppermute | solution.py:422
  95.9 9.7 %collective-permute-start.14 = (bf16[128,1024]{1,0:T(8,128)(2,1)S(1)}, bf16[128,1024]{1,0:T(8,128)(2,1)S(1)}, u32[]{:S(2)}, u32[]{:S(2)}) collective-permute-start(bf16[128,1024]{1,0:T(8,128)(2,1)S(1)} %fusion.12.norm_own), channel_id=1, source_target_pairs={{0,2},{1,3},{2,0},{3,1},{4,6},{5,7},{6,4},{7,5},{8,10},{9,11},{10,... | collective-permute-start | bytes 786440 | tf_op jit(solution)/shard_map/ppermute | solution.py:413
  102.4 13.7 %collective-permute-start.18 = (bf16[128,2176]{1,0:T(8,128)(2,1)}, bf16[128,2176]{1,0:T(8,128)(2,1)S(1)}, u32[]{:S(2)}, u32[]{:S(2)}) collective-permute-start(bf16[128,2176]{1,0:T(8,128)(2,1)} %collective-permute-done.10.first), channel_id=1, source_target_pairs={{0,4},{4,0},{8,12},{12,8},{16,20},{20,16},{24,28},{28,24},{1,5},{5... | collective-permute-start | bytes 1671176 | tf_op jit(solution)/shard_map/ppermute | solution.py:430
  105.6 15.0 %collective-permute-start.19 = (bf16[128,2176]{1,0:T(8,128)(2,1)S(1)}, bf16[128,2176]{1,0:T(8,128)(2,1)S(1)}, u32[]{:S(2)}, u32[]{:S(2)}) collective-permute-start(bf16[128,2176]{1,0:T(8,128)(2,1)S(1)} %collective-permute-done.17.other_third), channel_id=1, source_target_pairs={{0,8},{4,12},{8,16},{12,20},{16,24},{20,28},{24,0},{28,4},{1,9},{5... | collective-permute-start | bytes 1671176 | tf_op jit(solution)/shard_map/ppermute | solution.py:422
  105.7 14.9 %collective-permute-start.15 = (bf16[256,1024]{1,0:T(8,128)(2,1)S(1)}, bf16[256,1024]{1,0:T(8,128)(2,1)S(1)}, u32[]{:S(2)}, u32[]{:S(2)}) collective-permute-start(bf16[256,1024]{1,0:T(8,128)(2,1)S(1)} %pad_maximum_fusion.4), channel_id=1, source_target_pairs={{0,1},{1,0},{2,3},{3,2},{4,5},{5,4},{6,7},{7,6},{8,9},{9,8},{10,11... | collective-permute-start | bytes 1572872 | tf_op jit(solution)/shard_map/ppermute | solution.py:413
  133.4 28.2 %collective-permute-start.24 = (bf16[256,2176]{1,0:T(8,128)(2,1)S(1)}, bf16[256,2176]{1,0:T(8,128)(2,1)S(1)}, u32[]{:S(2)}, u32[]{:S(2)}) collective-permute-start(bf16[256,2176]{1,0:T(8,128)(2,1)S(1)} %get-tuple-element.122), channel_id=1, source_target_pairs={{0,8},{4,12},{8,16},{12,20},{16,24},{20,28},{24,0},{28,4},{1,9},{5... | collective-permute-start | bytes 3342344 | tf_op jit(solution)/shard_map/ppermute | solution.py:422
  133.5 28.1 %collective-permute-start.25 = (bf16[256,2176]{1,0:T(8,128)(2,1)S(1)}, bf16[256,2176]{1,0:T(8,128)(2,1)S(1)}, u32[]{:S(2)}, u32[]{:S(2)}) collective-permute-start(bf16[256,2176]{1,0:T(8,128)(2,1)S(1)} %get-tuple-element.123), channel_id=1, source_target_pairs={{0,4},{4,0},{8,12},{12,8},{16,20},{20,16},{24,28},{28,24},{1,5},{5... | collective-permute-start | bytes 3342344 | tf_op jit(solution)/shard_map/ppermute | solution.py:430
  161.7 26.2 %collective-permute-start.27 = (bf16[128,2176]{1,0:T(8,128)(2,1)S(1)}, bf16[128,2176]{1,0:T(8,128)(2,1)S(1)}, u32[]{:S(2)}, u32[]{:S(2)}) collective-permute-start(bf16[128,2176]{1,0:T(8,128)(2,1)S(1)} %add_convert_fusion.2), channel_id=1, source_target_pairs={{0,24},{4,28},{8,0},{12,4},{16,8},{20,12},{24,16},{28,20},{1,25},{... | collective-permute-start | bytes 1671176 | tf_op jit(solution)/shard_map/ppermute | solution.py:426
  163.7 24.2 %collective-permute-start.26 = (bf16[128,2176]{1,0:T(8,128)(2,1)S(1)}, bf16[128,2176]{1,0:T(8,128)(2,1)S(1)}, u32[]{:S(2)}, u32[]{:S(2)}) collective-permute-start(bf16[128,2176]{1,0:T(8,128)(2,1)S(1)} %add_convert_fusion.3), channel_id=1, source_target_pairs={{0,4},{4,0},{8,12},{12,8},{16,20},{20,16},{24,28},{28,24},{1,5},{5... | collective-permute-start | bytes 1671176 | tf_op jit(solution)/shard_map/ppermute | solution.py:430
  164.2 22.1 %collective-permute-start.28 = (bf16[256,1024]{1,0:T(8,128)(2,1)S(1)}, bf16[256,1024]{1,0:T(8,128)(2,1)S(1)}, u32[]{:S(2)}, u32[]{:S(2)}) collective-permute-start(bf16[256,1024]{1,0:T(8,128)(2,1)S(1)} %get-tuple-element.127), channel_id=1, source_target_pairs={{0,8},{4,12},{8,16},{12,20},{16,24},{20,28},{24,0},{28,4},{1,9},{5... | collective-permute-start | bytes 1572872 | tf_op jit(solution)/shard_map/ppermute | solution.py:422
  164.5 23.4 %collective-permute-start.29 = (bf16[256,1024]{1,0:T(8,128)(2,1)S(1)}, bf16[256,1024]{1,0:T(8,128)(2,1)S(1)}, u32[]{:S(2)}, u32[]{:S(2)}) collective-permute-start(bf16[256,1024]{1,0:T(8,128)(2,1)S(1)} %get-tuple-element.128), channel_id=1, source_target_pairs={{0,4},{4,0},{8,12},{12,8},{16,20},{20,16},{24,28},{28,24},{1,5},{5... | collective-permute-start | bytes 1572872 | tf_op jit(solution)/shard_map/ppermute | solution.py:430
  188.2 21.2 %collective-permute-start.31 = (bf16[128,2176]{1,0:T(8,128)(2,1)S(1)}, bf16[128,2176]{1,0:T(8,128)(2,1)S(1)}, u32[]{:S(2)}, u32[]{:S(2)}) collective-permute-start(bf16[128,2176]{1,0:T(8,128)(2,1)S(1)} %add_convert_fusion.1), channel_id=1, source_target_pairs={{0,8},{4,12},{8,16},{12,20},{16,24},{20,28},{24,0},{28,4},{1,9},{5... | collective-permute-start | bytes 1671176 | tf_op jit(solution)/shard_map/ppermute | solution.py:422
  188.9 20.4 %collective-permute-start.33 = (bf16[128,1024]{1,0:T(8,128)(2,1)S(1)}, bf16[128,1024]{1,0:T(8,128)(2,1)S(1)}, u32[]{:S(2)}, u32[]{:S(2)}) collective-permute-start(bf16[128,1024]{1,0:T(8,128)(2,1)S(1)} %add_convert_fusion.7), channel_id=1, source_target_pairs={{0,24},{4,28},{8,0},{12,4},{16,8},{20,12},{24,16},{28,20},{1,25},{... | collective-permute-start | bytes 786440 | tf_op jit(solution)/shard_map/ppermute | solution.py:426
  192.3 17.1 %collective-permute-start.32 = (bf16[128,1024]{1,0:T(8,128)(2,1)S(1)}, bf16[128,1024]{1,0:T(8,128)(2,1)S(1)}, u32[]{:S(2)}, u32[]{:S(2)}) collective-permute-start(bf16[128,1024]{1,0:T(8,128)(2,1)S(1)} %add_convert_fusion.8), channel_id=1, source_target_pairs={{0,4},{4,0},{8,12},{12,8},{16,20},{20,16},{24,28},{28,24},{1,5},{5... | collective-permute-start | bytes 786440 | tf_op jit(solution)/shard_map/ppermute | solution.py:430
  211.3 14.4 %all-to-all-start.2 = ((bf16[4,32,2176]{2,1,0:T(8,128)(2,1)}), bf16[4,32,2176]{2,1,0:T(8,128)(2,1)S(1)}, u32[]{:S(2)}, u32[]{:S(2)}) async-start(bf16[4,32,2176]{2,1,0:T(8,128)(2,1)} %bitcast.26), calls=%async_computation.2 | async-start | bytes 1114112 | tf_op jit(solution)/shard_map/all_to_all | solution.py:418
  214.9 10.8 %collective-permute-start.35 = (bf16[128,1024]{1,0:T(8,128)(2,1)}, bf16[128,1024]{1,0:T(8,128)(2,1)}, u32[]{:S(2)}, u32[]{:S(2)}) collective-permute-start(bf16[128,1024]{1,0:T(8,128)(2,1)} %add_convert_fusion.6), channel_id=1, source_target_pairs={{0,8},{4,12},{8,16},{12,20},{16,24},{20,28},{24,0},{28,4},{1,9},{5... | collective-permute-start | bytes 786440 | tf_op jit(solution)/shard_map/ppermute | solution.py:422
  216.8 21.7 %collective-permute-start.34 = (bf16[256,1024]{1,0:T(8,128)(2,1)}, bf16[256,1024]{1,0:T(8,128)(2,1)}, u32[]{:S(2)}, u32[]{:S(2)}) collective-permute-start(bf16[256,1024]{1,0:T(8,128)(2,1)} %add_convert_fusion.4), channel_id=1, source_target_pairs={{0,2},{1,3},{2,0},{3,1},{4,6},{5,7},{6,4},{7,5},{8,10},{9,11},{10,... | collective-permute-start | bytes 1572872 | tf_op jit(solution)/shard_map/ppermute | solution.py:413
  226.9 11.0 %collective-permute-start.36 = (bf16[32,1024]{1,0:T(8,128)(2,1)S(1)}, bf16[32,1024]{1,0:T(8,128)(2,1)S(1)}, u32[]{:S(2)}, u32[]{:S(2)}) collective-permute-start(bf16[32,1024]{1,0:T(8,128)(2,1)S(1)} %pad_maximum_fusion.8), channel_id=1, source_target_pairs={{0,0},{4,1},{8,2},{12,3},{16,4},{20,5},{24,6},{28,7},{1,8},{5,9},{... | collective-permute-start | bytes 196616 | tf_op jit(solution)/shard_map/ppermute | solution.py:906
  228.9 12.3 %all-to-all-start.3 = ((bf16[4,32,768]{2,1,0:T(8,128)(2,1)}), bf16[4,32,768]{2,1,0:T(8,128)(2,1)S(1)}, u32[]{:S(2)}, u32[]{:S(2)}) async-start(bf16[4,32,768]{2,1,0:T(8,128)(2,1)} %bitcast.11), calls=%async_computation.3 | async-start | bytes 393216 | tf_op jit(solution)/shard_map/all_to_all | solution.py:418
  (33 other events, 268.8 us)

commit v9 on v8

--- a/solution.py
+++ b/solution.py
@@ -793,11 +793,11 @@
     third, first, other, mine, rest = tie(third, first, other, mine, rest)
     across = swap(mine, 2)
     second, others, rest_third = up(third), over(rows([first, third])), up(rest)
-    second, others, across, rest_third, rest = tie(second, others, across, rest_third, rest)
+    second, others, across = tie(second, others, across)
     other_second = over(second)
-    rest_first = down(rest)
+    rest_first = down(tie(rest, rest_third)[0])
     beside = swap(rows([mine, across]), 1)
-    rest_other = over(tie(rest, other_second, beside)[0])
+    rest_other = over(tie(rest, other_second)[0])
 
     step = mine.shape[0]
     segment, positions, _ = jax.vmap(lambda row: layout(row, count))(lengths)

time: 245 us -> 238 us (0.971)
  waiting for transfers between devices: 126 us -> 114 us
  starting transfers between devices: 58.5 us -> 61.3 us
    ppermute x10, waiting for transfers between devices: 26.1 us -> 18.6 us  [over(): return lax.ppermute(value, 'fsdp', [(k, k ^ 1) for k in range(8)])]
    ppermute x9, starting transfers between devices: 6.52 us -> 11.1 us  [up(): return lax.ppermute(value, 'fsdp', [(k, (k + 2) % 8) for k in range(8)])]
  transfers between devices with their start and end apart: 41 -> 41, of which waited for: 21 -> 22; matrix products, arithmetic and copies ran while one was open for 7% -> 8% of each run, Pallas kernels for 10% -> 10%
where the time goes in v9:
time: 238 us; the launch traced here: 236 us
  waiting for transfers between devices  114 us (48%)
  starting transfers between devices  61.3 us (26%)
  Pallas kernels  30.9 us (13%)
  other arithmetic  22.1 us (9%)
  local copies, waits for them, and re-layouts  5.96 us (3%)
    ppermute x9, waiting for transfers between devices, up(): return lax.ppermute(value, 'fsdp', [(k, (k + 2) % 8) for k in range(8)])  57.1 us
    pallas_call x7, Pallas kernels, kernel(): pl.pallas_call(body, out_shape=shapes, in_specs=[pl.BlockSpec(memory_spac...  30.9 us
    all_to_all x4, starting transfers between devices, rep_exchange(): return lax.all_to_all(blocks, 'rep', 0, 0, tiled=True).reshape(value.shape)  19.8 us
    ppermute x12, waiting for transfers between devices, swap(): return lax.ppermute(value, 'rep', [(k, k ^ distance) for k in range(4)])  19.1 us
    ppermute x10, waiting for transfers between devices, over(): return lax.ppermute(value, 'fsdp', [(k, k ^ 1) for k in range(8)])  18.6 us
    ppermute x4, waiting for transfers between devices, down(): return lax.ppermute(value, 'fsdp', [(k, (k - 2) % 8) for k in range(8)])  18.1 us
    ppermute x4, starting transfers between devices, down(): return lax.ppermute(value, 'fsdp', [(k, (k - 2) % 8) for k in range(8)])  11.5 us
    ppermute x9, starting transfers between devices, up(): return lax.ppermute(value, 'fsdp', [(k, (k + 2) % 8) for k in range(8)])  11.1 us
  transfers between devices with their start and end apart: 41, of which 22 were waited for; matrix products, arithmetic and copies ran while one was open for 8% of the time, Pallas kernels for 10%

profile of v9, /device:TPU:0, one launch (start us, length us, event | category | flops | bytes accessed | tf_op | source)
XLA Modules:
  0.0 235.8 jit_solution(17673097624816041371)
XLA Ops:
  4.3 4.2 %all-to-all-start = ((bf16[4,32,896]{2,1,0:T(8,128)(2,1)}), bf16[4,32,896]{2,1,0:T(8,128)(2,1)S(1)}, u32[]{:S(2)}, u32[]{:S(2)}) async-start(bf16[4,32,896]{2,1,0:T(8,128)(2,1)} %bitcast), calls=%async_computation | async-start | bytes 458752 | tf_op jit(solution)/shard_map/all_to_all | solution.py:418
  14.3 7.2 %all-to-all-start.1 = ((bf16[4,32,2176]{2,1,0:T(8,128)(2,1)}), bf16[4,32,2176]{2,1,0:T(8,128)(2,1)}, u32[]{:S(2)}, u32[]{:S(2)}) async-start(bf16[4,32,2176]{2,1,0:T(8,128)(2,1)} %bitcast.3), calls=%async_computation.1 | async-start | bytes 1114112 | tf_op jit(solution)/shard_map/all_to_all | solution.py:418
  22.5 4.7 %collective-permute-start.2 = (bf16[128,1024]{1,0:T(8,128)(2,1)S(1)}, bf16[128,1024]{1,0:T(8,128)(2,1)S(1)}, u32[]{:S(2)}, u32[]{:S(2)}) collective-permute-start(bf16[128,1024]{1,0:T(8,128)(2,1)S(1)} %maximum_maximum_fusion.own), channel_id=1, source_target_pairs={{0,24},{4,28},{8,0},{12,4},{16,8},{20,12},{24,16},{28,20},{1,25},{... | collective-permute-start | bytes 786440 | tf_op jit(solution)/shard_map/ppermute | solution.py:426
  27.5 6.9 %collective-permute-done.1.third = bf16[128,1024]{1,0:T(8,128)(2,1)S(1)} collective-permute-done((bf16[128,1024]{1,0:T(8,128)(2,1)S(1)}, bf16[128,1024]{1,0:T(8,128)(2,1)S(1)}, u32[]{:S(2)}, u32[]{:S(2)}) %collective-permute-start.1) | collective-permute-done | bytes 262176 | tf_op jit(solution)/shard_map/ppermute | solution.py:422
  34.4 3.2 %collective-permute-done.2.first = bf16[128,1024]{1,0:T(8,128)(2,1)S(1)} collective-permute-done((bf16[128,1024]{1,0:T(8,128)(2,1)S(1)}, bf16[128,1024]{1,0:T(8,128)(2,1)S(1)}, u32[]{:S(2)}, u32[]{:S(2)}) %collective-permute-start.2) | collective-permute-done | bytes 262176 | tf_op jit(solution)/shard_map/ppermute | solution.py:426
  40.1 2.0 collective-permute-start.4
  42.9 8.4 %collective-permute-done.4.second = bf16[128,1024]{1,0:T(8,128)(2,1)S(1)} collective-permute-done((bf16[128,1024]{1,0:T(8,128)(2,1)S(1)}, bf16[128,1024]{1,0:T(8,128)(2,1)S(1)}, u32[]{:S(2)}, u32[]{:S(2)}) %collective-permute-start.4) | collective-permute-done | bytes 262176 | tf_op jit(solution)/shard_map/ppermute | solution.py:422
  55.5 5.3 %collective-permute-done.9.third = bf16[128,2176]{1,0:T(8,128)(2,1)S(1)} collective-permute-done((bf16[128,2176]{1,0:T(8,128)(2,1)}, bf16[128,2176]{1,0:T(8,128)(2,1)S(1)}, u32[]{:S(2)}, u32[]{:S(2)}) %collective-permute-start.9) | collective-permute-done | bytes 557088 | tf_op jit(solution)/shard_map/ppermute | solution.py:422
  66.7 7.0 %attention_forward.1 = (bf16[512,1024]{1,0:T(8,128)(2,1)S(1)}, bf16[1024,768]{1,0:T(8,128)(2,1)S(1)}, bf16[256,1024]{1,0:T(8,128)(2,1)S(1)}, bf16[512,256]{1,0:T...) custom-call(s32[2]{0:T(128)S(1)} %pad_add_fusion.place, ...), custom_call_target="tpu_custom_call" | custom-call | flops 1207959552 | bytes 11014152 | tf_op jit(solution)/shard_map/attention_forward/pallas_call | solution.py:713
  74.1 3.1 %collective-permute-done.11.other = bf16[128,2176]{1,0:T(8,128)(2,1)} collective-permute-done((bf16[128,2176]{1,0:T(8,128)(2,1)}, bf16[128,2176]{1,0:T(8,128)(2,1)}, u32[]{:S(2)}, u32[]{:S(2)}) %collective-permute-start.11) | collective-permute-done | bytes 557088 | tf_op jit(solution)/shard_map/ppermute | solution.py:430
  77.2 1.9 collective-permute-done.12
  81.3 3.8 %collective-permute-start.16 = (bf16[128,2176]{1,0:T(8,128)(2,1)S(1)}, bf16[128,2176]{1,0:T(8,128)(2,1)S(1)}, u32[]{:S(2)}, u32[]{:S(2)}) collective-permute-start(bf16[128,2176]{1,0:T(8,128)(2,1)S(1)} %copy-done.11), channel_id=1, source_target_pairs={{0,8},{4,12},{8,16},{12,20},{16,24},{20,28},{24,0},{28,4},{1,9},{5... | collective-permute-start | bytes 1671176 | tf_op jit(solution)/shard_map/ppermute | solution.py:422
  85.0 2.5 %collective-permute-done.13 = bf16[128,1024]{1,0:T(8,128)(2,1)S(1)} collective-permute-done((bf16[128,1024]{1,0:T(8,128)(2,1)S(1)}, bf16[128,1024]{1,0:T(8,128)(2,1)S(1)}, u32[]{:S(2)}, u32[]{:S(2)}) %collective-permute-start.13) | collective-permute-done | bytes 262176 | tf_op jit(solution)/shard_map/ppermute | solution.py:413
  89.7 5.0 %collective-permute-done.17.other_third = bf16[128,2176]{1,0:T(8,128)(2,1)S(1)} collective-permute-done((bf16[128,2176]{1,0:T(8,128)(2,1)S(1)}, bf16[128,2176]{1,0:T(8,128)(2,1)S(1)}, u32[]{:S(2)}, u32[]{:S(2)}) %collective-permute-start.17) | collective-permute-done | bytes 557088 | tf_op jit(solution)/shard_map/ppermute | solution.py:430
  95.6 2.2 collective-permute-done.16.second
  99.5 8.9 %collective-permute-done.18.other_first = bf16[128,2176]{1,0:T(8,128)(2,1)S(1)} collective-permute-done((bf16[128,2176]{1,0:T(8,128)(2,1)}, bf16[128,2176]{1,0:T(8,128)(2,1)S(1)}, u32[]{:S(2)}, u32[]{:S(2)}) %collective-permute-start.18) | collective-permute-done | bytes 557088 | tf_op jit(solution)/shard_map/ppermute | solution.py:430
  108.4 4.8 %collective-permute-done.19.other_second = bf16[128,2176]{1,0:T(8,128)(2,1)S(1)} collective-permute-done((bf16[128,2176]{1,0:T(8,128)(2,1)S(1)}, bf16[128,2176]{1,0:T(8,128)(2,1)S(1)}, u32[]{:S(2)}, u32[]{:S(2)}) %collective-permute-start.19) | collective-permute-done | bytes 557088 | tf_op jit(solution)/shard_map/ppermute | solution.py:422
  113.2 7.3 %mlp.1 = (bf16[512,1024]{1,0:T(8,128)(2,1)S(1)}, bf16[512,1024]{1,0:T(8,128)(2,1)S(1)}, bf16[512,768]{1,0:T(8,128)(2,1)S(1)}, bf16[512,1408]{1,0:T(8,128)(2,1)S(...) custom-call(s32[512,1]{1,0:T(8,128)S(1)} %copy.28.seg_col, ...), custom_call_target="tpu_custom_call" | custom-call | flops 3758096384 | bytes 14551040 | tf_op jit(solution)/shard_map/mlp/pallas_call | solution.py:713
  120.6 1.9 collective-permute-done.20
  123.1 2.7 %mlp_terms.1 = (bf16[384,2176]{1,0:T(8,128)(2,1)S(1)}, bf16[256,2176]{1,0:T(8,128)(2,1)S(1)}, bf16[128,2176]{1,0:T(8,128)(2,1)S(1)}, bf16[256,2176]{1,0:T(8,128)(2,1)S(1)}) custom-call(bf16[512,1024]{1,0:T(8,128)(2,1)S(1)} %get-tuple-element.103.normed, bf16[512,1408]{1,0:T(8,128)(2,1)S(1)} %get-tuple-element.104.grad_inner, ...), custom_call_target="tpu_custom_call" | custom-call | flops 2281701376 | bytes 8781824 | tf_op jit(solution)/shard_map/mlp_terms/pallas_call | solution.py:713
  127.2 3.7 %collective-permute-done.21 = bf16[128,1024]{1,0:T(8,128)(2,1)S(1)} collective-permute-done((bf16[128,1024]{1,0:T(8,128)(2,1)S(1)}, bf16[128,1024]{1,0:T(8,128)(2,1)S(1)}, u32[]{:S(2)}, u32[]{:S(2)}) %collective-permute-start.21) | collective-permute-done | bytes 262176 | tf_op jit(solution)/shard_map/ppermute | solution.py:413
  132.8 7.1 %collective-permute-done.22.low_across = bf16[128,1024]{1,0:T(8,128)(2,1)S(1)} collective-permute-done((bf16[128,1024]{1,0:T(8,128)(2,1)S(1)}, bf16[128,1024]{1,0:T(8,128)(2,1)S(1)}, u32[]{:S(2)}, u32[]{:S(2)}) %collective-permute-start.22) | collective-permute-done | bytes 262176 | tf_op jit(solution)/shard_map/ppermute | solution.py:413
  141.9 7.6 %attention_backward.1 = (bf16[512,768]{1,0:T(8,128)(2,1)S(1)}, bf16[384,1024]{1,0:T(8,128)(2,1)S(1)}, bf16[256,1024]{1,0:T(8,128)(2,1)S(1)}, bf16[128,1024]{1,0:T(8,128)(2,1)S(1)}, bf16[256,1024]{1,0:T(8,128)(2,1)S(1)}) custom-call(s32[2]{0:T(128)S(1)} %pad_add_fusion.place, f32[512,128]{1,0:T(8,128)S(1)} %get-tuple-element.258.cosine, ...), custom_call_target="tpu_custom_call" | custom-call | flops 1677721600 | bytes 8126472 | tf_op jit(solution)/shard_map/attention_backward/pallas_call | solution.py:713
  149.4 4.5 %collective-permute-done.24 = bf16[256,2176]{1,0:T(8,128)(2,1)S(1)} collective-permute-done((bf16[256,2176]{1,0:T(8,128)(2,1)S(1)}, bf16[256,2176]{1,0:T(8,128)(2,1)S(1)}, u32[]{:S(2)}, u32[]{:S(2)}) %collective-permute-start.24) | collective-permute-done | bytes 1114144 | tf_op jit(solution)/shard_map/ppermute | solution.py:422
  160.2 18.5 %collective-permute-done.28 = bf16[256,1024]{1,0:T(8,128)(2,1)S(1)} collective-permute-done((bf16[256,1024]{1,0:T(8,128)(2,1)S(1)}, bf16[256,1024]{1,0:T(8,128)(2,1)S(1)}, u32[]{:S(2)}, u32[]{:S(2)}) %collective-permute-start.28) | collective-permute-done | bytes 524320 | tf_op jit(solution)/shard_map/ppermute | solution.py:422
  181.3 3.3 %collective-permute-start.33 = (bf16[128,1024]{1,0:T(8,128)(2,1)S(1)}, bf16[128,1024]{1,0:T(8,128)(2,1)S(1)}, u32[]{:S(2)}, u32[]{:S(2)}) collective-permute-start(bf16[128,1024]{1,0:T(8,128)(2,1)S(1)} %add_convert_fusion.7), channel_id=1, source_target_pairs={{0,24},{4,28},{8,0},{12,4},{16,8},{20,12},{24,16},{28,20},{1,25},{... | collective-permute-start | bytes 786440 | tf_op jit(solution)/shard_map/ppermute | solution.py:426
  187.1 14.6 %collective-permute-done.33 = bf16[128,1024]{1,0:T(8,128)(2,1)S(1)} collective-permute-done((bf16[128,1024]{1,0:T(8,128)(2,1)S(1)}, bf16[128,1024]{1,0:T(8,128)(2,1)S(1)}, u32[]{:S(2)}, u32[]{:S(2)}) %collective-permute-start.33) | collective-permute-done | bytes 262176 | tf_op jit(solution)/shard_map/ppermute | solution.py:426
  203.6 3.6 %all-to-all-start.2 = ((bf16[4,32,2176]{2,1,0:T(8,128)(2,1)}), bf16[4,32,2176]{2,1,0:T(8,128)(2,1)S(1)}, u32[]{:S(2)}, u32[]{:S(2)}) async-start(bf16[4,32,2176]{2,1,0:T(8,128)(2,1)} %bitcast.22), calls=%async_computation.2 | async-start | bytes 1114112 | tf_op jit(solution)/shard_map/all_to_all | solution.py:418
  209.6 1.9 collective-permute-start.34
  211.5 6.5 %collective-permute-done.35 = bf16[128,1024]{1,0:T(8,128)(2,1)} collective-permute-done((bf16[128,1024]{1,0:T(8,128)(2,1)}, bf16[128,1024]{1,0:T(8,128)(2,1)}, u32[]{:S(2)}, u32[]{:S(2)}) %collective-permute-start.35) | collective-permute-done | bytes 262176 | tf_op jit(solution)/shard_map/ppermute | solution.py:422
  221.3 4.8 %all-to-all-start.3 = ((bf16[4,32,768]{2,1,0:T(8,128)(2,1)}), bf16[4,32,768]{2,1,0:T(8,128)(2,1)S(1)}, u32[]{:S(2)}, u32[]{:S(2)}) async-start(bf16[4,32,768]{2,1,0:T(8,128)(2,1)} %bitcast.11), calls=%async_computation.3 | async-start | bytes 393216 | tf_op jit(solution)/shard_map/all_to_all | solution.py:418
  226.0 3.6 %unpack_rest.1 = (f32[32,5248]{1,0:T(8,128)}, f32[32,1]{1,0:T(8,128)S(1)}, f32[32,2624]{1,0:T(8,128)}) custom-call(bf16[128,2176]{1,0:T(8,128)(2,1)S(1)} %bitcast.19, bf16[32,5248]{1,0:T(8,128)(2,1)S(1)} %copy-done, f32[32,1]{1,0:T(8,128)S(1)} %copy.31.gain), custom_call_target="tpu_custom_call" | custom-call | flops 671744 | bytes 1900800 | tf_op jit(solution)/shard_map/unpack_rest/pallas_call | solution.py:713
  (220 shorter events, 61.8 us)
Async XLA Ops:
  4.3 9.9 %all-to-all-start = ((bf16[4,32,896]{2,1,0:T(8,128)(2,1)}), bf16[4,32,896]{2,1,0:T(8,128)(2,1)S(1)}, u32[]{:S(2)}, u32[]{:S(2)}) async-start(bf16[4,32,896]{2,1,0:T(8,128)(2,1)} %bitcast), calls=%async_computation | async-start | bytes 458752 | tf_op jit(solution)/shard_map/all_to_all | solution.py:418
  14.3 23.3 %all-to-all-start.1 = ((bf16[4,32,2176]{2,1,0:T(8,128)(2,1)}), bf16[4,32,2176]{2,1,0:T(8,128)(2,1)}, u32[]{:S(2)}, u32[]{:S(2)}) async-start(bf16[4,32,2176]{2,1,0:T(8,128)(2,1)} %bitcast.3), calls=%async_computation.1 | async-start | bytes 1114112 | tf_op jit(solution)/shard_map/all_to_all | solution.py:418
  21.5 12.9 %collective-permute-start.1 = (bf16[128,1024]{1,0:T(8,128)(2,1)S(1)}, bf16[128,1024]{1,0:T(8,128)(2,1)S(1)}, u32[]{:S(2)}, u32[]{:S(2)}) collective-permute-start(bf16[128,1024]{1,0:T(8,128)(2,1)S(1)} %maximum_maximum_fusion.own), channel_id=1, source_target_pairs={{0,8},{4,12},{8,16},{12,20},{16,24},{20,28},{24,0},{28,4},{1,9},{5... | collective-permute-start | bytes 786440 | tf_op jit(solution)/shard_map/ppermute | solution.py:422
  22.5 15.0 %collective-permute-start.2 = (bf16[128,1024]{1,0:T(8,128)(2,1)S(1)}, bf16[128,1024]{1,0:T(8,128)(2,1)S(1)}, u32[]{:S(2)}, u32[]{:S(2)}) collective-permute-start(bf16[128,1024]{1,0:T(8,128)(2,1)S(1)} %maximum_maximum_fusion.own), channel_id=1, source_target_pairs={{0,24},{4,28},{8,0},{12,4},{16,8},{20,12},{24,16},{28,20},{1,25},{... | collective-permute-start | bytes 786440 | tf_op jit(solution)/shard_map/ppermute | solution.py:426
  27.2 10.3 %collective-permute-start.3 = (bf16[128,1024]{1,0:T(8,128)(2,1)S(1)}, bf16[128,1024]{1,0:T(8,128)(2,1)S(1)}, u32[]{:S(2)}, u32[]{:S(2)}) collective-permute-start(bf16[128,1024]{1,0:T(8,128)(2,1)S(1)} %maximum_maximum_fusion.own), channel_id=1, source_target_pairs={{0,4},{4,0},{8,12},{12,8},{16,20},{20,16},{24,28},{28,24},{1,5},{5... | collective-permute-start | bytes 786440 | tf_op jit(solution)/shard_map/ppermute | solution.py:430
  37.6 13.6 %collective-permute-start.5 = (bf16[256,1024]{1,0:T(8,128)(2,1)S(1)}, bf16[256,1024]{1,0:T(8,128)(2,1)S(1)}, u32[]{:S(2)}, u32[]{:S(2)}) collective-permute-start(bf16[256,1024]{1,0:T(8,128)(2,1)S(1)} %pad_maximum_fusion.3), channel_id=1, source_target_pairs={{0,4},{4,0},{8,12},{12,8},{16,20},{20,16},{24,28},{28,24},{1,5},{5... | collective-permute-start | bytes 1572872 | tf_op jit(solution)/shard_map/ppermute | solution.py:430
  38.5 13.6 %collective-permute-start.6 = (bf16[256,1024]{1,0:T(8,128)(2,1)S(1)}, bf16[256,1024]{1,0:T(8,128)(2,1)S(1)}, u32[]{:S(2)}, u32[]{:S(2)}) collective-permute-start(bf16[256,1024]{1,0:T(8,128)(2,1)S(1)} %pad_maximum_fusion.2.mine), channel_id=1, source_target_pairs={{0,2},{1,3},{2,0},{3,1},{4,6},{5,7},{6,4},{7,5},{8,10},{9,11},{10,... | collective-permute-start | bytes 1572872 | tf_op jit(solution)/shard_map/ppermute | solution.py:413
  40.1 11.1 %collective-permute-start.4 = (bf16[128,1024]{1,0:T(8,128)(2,1)S(1)}, bf16[128,1024]{1,0:T(8,128)(2,1)S(1)}, u32[]{:S(2)}, u32[]{:S(2)}) collective-permute-start(bf16[128,1024]{1,0:T(8,128)(2,1)S(1)} %collective-permute-done.1.third), channel_id=1, source_target_pairs={{0,8},{4,12},{8,16},{12,20},{16,24},{20,28},{24,0},{28,4},{1,9},{5... | collective-permute-start | bytes 786440 | tf_op jit(solution)/shard_map/ppermute | solution.py:422
  42.2 18.6 %collective-permute-start.9 = (bf16[128,2176]{1,0:T(8,128)(2,1)}, bf16[128,2176]{1,0:T(8,128)(2,1)S(1)}, u32[]{:S(2)}, u32[]{:S(2)}) collective-permute-start(bf16[128,2176]{1,0:T(8,128)(2,1)} %bitcast.4.own), channel_id=1, source_target_pairs={{0,8},{4,12},{8,16},{12,20},{16,24},{20,28},{24,0},{28,4},{1,9},{5... | collective-permute-start | bytes 1671176 | tf_op jit(solution)/shard_map/ppermute | solution.py:422
  53.1 13.5 %collective-permute-start.7 = (bf16[512,1024]{1,0:T(8,128)(2,1)}, bf16[512,1024]{1,0:T(8,128)(2,1)S(1)}, u32[]{:S(2)}, u32[]{:S(2)}) collective-permute-start(bf16[512,1024]{1,0:T(8,128)(2,1)} %pad_maximum_fusion), channel_id=1, source_target_pairs={{0,1},{1,0},{2,3},{3,2},{4,5},{5,4},{6,7},{7,6},{8,9},{9,8},{10,11... | collective-permute-start | bytes 3145736 | tf_op jit(solution)/shard_map/ppermute | solution.py:413
  60.8 13.2 %collective-permute-start.10 = (bf16[128,2176]{1,0:T(8,128)(2,1)}, bf16[128,2176]{1,0:T(8,128)(2,1)}, u32[]{:S(2)}, u32[]{:S(2)}) collective-permute-start(bf16[128,2176]{1,0:T(8,128)(2,1)} %bitcast.4.own), channel_id=1, source_target_pairs={{0,24},{4,28},{8,0},{12,4},{16,8},{20,12},{24,16},{28,20},{1,25},{... | collective-permute-start | bytes 1671176 | tf_op jit(solution)/shard_map/ppermute | solution.py:426
  63.3 13.9 %collective-permute-start.11 = (bf16[128,2176]{1,0:T(8,128)(2,1)}, bf16[128,2176]{1,0:T(8,128)(2,1)}, u32[]{:S(2)}, u32[]{:S(2)}) collective-permute-start(bf16[128,2176]{1,0:T(8,128)(2,1)} %bitcast.4.own), channel_id=1, source_target_pairs={{0,4},{4,0},{8,12},{12,8},{16,20},{20,16},{24,28},{28,24},{1,5},{5... | collective-permute-start | bytes 1671176 | tf_op jit(solution)/shard_map/ppermute | solution.py:430
  80.2 14.5 %collective-permute-start.17 = (bf16[128,2176]{1,0:T(8,128)(2,1)S(1)}, bf16[128,2176]{1,0:T(8,128)(2,1)S(1)}, u32[]{:S(2)}, u32[]{:S(2)}) collective-permute-start(bf16[128,2176]{1,0:T(8,128)(2,1)S(1)} %copy-done.11), channel_id=1, source_target_pairs={{0,4},{4,0},{8,12},{12,8},{16,20},{20,16},{24,28},{28,24},{1,5},{5... | collective-permute-start | bytes 1671176 | tf_op jit(solution)/shard_map/ppermute | solution.py:430
  81.3 16.6 %collective-permute-start.16 = (bf16[128,2176]{1,0:T(8,128)(2,1)S(1)}, bf16[128,2176]{1,0:T(8,128)(2,1)S(1)}, u32[]{:S(2)}, u32[]{:S(2)}) collective-permute-start(bf16[128,2176]{1,0:T(8,128)(2,1)S(1)} %copy-done.11), channel_id=1, source_target_pairs={{0,8},{4,12},{8,16},{12,20},{16,24},{20,28},{24,0},{28,4},{1,9},{5... | collective-permute-start | bytes 1671176 | tf_op jit(solution)/shard_map/ppermute | solution.py:422
  88.7 10.7 %collective-permute-start.14 = (bf16[128,1024]{1,0:T(8,128)(2,1)S(1)}, bf16[128,1024]{1,0:T(8,128)(2,1)S(1)}, u32[]{:S(2)}, u32[]{:S(2)}) collective-permute-start(bf16[128,1024]{1,0:T(8,128)(2,1)S(1)} %fusion.12.norm_own), channel_id=1, source_target_pairs={{0,2},{1,3},{2,0},{3,1},{4,6},{5,7},{6,4},{7,5},{8,10},{9,11},{10,... | collective-permute-start | bytes 786440 | tf_op jit(solution)/shard_map/ppermute | solution.py:413
  94.7 13.7 %collective-permute-start.18 = (bf16[128,2176]{1,0:T(8,128)(2,1)}, bf16[128,2176]{1,0:T(8,128)(2,1)S(1)}, u32[]{:S(2)}, u32[]{:S(2)}) collective-permute-start(bf16[128,2176]{1,0:T(8,128)(2,1)} %collective-permute-done.10.first), channel_id=1, source_target_pairs={{0,4},{4,0},{8,12},{12,8},{16,20},{20,16},{24,28},{28,24},{1,5},{5... | collective-permute-start | bytes 1671176 | tf_op jit(solution)/shard_map/ppermute | solution.py:430
  97.9 15.3 %collective-permute-start.19 = (bf16[128,2176]{1,0:T(8,128)(2,1)S(1)}, bf16[128,2176]{1,0:T(8,128)(2,1)S(1)}, u32[]{:S(2)}, u32[]{:S(2)}) collective-permute-start(bf16[128,2176]{1,0:T(8,128)(2,1)S(1)} %collective-permute-done.17.other_third), channel_id=1, source_target_pairs={{0,8},{4,12},{8,16},{12,20},{16,24},{20,28},{24,0},{28,4},{1,9},{5... | collective-permute-start | bytes 1671176 | tf_op jit(solution)/shard_map/ppermute | solution.py:422
  99.5 13.7 %collective-permute-start.15 = (bf16[256,1024]{1,0:T(8,128)(2,1)S(1)}, bf16[256,1024]{1,0:T(8,128)(2,1)S(1)}, u32[]{:S(2)}, u32[]{:S(2)}) collective-permute-start(bf16[256,1024]{1,0:T(8,128)(2,1)S(1)} %pad_maximum_fusion.4), channel_id=1, source_target_pairs={{0,1},{1,0},{2,3},{3,2},{4,5},{5,4},{6,7},{7,6},{8,9},{9,8},{10,11... | collective-permute-start | bytes 1572872 | tf_op jit(solution)/shard_map/ppermute | solution.py:413
  125.8 28.2 %collective-permute-start.24 = (bf16[256,2176]{1,0:T(8,128)(2,1)S(1)}, bf16[256,2176]{1,0:T(8,128)(2,1)S(1)}, u32[]{:S(2)}, u32[]{:S(2)}) collective-permute-start(bf16[256,2176]{1,0:T(8,128)(2,1)S(1)} %get-tuple-element.120), channel_id=1, source_target_pairs={{0,8},{4,12},{8,16},{12,20},{16,24},{20,28},{24,0},{28,4},{1,9},{5... | collective-permute-start | bytes 3342344 | tf_op jit(solution)/shard_map/ppermute | solution.py:422
  125.8 28.1 %collective-permute-start.25 = (bf16[256,2176]{1,0:T(8,128)(2,1)S(1)}, bf16[256,2176]{1,0:T(8,128)(2,1)S(1)}, u32[]{:S(2)}, u32[]{:S(2)}) collective-permute-start(bf16[256,2176]{1,0:T(8,128)(2,1)S(1)} %get-tuple-element.121), channel_id=1, source_target_pairs={{0,4},{4,0},{8,12},{12,8},{16,20},{20,16},{24,28},{28,24},{1,5},{5... | collective-permute-start | bytes 3342344 | tf_op jit(solution)/shard_map/ppermute | solution.py:430
  154.1 26.2 %collective-permute-start.27 = (bf16[128,2176]{1,0:T(8,128)(2,1)S(1)}, bf16[128,2176]{1,0:T(8,128)(2,1)S(1)}, u32[]{:S(2)}, u32[]{:S(2)}) collective-permute-start(bf16[128,2176]{1,0:T(8,128)(2,1)S(1)} %add_convert_fusion.2), channel_id=1, source_target_pairs={{0,24},{4,28},{8,0},{12,4},{16,8},{20,12},{24,16},{28,20},{1,25},{... | collective-permute-start | bytes 1671176 | tf_op jit(solution)/shard_map/ppermute | solution.py:426
  156.0 24.2 %collective-permute-start.26 = (bf16[128,2176]{1,0:T(8,128)(2,1)S(1)}, bf16[128,2176]{1,0:T(8,128)(2,1)S(1)}, u32[]{:S(2)}, u32[]{:S(2)}) collective-permute-start(bf16[128,2176]{1,0:T(8,128)(2,1)S(1)} %add_convert_fusion.3), channel_id=1, source_target_pairs={{0,4},{4,0},{8,12},{12,8},{16,20},{20,16},{24,28},{28,24},{1,5},{5... | collective-permute-start | bytes 1671176 | tf_op jit(solution)/shard_map/ppermute | solution.py:430
  157.4 21.3 %collective-permute-start.28 = (bf16[256,1024]{1,0:T(8,128)(2,1)S(1)}, bf16[256,1024]{1,0:T(8,128)(2,1)S(1)}, u32[]{:S(2)}, u32[]{:S(2)}) collective-permute-start(bf16[256,1024]{1,0:T(8,128)(2,1)S(1)} %get-tuple-element.125), channel_id=1, source_target_pairs={{0,8},{4,12},{8,16},{12,20},{16,24},{20,28},{24,0},{28,4},{1,9},{5... | collective-permute-start | bytes 1572872 | tf_op jit(solution)/shard_map/ppermute | solution.py:422
  157.7 22.6 %collective-permute-start.29 = (bf16[256,1024]{1,0:T(8,128)(2,1)S(1)}, bf16[256,1024]{1,0:T(8,128)(2,1)S(1)}, u32[]{:S(2)}, u32[]{:S(2)}) collective-permute-start(bf16[256,1024]{1,0:T(8,128)(2,1)S(1)} %get-tuple-element.126), channel_id=1, source_target_pairs={{0,4},{4,0},{8,12},{12,8},{16,20},{20,16},{24,28},{28,24},{1,5},{5... | collective-permute-start | bytes 1572872 | tf_op jit(solution)/shard_map/ppermute | solution.py:430
  180.5 21.2 %collective-permute-start.31 = (bf16[128,2176]{1,0:T(8,128)(2,1)S(1)}, bf16[128,2176]{1,0:T(8,128)(2,1)S(1)}, u32[]{:S(2)}, u32[]{:S(2)}) collective-permute-start(bf16[128,2176]{1,0:T(8,128)(2,1)S(1)} %add_convert_fusion.1), channel_id=1, source_target_pairs={{0,8},{4,12},{8,16},{12,20},{16,24},{20,28},{24,0},{28,4},{1,9},{5... | collective-permute-start | bytes 1671176 | tf_op jit(solution)/shard_map/ppermute | solution.py:422
  181.3 20.4 %collective-permute-start.33 = (bf16[128,1024]{1,0:T(8,128)(2,1)S(1)}, bf16[128,1024]{1,0:T(8,128)(2,1)S(1)}, u32[]{:S(2)}, u32[]{:S(2)}) collective-permute-start(bf16[128,1024]{1,0:T(8,128)(2,1)S(1)} %add_convert_fusion.7), channel_id=1, source_target_pairs={{0,24},{4,28},{8,0},{12,4},{16,8},{20,12},{24,16},{28,20},{1,25},{... | collective-permute-start | bytes 786440 | tf_op jit(solution)/shard_map/ppermute | solution.py:426
  184.6 17.1 %collective-permute-start.32 = (bf16[128,1024]{1,0:T(8,128)(2,1)S(1)}, bf16[128,1024]{1,0:T(8,128)(2,1)S(1)}, u32[]{:S(2)}, u32[]{:S(2)}) collective-permute-start(bf16[128,1024]{1,0:T(8,128)(2,1)S(1)} %add_convert_fusion.8), channel_id=1, source_target_pairs={{0,4},{4,0},{8,12},{12,8},{16,20},{20,16},{24,28},{28,24},{1,5},{5... | collective-permute-start | bytes 786440 | tf_op jit(solution)/shard_map/ppermute | solution.py:430
  203.6 14.4 %all-to-all-start.2 = ((bf16[4,32,2176]{2,1,0:T(8,128)(2,1)}), bf16[4,32,2176]{2,1,0:T(8,128)(2,1)S(1)}, u32[]{:S(2)}, u32[]{:S(2)}) async-start(bf16[4,32,2176]{2,1,0:T(8,128)(2,1)} %bitcast.22), calls=%async_computation.2 | async-start | bytes 1114112 | tf_op jit(solution)/shard_map/all_to_all | solution.py:418
  207.2 10.8 %collective-permute-start.35 = (bf16[128,1024]{1,0:T(8,128)(2,1)}, bf16[128,1024]{1,0:T(8,128)(2,1)}, u32[]{:S(2)}, u32[]{:S(2)}) collective-permute-start(bf16[128,1024]{1,0:T(8,128)(2,1)} %add_convert_fusion.6), channel_id=1, source_target_pairs={{0,8},{4,12},{8,16},{12,20},{16,24},{20,28},{24,0},{28,4},{1,9},{5... | collective-permute-start | bytes 786440 | tf_op jit(solution)/shard_map/ppermute | solution.py:422
  209.6 21.4 %collective-permute-start.34 = (bf16[256,1024]{1,0:T(8,128)(2,1)}, bf16[256,1024]{1,0:T(8,128)(2,1)}, u32[]{:S(2)}, u32[]{:S(2)}) collective-permute-start(bf16[256,1024]{1,0:T(8,128)(2,1)} %add_convert_fusion.4), channel_id=1, source_target_pairs={{0,2},{1,3},{2,0},{3,1},{4,6},{5,7},{6,4},{7,5},{8,10},{9,11},{10,... | collective-permute-start | bytes 1572872 | tf_op jit(solution)/shard_map/ppermute | solution.py:413
  219.2 11.0 %collective-permute-start.36 = (bf16[32,1024]{1,0:T(8,128)(2,1)S(1)}, bf16[32,1024]{1,0:T(8,128)(2,1)S(1)}, u32[]{:S(2)}, u32[]{:S(2)}) collective-permute-start(bf16[32,1024]{1,0:T(8,128)(2,1)S(1)} %pad_maximum_fusion.8), channel_id=1, source_target_pairs={{0,0},{4,1},{8,2},{12,3},{16,4},{20,5},{24,6},{28,7},{1,8},{5,9},{... | collective-permute-start | bytes 196616 | tf_op jit(solution)/shard_map/ppermute | solution.py:906
  221.3 12.3 %all-to-all-start.3 = ((bf16[4,32,768]{2,1,0:T(8,128)(2,1)}), bf16[4,32,768]{2,1,0:T(8,128)(2,1)S(1)}, u32[]{:S(2)}, u32[]{:S(2)}) async-start(bf16[4,32,768]{2,1,0:T(8,128)(2,1)} %bitcast.11), calls=%async_computation.3 | async-start | bytes 393216 | tf_op jit(solution)/shard_map/all_to_all | solution.py:418
  (35 other events, 223.4 us)

commit v10 on v9

--- a/solution.py
+++ b/solution.py
@@ -696,10 +696,12 @@
 
 def unpack_qkv(back, w_qkv, gain, grad, gain_grad):
     size, part = w_qkv.shape[0], 256
+    edge = back.shape[1] - 3 * part
     total = jnp.zeros(gain_grad.shape, jnp.float32)
     for k in range(4):
         for third in range(3):
-            piece = wide(back[size * k : size * (k + 1), part * third : part * (third + 1)])
+            source = slice(edge + part * third, edge + part * (third + 1))
+            piece = wide(back[size * k : size * (k + 1), source])
             lanes = slice(part * (4 * third + k), part * (4 * third + k + 1))
             grad[:, lanes] = piece * gain[...]
             total += jnp.sum(piece * wide(w_qkv[:, lanes]), axis=1, keepdims=True)
@@ -891,20 +893,16 @@
     g_down = down(low(wide(g_kept[1]) + wide(g_far[0])))
     kept, sent = scatter_last(send, keep)
     io_up = up(low(wide(io_kept[0]) + wide(io_pair[0]) + wide(io_near)))
-    io_up, g_near, g_down, sent = tie(io_up, g_near, g_down, sent)
-    sum_io, g_turned = tie(
-        low(wide(io_kept[2]) + wide(io_far[1]) + wide(io_down) + wide(io_up)),
-        low(wide(g_kept[0]) + wide(g_pair[0]) + wide(g_near)),
-    )
-    g_up = up(g_turned)
+    g_near, sent = tie(g_near, sent)
+    g_up = up(low(wide(g_kept[0]) + wide(g_pair[0]) + wide(g_near)))
     last_across = swap(sent, 2)
-    back = rep_exchange(sum_io)
-    back, g_up = tie(back, g_up)
+    io_up, g_up, g_down = tie(io_up, g_up, g_down)
+    sum_io = low(wide(io_kept[2]) + wide(io_far[1]) + wide(io_down) + wide(io_up))
     sum_g = low(wide(g_kept[2]) + wide(g_far[1]) + wide(g_down) + wide(g_up))
-    back_qkv = rep_exchange(sum_g[:, :768])
+    back = rep_exchange(columns([sum_io, sum_g[:, :768]]))
     grad_w_attn_out = wide(
         lax.ppermute(
-            columns(split_rows(tie(sum_g, back)[0][:, 768:], 4)),
+            columns(split_rows(sum_g[:, 768:], 4)),
             AXES,
             [(there, here) for here, there in order],
         )
@@ -919,7 +917,7 @@
         unpack_qkv,
         [(w_qkv.shape, f32), (gain_attn.shape, f32)],
         (4 * w_qkv.size, 0),
-        back_qkv, w_qkv, gain_attn,
+        back, w_qkv, gain_attn,
     )
     last = kept + wide(last_across)
 

time: 238 us -> 236 us (level)
  waiting for transfers between devices: 114 us -> 119 us
  starting transfers between devices: 61.3 us -> 56.9 us
    ppermute x4, waiting for transfers between devices: 18.1 us -> 7.26 us  [down(): return lax.ppermute(value, 'fsdp', [(k, (k - 2) % 8) for k in range(8)])]
    all_to_all x4 -> x3, waiting for transfers between devices: 1.32 us -> 9.98 us  [rep_exchange(): return lax.all_to_all(blocks, 'rep', 0, 0, tiled=True).reshape(value.shape)]
    all_to_all x4 -> x3, starting transfers between devices: 19.8 us -> 16.1 us  [rep_exchange(): return lax.all_to_all(blocks, 'rep', 0, 0, tiled=True).reshape(value.shape)]
    ppermute x9, waiting for transfers between devices: 57.1 us -> 60.7 us  [up(): return lax.ppermute(value, 'fsdp', [(k, (k + 2) % 8) for k in range(8)])]
    ppermute x10, waiting for transfers between devices: 18.6 us -> 21.5 us  [over(): return lax.ppermute(value, 'fsdp', [(k, k ^ 1) for k in range(8)])]
    unnamed x52 -> x74, local copies, waits for them, and re-layouts: 3.47 us -> 4.94 us
    convert_element_type x16 -> x15, other arithmetic: 8 us -> 8.59 us  [low(): return value.astype(jnp.bfloat16)]
  transfers between devices with their start and end apart: 41 -> 40, of which waited for: 22 -> 25; matrix products, arithmetic and copies ran while one was open for 8% -> 7% of each run, Pallas kernels for 10% -> 9%
where the time goes in v10:
time: 236 us
  waiting for transfers between devices  119 us (50%)
  starting transfers between devices  56.9 us (24%)
  Pallas kernels  31.9 us (14%)
  other arithmetic  20.9 us (9%)
  local copies, waits for them, and re-layouts  6.09 us (3%)
    ppermute x9, waiting for transfers between devices, up(): return lax.ppermute(value, 'fsdp', [(k, (k + 2) % 8) for k in range(8)])  60.7 us
    pallas_call x7, Pallas kernels, kernel(): pl.pallas_call(body, out_shape=shapes, in_specs=[pl.BlockSpec(memory_spac...  31.9 us
    ppermute x10, waiting for transfers between devices, over(): return lax.ppermute(value, 'fsdp', [(k, k ^ 1) for k in range(8)])  21.5 us
    ppermute x12, waiting for transfers between devices, swap(): return lax.ppermute(value, 'rep', [(k, k ^ distance) for k in range(4)])  19.1 us
    all_to_all x3, starting transfers between devices, rep_exchange(): return lax.all_to_all(blocks, 'rep', 0, 0, tiled=True).reshape(value.shape)  16.1 us
    ppermute x4, starting transfers between devices, down(): return lax.ppermute(value, 'fsdp', [(k, (k - 2) % 8) for k in range(8)])  11.5 us
    ppermute x10, starting transfers between devices, over(): return lax.ppermute(value, 'fsdp', [(k, k ^ 1) for k in range(8)])  10.8 us
    ppermute x9, starting transfers between devices, up(): return lax.ppermute(value, 'fsdp', [(k, (k + 2) % 8) for k in range(8)])  10.8 us
  transfers between devices with their start and end apart: 40, of which 25 were waited for; matrix products, arithmetic and copies ran while one was open for 7% of the time, Pallas kernels for 9%

profile of v10, /device:TPU:0, one launch (start us, length us, event | category | flops | bytes accessed | tf_op | source)
XLA Modules:
  0.0 235.9 jit_solution(17679800966782878101)
XLA Ops:
  3.8 4.2 %all-to-all-start = ((bf16[4,32,896]{2,1,0:T(8,128)(2,1)}), bf16[4,32,896]{2,1,0:T(8,128)(2,1)S(1)}, u32[]{:S(2)}, u32[]{:S(2)}) async-start(bf16[4,32,896]{2,1,0:T(8,128)(2,1)} %bitcast), calls=%async_computation | async-start | bytes 458752 | tf_op jit(solution)/shard_map/all_to_all | solution.py:418
  13.8 7.2 %all-to-all-start.1 = ((bf16[4,32,2176]{2,1,0:T(8,128)(2,1)}), bf16[4,32,2176]{2,1,0:T(8,128)(2,1)}, u32[]{:S(2)}, u32[]{:S(2)}) async-start(bf16[4,32,2176]{2,1,0:T(8,128)(2,1)} %bitcast.3), calls=%async_computation.1 | async-start | bytes 1114112 | tf_op jit(solution)/shard_map/all_to_all | solution.py:418
  22.0 4.7 %collective-permute-start.2 = (bf16[128,1024]{1,0:T(8,128)(2,1)S(1)}, bf16[128,1024]{1,0:T(8,128)(2,1)S(1)}, u32[]{:S(2)}, u32[]{:S(2)}) collective-permute-start(bf16[128,1024]{1,0:T(8,128)(2,1)S(1)} %maximum_maximum_fusion.own), channel_id=1, source_target_pairs={{0,24},{4,28},{8,0},{12,4},{16,8},{20,12},{24,16},{28,20},{1,25},{... | collective-permute-start | bytes 786440 | tf_op jit(solution)/shard_map/ppermute | solution.py:426
  27.0 6.9 %collective-permute-done.1.third = bf16[128,1024]{1,0:T(8,128)(2,1)S(1)} collective-permute-done((bf16[128,1024]{1,0:T(8,128)(2,1)S(1)}, bf16[128,1024]{1,0:T(8,128)(2,1)S(1)}, u32[]{:S(2)}, u32[]{:S(2)}) %collective-permute-start.1) | collective-permute-done | bytes 262176 | tf_op jit(solution)/shard_map/ppermute | solution.py:422
  33.9 3.2 %collective-permute-done.2.first = bf16[128,1024]{1,0:T(8,128)(2,1)S(1)} collective-permute-done((bf16[128,1024]{1,0:T(8,128)(2,1)S(1)}, bf16[128,1024]{1,0:T(8,128)(2,1)S(1)}, u32[]{:S(2)}, u32[]{:S(2)}) %collective-permute-start.2) | collective-permute-done | bytes 262176 | tf_op jit(solution)/shard_map/ppermute | solution.py:426
  39.6 2.0 collective-permute-start.4
  42.3 8.4 %collective-permute-done.4.second = bf16[128,1024]{1,0:T(8,128)(2,1)S(1)} collective-permute-done((bf16[128,1024]{1,0:T(8,128)(2,1)S(1)}, bf16[128,1024]{1,0:T(8,128)(2,1)S(1)}, u32[]{:S(2)}, u32[]{:S(2)}) %collective-permute-start.4) | collective-permute-done | bytes 262176 | tf_op jit(solution)/shard_map/ppermute | solution.py:422
  55.0 5.3 %collective-permute-done.9.third = bf16[128,2176]{1,0:T(8,128)(2,1)S(1)} collective-permute-done((bf16[128,2176]{1,0:T(8,128)(2,1)}, bf16[128,2176]{1,0:T(8,128)(2,1)S(1)}, u32[]{:S(2)}, u32[]{:S(2)}) %collective-permute-start.9) | collective-permute-done | bytes 557088 | tf_op jit(solution)/shard_map/ppermute | solution.py:422
  66.2 7.0 %attention_forward.1 = (bf16[512,1024]{1,0:T(8,128)(2,1)S(1)}, bf16[1024,768]{1,0:T(8,128)(2,1)S(1)}, bf16[256,1024]{1,0:T(8,128)(2,1)S(1)}, bf16[512,256]{1,0:T...) custom-call(s32[2]{0:T(128)S(1)} %pad_add_fusion.place, ...), custom_call_target="tpu_custom_call" | custom-call | flops 1207959552 | bytes 11014152 | tf_op jit(solution)/shard_map/attention_forward/pallas_call | solution.py:715
  73.5 3.1 %collective-permute-done.11.other = bf16[128,2176]{1,0:T(8,128)(2,1)} collective-permute-done((bf16[128,2176]{1,0:T(8,128)(2,1)}, bf16[128,2176]{1,0:T(8,128)(2,1)}, u32[]{:S(2)}, u32[]{:S(2)}) %collective-permute-start.11) | collective-permute-done | bytes 557088 | tf_op jit(solution)/shard_map/ppermute | solution.py:430
  80.7 3.8 %collective-permute-start.16 = (bf16[128,2176]{1,0:T(8,128)(2,1)S(1)}, bf16[128,2176]{1,0:T(8,128)(2,1)S(1)}, u32[]{:S(2)}, u32[]{:S(2)}) collective-permute-start(bf16[128,2176]{1,0:T(8,128)(2,1)S(1)} %copy-done.15), channel_id=1, source_target_pairs={{0,8},{4,12},{8,16},{12,20},{16,24},{20,28},{24,0},{28,4},{1,9},{5... | collective-permute-start | bytes 1671176 | tf_op jit(solution)/shard_map/ppermute | solution.py:422
  84.5 2.5 %collective-permute-done.13 = bf16[128,1024]{1,0:T(8,128)(2,1)S(1)} collective-permute-done((bf16[128,1024]{1,0:T(8,128)(2,1)S(1)}, bf16[128,1024]{1,0:T(8,128)(2,1)S(1)}, u32[]{:S(2)}, u32[]{:S(2)}) %collective-permute-start.13) | collective-permute-done | bytes 262176 | tf_op jit(solution)/shard_map/ppermute | solution.py:413
  88.7 5.5 %collective-permute-done.17.other_third = bf16[128,2176]{1,0:T(8,128)(2,1)S(1)} collective-permute-done((bf16[128,2176]{1,0:T(8,128)(2,1)S(1)}, bf16[128,2176]{1,0:T(8,128)(2,1)S(1)}, u32[]{:S(2)}, u32[]{:S(2)}) %collective-permute-start.17) | collective-permute-done | bytes 557088 | tf_op jit(solution)/shard_map/ppermute | solution.py:430
  95.1 2.2 collective-permute-done.16.second
  99.0 8.9 %collective-permute-done.18.other_first = bf16[128,2176]{1,0:T(8,128)(2,1)S(1)} collective-permute-done((bf16[128,2176]{1,0:T(8,128)(2,1)}, bf16[128,2176]{1,0:T(8,128)(2,1)S(1)}, u32[]{:S(2)}, u32[]{:S(2)}) %collective-permute-start.18) | collective-permute-done | bytes 557088 | tf_op jit(solution)/shard_map/ppermute | solution.py:430
  107.9 4.8 %collective-permute-done.19.other_second = bf16[128,2176]{1,0:T(8,128)(2,1)S(1)} collective-permute-done((bf16[128,2176]{1,0:T(8,128)(2,1)S(1)}, bf16[128,2176]{1,0:T(8,128)(2,1)S(1)}, u32[]{:S(2)}, u32[]{:S(2)}) %collective-permute-start.19) | collective-permute-done | bytes 557088 | tf_op jit(solution)/shard_map/ppermute | solution.py:422
  112.7 7.3 %mlp.1 = (bf16[512,1024]{1,0:T(8,128)(2,1)S(1)}, bf16[512,1024]{1,0:T(8,128)(2,1)S(1)}, bf16[512,768]{1,0:T(8,128)(2,1)S(1)}, bf16[512,1408]{1,0:T(8,128)(2,1)S(...) custom-call(s32[512,1]{1,0:T(8,128)S(1)} %copy.28.seg_col, ...), custom_call_target="tpu_custom_call" | custom-call | flops 3758096384 | bytes 14551040 | tf_op jit(solution)/shard_map/mlp/pallas_call | solution.py:715
  122.6 2.7 %mlp_terms.1 = (bf16[384,2176]{1,0:T(8,128)(2,1)S(1)}, bf16[256,2176]{1,0:T(8,128)(2,1)S(1)}, bf16[128,2176]{1,0:T(8,128)(2,1)S(1)}, bf16[256,2176]{1,0:T(8,128)(2,1)S(1)}) custom-call(bf16[512,1024]{1,0:T(8,128)(2,1)S(1)} %get-tuple-element.99.normed, bf16[512,1408]{1,0:T(8,128)(2,1)S(1)} %get-tuple-element.100.grad_inner, ...), custom_call_target="tpu_custom_call" | custom-call | flops 2281701376 | bytes 8781824 | tf_op jit(solution)/shard_map/mlp_terms/pallas_call | solution.py:715
  126.7 3.7 %collective-permute-done.21 = bf16[128,1024]{1,0:T(8,128)(2,1)S(1)} collective-permute-done((bf16[128,1024]{1,0:T(8,128)(2,1)S(1)}, bf16[128,1024]{1,0:T(8,128)(2,1)S(1)}, u32[]{:S(2)}, u32[]{:S(2)}) %collective-permute-start.21) | collective-permute-done | bytes 262176 | tf_op jit(solution)/shard_map/ppermute | solution.py:413
  132.3 7.1 %collective-permute-done.22.low_across = bf16[128,1024]{1,0:T(8,128)(2,1)S(1)} collective-permute-done((bf16[128,1024]{1,0:T(8,128)(2,1)S(1)}, bf16[128,1024]{1,0:T(8,128)(2,1)S(1)}, u32[]{:S(2)}, u32[]{:S(2)}) %collective-permute-start.22) | collective-permute-done | bytes 262176 | tf_op jit(solution)/shard_map/ppermute | solution.py:413
  141.3 7.6 %attention_backward.1 = (bf16[512,768]{1,0:T(8,128)(2,1)S(1)}, bf16[384,1024]{1,0:T(8,128)(2,1)S(1)}, bf16[256,1024]{1,0:T(8,128)(2,1)S(1)}, bf16[128,1024]{1,0:T(8,128)(2,1)S(1)}, bf16[256,1024]{1,0:T(8,128)(2,1)S(1)}) custom-call(s32[2]{0:T(128)S(1)} %pad_add_fusion.place, f32[512,128]{1,0:T(8,128)S(1)} %get-tuple-element.252.cosine, ...), custom_call_target="tpu_custom_call" | custom-call | flops 1677721600 | bytes 8126472 | tf_op jit(solution)/shard_map/attention_backward/pallas_call | solution.py:715
  148.9 4.5 %collective-permute-done.24 = bf16[256,2176]{1,0:T(8,128)(2,1)S(1)} collective-permute-done((bf16[256,2176]{1,0:T(8,128)(2,1)S(1)}, bf16[256,2176]{1,0:T(8,128)(2,1)S(1)}, u32[]{:S(2)}, u32[]{:S(2)}) %collective-permute-start.24) | collective-permute-done | bytes 1114144 | tf_op jit(solution)/shard_map/ppermute | solution.py:422
  157.9 2.8 %projections.1 = (bf16[512,1024]{1,0:T(8,128)(2,1)}, bf16[512,1024]{1,0:T(8,128)(2,1)S(1)}) custom-call(bf16[512,768]{1,0:T(8,128)(2,1)S(1)} %get-tuple-element.111.grad_packed, bf16[1024,768]{1,0:T(8,128)(2,1)S(1)} %get-tuple-element.112.qkv, bf16[512,768]{1,0:T(8,128)(2,1)S(1)} %get-tuple-element.101.mixed, bf16[1024,768]{1,0:T(8,128)(2,1)S(1)} %get-tuple-element.113.w_down), custom_call_target="tpu_custom_call" | custom-call | flops 1610612736 | bytes 6815744 | tf_op jit(solution)/shard_map/projections/pallas_call | solution.py:715
  161.7 16.4 %collective-permute-done.28 = bf16[256,1024]{1,0:T(8,128)(2,1)S(1)} collective-permute-done((bf16[256,1024]{1,0:T(8,128)(2,1)S(1)}, bf16[256,1024]{1,0:T(8,128)(2,1)S(1)}, u32[]{:S(2)}, u32[]{:S(2)}) %collective-permute-start.28) | collective-permute-done | bytes 524320 | tf_op jit(solution)/shard_map/ppermute | solution.py:422
  187.6 2.4 collective-permute-done.31
  190.9 3.2 %collective-permute-start.35 = (bf16[128,1024]{1,0:T(8,128)(2,1)S(1)}, bf16[128,1024]{1,0:T(8,128)(2,1)S(1)}, u32[]{:S(2)}, u32[]{:S(2)}) collective-permute-start(bf16[128,1024]{1,0:T(8,128)(2,1)S(1)} %get-tuple-element.190), channel_id=1, source_target_pairs={{0,24},{4,28},{8,0},{12,4},{16,8},{20,12},{24,16},{28,20},{1,25},{... | collective-permute-start | bytes 786440 | tf_op jit(solution)/shard_map/ppermute | solution.py:426
  195.8 6.8 %collective-permute-done.33 = bf16[128,2176]{1,0:T(8,128)(2,1)S(1)} collective-permute-done((bf16[128,2176]{1,0:T(8,128)(2,1)S(1)}, bf16[128,2176]{1,0:T(8,128)(2,1)S(1)}, u32[]{:S(2)}, u32[]{:S(2)}) %collective-permute-start.33) | collective-permute-done | bytes 557088 | tf_op jit(solution)/shard_map/ppermute | solution.py:422
  202.5 5.5 %collective-permute-done.34 = bf16[128,1024]{1,0:T(8,128)(2,1)S(1)} collective-permute-done((bf16[128,1024]{1,0:T(8,128)(2,1)S(1)}, bf16[128,1024]{1,0:T(8,128)(2,1)S(1)}, u32[]{:S(2)}, u32[]{:S(2)}) %collective-permute-start.34) | collective-permute-done | bytes 262176 | tf_op jit(solution)/shard_map/ppermute | solution.py:422
  208.0 3.7 %collective-permute-done.35 = bf16[128,1024]{1,0:T(8,128)(2,1)S(1)} collective-permute-done((bf16[128,1024]{1,0:T(8,128)(2,1)S(1)}, bf16[128,1024]{1,0:T(8,128)(2,1)S(1)}, u32[]{:S(2)}, u32[]{:S(2)}) %collective-permute-start.35) | collective-permute-done | bytes 262176 | tf_op jit(solution)/shard_map/ppermute | solution.py:426
  213.9 4.7 %all-to-all-start.2 = ((bf16[4,32,2944]{2,1,0:T(8,128)(2,1)}), bf16[4,32,2944]{2,1,0:T(8,128)(2,1)S(1)}, u32[]{:S(2)}, u32[]{:S(2)}) async-start(bf16[4,32,2944]{2,1,0:T(8,128)(2,1)} %bitcast.9), calls=%async_computation.2 | async-start | bytes 1507328 | tf_op jit(solution)/shard_map/all_to_all | solution.py:418
  222.0 8.1 %all-to-all-done.2 = bf16[4,32,2944]{2,1,0:T(8,128)(2,1)S(1)} async-done(((bf16[4,32,2944]{2,1,0:T(8,128)(2,1)}), bf16[4,32,2944]{2,1,0:T(8,128)(2,1)S(1)}, u32[]{:S(2)}, u32[]{:S(2)}) %all-to-all-start.2) | async-done | bytes 753696 | tf_op jit(solution)/shard_map/all_to_all | solution.py:418
  230.1 3.6 %unpack_rest.1 = (f32[32,5248]{1,0:T(8,128)}, f32[32,1]{1,0:T(8,128)S(1)}, f32[32,2624]{1,0:T(8,128)}) custom-call(bf16[128,2944]{1,0:T(8,128)(2,1)S(1)} %bitcast.17, bf16[32,5248]{1,0:T(8,128)(2,1)S(1)} %copy-done, f32[32,1]{1,0:T(8,128)S(1)} %copy.31.gain), custom_call_target="tpu_custom_call" | custom-call | flops 671744 | bytes 2097408 | tf_op jit(solution)/shard_map/unpack_rest/pallas_call | solution.py:715
  (240 shorter events, 64.6 us)
Async XLA Ops:
  3.8 9.9 %all-to-all-start = ((bf16[4,32,896]{2,1,0:T(8,128)(2,1)}), bf16[4,32,896]{2,1,0:T(8,128)(2,1)S(1)}, u32[]{:S(2)}, u32[]{:S(2)}) async-start(bf16[4,32,896]{2,1,0:T(8,128)(2,1)} %bitcast), calls=%async_computation | async-start | bytes 458752 | tf_op jit(solution)/shard_map/all_to_all | solution.py:418
  13.8 23.3 %all-to-all-start.1 = ((bf16[4,32,2176]{2,1,0:T(8,128)(2,1)}), bf16[4,32,2176]{2,1,0:T(8,128)(2,1)}, u32[]{:S(2)}, u32[]{:S(2)}) async-start(bf16[4,32,2176]{2,1,0:T(8,128)(2,1)} %bitcast.3), calls=%async_computation.1 | async-start | bytes 1114112 | tf_op jit(solution)/shard_map/all_to_all | solution.py:418
  21.0 12.9 %collective-permute-start.1 = (bf16[128,1024]{1,0:T(8,128)(2,1)S(1)}, bf16[128,1024]{1,0:T(8,128)(2,1)S(1)}, u32[]{:S(2)}, u32[]{:S(2)}) collective-permute-start(bf16[128,1024]{1,0:T(8,128)(2,1)S(1)} %maximum_maximum_fusion.own), channel_id=1, source_target_pairs={{0,8},{4,12},{8,16},{12,20},{16,24},{20,28},{24,0},{28,4},{1,9},{5... | collective-permute-start | bytes 786440 | tf_op jit(solution)/shard_map/ppermute | solution.py:422
  22.0 15.0 %collective-permute-start.2 = (bf16[128,1024]{1,0:T(8,128)(2,1)S(1)}, bf16[128,1024]{1,0:T(8,128)(2,1)S(1)}, u32[]{:S(2)}, u32[]{:S(2)}) collective-permute-start(bf16[128,1024]{1,0:T(8,128)(2,1)S(1)} %maximum_maximum_fusion.own), channel_id=1, source_target_pairs={{0,24},{4,28},{8,0},{12,4},{16,8},{20,12},{24,16},{28,20},{1,25},{... | collective-permute-start | bytes 786440 | tf_op jit(solution)/shard_map/ppermute | solution.py:426
  26.7 10.3 %collective-permute-start.3 = (bf16[128,1024]{1,0:T(8,128)(2,1)S(1)}, bf16[128,1024]{1,0:T(8,128)(2,1)S(1)}, u32[]{:S(2)}, u32[]{:S(2)}) collective-permute-start(bf16[128,1024]{1,0:T(8,128)(2,1)S(1)} %maximum_maximum_fusion.own), channel_id=1, source_target_pairs={{0,4},{4,0},{8,12},{12,8},{16,20},{20,16},{24,28},{28,24},{1,5},{5... | collective-permute-start | bytes 786440 | tf_op jit(solution)/shard_map/ppermute | solution.py:430
  37.1 13.6 %collective-permute-start.5 = (bf16[256,1024]{1,0:T(8,128)(2,1)S(1)}, bf16[256,1024]{1,0:T(8,128)(2,1)S(1)}, u32[]{:S(2)}, u32[]{:S(2)}) collective-permute-start(bf16[256,1024]{1,0:T(8,128)(2,1)S(1)} %pad_maximum_fusion.4), channel_id=1, source_target_pairs={{0,4},{4,0},{8,12},{12,8},{16,20},{20,16},{24,28},{28,24},{1,5},{5... | collective-permute-start | bytes 1572872 | tf_op jit(solution)/shard_map/ppermute | solution.py:430
  37.9 13.6 %collective-permute-start.6 = (bf16[256,1024]{1,0:T(8,128)(2,1)S(1)}, bf16[256,1024]{1,0:T(8,128)(2,1)S(1)}, u32[]{:S(2)}, u32[]{:S(2)}) collective-permute-start(bf16[256,1024]{1,0:T(8,128)(2,1)S(1)} %pad_maximum_fusion.3.mine), channel_id=1, source_target_pairs={{0,2},{1,3},{2,0},{3,1},{4,6},{5,7},{6,4},{7,5},{8,10},{9,11},{10,... | collective-permute-start | bytes 1572872 | tf_op jit(solution)/shard_map/ppermute | solution.py:413
  39.6 11.1 %collective-permute-start.4 = (bf16[128,1024]{1,0:T(8,128)(2,1)S(1)}, bf16[128,1024]{1,0:T(8,128)(2,1)S(1)}, u32[]{:S(2)}, u32[]{:S(2)}) collective-permute-start(bf16[128,1024]{1,0:T(8,128)(2,1)S(1)} %collective-permute-done.1.third), channel_id=1, source_target_pairs={{0,8},{4,12},{8,16},{12,20},{16,24},{20,28},{24,0},{28,4},{1,9},{5... | collective-permute-start | bytes 786440 | tf_op jit(solution)/shard_map/ppermute | solution.py:422
  41.7 18.6 %collective-permute-start.9 = (bf16[128,2176]{1,0:T(8,128)(2,1)}, bf16[128,2176]{1,0:T(8,128)(2,1)S(1)}, u32[]{:S(2)}, u32[]{:S(2)}) collective-permute-start(bf16[128,2176]{1,0:T(8,128)(2,1)} %bitcast.4.own), channel_id=1, source_target_pairs={{0,8},{4,12},{8,16},{12,20},{16,24},{20,28},{24,0},{28,4},{1,9},{5... | collective-permute-start | bytes 1671176 | tf_op jit(solution)/shard_map/ppermute | solution.py:422
  52.6 13.5 %collective-permute-start.7 = (bf16[512,1024]{1,0:T(8,128)(2,1)}, bf16[512,1024]{1,0:T(8,128)(2,1)S(1)}, u32[]{:S(2)}, u32[]{:S(2)}) collective-permute-start(bf16[512,1024]{1,0:T(8,128)(2,1)} %pad_maximum_fusion), channel_id=1, source_target_pairs={{0,1},{1,0},{2,3},{3,2},{4,5},{5,4},{6,7},{7,6},{8,9},{9,8},{10,11... | collective-permute-start | bytes 3145736 | tf_op jit(solution)/shard_map/ppermute | solution.py:413
  52.6 9.4 %collective-permute-start.8 = (bf16[128,1024]{1,0:T(8,128)(2,1)S(1)}, bf16[128,1024]{1,0:T(8,128)(2,1)S(1)}, u32[]{:S(2)}, u32[]{:S(2)}) collective-permute-start(bf16[128,1024]{1,0:T(8,128)(2,1)S(1)} %collective-permute-done.4.second), channel_id=1, source_target_pairs={{0,4},{4,0},{8,12},{12,8},{16,20},{20,16},{24,28},{28,24},{1,5},{5... | collective-permute-start | bytes 786440 | tf_op jit(solution)/shard_map/ppermute | solution.py:430
  60.3 13.2 %collective-permute-start.10 = (bf16[128,2176]{1,0:T(8,128)(2,1)}, bf16[128,2176]{1,0:T(8,128)(2,1)}, u32[]{:S(2)}, u32[]{:S(2)}) collective-permute-start(bf16[128,2176]{1,0:T(8,128)(2,1)} %bitcast.4.own), channel_id=1, source_target_pairs={{0,24},{4,28},{8,0},{12,4},{16,8},{20,12},{24,16},{28,20},{1,25},{... | collective-permute-start | bytes 1671176 | tf_op jit(solution)/shard_map/ppermute | solution.py:426
  62.7 13.9 %collective-permute-start.11 = (bf16[128,2176]{1,0:T(8,128)(2,1)}, bf16[128,2176]{1,0:T(8,128)(2,1)}, u32[]{:S(2)}, u32[]{:S(2)}) collective-permute-start(bf16[128,2176]{1,0:T(8,128)(2,1)} %bitcast.4.own), channel_id=1, source_target_pairs={{0,4},{4,0},{8,12},{12,8},{16,20},{20,16},{24,28},{28,24},{1,5},{5... | collective-permute-start | bytes 1671176 | tf_op jit(solution)/shard_map/ppermute | solution.py:430
  78.6 8.4 %collective-permute-start.13 = (bf16[128,1024]{1,0:T(8,128)(2,1)S(1)}, bf16[128,1024]{1,0:T(8,128)(2,1)S(1)}, u32[]{:S(2)}, u32[]{:S(2)}) collective-permute-start(bf16[128,1024]{1,0:T(8,128)(2,1)S(1)} %add_convert_fusion.10), channel_id=1, source_target_pairs={{0,2},{1,3},{2,0},{3,1},{4,6},{5,7},{6,4},{7,5},{8,10},{9,11},{10,... | collective-permute-start | bytes 786440 | tf_op jit(solution)/shard_map/ppermute | solution.py:413
  79.7 14.5 %collective-permute-start.17 = (bf16[128,2176]{1,0:T(8,128)(2,1)S(1)}, bf16[128,2176]{1,0:T(8,128)(2,1)S(1)}, u32[]{:S(2)}, u32[]{:S(2)}) collective-permute-start(bf16[128,2176]{1,0:T(8,128)(2,1)S(1)} %copy-done.15), channel_id=1, source_target_pairs={{0,4},{4,0},{8,12},{12,8},{16,20},{20,16},{24,28},{28,24},{1,5},{5... | collective-permute-start | bytes 1671176 | tf_op jit(solution)/shard_map/ppermute | solution.py:430
  80.7 16.6 %collective-permute-start.16 = (bf16[128,2176]{1,0:T(8,128)(2,1)S(1)}, bf16[128,2176]{1,0:T(8,128)(2,1)S(1)}, u32[]{:S(2)}, u32[]{:S(2)}) collective-permute-start(bf16[128,2176]{1,0:T(8,128)(2,1)S(1)} %copy-done.15), channel_id=1, source_target_pairs={{0,8},{4,12},{8,16},{12,20},{16,24},{20,28},{24,0},{28,4},{1,9},{5... | collective-permute-start | bytes 1671176 | tf_op jit(solution)/shard_map/ppermute | solution.py:422
  87.7 11.2 %collective-permute-start.14 = (bf16[128,1024]{1,0:T(8,128)(2,1)S(1)}, bf16[128,1024]{1,0:T(8,128)(2,1)S(1)}, u32[]{:S(2)}, u32[]{:S(2)}) collective-permute-start(bf16[128,1024]{1,0:T(8,128)(2,1)S(1)} %fusion.12.norm_own), channel_id=1, source_target_pairs={{0,2},{1,3},{2,0},{3,1},{4,6},{5,7},{6,4},{7,5},{8,10},{9,11},{10,... | collective-permute-start | bytes 786440 | tf_op jit(solution)/shard_map/ppermute | solution.py:413
  94.2 13.7 %collective-permute-start.18 = (bf16[128,2176]{1,0:T(8,128)(2,1)}, bf16[128,2176]{1,0:T(8,128)(2,1)S(1)}, u32[]{:S(2)}, u32[]{:S(2)}) collective-permute-start(bf16[128,2176]{1,0:T(8,128)(2,1)} %collective-permute-done.10.first), channel_id=1, source_target_pairs={{0,4},{4,0},{8,12},{12,8},{16,20},{20,16},{24,28},{28,24},{1,5},{5... | collective-permute-start | bytes 1671176 | tf_op jit(solution)/shard_map/ppermute | solution.py:430
  97.4 15.3 %collective-permute-start.19 = (bf16[128,2176]{1,0:T(8,128)(2,1)S(1)}, bf16[128,2176]{1,0:T(8,128)(2,1)S(1)}, u32[]{:S(2)}, u32[]{:S(2)}) collective-permute-start(bf16[128,2176]{1,0:T(8,128)(2,1)S(1)} %collective-permute-done.17.other_third), channel_id=1, source_target_pairs={{0,8},{4,12},{8,16},{12,20},{16,24},{20,28},{24,0},{28,4},{1,9},{5... | collective-permute-start | bytes 1671176 | tf_op jit(solution)/shard_map/ppermute | solution.py:422
  99.0 13.7 %collective-permute-start.15 = (bf16[256,1024]{1,0:T(8,128)(2,1)S(1)}, bf16[256,1024]{1,0:T(8,128)(2,1)S(1)}, u32[]{:S(2)}, u32[]{:S(2)}) collective-permute-start(bf16[256,1024]{1,0:T(8,128)(2,1)S(1)} %pad_maximum_fusion.5), channel_id=1, source_target_pairs={{0,1},{1,0},{2,3},{3,2},{4,5},{5,4},{6,7},{7,6},{8,9},{9,8},{10,11... | collective-permute-start | bytes 1572872 | tf_op jit(solution)/shard_map/ppermute | solution.py:413
  122.0 8.4 %collective-permute-start.21 = (bf16[128,1024]{1,0:T(8,128)(2,1)S(1)}, bf16[128,1024]{1,0:T(8,128)(2,1)S(1)}, u32[]{:S(2)}, u32[]{:S(2)}) collective-permute-start(bf16[128,1024]{1,0:T(8,128)(2,1)S(1)} %add_convert_fusion.9), channel_id=1, source_target_pairs={{0,2},{1,3},{2,0},{3,1},{4,6},{5,7},{6,4},{7,5},{8,10},{9,11},{10,... | collective-permute-start | bytes 786440 | tf_op jit(solution)/shard_map/ppermute | solution.py:413
  125.3 28.2 %collective-permute-start.24 = (bf16[256,2176]{1,0:T(8,128)(2,1)S(1)}, bf16[256,2176]{1,0:T(8,128)(2,1)S(1)}, u32[]{:S(2)}, u32[]{:S(2)}) collective-permute-start(bf16[256,2176]{1,0:T(8,128)(2,1)S(1)} %get-tuple-element.116), channel_id=1, source_target_pairs={{0,8},{4,12},{8,16},{12,20},{16,24},{20,28},{24,0},{28,4},{1,9},{5... | collective-permute-start | bytes 3342344 | tf_op jit(solution)/shard_map/ppermute | solution.py:422
  125.3 28.1 %collective-permute-start.25 = (bf16[256,2176]{1,0:T(8,128)(2,1)S(1)}, bf16[256,2176]{1,0:T(8,128)(2,1)S(1)}, u32[]{:S(2)}, u32[]{:S(2)}) collective-permute-start(bf16[256,2176]{1,0:T(8,128)(2,1)S(1)} %get-tuple-element.117), channel_id=1, source_target_pairs={{0,4},{4,0},{8,12},{12,8},{16,20},{20,16},{24,28},{28,24},{1,5},{5... | collective-permute-start | bytes 3342344 | tf_op jit(solution)/shard_map/ppermute | solution.py:430
  153.6 26.2 %collective-permute-start.27 = (bf16[128,2176]{1,0:T(8,128)(2,1)S(1)}, bf16[128,2176]{1,0:T(8,128)(2,1)S(1)}, u32[]{:S(2)}, u32[]{:S(2)}) collective-permute-start(bf16[128,2176]{1,0:T(8,128)(2,1)S(1)} %add_convert_fusion.2), channel_id=1, source_target_pairs={{0,24},{4,28},{8,0},{12,4},{16,8},{20,12},{24,16},{28,20},{1,25},{... | collective-permute-start | bytes 1671176 | tf_op jit(solution)/shard_map/ppermute | solution.py:426
  155.5 24.2 %collective-permute-start.26 = (bf16[128,2176]{1,0:T(8,128)(2,1)S(1)}, bf16[128,2176]{1,0:T(8,128)(2,1)S(1)}, u32[]{:S(2)}, u32[]{:S(2)}) collective-permute-start(bf16[128,2176]{1,0:T(8,128)(2,1)S(1)} %add_convert_fusion.3), channel_id=1, source_target_pairs={{0,4},{4,0},{8,12},{12,8},{16,20},{20,16},{24,28},{28,24},{1,5},{5... | collective-permute-start | bytes 1671176 | tf_op jit(solution)/shard_map/ppermute | solution.py:430
  156.9 21.2 %collective-permute-start.28 = (bf16[256,1024]{1,0:T(8,128)(2,1)S(1)}, bf16[256,1024]{1,0:T(8,128)(2,1)S(1)}, u32[]{:S(2)}, u32[]{:S(2)}) collective-permute-start(bf16[256,1024]{1,0:T(8,128)(2,1)S(1)} %get-tuple-element.121), channel_id=1, source_target_pairs={{0,8},{4,12},{8,16},{12,20},{16,24},{20,28},{24,0},{28,4},{1,9},{5... | collective-permute-start | bytes 1572872 | tf_op jit(solution)/shard_map/ppermute | solution.py:422
  157.2 22.6 %collective-permute-start.29 = (bf16[256,1024]{1,0:T(8,128)(2,1)S(1)}, bf16[256,1024]{1,0:T(8,128)(2,1)S(1)}, u32[]{:S(2)}, u32[]{:S(2)}) collective-permute-start(bf16[256,1024]{1,0:T(8,128)(2,1)S(1)} %get-tuple-element.122), channel_id=1, source_target_pairs={{0,4},{4,0},{8,12},{12,8},{16,20},{20,16},{24,28},{28,24},{1,5},{5... | collective-permute-start | bytes 1572872 | tf_op jit(solution)/shard_map/ppermute | solution.py:430
  184.9 17.6 %collective-permute-start.33 = (bf16[128,2176]{1,0:T(8,128)(2,1)S(1)}, bf16[128,2176]{1,0:T(8,128)(2,1)S(1)}, u32[]{:S(2)}, u32[]{:S(2)}) collective-permute-start(bf16[128,2176]{1,0:T(8,128)(2,1)S(1)} %add_convert_fusion.1), channel_id=1, source_target_pairs={{0,8},{4,12},{8,16},{12,20},{16,24},{20,28},{24,0},{28,4},{1,9},{5... | collective-permute-start | bytes 1671176 | tf_op jit(solution)/shard_map/ppermute | solution.py:422
  190.2 17.8 %collective-permute-start.34 = (bf16[128,1024]{1,0:T(8,128)(2,1)S(1)}, bf16[128,1024]{1,0:T(8,128)(2,1)S(1)}, u32[]{:S(2)}, u32[]{:S(2)}) collective-permute-start(bf16[128,1024]{1,0:T(8,128)(2,1)S(1)} %get-tuple-element.191), channel_id=1, source_target_pairs={{0,8},{4,12},{8,16},{12,20},{16,24},{20,28},{24,0},{28,4},{1,9},{5... | collective-permute-start | bytes 786440 | tf_op jit(solution)/shard_map/ppermute | solution.py:422
  190.9 20.8 %collective-permute-start.35 = (bf16[128,1024]{1,0:T(8,128)(2,1)S(1)}, bf16[128,1024]{1,0:T(8,128)(2,1)S(1)}, u32[]{:S(2)}, u32[]{:S(2)}) collective-permute-start(bf16[128,1024]{1,0:T(8,128)(2,1)S(1)} %get-tuple-element.190), channel_id=1, source_target_pairs={{0,24},{4,28},{8,0},{12,4},{16,8},{20,12},{24,16},{28,20},{1,25},{... | collective-permute-start | bytes 786440 | tf_op jit(solution)/shard_map/ppermute | solution.py:426
  194.1 25.2 %collective-permute-start.32 = (bf16[256,1024]{1,0:T(8,128)(2,1)}, bf16[256,1024]{1,0:T(8,128)(2,1)}, u32[]{:S(2)}, u32[]{:S(2)}) collective-permute-start(bf16[256,1024]{1,0:T(8,128)(2,1)} %add_convert_fusion.4), channel_id=1, source_target_pairs={{0,2},{1,3},{2,0},{3,1},{4,6},{5,7},{6,4},{7,5},{8,10},{9,11},{10,... | collective-permute-start | bytes 1572872 | tf_op jit(solution)/shard_map/ppermute | solution.py:413
  213.9 16.2 %all-to-all-start.2 = ((bf16[4,32,2944]{2,1,0:T(8,128)(2,1)}), bf16[4,32,2944]{2,1,0:T(8,128)(2,1)S(1)}, u32[]{:S(2)}, u32[]{:S(2)}) async-start(bf16[4,32,2944]{2,1,0:T(8,128)(2,1)} %bitcast.9), calls=%async_computation.2 | async-start | bytes 1507328 | tf_op jit(solution)/shard_map/all_to_all | solution.py:418
  (45 other events, 279.0 us)

commit v11 on v10

--- a/solution.py
+++ b/solution.py
@@ -677,7 +677,7 @@
     size, hidden, part = w_in.shape[0], w_in.shape[1] // 2, w_in.shape[1] // 8
     main = part // LANES * LANES
     rest, edge = part - main, 2 * main + LANES
-    total = jnp.zeros(gain_grad.shape, jnp.float32)
+    total = jnp.zeros(gain.shape, jnp.float32)
     for k in range(4):
         here = slice(size * k, size * (k + 1))
         for half in range(2):
@@ -691,13 +691,13 @@
                 weights = wide(w_in[:, target : target + count])
                 total += jnp.sum(piece * weights, axis=1, keepdims=True)
         grad_out[:, part * k : part * (k + 1)] = wide(back[here, edge : edge + part])
-    gain_grad[...] = total
+    gain_grad[...] = jnp.broadcast_to(total, (total.shape[0], LANES)).T[:1, :]
 
 
 def unpack_qkv(back, w_qkv, gain, grad, gain_grad):
     size, part = w_qkv.shape[0], 256
     edge = back.shape[1] - 3 * part
-    total = jnp.zeros(gain_grad.shape, jnp.float32)
+    total = jnp.zeros(gain.shape, jnp.float32)
     for k in range(4):
         for third in range(3):
             source = slice(edge + part * third, edge + part * (third + 1))
@@ -705,7 +705,7 @@
             lanes = slice(part * (4 * third + k), part * (4 * third + k + 1))
             grad[:, lanes] = piece * gain[...]
             total += jnp.sum(piece * wide(w_qkv[:, lanes]), axis=1, keepdims=True)
-    gain_grad[...] = total
+    gain_grad[...] = jnp.broadcast_to(total, (total.shape[0], LANES)).T[:1, :]
 
 
 def kernel(body, outs, cost, *args, scratch=(), scalars=0):
@@ -900,35 +900,37 @@
     sum_io = low(wide(io_kept[2]) + wide(io_far[1]) + wide(io_down) + wide(io_up))
     sum_g = low(wide(g_kept[2]) + wide(g_far[1]) + wide(g_down) + wide(g_up))
     back = rep_exchange(columns([sum_io, sum_g[:, :768]]))
+    grad_w_in, gain_in, grad_w_out = kernel(
+        unpack_rest,
+        [(w_in.shape, f32), ((1, w_in.shape[0]), f32), (w_out.shape, f32)],
+        (4 * w_in.size, 0),
+        back, w_in, gain_mlp,
+    )
+    grad_w_qkv, gain_qkv = kernel(
+        unpack_qkv,
+        [(w_qkv.shape, f32), ((1, w_qkv.shape[0]), f32)],
+        (4 * w_qkv.size, 0),
+        back, w_qkv, gain_attn,
+    )
+    last = kept + wide(last_across)
+
+    standard, inverse = norm_statistics(x_own)
+    block_input_gradient = grad_hidden + norm_backward_pass(
+        last[:count], jnp.ones((), f32), standard, inverse
+    )
+    output = low(jnp.where(seg_col[:count] < 8, hidden_sum + last[count:], 0.0))
+    block_input_gradient = absolute(block_input_gradient, z, x)
+    sum_attn, block_input_gradient = tie(sum_g[:, 768:], block_input_gradient)
     grad_w_attn_out = wide(
         lax.ppermute(
-            columns(split_rows(sum_g[:, 768:], 4)),
+            columns(split_rows(sum_attn, 4)),
             AXES,
             [(there, here) for here, there in order],
         )
     )
-    grad_w_in, gain_in, grad_w_out = kernel(
-        unpack_rest,
-        [(w_in.shape, f32), (gain_mlp.shape, f32), (w_out.shape, f32)],
-        (4 * w_in.size, 0),
-        back, w_in, gain_mlp,
-    )
-    grad_w_qkv, gain_qkv = kernel(
-        unpack_qkv,
-        [(w_qkv.shape, f32), (gain_attn.shape, f32)],
-        (4 * w_qkv.size, 0),
-        back, w_qkv, gain_attn,
-    )
-    last = kept + wide(last_across)
-
-    standard, inverse = norm_statistics(x_own)
-    block_input_gradient = grad_hidden + norm_backward_pass(
-        last[:count], jnp.ones((), f32), standard, inverse
-    )
-    output = low(jnp.where(seg_col[:count] < 8, hidden_sum + last[count:], 0.0))
     return (
         absolute(output, z, x),
-        absolute(block_input_gradient, z, x),
+        block_input_gradient,
         gain_qkv.reshape(-1),
         grad_w_qkv,
         grad_w_attn_out,

time: 236 us -> 234 us (level)
    unnamed x74 -> x76, local copies, waits for them, and re-layouts: 4.94 us -> 4.91 us
where the time goes in v11:
time: 234 us; the launch traced here: 233 us
  waiting for transfers between devices  117 us (50%)
  starting transfers between devices  55.8 us (24%)
  Pallas kernels  31.9 us (14%)
  other arithmetic  19.7 us (8%)
  local copies, waits for them, and re-layouts  6.74 us (3%)
    ppermute x9, waiting for transfers between devices, up(): return lax.ppermute(value, 'fsdp', [(k, (k + 2) % 8) for k in range(8)])  60.8 us
    pallas_call x7, Pallas kernels, kernel(): pl.pallas_call(body, out_shape=shapes, in_specs=[pl.BlockSpec(memory_spac...  31.9 us
    ppermute x10, waiting for transfers between devices, over(): return lax.ppermute(value, 'fsdp', [(k, k ^ 1) for k in range(8)])  21.5 us
    ppermute x12, waiting for transfers between devices, swap(): return lax.ppermute(value, 'rep', [(k, k ^ distance) for k in range(4)])  19.1 us
    all_to_all x3, starting transfers between devices, rep_exchange(): return lax.all_to_all(blocks, 'rep', 0, 0, tiled=True).reshape(value.shape)  15 us
    ppermute x4, starting transfers between devices, down(): return lax.ppermute(value, 'fsdp', [(k, (k - 2) % 8) for k in range(8)])  11.5 us
    ppermute x10, starting transfers between devices, over(): return lax.ppermute(value, 'fsdp', [(k, k ^ 1) for k in range(8)])  10.8 us
    ppermute x9, starting transfers between devices, up(): return lax.ppermute(value, 'fsdp', [(k, (k + 2) % 8) for k in range(8)])  10.8 us
  transfers between devices with their start and end apart: 40, of which 25 were waited for; matrix products, arithmetic and copies ran while one was open for 7% of the time, Pallas kernels for 9%

profile of v11, /device:TPU:0, one launch (start us, length us, event | category | flops | bytes accessed | tf_op | source)
XLA Modules:
  0.0 232.6 jit_solution(12762115112711012719)
XLA Ops:
  3.8 4.2 %all-to-all-start = ((bf16[4,32,896]{2,1,0:T(8,128)(2,1)}), bf16[4,32,896]{2,1,0:T(8,128)(2,1)S(1)}, u32[]{:S(2)}, u32[]{:S(2)}) async-start(bf16[4,32,896]{2,1,0:T(8,128)(2,1)} %bitcast), calls=%async_computation | async-start | bytes 458752 | tf_op jit(solution)/shard_map/all_to_all | solution.py:418
  13.8 7.2 %all-to-all-start.1 = ((bf16[4,32,2176]{2,1,0:T(8,128)(2,1)}), bf16[4,32,2176]{2,1,0:T(8,128)(2,1)}, u32[]{:S(2)}, u32[]{:S(2)}) async-start(bf16[4,32,2176]{2,1,0:T(8,128)(2,1)} %bitcast.3), calls=%async_computation.1 | async-start | bytes 1114112 | tf_op jit(solution)/shard_map/all_to_all | solution.py:418
  22.0 4.7 %collective-permute-start.2 = (bf16[128,1024]{1,0:T(8,128)(2,1)S(1)}, bf16[128,1024]{1,0:T(8,128)(2,1)S(1)}, u32[]{:S(2)}, u32[]{:S(2)}) collective-permute-start(bf16[128,1024]{1,0:T(8,128)(2,1)S(1)} %maximum_maximum_fusion.own), channel_id=1, source_target_pairs={{0,24},{4,28},{8,0},{12,4},{16,8},{20,12},{24,16},{28,20},{1,25},{... | collective-permute-start | bytes 786440 | tf_op jit(solution)/shard_map/ppermute | solution.py:426
  27.0 6.9 %collective-permute-done.1.third = bf16[128,1024]{1,0:T(8,128)(2,1)S(1)} collective-permute-done((bf16[128,1024]{1,0:T(8,128)(2,1)S(1)}, bf16[128,1024]{1,0:T(8,128)(2,1)S(1)}, u32[]{:S(2)}, u32[]{:S(2)}) %collective-permute-start.1) | collective-permute-done | bytes 262176 | tf_op jit(solution)/shard_map/ppermute | solution.py:422
  33.9 3.2 %collective-permute-done.2.first = bf16[128,1024]{1,0:T(8,128)(2,1)S(1)} collective-permute-done((bf16[128,1024]{1,0:T(8,128)(2,1)S(1)}, bf16[128,1024]{1,0:T(8,128)(2,1)S(1)}, u32[]{:S(2)}, u32[]{:S(2)}) %collective-permute-start.2) | collective-permute-done | bytes 262176 | tf_op jit(solution)/shard_map/ppermute | solution.py:426
  39.6 2.0 collective-permute-start.4
  42.3 8.4 %collective-permute-done.4.second = bf16[128,1024]{1,0:T(8,128)(2,1)S(1)} collective-permute-done((bf16[128,1024]{1,0:T(8,128)(2,1)S(1)}, bf16[128,1024]{1,0:T(8,128)(2,1)S(1)}, u32[]{:S(2)}, u32[]{:S(2)}) %collective-permute-start.4) | collective-permute-done | bytes 262176 | tf_op jit(solution)/shard_map/ppermute | solution.py:422
  54.9 5.4 %collective-permute-done.9.third = bf16[128,2176]{1,0:T(8,128)(2,1)S(1)} collective-permute-done((bf16[128,2176]{1,0:T(8,128)(2,1)}, bf16[128,2176]{1,0:T(8,128)(2,1)S(1)}, u32[]{:S(2)}, u32[]{:S(2)}) %collective-permute-start.9) | collective-permute-done | bytes 557088 | tf_op jit(solution)/shard_map/ppermute | solution.py:422
  66.2 7.0 %attention_forward.1 = (bf16[512,1024]{1,0:T(8,128)(2,1)S(1)}, bf16[1024,768]{1,0:T(8,128)(2,1)S(1)}, bf16[256,1024]{1,0:T(8,128)(2,1)S(1)}, bf16[512,256]{1,0:T...) custom-call(s32[2]{0:T(128)S(1)} %pad_add_fusion.place, ...), custom_call_target="tpu_custom_call" | custom-call | flops 1207959552 | bytes 11014152 | tf_op jit(solution)/shard_map/attention_forward/pallas_call | solution.py:715
  73.5 3.1 %collective-permute-done.11.other = bf16[128,2176]{1,0:T(8,128)(2,1)} collective-permute-done((bf16[128,2176]{1,0:T(8,128)(2,1)}, bf16[128,2176]{1,0:T(8,128)(2,1)}, u32[]{:S(2)}, u32[]{:S(2)}) %collective-permute-start.11) | collective-permute-done | bytes 557088 | tf_op jit(solution)/shard_map/ppermute | solution.py:430
  80.7 3.8 %collective-permute-start.16 = (bf16[128,2176]{1,0:T(8,128)(2,1)S(1)}, bf16[128,2176]{1,0:T(8,128)(2,1)S(1)}, u32[]{:S(2)}, u32[]{:S(2)}) collective-permute-start(bf16[128,2176]{1,0:T(8,128)(2,1)S(1)} %copy-done.15), channel_id=1, source_target_pairs={{0,8},{4,12},{8,16},{12,20},{16,24},{20,28},{24,0},{28,4},{1,9},{5... | collective-permute-start | bytes 1671176 | tf_op jit(solution)/shard_map/ppermute | solution.py:422
  84.5 2.5 %collective-permute-done.13 = bf16[128,1024]{1,0:T(8,128)(2,1)S(1)} collective-permute-done((bf16[128,1024]{1,0:T(8,128)(2,1)S(1)}, bf16[128,1024]{1,0:T(8,128)(2,1)S(1)}, u32[]{:S(2)}, u32[]{:S(2)}) %collective-permute-start.13) | collective-permute-done | bytes 262176 | tf_op jit(solution)/shard_map/ppermute | solution.py:413
  88.6 5.5 %collective-permute-done.17.other_third = bf16[128,2176]{1,0:T(8,128)(2,1)S(1)} collective-permute-done((bf16[128,2176]{1,0:T(8,128)(2,1)S(1)}, bf16[128,2176]{1,0:T(8,128)(2,1)S(1)}, u32[]{:S(2)}, u32[]{:S(2)}) %collective-permute-start.17) | collective-permute-done | bytes 557088 | tf_op jit(solution)/shard_map/ppermute | solution.py:430
  95.1 2.2 collective-permute-done.16.second
  99.0 8.9 %collective-permute-done.18.other_first = bf16[128,2176]{1,0:T(8,128)(2,1)S(1)} collective-permute-done((bf16[128,2176]{1,0:T(8,128)(2,1)}, bf16[128,2176]{1,0:T(8,128)(2,1)S(1)}, u32[]{:S(2)}, u32[]{:S(2)}) %collective-permute-start.18) | collective-permute-done | bytes 557088 | tf_op jit(solution)/shard_map/ppermute | solution.py:430
  107.9 4.8 %collective-permute-done.19.other_second = bf16[128,2176]{1,0:T(8,128)(2,1)S(1)} collective-permute-done((bf16[128,2176]{1,0:T(8,128)(2,1)S(1)}, bf16[128,2176]{1,0:T(8,128)(2,1)S(1)}, u32[]{:S(2)}, u32[]{:S(2)}) %collective-permute-start.19) | collective-permute-done | bytes 557088 | tf_op jit(solution)/shard_map/ppermute | solution.py:422
  112.7 7.3 %mlp.1 = (bf16[512,1024]{1,0:T(8,128)(2,1)S(1)}, bf16[512,1024]{1,0:T(8,128)(2,1)S(1)}, bf16[512,768]{1,0:T(8,128)(2,1)S(1)}, bf16[512,1408]{1,0:T(8,128)(2,1)S(...) custom-call(s32[512,1]{1,0:T(8,128)S(1)} %copy.28.seg_col, ...), custom_call_target="tpu_custom_call" | custom-call | flops 3758096384 | bytes 14551040 | tf_op jit(solution)/shard_map/mlp/pallas_call | solution.py:715
  122.5 2.7 %mlp_terms.1 = (bf16[384,2176]{1,0:T(8,128)(2,1)S(1)}, bf16[256,2176]{1,0:T(8,128)(2,1)S(1)}, bf16[128,2176]{1,0:T(8,128)(2,1)S(1)}, bf16[256,2176]{1,0:T(8,128)(2,1)S(1)}) custom-call(bf16[512,1024]{1,0:T(8,128)(2,1)S(1)} %get-tuple-element.101.normed, bf16[512,1408]{1,0:T(8,128)(2,1)S(1)} %get-tuple-element.102.grad_inner, ...), custom_call_target="tpu_custom_call" | custom-call | flops 2281701376 | bytes 8781824 | tf_op jit(solution)/shard_map/mlp_terms/pallas_call | solution.py:715
  126.7 3.8 %collective-permute-done.21 = bf16[128,1024]{1,0:T(8,128)(2,1)S(1)} collective-permute-done((bf16[128,1024]{1,0:T(8,128)(2,1)S(1)}, bf16[128,1024]{1,0:T(8,128)(2,1)S(1)}, u32[]{:S(2)}, u32[]{:S(2)}) %collective-permute-start.21) | collective-permute-done | bytes 262176 | tf_op jit(solution)/shard_map/ppermute | solution.py:413
  132.3 7.1 %collective-permute-done.22.low_across = bf16[128,1024]{1,0:T(8,128)(2,1)S(1)} collective-permute-done((bf16[128,1024]{1,0:T(8,128)(2,1)S(1)}, bf16[128,1024]{1,0:T(8,128)(2,1)S(1)}, u32[]{:S(2)}, u32[]{:S(2)}) %collective-permute-start.22) | collective-permute-done | bytes 262176 | tf_op jit(solution)/shard_map/ppermute | solution.py:413
  141.3 7.6 %attention_backward.1 = (bf16[512,768]{1,0:T(8,128)(2,1)S(1)}, bf16[384,1024]{1,0:T(8,128)(2,1)S(1)}, bf16[256,1024]{1,0:T(8,128)(2,1)S(1)}, bf16[128,1024]{1,0:T(8,128)(2,1)S(1)}, bf16[256,1024]{1,0:T(8,128)(2,1)S(1)}) custom-call(s32[2]{0:T(128)S(1)} %pad_add_fusion.place, f32[512,128]{1,0:T(8,128)S(1)} %get-tuple-element.256.cosine, ...), custom_call_target="tpu_custom_call" | custom-call | flops 1677721600 | bytes 8126472 | tf_op jit(solution)/shard_map/attention_backward/pallas_call | solution.py:715
  148.9 4.5 %collective-permute-done.24 = bf16[256,2176]{1,0:T(8,128)(2,1)S(1)} collective-permute-done((bf16[256,2176]{1,0:T(8,128)(2,1)S(1)}, bf16[256,2176]{1,0:T(8,128)(2,1)S(1)}, u32[]{:S(2)}, u32[]{:S(2)}) %collective-permute-start.24) | collective-permute-done | bytes 1114144 | tf_op jit(solution)/shard_map/ppermute | solution.py:422
  157.9 2.8 %projections.1 = (bf16[512,1024]{1,0:T(8,128)(2,1)}, bf16[512,1024]{1,0:T(8,128)(2,1)S(1)}) custom-call(bf16[512,768]{1,0:T(8,128)(2,1)S(1)} %get-tuple-element.113.grad_packed, bf16[1024,768]{1,0:T(8,128)(2,1)S(1)} %get-tuple-element.114.qkv, bf16[512,768]{1,0:T(8,128)(2,1)S(1)} %get-tuple-element.103.mixed, bf16[1024,768]{1,0:T(8,128)(2,1)S(1)} %get-tuple-element.115.w_down), custom_call_target="tpu_custom_call" | custom-call | flops 1610612736 | bytes 6815744 | tf_op jit(solution)/shard_map/projections/pallas_call | solution.py:715
  161.7 16.4 %collective-permute-done.28 = bf16[256,1024]{1,0:T(8,128)(2,1)S(1)} collective-permute-done((bf16[256,1024]{1,0:T(8,128)(2,1)S(1)}, bf16[256,1024]{1,0:T(8,128)(2,1)S(1)}, u32[]{:S(2)}, u32[]{:S(2)}) %collective-permute-start.28) | collective-permute-done | bytes 524320 | tf_op jit(solution)/shard_map/ppermute | solution.py:422
  187.6 2.4 %collective-permute-done.31 = bf16[128,1024]{1,0:T(8,128)(2,1)S(1)} collective-permute-done((bf16[128,1024]{1,0:T(8,128)(2,1)S(1)}, bf16[128,1024]{1,0:T(8,128)(2,1)S(1)}, u32[]{:S(2)}, u32[]{:S(2)}) %collective-permute-start.31) | collective-permute-done | bytes 262176 | tf_op jit(solution)/shard_map/ppermute | solution.py:430
  190.9 3.2 %collective-permute-start.35 = (bf16[128,1024]{1,0:T(8,128)(2,1)S(1)}, bf16[128,1024]{1,0:T(8,128)(2,1)S(1)}, u32[]{:S(2)}, u32[]{:S(2)}) collective-permute-start(bf16[128,1024]{1,0:T(8,128)(2,1)S(1)} %get-tuple-element.194), channel_id=1, source_target_pairs={{0,24},{4,28},{8,0},{12,4},{16,8},{20,12},{24,16},{28,20},{1,25},{... | collective-permute-start | bytes 786440 | tf_op jit(solution)/shard_map/ppermute | solution.py:426
  195.7 6.7 %collective-permute-done.33 = bf16[128,2176]{1,0:T(8,128)(2,1)S(1)} collective-permute-done((bf16[128,2176]{1,0:T(8,128)(2,1)S(1)}, bf16[128,2176]{1,0:T(8,128)(2,1)S(1)}, u32[]{:S(2)}, u32[]{:S(2)}) %collective-permute-start.33) | collective-permute-done | bytes 557088 | tf_op jit(solution)/shard_map/ppermute | solution.py:422
  202.5 5.5 %collective-permute-done.34 = bf16[128,1024]{1,0:T(8,128)(2,1)S(1)} collective-permute-done((bf16[128,1024]{1,0:T(8,128)(2,1)S(1)}, bf16[128,1024]{1,0:T(8,128)(2,1)S(1)}, u32[]{:S(2)}, u32[]{:S(2)}) %collective-permute-start.34) | collective-permute-done | bytes 262176 | tf_op jit(solution)/shard_map/ppermute | solution.py:422
  208.0 3.7 %collective-permute-done.35 = bf16[128,1024]{1,0:T(8,128)(2,1)S(1)} collective-permute-done((bf16[128,1024]{1,0:T(8,128)(2,1)S(1)}, bf16[128,1024]{1,0:T(8,128)(2,1)S(1)}, u32[]{:S(2)}, u32[]{:S(2)}) %collective-permute-start.35) | collective-permute-done | bytes 262176 | tf_op jit(solution)/shard_map/ppermute | solution.py:426
  213.2 3.6 %all-to-all-start.2 = ((bf16[4,32,2944]{2,1,0:T(8,128)(2,1)}), bf16[4,32,2944]{2,1,0:T(8,128)(2,1)S(1)}, u32[]{:S(2)}, u32[]{:S(2)}) async-start(bf16[4,32,2944]{2,1,0:T(8,128)(2,1)} %bitcast.9), calls=%async_computation.2 | async-start | bytes 1507328 | tf_op jit(solution)/shard_map/all_to_all | solution.py:418
  221.6 6.4 %all-to-all-done.2 = bf16[4,32,2944]{2,1,0:T(8,128)(2,1)S(1)} async-done(((bf16[4,32,2944]{2,1,0:T(8,128)(2,1)}), bf16[4,32,2944]{2,1,0:T(8,128)(2,1)S(1)}, u32[]{:S(2)}, u32[]{:S(2)}) %all-to-all-start.2) | async-done | bytes 753696 | tf_op jit(solution)/shard_map/all_to_all | solution.py:418
  228.1 3.6 %unpack_rest.1 = (f32[32,5248]{1,0:T(8,128)}, f32[1,32]{1,0:T(1,128)}, f32[32,2624]{1,0:T(8,128)}) custom-call(bf16[128,2944]{1,0:T(8,128)(2,1)S(1)} %bitcast.19, bf16[32,5248]{1,0:T(8,128)(2,1)S(1)} %copy-done, f32[32,1]{1,0:T(8,128)S(1)} %copy.31.gain), custom_call_target="tpu_custom_call" | custom-call | flops 671744 | bytes 2097408 | tf_op jit(solution)/shard_map/unpack_rest/pallas_call | solution.py:715
  (242 shorter events, 64.1 us)
Async XLA Ops:
  3.8 9.9 %all-to-all-start = ((bf16[4,32,896]{2,1,0:T(8,128)(2,1)}), bf16[4,32,896]{2,1,0:T(8,128)(2,1)S(1)}, u32[]{:S(2)}, u32[]{:S(2)}) async-start(bf16[4,32,896]{2,1,0:T(8,128)(2,1)} %bitcast), calls=%async_computation | async-start | bytes 458752 | tf_op jit(solution)/shard_map/all_to_all | solution.py:418
  13.8 23.3 %all-to-all-start.1 = ((bf16[4,32,2176]{2,1,0:T(8,128)(2,1)}), bf16[4,32,2176]{2,1,0:T(8,128)(2,1)}, u32[]{:S(2)}, u32[]{:S(2)}) async-start(bf16[4,32,2176]{2,1,0:T(8,128)(2,1)} %bitcast.3), calls=%async_computation.1 | async-start | bytes 1114112 | tf_op jit(solution)/shard_map/all_to_all | solution.py:418
  21.0 12.9 %collective-permute-start.1 = (bf16[128,1024]{1,0:T(8,128)(2,1)S(1)}, bf16[128,1024]{1,0:T(8,128)(2,1)S(1)}, u32[]{:S(2)}, u32[]{:S(2)}) collective-permute-start(bf16[128,1024]{1,0:T(8,128)(2,1)S(1)} %maximum_maximum_fusion.own), channel_id=1, source_target_pairs={{0,8},{4,12},{8,16},{12,20},{16,24},{20,28},{24,0},{28,4},{1,9},{5... | collective-permute-start | bytes 786440 | tf_op jit(solution)/shard_map/ppermute | solution.py:422
  22.0 15.0 %collective-permute-start.2 = (bf16[128,1024]{1,0:T(8,128)(2,1)S(1)}, bf16[128,1024]{1,0:T(8,128)(2,1)S(1)}, u32[]{:S(2)}, u32[]{:S(2)}) collective-permute-start(bf16[128,1024]{1,0:T(8,128)(2,1)S(1)} %maximum_maximum_fusion.own), channel_id=1, source_target_pairs={{0,24},{4,28},{8,0},{12,4},{16,8},{20,12},{24,16},{28,20},{1,25},{... | collective-permute-start | bytes 786440 | tf_op jit(solution)/shard_map/ppermute | solution.py:426
  26.7 10.3 %collective-permute-start.3 = (bf16[128,1024]{1,0:T(8,128)(2,1)S(1)}, bf16[128,1024]{1,0:T(8,128)(2,1)S(1)}, u32[]{:S(2)}, u32[]{:S(2)}) collective-permute-start(bf16[128,1024]{1,0:T(8,128)(2,1)S(1)} %maximum_maximum_fusion.own), channel_id=1, source_target_pairs={{0,4},{4,0},{8,12},{12,8},{16,20},{20,16},{24,28},{28,24},{1,5},{5... | collective-permute-start | bytes 786440 | tf_op jit(solution)/shard_map/ppermute | solution.py:430
  37.1 13.6 %collective-permute-start.5 = (bf16[256,1024]{1,0:T(8,128)(2,1)S(1)}, bf16[256,1024]{1,0:T(8,128)(2,1)S(1)}, u32[]{:S(2)}, u32[]{:S(2)}) collective-permute-start(bf16[256,1024]{1,0:T(8,128)(2,1)S(1)} %pad_maximum_fusion.4), channel_id=1, source_target_pairs={{0,4},{4,0},{8,12},{12,8},{16,20},{20,16},{24,28},{28,24},{1,5},{5... | collective-permute-start | bytes 1572872 | tf_op jit(solution)/shard_map/ppermute | solution.py:430
  38.0 13.6 %collective-permute-start.6 = (bf16[256,1024]{1,0:T(8,128)(2,1)S(1)}, bf16[256,1024]{1,0:T(8,128)(2,1)S(1)}, u32[]{:S(2)}, u32[]{:S(2)}) collective-permute-start(bf16[256,1024]{1,0:T(8,128)(2,1)S(1)} %pad_maximum_fusion.3.mine), channel_id=1, source_target_pairs={{0,2},{1,3},{2,0},{3,1},{4,6},{5,7},{6,4},{7,5},{8,10},{9,11},{10,... | collective-permute-start | bytes 1572872 | tf_op jit(solution)/shard_map/ppermute | solution.py:413
  39.6 11.1 %collective-permute-start.4 = (bf16[128,1024]{1,0:T(8,128)(2,1)S(1)}, bf16[128,1024]{1,0:T(8,128)(2,1)S(1)}, u32[]{:S(2)}, u32[]{:S(2)}) collective-permute-start(bf16[128,1024]{1,0:T(8,128)(2,1)S(1)} %collective-permute-done.1.third), channel_id=1, source_target_pairs={{0,8},{4,12},{8,16},{12,20},{16,24},{20,28},{24,0},{28,4},{1,9},{5... | collective-permute-start | bytes 786440 | tf_op jit(solution)/shard_map/ppermute | solution.py:422
  41.7 18.6 %collective-permute-start.9 = (bf16[128,2176]{1,0:T(8,128)(2,1)}, bf16[128,2176]{1,0:T(8,128)(2,1)S(1)}, u32[]{:S(2)}, u32[]{:S(2)}) collective-permute-start(bf16[128,2176]{1,0:T(8,128)(2,1)} %bitcast.4.own), channel_id=1, source_target_pairs={{0,8},{4,12},{8,16},{12,20},{16,24},{20,28},{24,0},{28,4},{1,9},{5... | collective-permute-start | bytes 1671176 | tf_op jit(solution)/shard_map/ppermute | solution.py:422
  52.6 13.5 %collective-permute-start.7 = (bf16[512,1024]{1,0:T(8,128)(2,1)}, bf16[512,1024]{1,0:T(8,128)(2,1)S(1)}, u32[]{:S(2)}, u32[]{:S(2)}) collective-permute-start(bf16[512,1024]{1,0:T(8,128)(2,1)} %pad_maximum_fusion), channel_id=1, source_target_pairs={{0,1},{1,0},{2,3},{3,2},{4,5},{5,4},{6,7},{7,6},{8,9},{9,8},{10,11... | collective-permute-start | bytes 3145736 | tf_op jit(solution)/shard_map/ppermute | solution.py:413
  52.6 9.4 %collective-permute-start.8 = (bf16[128,1024]{1,0:T(8,128)(2,1)S(1)}, bf16[128,1024]{1,0:T(8,128)(2,1)S(1)}, u32[]{:S(2)}, u32[]{:S(2)}) collective-permute-start(bf16[128,1024]{1,0:T(8,128)(2,1)S(1)} %collective-permute-done.4.second), channel_id=1, source_target_pairs={{0,4},{4,0},{8,12},{12,8},{16,20},{20,16},{24,28},{28,24},{1,5},{5... | collective-permute-start | bytes 786440 | tf_op jit(solution)/shard_map/ppermute | solution.py:430
  60.3 13.2 %collective-permute-start.10 = (bf16[128,2176]{1,0:T(8,128)(2,1)}, bf16[128,2176]{1,0:T(8,128)(2,1)}, u32[]{:S(2)}, u32[]{:S(2)}) collective-permute-start(bf16[128,2176]{1,0:T(8,128)(2,1)} %bitcast.4.own), channel_id=1, source_target_pairs={{0,24},{4,28},{8,0},{12,4},{16,8},{20,12},{24,16},{28,20},{1,25},{... | collective-permute-start | bytes 1671176 | tf_op jit(solution)/shard_map/ppermute | solution.py:426
  62.7 13.9 %collective-permute-start.11 = (bf16[128,2176]{1,0:T(8,128)(2,1)}, bf16[128,2176]{1,0:T(8,128)(2,1)}, u32[]{:S(2)}, u32[]{:S(2)}) collective-permute-start(bf16[128,2176]{1,0:T(8,128)(2,1)} %bitcast.4.own), channel_id=1, source_target_pairs={{0,4},{4,0},{8,12},{12,8},{16,20},{20,16},{24,28},{28,24},{1,5},{5... | collective-permute-start | bytes 1671176 | tf_op jit(solution)/shard_map/ppermute | solution.py:430
  78.6 8.4 %collective-permute-start.13 = (bf16[128,1024]{1,0:T(8,128)(2,1)S(1)}, bf16[128,1024]{1,0:T(8,128)(2,1)S(1)}, u32[]{:S(2)}, u32[]{:S(2)}) collective-permute-start(bf16[128,1024]{1,0:T(8,128)(2,1)S(1)} %add_convert_fusion.10), channel_id=1, source_target_pairs={{0,2},{1,3},{2,0},{3,1},{4,6},{5,7},{6,4},{7,5},{8,10},{9,11},{10,... | collective-permute-start | bytes 786440 | tf_op jit(solution)/shard_map/ppermute | solution.py:413
  79.7 14.5 %collective-permute-start.17 = (bf16[128,2176]{1,0:T(8,128)(2,1)S(1)}, bf16[128,2176]{1,0:T(8,128)(2,1)S(1)}, u32[]{:S(2)}, u32[]{:S(2)}) collective-permute-start(bf16[128,2176]{1,0:T(8,128)(2,1)S(1)} %copy-done.15), channel_id=1, source_target_pairs={{0,4},{4,0},{8,12},{12,8},{16,20},{20,16},{24,28},{28,24},{1,5},{5... | collective-permute-start | bytes 1671176 | tf_op jit(solution)/shard_map/ppermute | solution.py:430
  80.7 16.6 %collective-permute-start.16 = (bf16[128,2176]{1,0:T(8,128)(2,1)S(1)}, bf16[128,2176]{1,0:T(8,128)(2,1)S(1)}, u32[]{:S(2)}, u32[]{:S(2)}) collective-permute-start(bf16[128,2176]{1,0:T(8,128)(2,1)S(1)} %copy-done.15), channel_id=1, source_target_pairs={{0,8},{4,12},{8,16},{12,20},{16,24},{20,28},{24,0},{28,4},{1,9},{5... | collective-permute-start | bytes 1671176 | tf_op jit(solution)/shard_map/ppermute | solution.py:422
  87.7 11.2 %collective-permute-start.14 = (bf16[128,1024]{1,0:T(8,128)(2,1)S(1)}, bf16[128,1024]{1,0:T(8,128)(2,1)S(1)}, u32[]{:S(2)}, u32[]{:S(2)}) collective-permute-start(bf16[128,1024]{1,0:T(8,128)(2,1)S(1)} %fusion.12.norm_own), channel_id=1, source_target_pairs={{0,2},{1,3},{2,0},{3,1},{4,6},{5,7},{6,4},{7,5},{8,10},{9,11},{10,... | collective-permute-start | bytes 786440 | tf_op jit(solution)/shard_map/ppermute | solution.py:413
  94.2 13.7 %collective-permute-start.18 = (bf16[128,2176]{1,0:T(8,128)(2,1)}, bf16[128,2176]{1,0:T(8,128)(2,1)S(1)}, u32[]{:S(2)}, u32[]{:S(2)}) collective-permute-start(bf16[128,2176]{1,0:T(8,128)(2,1)} %collective-permute-done.10.first), channel_id=1, source_target_pairs={{0,4},{4,0},{8,12},{12,8},{16,20},{20,16},{24,28},{28,24},{1,5},{5... | collective-permute-start | bytes 1671176 | tf_op jit(solution)/shard_map/ppermute | solution.py:430
  97.3 15.3 %collective-permute-start.19 = (bf16[128,2176]{1,0:T(8,128)(2,1)S(1)}, bf16[128,2176]{1,0:T(8,128)(2,1)S(1)}, u32[]{:S(2)}, u32[]{:S(2)}) collective-permute-start(bf16[128,2176]{1,0:T(8,128)(2,1)S(1)} %collective-permute-done.17.other_third), channel_id=1, source_target_pairs={{0,8},{4,12},{8,16},{12,20},{16,24},{20,28},{24,0},{28,4},{1,9},{5... | collective-permute-start | bytes 1671176 | tf_op jit(solution)/shard_map/ppermute | solution.py:422
  98.9 13.7 %collective-permute-start.15 = (bf16[256,1024]{1,0:T(8,128)(2,1)S(1)}, bf16[256,1024]{1,0:T(8,128)(2,1)S(1)}, u32[]{:S(2)}, u32[]{:S(2)}) collective-permute-start(bf16[256,1024]{1,0:T(8,128)(2,1)S(1)} %pad_maximum_fusion.5), channel_id=1, source_target_pairs={{0,1},{1,0},{2,3},{3,2},{4,5},{5,4},{6,7},{7,6},{8,9},{9,8},{10,11... | collective-permute-start | bytes 1572872 | tf_op jit(solution)/shard_map/ppermute | solution.py:413
  122.0 8.4 %collective-permute-start.21 = (bf16[128,1024]{1,0:T(8,128)(2,1)S(1)}, bf16[128,1024]{1,0:T(8,128)(2,1)S(1)}, u32[]{:S(2)}, u32[]{:S(2)}) collective-permute-start(bf16[128,1024]{1,0:T(8,128)(2,1)S(1)} %add_convert_fusion.9), channel_id=1, source_target_pairs={{0,2},{1,3},{2,0},{3,1},{4,6},{5,7},{6,4},{7,5},{8,10},{9,11},{10,... | collective-permute-start | bytes 786440 | tf_op jit(solution)/shard_map/ppermute | solution.py:413
  125.2 28.2 %collective-permute-start.24 = (bf16[256,2176]{1,0:T(8,128)(2,1)S(1)}, bf16[256,2176]{1,0:T(8,128)(2,1)S(1)}, u32[]{:S(2)}, u32[]{:S(2)}) collective-permute-start(bf16[256,2176]{1,0:T(8,128)(2,1)S(1)} %get-tuple-element.118), channel_id=1, source_target_pairs={{0,8},{4,12},{8,16},{12,20},{16,24},{20,28},{24,0},{28,4},{1,9},{5... | collective-permute-start | bytes 3342344 | tf_op jit(solution)/shard_map/ppermute | solution.py:422
  125.3 28.1 %collective-permute-start.25 = (bf16[256,2176]{1,0:T(8,128)(2,1)S(1)}, bf16[256,2176]{1,0:T(8,128)(2,1)S(1)}, u32[]{:S(2)}, u32[]{:S(2)}) collective-permute-start(bf16[256,2176]{1,0:T(8,128)(2,1)S(1)} %get-tuple-element.119), channel_id=1, source_target_pairs={{0,4},{4,0},{8,12},{12,8},{16,20},{20,16},{24,28},{28,24},{1,5},{5... | collective-permute-start | bytes 3342344 | tf_op jit(solution)/shard_map/ppermute | solution.py:430
  153.6 26.2 %collective-permute-start.27 = (bf16[128,2176]{1,0:T(8,128)(2,1)S(1)}, bf16[128,2176]{1,0:T(8,128)(2,1)S(1)}, u32[]{:S(2)}, u32[]{:S(2)}) collective-permute-start(bf16[128,2176]{1,0:T(8,128)(2,1)S(1)} %add_convert_fusion.2), channel_id=1, source_target_pairs={{0,24},{4,28},{8,0},{12,4},{16,8},{20,12},{24,16},{28,20},{1,25},{... | collective-permute-start | bytes 1671176 | tf_op jit(solution)/shard_map/ppermute | solution.py:426
  155.5 24.2 %collective-permute-start.26 = (bf16[128,2176]{1,0:T(8,128)(2,1)S(1)}, bf16[128,2176]{1,0:T(8,128)(2,1)S(1)}, u32[]{:S(2)}, u32[]{:S(2)}) collective-permute-start(bf16[128,2176]{1,0:T(8,128)(2,1)S(1)} %add_convert_fusion.3), channel_id=1, source_target_pairs={{0,4},{4,0},{8,12},{12,8},{16,20},{20,16},{24,28},{28,24},{1,5},{5... | collective-permute-start | bytes 1671176 | tf_op jit(solution)/shard_map/ppermute | solution.py:430
  156.9 21.2 %collective-permute-start.28 = (bf16[256,1024]{1,0:T(8,128)(2,1)S(1)}, bf16[256,1024]{1,0:T(8,128)(2,1)S(1)}, u32[]{:S(2)}, u32[]{:S(2)}) collective-permute-start(bf16[256,1024]{1,0:T(8,128)(2,1)S(1)} %get-tuple-element.123), channel_id=1, source_target_pairs={{0,8},{4,12},{8,16},{12,20},{16,24},{20,28},{24,0},{28,4},{1,9},{5... | collective-permute-start | bytes 1572872 | tf_op jit(solution)/shard_map/ppermute | solution.py:422
  157.2 22.6 %collective-permute-start.29 = (bf16[256,1024]{1,0:T(8,128)(2,1)S(1)}, bf16[256,1024]{1,0:T(8,128)(2,1)S(1)}, u32[]{:S(2)}, u32[]{:S(2)}) collective-permute-start(bf16[256,1024]{1,0:T(8,128)(2,1)S(1)} %get-tuple-element.124), channel_id=1, source_target_pairs={{0,4},{4,0},{8,12},{12,8},{16,20},{20,16},{24,28},{28,24},{1,5},{5... | collective-permute-start | bytes 1572872 | tf_op jit(solution)/shard_map/ppermute | solution.py:430
  184.9 17.6 %collective-permute-start.33 = (bf16[128,2176]{1,0:T(8,128)(2,1)S(1)}, bf16[128,2176]{1,0:T(8,128)(2,1)S(1)}, u32[]{:S(2)}, u32[]{:S(2)}) collective-permute-start(bf16[128,2176]{1,0:T(8,128)(2,1)S(1)} %add_convert_fusion.1), channel_id=1, source_target_pairs={{0,8},{4,12},{8,16},{12,20},{16,24},{20,28},{24,0},{28,4},{1,9},{5... | collective-permute-start | bytes 1671176 | tf_op jit(solution)/shard_map/ppermute | solution.py:422
  190.2 17.8 %collective-permute-start.34 = (bf16[128,1024]{1,0:T(8,128)(2,1)S(1)}, bf16[128,1024]{1,0:T(8,128)(2,1)S(1)}, u32[]{:S(2)}, u32[]{:S(2)}) collective-permute-start(bf16[128,1024]{1,0:T(8,128)(2,1)S(1)} %get-tuple-element.195), channel_id=1, source_target_pairs={{0,8},{4,12},{8,16},{12,20},{16,24},{20,28},{24,0},{28,4},{1,9},{5... | collective-permute-start | bytes 786440 | tf_op jit(solution)/shard_map/ppermute | solution.py:422
  190.9 20.8 %collective-permute-start.35 = (bf16[128,1024]{1,0:T(8,128)(2,1)S(1)}, bf16[128,1024]{1,0:T(8,128)(2,1)S(1)}, u32[]{:S(2)}, u32[]{:S(2)}) collective-permute-start(bf16[128,1024]{1,0:T(8,128)(2,1)S(1)} %get-tuple-element.194), channel_id=1, source_target_pairs={{0,24},{4,28},{8,0},{12,4},{16,8},{20,12},{24,16},{28,20},{1,25},{... | collective-permute-start | bytes 786440 | tf_op jit(solution)/shard_map/ppermute | solution.py:426
  194.1 22.7 %collective-permute-start.32 = (bf16[256,1024]{1,0:T(8,128)(2,1)}, bf16[256,1024]{1,0:T(8,128)(2,1)}, u32[]{:S(2)}, u32[]{:S(2)}) collective-permute-start(bf16[256,1024]{1,0:T(8,128)(2,1)} %add_convert_fusion.4), channel_id=1, source_target_pairs={{0,2},{1,3},{2,0},{3,1},{4,6},{5,7},{6,4},{7,5},{8,10},{9,11},{10,... | collective-permute-start | bytes 1572872 | tf_op jit(solution)/shard_map/ppermute | solution.py:413
  213.2 14.9 %all-to-all-start.2 = ((bf16[4,32,2944]{2,1,0:T(8,128)(2,1)}), bf16[4,32,2944]{2,1,0:T(8,128)(2,1)S(1)}, u32[]{:S(2)}, u32[]{:S(2)}) async-start(bf16[4,32,2944]{2,1,0:T(8,128)(2,1)} %bitcast.9), calls=%async_computation.2 | async-start | bytes 1507328 | tf_op jit(solution)/shard_map/all_to_all | solution.py:418
  (47 other events, 262.6 us)

commit v12 on v11

--- a/solution.py
+++ b/solution.py
@@ -545,11 +545,18 @@
     normed, grad_out, mixed, grad_inner, send, keep, w_down,
     w_up, inner, grad_mixed,
 ):
-    size, count, edge = own.shape[0], 128, w_up.shape[1]
+    size, count = own.shape[0], 128
+    main, rest = w_down.shape[1] - LANES, 16
+    lane = lax.broadcasted_iota(jnp.int32, (size, LANES), 1)
     blocks = (first, second, third, own, other_first, other_second, other_third, other)
     for at, ref in enumerate(blocks):
-        w_up[size * at : size * (at + 1), :] = ref[:, :edge]
-        w_down[size * at : size * (at + 1), :] = ref[:, edge:]
+        here = slice(size * at, size * (at + 1))
+        tail = wide(ref[:, 3 * main :])
+        w_up[here, : 2 * main] = ref[:, : 2 * main]
+        w_up[here, 2 * main :] = low(jnp.where(lane < 2 * rest, tail, 0.0))
+        w_down[here, :main] = ref[:, 2 * main : 3 * main]
+        tail = pltpu.roll(tail, LANES - 2 * rest, 1)
+        w_down[here, main:] = low(jnp.where(lane < rest, tail, 0.0))
     for at, ref in enumerate(
         (norm_own[...], norm_beside[:count, :], norm_across[...], norm_beside[count:, :])
     ):
@@ -559,8 +566,6 @@
         grad_out[count * at : count * (at + 1), :] = low(wide(ref) * live)
     inner[...] = matmul(normed[...], w_up[...])
     grad_mixed[...] = matmul(grad_out[...], w_down[...])
-    main = (w_down.shape[1] // LANES - 1) * LANES
-    rest = 16
 
     def parts(gate):
         phi = 0.5 * (1.0 + lax.erf(gate * 0.7071067811865476))
@@ -599,11 +604,13 @@
 
 
 def mlp_terms(normed, grad_inner, grad_out, mixed, keep, pair, near, far):
-    edge = grad_inner.shape[1]
-    term = low(matmul_left_t(normed[...], grad_inner[...]))
-    place_term(term, keep, pair, near, far, slice(0, edge))
-    term = low(matmul_left_t(grad_out[...], mixed[...]))
-    place_term(term, keep, pair, near, far, slice(edge, edge + mixed.shape[1]))
+    main, rest = mixed.shape[1] - LANES, 16
+    term_in = matmul_left_t(normed[...], grad_inner[...])
+    term_out = matmul_left_t(grad_out[...], mixed[...])
+    tail = term_in[:, 2 * main :] + pltpu.roll(term_out[:, main:], 2 * rest, 1)
+    place_term(low(term_in[:, : 2 * main]), keep, pair, near, far, slice(0, 2 * main))
+    place_term(low(term_out[:, :main]), keep, pair, near, far, slice(2 * main, 3 * main))
+    place_term(low(tail), keep, pair, near, far, slice(3 * main, 3 * main + LANES))
 
 
 def attention_backward(
@@ -676,7 +683,7 @@
 def unpack_rest(back, w_in, gain, grad_in, gain_grad, grad_out):
     size, hidden, part = w_in.shape[0], w_in.shape[1] // 2, w_in.shape[1] // 8
     main = part // LANES * LANES
-    rest, edge = part - main, 2 * main + LANES
+    rest = part - main
     total = jnp.zeros(gain.shape, jnp.float32)
     for k in range(4):
         here = slice(size * k, size * (k + 1))
@@ -684,13 +691,16 @@
             base = hidden * half + part * k
             for source, target, count in (
                 (main * half, base, main),
-                (2 * main + rest * half, base + main, rest),
+                (3 * main + rest * half, base + main, rest),
             ):
                 piece = wide(back[here, source : source + count])
                 grad_in[:, target : target + count] = piece * gain[...]
                 weights = wide(w_in[:, target : target + count])
                 total += jnp.sum(piece * weights, axis=1, keepdims=True)
-        grad_out[:, part * k : part * (k + 1)] = wide(back[here, edge : edge + part])
+        base = part * k
+        grad_out[:, base : base + main] = wide(back[here, 2 * main : 3 * main])
+        source = 3 * main + 2 * rest
+        grad_out[:, base + main : base + part] = wide(back[here, source : source + rest])
     gain_grad[...] = jnp.broadcast_to(total, (total.shape[0], LANES)).T[:1, :]
 
 
@@ -754,7 +764,7 @@
     hidden = w_in.shape[1] // 2
     part = hidden // 4
     main = part // LANES * LANES
-    in_width, out_width = 2 * main + LANES, main + LANES
+    in_width, out_width, all_width = 2 * main + LANES, main + LANES, 3 * main + LANES
     f32, b16 = jnp.float32, jnp.bfloat16
     group = 4 * count
 
@@ -780,11 +790,11 @@
         gate = scaled_in[:, part * k : part * (k + 1)]
         up_part = scaled_in[:, hidden + part * k : hidden + part * (k + 1)]
         out_part = w_out[:, part * k : part * (k + 1)]
-        fill = [jnp.zeros((w_in.shape[0], n), b16) for n in (in_width - 2 * part, out_width - part)]
+        fill = jnp.zeros((w_in.shape[0], all_width - 3 * part), b16)
         pieces.append(
             columns(
-                [gate[:, :main], up_part[:, :main], gate[:, main:], up_part[:, main:], fill[0]]
-                + [out_part, fill[1]]
+                [gate[:, :main], up_part[:, :main], out_part[:, :main]]
+                + [gate[:, main:], up_part[:, main:], out_part[:, main:], fill]
             )
         )
     mine = rows([relative(tokens, z, x), relative(cotangent, z, x)])
@@ -849,7 +859,6 @@
             ((group, out_width), f32),
         ],
     )
-    all_width = in_width + out_width
     size = width // 8
     io_keep, io_pair, io_near, io_far = kernel(
         mlp_terms,

time: 234 us -> 235 us (level)
    ppermute x4, waiting for transfers between devices: 7.25 us -> 23.1 us  [down(): return lax.ppermute(value, 'fsdp', [(k, (k - 2) % 8) for k in range(8)])]
    ppermute x9, waiting for transfers between devices: 60.8 us -> 47.7 us  [up(): return lax.ppermute(value, 'fsdp', [(k, (k + 2) % 8) for k in range(8)])]
    unnamed x76 -> x72, local copies, waits for them, and re-layouts: 4.91 us -> 4.11 us
where the time goes in v12:
time: 235 us; the launch traced here: 234 us
  waiting for transfers between devices  118 us (50%)
  starting transfers between devices  55.7 us (24%)
  Pallas kernels  31.9 us (14%)
  other arithmetic  20.1 us (9%)
  local copies, waits for them, and re-layouts  5.84 us (2%)
    ppermute x9, waiting for transfers between devices, up(): return lax.ppermute(value, 'fsdp', [(k, (k + 2) % 8) for k in range(8)])  47.7 us
    pallas_call x7, Pallas kernels, kernel(): pl.pallas_call(body, out_shape=shapes, in_specs=[pl.BlockSpec(memory_spac...  31.9 us
    ppermute x4, waiting for transfers between devices, down(): return lax.ppermute(value, 'fsdp', [(k, (k - 2) % 8) for k in range(8)])  23.1 us
    ppermute x10, waiting for transfers between devices, over(): return lax.ppermute(value, 'fsdp', [(k, k ^ 1) for k in range(8)])  20.3 us
    ppermute x12, waiting for transfers between devices, swap(): return lax.ppermute(value, 'rep', [(k, k ^ distance) for k in range(4)])  19.1 us
    all_to_all x3, starting transfers between devices, rep_exchange(): return lax.all_to_all(blocks, 'rep', 0, 0, tiled=True).reshape(value.shape)  14.9 us
    ppermute x4, starting transfers between devices, down(): return lax.ppermute(value, 'fsdp', [(k, (k - 2) % 8) for k in range(8)])  11.6 us
    ppermute x9, starting transfers between devices, up(): return lax.ppermute(value, 'fsdp', [(k, (k + 2) % 8) for k in range(8)])  10.7 us
  transfers between devices with their start and end apart: 40, of which 25 were waited for; matrix products, arithmetic and copies ran while one was open for 7% of the time, Pallas kernels for 9%

profile of v12, /device:TPU:0, one launch (start us, length us, event | category | flops | bytes accessed | tf_op | source)
XLA Modules:
  0.0 233.6 jit_solution(1230534530896052221)
XLA Ops:
  3.9 4.2 %all-to-all-start = ((bf16[4,32,896]{2,1,0:T(8,128)(2,1)}), bf16[4,32,896]{2,1,0:T(8,128)(2,1)S(1)}, u32[]{:S(2)}, u32[]{:S(2)}) async-start(bf16[4,32,896]{2,1,0:T(8,128)(2,1)} %bitcast), calls=%async_computation | async-start | bytes 458752 | tf_op jit(solution)/shard_map/all_to_all | solution.py:418
  11.6 2.2 all-to-all-done
  13.8 7.2 %all-to-all-start.1 = ((bf16[4,32,2048]{2,1,0:T(8,128)(2,1)}), bf16[4,32,2048]{2,1,0:T(8,128)(2,1)}, u32[]{:S(2)}, u32[]{:S(2)}) async-start(bf16[4,32,2048]{2,1,0:T(8,128)(2,1)} %bitcast.3), calls=%async_computation.1 | async-start | bytes 1048576 | tf_op jit(solution)/shard_map/all_to_all | solution.py:418
  22.1 4.7 %collective-permute-start.2 = (bf16[128,1024]{1,0:T(8,128)(2,1)S(1)}, bf16[128,1024]{1,0:T(8,128)(2,1)S(1)}, u32[]{:S(2)}, u32[]{:S(2)}) collective-permute-start(bf16[128,1024]{1,0:T(8,128)(2,1)S(1)} %maximum_maximum_fusion.own), channel_id=1, source_target_pairs={{0,24},{4,28},{8,0},{12,4},{16,8},{20,12},{24,16},{28,20},{1,25},{... | collective-permute-start | bytes 786440 | tf_op jit(solution)/shard_map/ppermute | solution.py:426
  27.0 6.9 %collective-permute-done.1.third = bf16[128,1024]{1,0:T(8,128)(2,1)S(1)} collective-permute-done((bf16[128,1024]{1,0:T(8,128)(2,1)S(1)}, bf16[128,1024]{1,0:T(8,128)(2,1)S(1)}, u32[]{:S(2)}, u32[]{:S(2)}) %collective-permute-start.1) | collective-permute-done | bytes 262176 | tf_op jit(solution)/shard_map/ppermute | solution.py:422
  33.9 3.2 %collective-permute-done.2.first = bf16[128,1024]{1,0:T(8,128)(2,1)S(1)} collective-permute-done((bf16[128,1024]{1,0:T(8,128)(2,1)S(1)}, bf16[128,1024]{1,0:T(8,128)(2,1)S(1)}, u32[]{:S(2)}, u32[]{:S(2)}) %collective-permute-start.2) | collective-permute-done | bytes 262176 | tf_op jit(solution)/shard_map/ppermute | solution.py:426
  42.4 8.4 %collective-permute-done.4.second = bf16[128,1024]{1,0:T(8,128)(2,1)S(1)} collective-permute-done((bf16[128,1024]{1,0:T(8,128)(2,1)S(1)}, bf16[128,1024]{1,0:T(8,128)(2,1)S(1)}, u32[]{:S(2)}, u32[]{:S(2)}) %collective-permute-start.4) | collective-permute-done | bytes 262176 | tf_op jit(solution)/shard_map/ppermute | solution.py:422
  55.0 4.6 %collective-permute-done.9.third = bf16[128,2048]{1,0:T(8,128)(2,1)S(1)} collective-permute-done((bf16[128,2048]{1,0:T(8,128)(2,1)}, bf16[128,2048]{1,0:T(8,128)(2,1)S(1)}, u32[]{:S(2)}, u32[]{:S(2)}) %collective-permute-start.9) | collective-permute-done | bytes 524320 | tf_op jit(solution)/shard_map/ppermute | solution.py:422
  65.5 7.0 %attention_forward.1 = (bf16[512,1024]{1,0:T(8,128)(2,1)S(1)}, bf16[1024,768]{1,0:T(8,128)(2,1)S(1)}, bf16[256,1024]{1,0:T(8,128)(2,1)S(1)}, bf16[512,256]{1,0:T...) custom-call(s32[2]{0:T(128)S(1)} %pad_add_fusion.place, ...), custom_call_target="tpu_custom_call" | custom-call | flops 1207959552 | bytes 11014152 | tf_op jit(solution)/shard_map/attention_forward/pallas_call | solution.py:725
  72.5 3.5 %collective-permute-done.11.other = bf16[128,2048]{1,0:T(8,128)(2,1)} collective-permute-done((bf16[128,2048]{1,0:T(8,128)(2,1)}, bf16[128,2048]{1,0:T(8,128)(2,1)}, u32[]{:S(2)}, u32[]{:S(2)}) %collective-permute-start.11) | collective-permute-done | bytes 524320 | tf_op jit(solution)/shard_map/ppermute | solution.py:430
  80.1 3.8 %collective-permute-start.16 = (bf16[128,2048]{1,0:T(8,128)(2,1)S(1)}, bf16[128,2048]{1,0:T(8,128)(2,1)S(1)}, u32[]{:S(2)}, u32[]{:S(2)}) collective-permute-start(bf16[128,2048]{1,0:T(8,128)(2,1)S(1)} %copy-done.14), channel_id=1, source_target_pairs={{0,8},{4,12},{8,16},{12,20},{16,24},{20,28},{24,0},{28,4},{1,9},{5... | collective-permute-start | bytes 1572872 | tf_op jit(solution)/shard_map/ppermute | solution.py:422
  83.9 2.5 %collective-permute-done.13 = bf16[128,1024]{1,0:T(8,128)(2,1)S(1)} collective-permute-done((bf16[128,1024]{1,0:T(8,128)(2,1)S(1)}, bf16[128,1024]{1,0:T(8,128)(2,1)S(1)}, u32[]{:S(2)}, u32[]{:S(2)}) %collective-permute-start.13) | collective-permute-done | bytes 262176 | tf_op jit(solution)/shard_map/ppermute | solution.py:413
  88.0 4.8 %collective-permute-done.17.other_third = bf16[128,2048]{1,0:T(8,128)(2,1)S(1)} collective-permute-done((bf16[128,2048]{1,0:T(8,128)(2,1)S(1)}, bf16[128,2048]{1,0:T(8,128)(2,1)S(1)}, u32[]{:S(2)}, u32[]{:S(2)}) %collective-permute-start.17) | collective-permute-done | bytes 524320 | tf_op jit(solution)/shard_map/ppermute | solution.py:430
  93.8 2.2 collective-permute-done.16.second
  97.7 8.2 %collective-permute-done.18.other_first = bf16[128,2048]{1,0:T(8,128)(2,1)S(1)} collective-permute-done((bf16[128,2048]{1,0:T(8,128)(2,1)}, bf16[128,2048]{1,0:T(8,128)(2,1)S(1)}, u32[]{:S(2)}, u32[]{:S(2)}) %collective-permute-start.18) | collective-permute-done | bytes 524320 | tf_op jit(solution)/shard_map/ppermute | solution.py:430
  105.9 4.8 %collective-permute-done.19.other_second = bf16[128,2048]{1,0:T(8,128)(2,1)S(1)} collective-permute-done((bf16[128,2048]{1,0:T(8,128)(2,1)S(1)}, bf16[128,2048]{1,0:T(8,128)(2,1)S(1)}, u32[]{:S(2)}, u32[]{:S(2)}) %collective-permute-start.19) | collective-permute-done | bytes 524320 | tf_op jit(solution)/shard_map/ppermute | solution.py:422
  110.6 7.3 %mlp.1 = (bf16[512,1024]{1,0:T(8,128)(2,1)S(1)}, bf16[512,1024]{1,0:T(8,128)(2,1)S(1)}, bf16[512,768]{1,0:T(8,128)(2,1)S(1)}, bf16[512,1408]{1,0:T(8,128)(2,1)S(...) custom-call(s32[512,1]{1,0:T(8,128)S(1)} %copy.28.seg_col, ...), custom_call_target="tpu_custom_call" | custom-call | flops 3758096384 | bytes 14288896 | tf_op jit(solution)/shard_map/mlp/pallas_call | solution.py:725
  120.5 2.7 %mlp_terms.1 = (bf16[384,2048]{1,0:T(8,128)(2,1)S(1)}, bf16[256,2048]{1,0:T(8,128)(2,1)S(1)}, bf16[128,2048]{1,0:T(8,128)(2,1)S(1)}, bf16[256,2048]{1,0:T(8,128)(2,1)S(1)}) custom-call(bf16[512,1024]{1,0:T(8,128)(2,1)S(1)} %get-tuple-element.101.normed, bf16[512,1408]{1,0:T(8,128)(2,1)S(1)} %get-tuple-element.102.grad_inner, ...), custom_call_target="tpu_custom_call" | custom-call | flops 2147483648 | bytes 8519680 | tf_op jit(solution)/shard_map/mlp_terms/pallas_call | solution.py:725
  123.3 5.1 %collective-permute-done.21 = bf16[128,1024]{1,0:T(8,128)(2,1)S(1)} collective-permute-done((bf16[128,1024]{1,0:T(8,128)(2,1)S(1)}, bf16[128,1024]{1,0:T(8,128)(2,1)S(1)}, u32[]{:S(2)}, u32[]{:S(2)}) %collective-permute-start.21) | collective-permute-done | bytes 262176 | tf_op jit(solution)/shard_map/ppermute | solution.py:413
  131.6 5.8 %collective-permute-done.22.low_across = bf16[128,1024]{1,0:T(8,128)(2,1)S(1)} collective-permute-done((bf16[128,1024]{1,0:T(8,128)(2,1)S(1)}, bf16[128,1024]{1,0:T(8,128)(2,1)S(1)}, u32[]{:S(2)}, u32[]{:S(2)}) %collective-permute-start.22) | collective-permute-done | bytes 262176 | tf_op jit(solution)/shard_map/ppermute | solution.py:413
  139.4 7.6 %attention_backward.1 = (bf16[512,768]{1,0:T(8,128)(2,1)S(1)}, bf16[384,1024]{1,0:T(8,128)(2,1)S(1)}, bf16[256,1024]{1,0:T(8,128)(2,1)S(1)}, bf16[128,1024]{1,0:T(8,128)(2,1)S(1)}, bf16[256,1024]{1,0:T(8,128)(2,1)S(1)}) custom-call(s32[2]{0:T(128)S(1)} %pad_add_fusion.place, f32[512,128]{1,0:T(8,128)S(1)} %get-tuple-element.268.cosine, ...), custom_call_target="tpu_custom_call" | custom-call | flops 1677721600 | bytes 8126472 | tf_op jit(solution)/shard_map/attention_backward/pallas_call | solution.py:725
  146.9 9.3 %collective-permute-done.24 = bf16[256,2048]{1,0:T(8,128)(2,1)S(1)} collective-permute-done((bf16[256,2048]{1,0:T(8,128)(2,1)S(1)}, bf16[256,2048]{1,0:T(8,128)(2,1)S(1)}, u32[]{:S(2)}, u32[]{:S(2)}) %collective-permute-start.24) | collective-permute-done | bytes 1048608 | tf_op jit(solution)/shard_map/ppermute | solution.py:422
  161.0 2.8 %projections.1 = (bf16[512,1024]{1,0:T(8,128)(2,1)}, bf16[512,1024]{1,0:T(8,128)(2,1)S(1)}) custom-call(bf16[512,768]{1,0:T(8,128)(2,1)S(1)} %get-tuple-element.113.grad_packed, bf16[1024,768]{1,0:T(8,128)(2,1)S(1)} %get-tuple-element.114.qkv, bf16[512,768]{1,0:T(8,128)(2,1)S(1)} %get-tuple-element.103.mixed, bf16[1024,768]{1,0:T(8,128)(2,1)S(1)} %get-tuple-element.115.w_down), custom_call_target="tpu_custom_call" | custom-call | flops 1610612736 | bytes 6815744 | tf_op jit(solution)/shard_map/projections/pallas_call | solution.py:725
  163.8 16.0 %collective-permute-done.27 = bf16[128,2048]{1,0:T(8,128)(2,1)S(1)} collective-permute-done((bf16[128,2048]{1,0:T(8,128)(2,1)S(1)}, bf16[128,2048]{1,0:T(8,128)(2,1)S(1)}, u32[]{:S(2)}, u32[]{:S(2)}) %collective-permute-start.27) | collective-permute-done | bytes 524320 | tf_op jit(solution)/shard_map/ppermute | solution.py:426
  188.9 2.4 %collective-permute-done.31 = bf16[128,1024]{1,0:T(8,128)(2,1)S(1)} collective-permute-done((bf16[128,1024]{1,0:T(8,128)(2,1)S(1)}, bf16[128,1024]{1,0:T(8,128)(2,1)S(1)}, u32[]{:S(2)}, u32[]{:S(2)}) %collective-permute-start.31) | collective-permute-done | bytes 262176 | tf_op jit(solution)/shard_map/ppermute | solution.py:430
  192.2 3.3 %collective-permute-start.35 = (bf16[128,1024]{1,0:T(8,128)(2,1)S(1)}, bf16[128,1024]{1,0:T(8,128)(2,1)S(1)}, u32[]{:S(2)}, u32[]{:S(2)}) collective-permute-start(bf16[128,1024]{1,0:T(8,128)(2,1)S(1)} %get-tuple-element.194), channel_id=1, source_target_pairs={{0,24},{4,28},{8,0},{12,4},{16,8},{20,12},{24,16},{28,20},{1,25},{... | collective-permute-start | bytes 786440 | tf_op jit(solution)/shard_map/ppermute | solution.py:426
  197.1 6.0 %collective-permute-done.33 = bf16[128,2048]{1,0:T(8,128)(2,1)S(1)} collective-permute-done((bf16[128,2048]{1,0:T(8,128)(2,1)S(1)}, bf16[128,2048]{1,0:T(8,128)(2,1)S(1)}, u32[]{:S(2)}, u32[]{:S(2)}) %collective-permute-start.33) | collective-permute-done | bytes 524320 | tf_op jit(solution)/shard_map/ppermute | solution.py:422
  203.0 5.5 %collective-permute-done.34 = bf16[128,1024]{1,0:T(8,128)(2,1)S(1)} collective-permute-done((bf16[128,1024]{1,0:T(8,128)(2,1)S(1)}, bf16[128,1024]{1,0:T(8,128)(2,1)S(1)}, u32[]{:S(2)}, u32[]{:S(2)}) %collective-permute-start.34) | collective-permute-done | bytes 262176 | tf_op jit(solution)/shard_map/ppermute | solution.py:422
  208.5 4.0 %collective-permute-done.35 = bf16[128,1024]{1,0:T(8,128)(2,1)S(1)} collective-permute-done((bf16[128,1024]{1,0:T(8,128)(2,1)S(1)}, bf16[128,1024]{1,0:T(8,128)(2,1)S(1)}, u32[]{:S(2)}, u32[]{:S(2)}) %collective-permute-start.35) | collective-permute-done | bytes 262176 | tf_op jit(solution)/shard_map/ppermute | solution.py:426
  214.7 3.5 %all-to-all-start.2 = ((bf16[4,32,2816]{2,1,0:T(8,128)(2,1)}), bf16[4,32,2816]{2,1,0:T(8,128)(2,1)S(1)}, u32[]{:S(2)}, u32[]{:S(2)}) async-start(bf16[4,32,2816]{2,1,0:T(8,128)(2,1)} %bitcast.9), calls=%async_computation.2 | async-start | bytes 1441792 | tf_op jit(solution)/shard_map/all_to_all | solution.py:418
  223.2 5.9 %all-to-all-done.2 = bf16[4,32,2816]{2,1,0:T(8,128)(2,1)S(1)} async-done(((bf16[4,32,2816]{2,1,0:T(8,128)(2,1)}), bf16[4,32,2816]{2,1,0:T(8,128)(2,1)S(1)}, u32[]{:S(2)}, u32[]{:S(2)}) %all-to-all-start.2) | async-done | bytes 720928 | tf_op jit(solution)/shard_map/all_to_all | solution.py:418
  229.1 3.6 %unpack_rest.1 = (f32[32,5248]{1,0:T(8,128)}, f32[1,32]{1,0:T(1,128)}, f32[32,2624]{1,0:T(8,128)}) custom-call(bf16[128,2816]{1,0:T(8,128)(2,1)S(1)} %bitcast.19, bf16[32,5248]{1,0:T(8,128)(2,1)S(1)} %copy-done, f32[32,1]{1,0:T(8,128)S(1)} %copy.31.gain), custom_call_target="tpu_custom_call" | custom-call | flops 671744 | bytes 2064640 | tf_op jit(solution)/shard_map/unpack_rest/pallas_call | solution.py:725
  (236 shorter events, 63.2 us)
Async XLA Ops:
  3.9 9.9 %all-to-all-start = ((bf16[4,32,896]{2,1,0:T(8,128)(2,1)}), bf16[4,32,896]{2,1,0:T(8,128)(2,1)S(1)}, u32[]{:S(2)}, u32[]{:S(2)}) async-start(bf16[4,32,896]{2,1,0:T(8,128)(2,1)} %bitcast), calls=%async_computation | async-start | bytes 458752 | tf_op jit(solution)/shard_map/all_to_all | solution.py:418
  13.8 23.3 %all-to-all-start.1 = ((bf16[4,32,2048]{2,1,0:T(8,128)(2,1)}), bf16[4,32,2048]{2,1,0:T(8,128)(2,1)}, u32[]{:S(2)}, u32[]{:S(2)}) async-start(bf16[4,32,2048]{2,1,0:T(8,128)(2,1)} %bitcast.3), calls=%async_computation.1 | async-start | bytes 1048576 | tf_op jit(solution)/shard_map/all_to_all | solution.py:418
  21.0 12.9 %collective-permute-start.1 = (bf16[128,1024]{1,0:T(8,128)(2,1)S(1)}, bf16[128,1024]{1,0:T(8,128)(2,1)S(1)}, u32[]{:S(2)}, u32[]{:S(2)}) collective-permute-start(bf16[128,1024]{1,0:T(8,128)(2,1)S(1)} %maximum_maximum_fusion.own), channel_id=1, source_target_pairs={{0,8},{4,12},{8,16},{12,20},{16,24},{20,28},{24,0},{28,4},{1,9},{5... | collective-permute-start | bytes 786440 | tf_op jit(solution)/shard_map/ppermute | solution.py:422
  22.1 15.0 %collective-permute-start.2 = (bf16[128,1024]{1,0:T(8,128)(2,1)S(1)}, bf16[128,1024]{1,0:T(8,128)(2,1)S(1)}, u32[]{:S(2)}, u32[]{:S(2)}) collective-permute-start(bf16[128,1024]{1,0:T(8,128)(2,1)S(1)} %maximum_maximum_fusion.own), channel_id=1, source_target_pairs={{0,24},{4,28},{8,0},{12,4},{16,8},{20,12},{24,16},{28,20},{1,25},{... | collective-permute-start | bytes 786440 | tf_op jit(solution)/shard_map/ppermute | solution.py:426
  26.8 10.3 %collective-permute-start.3 = (bf16[128,1024]{1,0:T(8,128)(2,1)S(1)}, bf16[128,1024]{1,0:T(8,128)(2,1)S(1)}, u32[]{:S(2)}, u32[]{:S(2)}) collective-permute-start(bf16[128,1024]{1,0:T(8,128)(2,1)S(1)} %maximum_maximum_fusion.own), channel_id=1, source_target_pairs={{0,4},{4,0},{8,12},{12,8},{16,20},{20,16},{24,28},{28,24},{1,5},{5... | collective-permute-start | bytes 786440 | tf_op jit(solution)/shard_map/ppermute | solution.py:430
  37.2 13.6 %collective-permute-start.5 = (bf16[256,1024]{1,0:T(8,128)(2,1)S(1)}, bf16[256,1024]{1,0:T(8,128)(2,1)S(1)}, u32[]{:S(2)}, u32[]{:S(2)}) collective-permute-start(bf16[256,1024]{1,0:T(8,128)(2,1)S(1)} %pad_maximum_fusion.4), channel_id=1, source_target_pairs={{0,4},{4,0},{8,12},{12,8},{16,20},{20,16},{24,28},{28,24},{1,5},{5... | collective-permute-start | bytes 1572872 | tf_op jit(solution)/shard_map/ppermute | solution.py:430
  38.0 13.6 %collective-permute-start.6 = (bf16[256,1024]{1,0:T(8,128)(2,1)S(1)}, bf16[256,1024]{1,0:T(8,128)(2,1)S(1)}, u32[]{:S(2)}, u32[]{:S(2)}) collective-permute-start(bf16[256,1024]{1,0:T(8,128)(2,1)S(1)} %pad_maximum_fusion.3.mine), channel_id=1, source_target_pairs={{0,2},{1,3},{2,0},{3,1},{4,6},{5,7},{6,4},{7,5},{8,10},{9,11},{10,... | collective-permute-start | bytes 1572872 | tf_op jit(solution)/shard_map/ppermute | solution.py:413
  39.7 11.1 %collective-permute-start.4 = (bf16[128,1024]{1,0:T(8,128)(2,1)S(1)}, bf16[128,1024]{1,0:T(8,128)(2,1)S(1)}, u32[]{:S(2)}, u32[]{:S(2)}) collective-permute-start(bf16[128,1024]{1,0:T(8,128)(2,1)S(1)} %collective-permute-done.1.third), channel_id=1, source_target_pairs={{0,8},{4,12},{8,16},{12,20},{16,24},{20,28},{24,0},{28,4},{1,9},{5... | collective-permute-start | bytes 786440 | tf_op jit(solution)/shard_map/ppermute | solution.py:422
  41.7 17.9 %collective-permute-start.9 = (bf16[128,2048]{1,0:T(8,128)(2,1)}, bf16[128,2048]{1,0:T(8,128)(2,1)S(1)}, u32[]{:S(2)}, u32[]{:S(2)}) collective-permute-start(bf16[128,2048]{1,0:T(8,128)(2,1)} %bitcast.4.own), channel_id=1, source_target_pairs={{0,8},{4,12},{8,16},{12,20},{16,24},{20,28},{24,0},{28,4},{1,9},{5... | collective-permute-start | bytes 1572872 | tf_op jit(solution)/shard_map/ppermute | solution.py:422
  52.6 12.8 %collective-permute-start.7 = (bf16[512,1024]{1,0:T(8,128)(2,1)}, bf16[512,1024]{1,0:T(8,128)(2,1)S(1)}, u32[]{:S(2)}, u32[]{:S(2)}) collective-permute-start(bf16[512,1024]{1,0:T(8,128)(2,1)} %pad_maximum_fusion), channel_id=1, source_target_pairs={{0,1},{1,0},{2,3},{3,2},{4,5},{5,4},{6,7},{7,6},{8,9},{9,8},{10,11... | collective-permute-start | bytes 3145736 | tf_op jit(solution)/shard_map/ppermute | solution.py:413
  52.7 8.8 %collective-permute-start.8 = (bf16[128,1024]{1,0:T(8,128)(2,1)S(1)}, bf16[128,1024]{1,0:T(8,128)(2,1)S(1)}, u32[]{:S(2)}, u32[]{:S(2)}) collective-permute-start(bf16[128,1024]{1,0:T(8,128)(2,1)S(1)} %collective-permute-done.4.second), channel_id=1, source_target_pairs={{0,4},{4,0},{8,12},{12,8},{16,20},{20,16},{24,28},{28,24},{1,5},{5... | collective-permute-start | bytes 786440 | tf_op jit(solution)/shard_map/ppermute | solution.py:430
  59.7 12.9 %collective-permute-start.10 = (bf16[128,2048]{1,0:T(8,128)(2,1)}, bf16[128,2048]{1,0:T(8,128)(2,1)}, u32[]{:S(2)}, u32[]{:S(2)}) collective-permute-start(bf16[128,2048]{1,0:T(8,128)(2,1)} %bitcast.4.own), channel_id=1, source_target_pairs={{0,24},{4,28},{8,0},{12,4},{16,8},{20,12},{24,16},{28,20},{1,25},{... | collective-permute-start | bytes 1572872 | tf_op jit(solution)/shard_map/ppermute | solution.py:426
  62.2 13.9 %collective-permute-start.11 = (bf16[128,2048]{1,0:T(8,128)(2,1)}, bf16[128,2048]{1,0:T(8,128)(2,1)}, u32[]{:S(2)}, u32[]{:S(2)}) collective-permute-start(bf16[128,2048]{1,0:T(8,128)(2,1)} %bitcast.4.own), channel_id=1, source_target_pairs={{0,4},{4,0},{8,12},{12,8},{16,20},{20,16},{24,28},{28,24},{1,5},{5... | collective-permute-start | bytes 1572872 | tf_op jit(solution)/shard_map/ppermute | solution.py:430
  78.0 8.4 %collective-permute-start.13 = (bf16[128,1024]{1,0:T(8,128)(2,1)S(1)}, bf16[128,1024]{1,0:T(8,128)(2,1)S(1)}, u32[]{:S(2)}, u32[]{:S(2)}) collective-permute-start(bf16[128,1024]{1,0:T(8,128)(2,1)S(1)} %add_convert_fusion.10), channel_id=1, source_target_pairs={{0,2},{1,3},{2,0},{3,1},{4,6},{5,7},{6,4},{7,5},{8,10},{9,11},{10,... | collective-permute-start | bytes 786440 | tf_op jit(solution)/shard_map/ppermute | solution.py:413
  79.1 13.8 %collective-permute-start.17 = (bf16[128,2048]{1,0:T(8,128)(2,1)S(1)}, bf16[128,2048]{1,0:T(8,128)(2,1)S(1)}, u32[]{:S(2)}, u32[]{:S(2)}) collective-permute-start(bf16[128,2048]{1,0:T(8,128)(2,1)S(1)} %copy-done.14), channel_id=1, source_target_pairs={{0,4},{4,0},{8,12},{12,8},{16,20},{20,16},{24,28},{28,24},{1,5},{5... | collective-permute-start | bytes 1572872 | tf_op jit(solution)/shard_map/ppermute | solution.py:430
  80.1 15.9 %collective-permute-start.16 = (bf16[128,2048]{1,0:T(8,128)(2,1)S(1)}, bf16[128,2048]{1,0:T(8,128)(2,1)S(1)}, u32[]{:S(2)}, u32[]{:S(2)}) collective-permute-start(bf16[128,2048]{1,0:T(8,128)(2,1)S(1)} %copy-done.14), channel_id=1, source_target_pairs={{0,8},{4,12},{8,16},{12,20},{16,24},{20,28},{24,0},{28,4},{1,9},{5... | collective-permute-start | bytes 1572872 | tf_op jit(solution)/shard_map/ppermute | solution.py:422
  87.1 10.5 %collective-permute-start.14 = (bf16[128,1024]{1,0:T(8,128)(2,1)S(1)}, bf16[128,1024]{1,0:T(8,128)(2,1)S(1)}, u32[]{:S(2)}, u32[]{:S(2)}) collective-permute-start(bf16[128,1024]{1,0:T(8,128)(2,1)S(1)} %fusion.12.norm_own), channel_id=1, source_target_pairs={{0,2},{1,3},{2,0},{3,1},{4,6},{5,7},{6,4},{7,5},{8,10},{9,11},{10,... | collective-permute-start | bytes 786440 | tf_op jit(solution)/shard_map/ppermute | solution.py:413
  92.8 13.0 %collective-permute-start.18 = (bf16[128,2048]{1,0:T(8,128)(2,1)}, bf16[128,2048]{1,0:T(8,128)(2,1)S(1)}, u32[]{:S(2)}, u32[]{:S(2)}) collective-permute-start(bf16[128,2048]{1,0:T(8,128)(2,1)} %collective-permute-done.10.first), channel_id=1, source_target_pairs={{0,4},{4,0},{8,12},{12,8},{16,20},{20,16},{24,28},{28,24},{1,5},{5... | collective-permute-start | bytes 1572872 | tf_op jit(solution)/shard_map/ppermute | solution.py:430
  96.0 14.6 %collective-permute-start.19 = (bf16[128,2048]{1,0:T(8,128)(2,1)S(1)}, bf16[128,2048]{1,0:T(8,128)(2,1)S(1)}, u32[]{:S(2)}, u32[]{:S(2)}) collective-permute-start(bf16[128,2048]{1,0:T(8,128)(2,1)S(1)} %collective-permute-done.17.other_third), channel_id=1, source_target_pairs={{0,8},{4,12},{8,16},{12,20},{16,24},{20,28},{24,0},{28,4},{1,9},{5... | collective-permute-start | bytes 1572872 | tf_op jit(solution)/shard_map/ppermute | solution.py:422
  97.6 13.0 %collective-permute-start.15 = (bf16[256,1024]{1,0:T(8,128)(2,1)S(1)}, bf16[256,1024]{1,0:T(8,128)(2,1)S(1)}, u32[]{:S(2)}, u32[]{:S(2)}) collective-permute-start(bf16[256,1024]{1,0:T(8,128)(2,1)S(1)} %pad_maximum_fusion.5), channel_id=1, source_target_pairs={{0,1},{1,0},{2,3},{3,2},{4,5},{5,4},{6,7},{7,6},{8,9},{9,8},{10,11... | collective-permute-start | bytes 1572872 | tf_op jit(solution)/shard_map/ppermute | solution.py:413
  120.0 8.4 %collective-permute-start.21 = (bf16[128,1024]{1,0:T(8,128)(2,1)S(1)}, bf16[128,1024]{1,0:T(8,128)(2,1)S(1)}, u32[]{:S(2)}, u32[]{:S(2)}) collective-permute-start(bf16[128,1024]{1,0:T(8,128)(2,1)S(1)} %add_convert_fusion.9), channel_id=1, source_target_pairs={{0,2},{1,3},{2,0},{3,1},{4,6},{5,7},{6,4},{7,5},{8,10},{9,11},{10,... | collective-permute-start | bytes 786440 | tf_op jit(solution)/shard_map/ppermute | solution.py:413
  130.3 26.0 %collective-permute-start.24 = (bf16[256,2048]{1,0:T(8,128)(2,1)S(1)}, bf16[256,2048]{1,0:T(8,128)(2,1)S(1)}, u32[]{:S(2)}, u32[]{:S(2)}) collective-permute-start(bf16[256,2048]{1,0:T(8,128)(2,1)S(1)} %get-tuple-element.118), channel_id=1, source_target_pairs={{0,8},{4,12},{8,16},{12,20},{16,24},{20,28},{24,0},{28,4},{1,9},{5... | collective-permute-start | bytes 3145736 | tf_op jit(solution)/shard_map/ppermute | solution.py:422
  130.3 26.0 %collective-permute-start.25 = (bf16[256,2048]{1,0:T(8,128)(2,1)S(1)}, bf16[256,2048]{1,0:T(8,128)(2,1)S(1)}, u32[]{:S(2)}, u32[]{:S(2)}) collective-permute-start(bf16[256,2048]{1,0:T(8,128)(2,1)S(1)} %get-tuple-element.119), channel_id=1, source_target_pairs={{0,4},{4,0},{8,12},{12,8},{16,20},{20,16},{24,28},{28,24},{1,5},{5... | collective-permute-start | bytes 3145736 | tf_op jit(solution)/shard_map/ppermute | solution.py:430
  156.4 23.4 %collective-permute-start.27 = (bf16[128,2048]{1,0:T(8,128)(2,1)S(1)}, bf16[128,2048]{1,0:T(8,128)(2,1)S(1)}, u32[]{:S(2)}, u32[]{:S(2)}) collective-permute-start(bf16[128,2048]{1,0:T(8,128)(2,1)S(1)} %add_convert_fusion.3), channel_id=1, source_target_pairs={{0,24},{4,28},{8,0},{12,4},{16,8},{20,12},{24,16},{28,20},{1,25},{... | collective-permute-start | bytes 1572872 | tf_op jit(solution)/shard_map/ppermute | solution.py:426
  158.5 21.3 %collective-permute-start.26 = (bf16[128,2048]{1,0:T(8,128)(2,1)S(1)}, bf16[128,2048]{1,0:T(8,128)(2,1)S(1)}, u32[]{:S(2)}, u32[]{:S(2)}) collective-permute-start(bf16[128,2048]{1,0:T(8,128)(2,1)S(1)} %add_convert_fusion.4), channel_id=1, source_target_pairs={{0,4},{4,0},{8,12},{12,8},{16,20},{20,16},{24,28},{28,24},{1,5},{5... | collective-permute-start | bytes 1572872 | tf_op jit(solution)/shard_map/ppermute | solution.py:430
  159.9 19.9 %collective-permute-start.28 = (bf16[256,1024]{1,0:T(8,128)(2,1)S(1)}, bf16[256,1024]{1,0:T(8,128)(2,1)S(1)}, u32[]{:S(2)}, u32[]{:S(2)}) collective-permute-start(bf16[256,1024]{1,0:T(8,128)(2,1)S(1)} %get-tuple-element.123), channel_id=1, source_target_pairs={{0,8},{4,12},{8,16},{12,20},{16,24},{20,28},{24,0},{28,4},{1,9},{5... | collective-permute-start | bytes 1572872 | tf_op jit(solution)/shard_map/ppermute | solution.py:422
  160.2 21.0 %collective-permute-start.29 = (bf16[256,1024]{1,0:T(8,128)(2,1)S(1)}, bf16[256,1024]{1,0:T(8,128)(2,1)S(1)}, u32[]{:S(2)}, u32[]{:S(2)}) collective-permute-start(bf16[256,1024]{1,0:T(8,128)(2,1)S(1)} %get-tuple-element.124), channel_id=1, source_target_pairs={{0,4},{4,0},{8,12},{12,8},{16,20},{20,16},{24,28},{28,24},{1,5},{5... | collective-permute-start | bytes 1572872 | tf_op jit(solution)/shard_map/ppermute | solution.py:430
  186.1 16.9 %collective-permute-start.33 = (bf16[128,2048]{1,0:T(8,128)(2,1)S(1)}, bf16[128,2048]{1,0:T(8,128)(2,1)S(1)}, u32[]{:S(2)}, u32[]{:S(2)}) collective-permute-start(bf16[128,2048]{1,0:T(8,128)(2,1)S(1)} %add_convert_fusion.1), channel_id=1, source_target_pairs={{0,8},{4,12},{8,16},{12,20},{16,24},{20,28},{24,0},{28,4},{1,9},{5... | collective-permute-start | bytes 1572872 | tf_op jit(solution)/shard_map/ppermute | solution.py:422
  191.6 17.0 %collective-permute-start.34 = (bf16[128,1024]{1,0:T(8,128)(2,1)S(1)}, bf16[128,1024]{1,0:T(8,128)(2,1)S(1)}, u32[]{:S(2)}, u32[]{:S(2)}) collective-permute-start(bf16[128,1024]{1,0:T(8,128)(2,1)S(1)} %get-tuple-element.195), channel_id=1, source_target_pairs={{0,8},{4,12},{8,16},{12,20},{16,24},{20,28},{24,0},{28,4},{1,9},{5... | collective-permute-start | bytes 786440 | tf_op jit(solution)/shard_map/ppermute | solution.py:422
  192.2 20.3 %collective-permute-start.35 = (bf16[128,1024]{1,0:T(8,128)(2,1)S(1)}, bf16[128,1024]{1,0:T(8,128)(2,1)S(1)}, u32[]{:S(2)}, u32[]{:S(2)}) collective-permute-start(bf16[128,1024]{1,0:T(8,128)(2,1)S(1)} %get-tuple-element.194), channel_id=1, source_target_pairs={{0,24},{4,28},{8,0},{12,4},{16,8},{20,12},{24,16},{28,20},{1,25},{... | collective-permute-start | bytes 786440 | tf_op jit(solution)/shard_map/ppermute | solution.py:426
  195.4 22.8 %collective-permute-start.32 = (bf16[256,1024]{1,0:T(8,128)(2,1)}, bf16[256,1024]{1,0:T(8,128)(2,1)}, u32[]{:S(2)}, u32[]{:S(2)}) collective-permute-start(bf16[256,1024]{1,0:T(8,128)(2,1)} %add_convert_fusion.2), channel_id=1, source_target_pairs={{0,2},{1,3},{2,0},{3,1},{4,6},{5,7},{6,4},{7,5},{8,10},{9,11},{10,... | collective-permute-start | bytes 1572872 | tf_op jit(solution)/shard_map/ppermute | solution.py:413
  214.7 14.4 %all-to-all-start.2 = ((bf16[4,32,2816]{2,1,0:T(8,128)(2,1)}), bf16[4,32,2816]{2,1,0:T(8,128)(2,1)S(1)}, u32[]{:S(2)}, u32[]{:S(2)}) async-start(bf16[4,32,2816]{2,1,0:T(8,128)(2,1)} %bitcast.9), calls=%async_computation.2 | async-start | bytes 1441792 | tf_op jit(solution)/shard_map/all_to_all | solution.py:418
  (45 other events, 302.5 us)

commit v13 on v12

--- a/solution.py
+++ b/solution.py
@@ -722,6 +722,7 @@
     flops, transcendentals = cost
     shapes = [jax.ShapeDtypeStruct(shape, kind) for shape, kind in outs]
     moved = sum(arg.size * arg.dtype.itemsize for arg in (*args, *shapes))
+    moved = moved // 4 if body is attention_backward else moved
     return pl.pallas_call(
         body,
         out_shape=shapes,
@@ -879,7 +880,7 @@
     grad_packed, g_keep, g_pair, g_near, g_far = kernel(
         attention_backward,
         [((group, 768), b16)] + [((size * n, width), b16) for n in (3, 2, 1, 2)],
-        (2 * group * width * (768 + 512) + 10 * 16 * count * count * LANES, 0),
+        (group * width * (768 + 512), 0),
         place, cosine, sine, low_own, low_across, low_beside, attn, query, key, value, probs,
         attended, normed,
         scratch=[((group, width), b16), ((group, 256), b16), ((256, width), b16)],

time: 235 us -> 230 us (0.979)
  waiting for transfers between devices: 118 us -> 113 us
    ppermute x9, waiting for transfers between devices: 47.7 us -> 41.5 us  [up(): return lax.ppermute(value, 'fsdp', [(k, (k + 2) % 8) for k in range(8)])]
  transfers between devices with their start and end apart: 40 -> 40, of which waited for: 25 -> 25; matrix products, arithmetic and copies ran while one was open for 7% -> 8% of each run, Pallas kernels for 9% -> 9%
where the time goes in v13:
time: 230 us; the launch traced here: 228 us
  waiting for transfers between devices  113 us (49%)
  starting transfers between devices  55.9 us (24%)
  Pallas kernels  31.9 us (14%)
  other arithmetic  20.1 us (9%)
  local copies, waits for them, and re-layouts  5.84 us (3%)
    ppermute x9, waiting for transfers between devices, up(): return lax.ppermute(value, 'fsdp', [(k, (k + 2) % 8) for k in range(8)])  41.5 us
    pallas_call x7, Pallas kernels, kernel(): pl.pallas_call(body, out_shape=shapes, in_specs=[pl.BlockSpec(memory_spac...  31.9 us
    ppermute x4, waiting for transfers between devices, down(): return lax.ppermute(value, 'fsdp', [(k, (k - 2) % 8) for k in range(8)])  24.1 us
    ppermute x10, waiting for transfers between devices, over(): return lax.ppermute(value, 'fsdp', [(k, k ^ 1) for k in range(8)])  20.2 us
    ppermute x12, waiting for transfers between devices, swap(): return lax.ppermute(value, 'rep', [(k, k ^ distance) for k in range(4)])  19 us
    all_to_all x3, starting transfers between devices, rep_exchange(): return lax.all_to_all(blocks, 'rep', 0, 0, tiled=True).reshape(value.shape)  14.9 us
    ppermute x4, starting transfers between devices, down(): return lax.ppermute(value, 'fsdp', [(k, (k - 2) % 8) for k in range(8)])  11.7 us
    ppermute x9, starting transfers between devices, up(): return lax.ppermute(value, 'fsdp', [(k, (k + 2) % 8) for k in range(8)])  10.7 us
  transfers between devices with their start and end apart: 40, of which 25 were waited for; matrix products, arithmetic and copies ran while one was open for 8% of the time, Pallas kernels for 9%

profile of v13, /device:TPU:0, one launch (start us, length us, event | category | flops | bytes accessed | tf_op | source)
XLA Modules:
  0.0 228.3 jit_solution(14650201866108360031)
XLA Ops:
  3.9 4.2 %all-to-all-start = ((bf16[4,32,896]{2,1,0:T(8,128)(2,1)}), bf16[4,32,896]{2,1,0:T(8,128)(2,1)S(1)}, u32[]{:S(2)}, u32[]{:S(2)}) async-start(bf16[4,32,896]{2,1,0:T(8,128)(2,1)} %bitcast), calls=%async_computation | async-start | bytes 458752 | tf_op jit(solution)/shard_map/all_to_all | solution.py:418
  11.6 2.2 all-to-all-done
  13.8 7.2 %all-to-all-start.1 = ((bf16[4,32,2048]{2,1,0:T(8,128)(2,1)}), bf16[4,32,2048]{2,1,0:T(8,128)(2,1)}, u32[]{:S(2)}, u32[]{:S(2)}) async-start(bf16[4,32,2048]{2,1,0:T(8,128)(2,1)} %bitcast.3), calls=%async_computation.1 | async-start | bytes 1048576 | tf_op jit(solution)/shard_map/all_to_all | solution.py:418
  22.1 4.7 %collective-permute-start.2 = (bf16[128,1024]{1,0:T(8,128)(2,1)S(1)}, bf16[128,1024]{1,0:T(8,128)(2,1)S(1)}, u32[]{:S(2)}, u32[]{:S(2)}) collective-permute-start(bf16[128,1024]{1,0:T(8,128)(2,1)S(1)} %maximum_maximum_fusion.own), channel_id=1, source_target_pairs={{0,24},{4,28},{8,0},{12,4},{16,8},{20,12},{24,16},{28,20},{1,25},{... | collective-permute-start | bytes 786440 | tf_op jit(solution)/shard_map/ppermute | solution.py:426
  27.0 6.9 %collective-permute-done.1.third = bf16[128,1024]{1,0:T(8,128)(2,1)S(1)} collective-permute-done((bf16[128,1024]{1,0:T(8,128)(2,1)S(1)}, bf16[128,1024]{1,0:T(8,128)(2,1)S(1)}, u32[]{:S(2)}, u32[]{:S(2)}) %collective-permute-start.1) | collective-permute-done | bytes 262176 | tf_op jit(solution)/shard_map/ppermute | solution.py:422
  33.9 3.2 %collective-permute-done.2.first = bf16[128,1024]{1,0:T(8,128)(2,1)S(1)} collective-permute-done((bf16[128,1024]{1,0:T(8,128)(2,1)S(1)}, bf16[128,1024]{1,0:T(8,128)(2,1)S(1)}, u32[]{:S(2)}, u32[]{:S(2)}) %collective-permute-start.2) | collective-permute-done | bytes 262176 | tf_op jit(solution)/shard_map/ppermute | solution.py:426
  42.4 8.4 %collective-permute-done.4.second = bf16[128,1024]{1,0:T(8,128)(2,1)S(1)} collective-permute-done((bf16[128,1024]{1,0:T(8,128)(2,1)S(1)}, bf16[128,1024]{1,0:T(8,128)(2,1)S(1)}, u32[]{:S(2)}, u32[]{:S(2)}) %collective-permute-start.4) | collective-permute-done | bytes 262176 | tf_op jit(solution)/shard_map/ppermute | solution.py:422
  55.0 4.6 %collective-permute-done.9.third = bf16[128,2048]{1,0:T(8,128)(2,1)S(1)} collective-permute-done((bf16[128,2048]{1,0:T(8,128)(2,1)}, bf16[128,2048]{1,0:T(8,128)(2,1)S(1)}, u32[]{:S(2)}, u32[]{:S(2)}) %collective-permute-start.9) | collective-permute-done | bytes 524320 | tf_op jit(solution)/shard_map/ppermute | solution.py:422
  65.5 7.0 %attention_forward.1 = (bf16[512,1024]{1,0:T(8,128)(2,1)S(1)}, bf16[1024,768]{1,0:T(8,128)(2,1)S(1)}, bf16[256,1024]{1,0:T(8,128)(2,1)S(1)}, bf16[512,256]{1,0:T...) custom-call(s32[2]{0:T(128)S(1)} %pad_add_fusion.place, ...), custom_call_target="tpu_custom_call" | custom-call | flops 1207959552 | bytes 11014152 | tf_op jit(solution)/shard_map/attention_forward/pallas_call | solution.py:726
  72.5 3.5 %collective-permute-done.11.other = bf16[128,2048]{1,0:T(8,128)(2,1)} collective-permute-done((bf16[128,2048]{1,0:T(8,128)(2,1)}, bf16[128,2048]{1,0:T(8,128)(2,1)}, u32[]{:S(2)}, u32[]{:S(2)}) %collective-permute-start.11) | collective-permute-done | bytes 524320 | tf_op jit(solution)/shard_map/ppermute | solution.py:430
  80.1 3.8 %collective-permute-start.16 = (bf16[128,2048]{1,0:T(8,128)(2,1)S(1)}, bf16[128,2048]{1,0:T(8,128)(2,1)S(1)}, u32[]{:S(2)}, u32[]{:S(2)}) collective-permute-start(bf16[128,2048]{1,0:T(8,128)(2,1)S(1)} %copy-done.14), channel_id=1, source_target_pairs={{0,8},{4,12},{8,16},{12,20},{16,24},{20,28},{24,0},{28,4},{1,9},{5... | collective-permute-start | bytes 1572872 | tf_op jit(solution)/shard_map/ppermute | solution.py:422
  83.9 2.5 %collective-permute-done.13 = bf16[128,1024]{1,0:T(8,128)(2,1)S(1)} collective-permute-done((bf16[128,1024]{1,0:T(8,128)(2,1)S(1)}, bf16[128,1024]{1,0:T(8,128)(2,1)S(1)}, u32[]{:S(2)}, u32[]{:S(2)}) %collective-permute-start.13) | collective-permute-done | bytes 262176 | tf_op jit(solution)/shard_map/ppermute | solution.py:413
  88.0 4.8 %collective-permute-done.17.other_third = bf16[128,2048]{1,0:T(8,128)(2,1)S(1)} collective-permute-done((bf16[128,2048]{1,0:T(8,128)(2,1)S(1)}, bf16[128,2048]{1,0:T(8,128)(2,1)S(1)}, u32[]{:S(2)}, u32[]{:S(2)}) %collective-permute-start.17) | collective-permute-done | bytes 524320 | tf_op jit(solution)/shard_map/ppermute | solution.py:430
  93.8 2.2 collective-permute-done.16.second
  97.7 8.2 %collective-permute-done.18.other_first = bf16[128,2048]{1,0:T(8,128)(2,1)S(1)} collective-permute-done((bf16[128,2048]{1,0:T(8,128)(2,1)}, bf16[128,2048]{1,0:T(8,128)(2,1)S(1)}, u32[]{:S(2)}, u32[]{:S(2)}) %collective-permute-start.18) | collective-permute-done | bytes 524320 | tf_op jit(solution)/shard_map/ppermute | solution.py:430
  105.9 4.8 %collective-permute-done.19.other_second = bf16[128,2048]{1,0:T(8,128)(2,1)S(1)} collective-permute-done((bf16[128,2048]{1,0:T(8,128)(2,1)S(1)}, bf16[128,2048]{1,0:T(8,128)(2,1)S(1)}, u32[]{:S(2)}, u32[]{:S(2)}) %collective-permute-start.19) | collective-permute-done | bytes 524320 | tf_op jit(solution)/shard_map/ppermute | solution.py:422
  110.6 7.3 %mlp.1 = (bf16[512,1024]{1,0:T(8,128)(2,1)S(1)}, bf16[512,1024]{1,0:T(8,128)(2,1)S(1)}, bf16[512,768]{1,0:T(8,128)(2,1)S(1)}, bf16[512,1408]{1,0:T(8,128)(2,1)S(...) custom-call(s32[512,1]{1,0:T(8,128)S(1)} %copy.28.seg_col, ...), custom_call_target="tpu_custom_call" | custom-call | flops 3758096384 | bytes 14288896 | tf_op jit(solution)/shard_map/mlp/pallas_call | solution.py:726
  120.5 2.7 %mlp_terms.1 = (bf16[384,2048]{1,0:T(8,128)(2,1)S(1)}, bf16[256,2048]{1,0:T(8,128)(2,1)S(1)}, bf16[128,2048]{1,0:T(8,128)(2,1)S(1)}, bf16[256,2048]{1,0:T(8,128)(2,1)S(1)}) custom-call(bf16[512,1024]{1,0:T(8,128)(2,1)S(1)} %get-tuple-element.101.normed, bf16[512,1408]{1,0:T(8,128)(2,1)S(1)} %get-tuple-element.102.grad_inner, ...), custom_call_target="tpu_custom_call" | custom-call | flops 2147483648 | bytes 8519680 | tf_op jit(solution)/shard_map/mlp_terms/pallas_call | solution.py:726
  124.7 3.7 %collective-permute-done.21 = bf16[128,1024]{1,0:T(8,128)(2,1)S(1)} collective-permute-done((bf16[128,1024]{1,0:T(8,128)(2,1)S(1)}, bf16[128,1024]{1,0:T(8,128)(2,1)S(1)}, u32[]{:S(2)}, u32[]{:S(2)}) %collective-permute-start.21) | collective-permute-done | bytes 262176 | tf_op jit(solution)/shard_map/ppermute | solution.py:413
  130.3 7.0 %collective-permute-done.22.low_across = bf16[128,1024]{1,0:T(8,128)(2,1)S(1)} collective-permute-done((bf16[128,1024]{1,0:T(8,128)(2,1)S(1)}, bf16[128,1024]{1,0:T(8,128)(2,1)S(1)}, u32[]{:S(2)}, u32[]{:S(2)}) %collective-permute-start.22) | collective-permute-done | bytes 262176 | tf_op jit(solution)/shard_map/ppermute | solution.py:413
  139.3 7.6 %attention_backward.1 = (bf16[512,768]{1,0:T(8,128)(2,1)S(1)}, bf16[384,1024]{1,0:T(8,128)(2,1)S(1)}, bf16[256,1024]{1,0:T(8,128)(2,1)S(1)}, bf16[128,1024]{1,0:T(8,128)(2,1)S(1)}, bf16[256,1024]{1,0:T(8,128)(2,1)S(1)}) custom-call(s32[2]{0:T(128)S(1)} %pad_add_fusion.place, f32[512,128]{1,0:T(8,128)S(1)} %get-tuple-element.268.cosine, ...), custom_call_target="tpu_custom_call" | custom-call | flops 671088640 | bytes 2031618 | tf_op jit(solution)/shard_map/attention_backward/pallas_call | solution.py:726
  146.9 3.1 %collective-permute-done.24 = bf16[256,2048]{1,0:T(8,128)(2,1)S(1)} collective-permute-done((bf16[256,2048]{1,0:T(8,128)(2,1)S(1)}, bf16[256,2048]{1,0:T(8,128)(2,1)S(1)}, u32[]{:S(2)}, u32[]{:S(2)}) %collective-permute-start.24) | collective-permute-done | bytes 1048608 | tf_op jit(solution)/shard_map/ppermute | solution.py:422
  154.8 2.8 %projections.1 = (bf16[512,1024]{1,0:T(8,128)(2,1)}, bf16[512,1024]{1,0:T(8,128)(2,1)S(1)}) custom-call(bf16[512,768]{1,0:T(8,128)(2,1)S(1)} %get-tuple-element.113.grad_packed, bf16[1024,768]{1,0:T(8,128)(2,1)S(1)} %get-tuple-element.114.qkv, bf16[512,768]{1,0:T(8,128)(2,1)S(1)} %get-tuple-element.103.mixed, bf16[1024,768]{1,0:T(8,128)(2,1)S(1)} %get-tuple-element.115.w_down), custom_call_target="tpu_custom_call" | custom-call | flops 1610612736 | bytes 6815744 | tf_op jit(solution)/shard_map/projections/pallas_call | solution.py:726
  157.6 17.0 %collective-permute-done.27 = bf16[128,2048]{1,0:T(8,128)(2,1)S(1)} collective-permute-done((bf16[128,2048]{1,0:T(8,128)(2,1)S(1)}, bf16[128,2048]{1,0:T(8,128)(2,1)S(1)}, u32[]{:S(2)}, u32[]{:S(2)}) %collective-permute-start.27) | collective-permute-done | bytes 524320 | tf_op jit(solution)/shard_map/ppermute | solution.py:426
  183.7 2.3 %collective-permute-done.31 = bf16[128,1024]{1,0:T(8,128)(2,1)S(1)} collective-permute-done((bf16[128,1024]{1,0:T(8,128)(2,1)S(1)}, bf16[128,1024]{1,0:T(8,128)(2,1)S(1)}, u32[]{:S(2)}, u32[]{:S(2)}) %collective-permute-start.31) | collective-permute-done | bytes 262176 | tf_op jit(solution)/shard_map/ppermute | solution.py:430
  186.9 3.2 %collective-permute-start.35 = (bf16[128,1024]{1,0:T(8,128)(2,1)S(1)}, bf16[128,1024]{1,0:T(8,128)(2,1)S(1)}, u32[]{:S(2)}, u32[]{:S(2)}) collective-permute-start(bf16[128,1024]{1,0:T(8,128)(2,1)S(1)} %get-tuple-element.194), channel_id=1, source_target_pairs={{0,24},{4,28},{8,0},{12,4},{16,8},{20,12},{24,16},{28,20},{1,25},{... | collective-permute-start | bytes 786440 | tf_op jit(solution)/shard_map/ppermute | solution.py:426
  191.8 6.0 %collective-permute-done.33 = bf16[128,2048]{1,0:T(8,128)(2,1)S(1)} collective-permute-done((bf16[128,2048]{1,0:T(8,128)(2,1)S(1)}, bf16[128,2048]{1,0:T(8,128)(2,1)S(1)}, u32[]{:S(2)}, u32[]{:S(2)}) %collective-permute-start.33) | collective-permute-done | bytes 524320 | tf_op jit(solution)/shard_map/ppermute | solution.py:422
  197.7 5.5 %collective-permute-done.34 = bf16[128,1024]{1,0:T(8,128)(2,1)S(1)} collective-permute-done((bf16[128,1024]{1,0:T(8,128)(2,1)S(1)}, bf16[128,1024]{1,0:T(8,128)(2,1)S(1)}, u32[]{:S(2)}, u32[]{:S(2)}) %collective-permute-start.34) | collective-permute-done | bytes 262176 | tf_op jit(solution)/shard_map/ppermute | solution.py:422
  203.2 4.0 %collective-permute-done.35 = bf16[128,1024]{1,0:T(8,128)(2,1)S(1)} collective-permute-done((bf16[128,1024]{1,0:T(8,128)(2,1)S(1)}, bf16[128,1024]{1,0:T(8,128)(2,1)S(1)}, u32[]{:S(2)}, u32[]{:S(2)}) %collective-permute-start.35) | collective-permute-done | bytes 262176 | tf_op jit(solution)/shard_map/ppermute | solution.py:426
  209.4 3.5 %all-to-all-start.2 = ((bf16[4,32,2816]{2,1,0:T(8,128)(2,1)}), bf16[4,32,2816]{2,1,0:T(8,128)(2,1)S(1)}, u32[]{:S(2)}, u32[]{:S(2)}) async-start(bf16[4,32,2816]{2,1,0:T(8,128)(2,1)} %bitcast.9), calls=%async_computation.2 | async-start | bytes 1441792 | tf_op jit(solution)/shard_map/all_to_all | solution.py:418
  217.8 5.9 %all-to-all-done.2 = bf16[4,32,2816]{2,1,0:T(8,128)(2,1)S(1)} async-done(((bf16[4,32,2816]{2,1,0:T(8,128)(2,1)}), bf16[4,32,2816]{2,1,0:T(8,128)(2,1)S(1)}, u32[]{:S(2)}, u32[]{:S(2)}) %all-to-all-start.2) | async-done | bytes 720928 | tf_op jit(solution)/shard_map/all_to_all | solution.py:418
  223.8 3.6 %unpack_rest.1 = (f32[32,5248]{1,0:T(8,128)}, f32[1,32]{1,0:T(1,128)}, f32[32,2624]{1,0:T(8,128)}) custom-call(bf16[128,2816]{1,0:T(8,128)(2,1)S(1)} %bitcast.19, bf16[32,5248]{1,0:T(8,128)(2,1)S(1)} %copy-done, f32[32,1]{1,0:T(8,128)S(1)} %copy.31.gain), custom_call_target="tpu_custom_call" | custom-call | flops 671744 | bytes 2064640 | tf_op jit(solution)/shard_map/unpack_rest/pallas_call | solution.py:726
  (236 shorter events, 63.4 us)
Async XLA Ops:
  3.9 9.9 %all-to-all-start = ((bf16[4,32,896]{2,1,0:T(8,128)(2,1)}), bf16[4,32,896]{2,1,0:T(8,128)(2,1)S(1)}, u32[]{:S(2)}, u32[]{:S(2)}) async-start(bf16[4,32,896]{2,1,0:T(8,128)(2,1)} %bitcast), calls=%async_computation | async-start | bytes 458752 | tf_op jit(solution)/shard_map/all_to_all | solution.py:418
  13.8 23.3 %all-to-all-start.1 = ((bf16[4,32,2048]{2,1,0:T(8,128)(2,1)}), bf16[4,32,2048]{2,1,0:T(8,128)(2,1)}, u32[]{:S(2)}, u32[]{:S(2)}) async-start(bf16[4,32,2048]{2,1,0:T(8,128)(2,1)} %bitcast.3), calls=%async_computation.1 | async-start | bytes 1048576 | tf_op jit(solution)/shard_map/all_to_all | solution.py:418
  21.0 12.9 %collective-permute-start.1 = (bf16[128,1024]{1,0:T(8,128)(2,1)S(1)}, bf16[128,1024]{1,0:T(8,128)(2,1)S(1)}, u32[]{:S(2)}, u32[]{:S(2)}) collective-permute-start(bf16[128,1024]{1,0:T(8,128)(2,1)S(1)} %maximum_maximum_fusion.own), channel_id=1, source_target_pairs={{0,8},{4,12},{8,16},{12,20},{16,24},{20,28},{24,0},{28,4},{1,9},{5... | collective-permute-start | bytes 786440 | tf_op jit(solution)/shard_map/ppermute | solution.py:422
  22.1 15.0 %collective-permute-start.2 = (bf16[128,1024]{1,0:T(8,128)(2,1)S(1)}, bf16[128,1024]{1,0:T(8,128)(2,1)S(1)}, u32[]{:S(2)}, u32[]{:S(2)}) collective-permute-start(bf16[128,1024]{1,0:T(8,128)(2,1)S(1)} %maximum_maximum_fusion.own), channel_id=1, source_target_pairs={{0,24},{4,28},{8,0},{12,4},{16,8},{20,12},{24,16},{28,20},{1,25},{... | collective-permute-start | bytes 786440 | tf_op jit(solution)/shard_map/ppermute | solution.py:426
  26.8 10.3 %collective-permute-start.3 = (bf16[128,1024]{1,0:T(8,128)(2,1)S(1)}, bf16[128,1024]{1,0:T(8,128)(2,1)S(1)}, u32[]{:S(2)}, u32[]{:S(2)}) collective-permute-start(bf16[128,1024]{1,0:T(8,128)(2,1)S(1)} %maximum_maximum_fusion.own), channel_id=1, source_target_pairs={{0,4},{4,0},{8,12},{12,8},{16,20},{20,16},{24,28},{28,24},{1,5},{5... | collective-permute-start | bytes 786440 | tf_op jit(solution)/shard_map/ppermute | solution.py:430
  37.2 13.6 %collective-permute-start.5 = (bf16[256,1024]{1,0:T(8,128)(2,1)S(1)}, bf16[256,1024]{1,0:T(8,128)(2,1)S(1)}, u32[]{:S(2)}, u32[]{:S(2)}) collective-permute-start(bf16[256,1024]{1,0:T(8,128)(2,1)S(1)} %pad_maximum_fusion.4), channel_id=1, source_target_pairs={{0,4},{4,0},{8,12},{12,8},{16,20},{20,16},{24,28},{28,24},{1,5},{5... | collective-permute-start | bytes 1572872 | tf_op jit(solution)/shard_map/ppermute | solution.py:430
  38.0 13.6 %collective-permute-start.6 = (bf16[256,1024]{1,0:T(8,128)(2,1)S(1)}, bf16[256,1024]{1,0:T(8,128)(2,1)S(1)}, u32[]{:S(2)}, u32[]{:S(2)}) collective-permute-start(bf16[256,1024]{1,0:T(8,128)(2,1)S(1)} %pad_maximum_fusion.3.mine), channel_id=1, source_target_pairs={{0,2},{1,3},{2,0},{3,1},{4,6},{5,7},{6,4},{7,5},{8,10},{9,11},{10,... | collective-permute-start | bytes 1572872 | tf_op jit(solution)/shard_map/ppermute | solution.py:413
  39.7 11.1 %collective-permute-start.4 = (bf16[128,1024]{1,0:T(8,128)(2,1)S(1)}, bf16[128,1024]{1,0:T(8,128)(2,1)S(1)}, u32[]{:S(2)}, u32[]{:S(2)}) collective-permute-start(bf16[128,1024]{1,0:T(8,128)(2,1)S(1)} %collective-permute-done.1.third), channel_id=1, source_target_pairs={{0,8},{4,12},{8,16},{12,20},{16,24},{20,28},{24,0},{28,4},{1,9},{5... | collective-permute-start | bytes 786440 | tf_op jit(solution)/shard_map/ppermute | solution.py:422
  41.7 17.9 %collective-permute-start.9 = (bf16[128,2048]{1,0:T(8,128)(2,1)}, bf16[128,2048]{1,0:T(8,128)(2,1)S(1)}, u32[]{:S(2)}, u32[]{:S(2)}) collective-permute-start(bf16[128,2048]{1,0:T(8,128)(2,1)} %bitcast.4.own), channel_id=1, source_target_pairs={{0,8},{4,12},{8,16},{12,20},{16,24},{20,28},{24,0},{28,4},{1,9},{5... | collective-permute-start | bytes 1572872 | tf_op jit(solution)/shard_map/ppermute | solution.py:422
  52.6 12.8 %collective-permute-start.7 = (bf16[512,1024]{1,0:T(8,128)(2,1)}, bf16[512,1024]{1,0:T(8,128)(2,1)S(1)}, u32[]{:S(2)}, u32[]{:S(2)}) collective-permute-start(bf16[512,1024]{1,0:T(8,128)(2,1)} %pad_maximum_fusion), channel_id=1, source_target_pairs={{0,1},{1,0},{2,3},{3,2},{4,5},{5,4},{6,7},{7,6},{8,9},{9,8},{10,11... | collective-permute-start | bytes 3145736 | tf_op jit(solution)/shard_map/ppermute | solution.py:413
  52.7 8.8 %collective-permute-start.8 = (bf16[128,1024]{1,0:T(8,128)(2,1)S(1)}, bf16[128,1024]{1,0:T(8,128)(2,1)S(1)}, u32[]{:S(2)}, u32[]{:S(2)}) collective-permute-start(bf16[128,1024]{1,0:T(8,128)(2,1)S(1)} %collective-permute-done.4.second), channel_id=1, source_target_pairs={{0,4},{4,0},{8,12},{12,8},{16,20},{20,16},{24,28},{28,24},{1,5},{5... | collective-permute-start | bytes 786440 | tf_op jit(solution)/shard_map/ppermute | solution.py:430
  59.7 12.9 %collective-permute-start.10 = (bf16[128,2048]{1,0:T(8,128)(2,1)}, bf16[128,2048]{1,0:T(8,128)(2,1)}, u32[]{:S(2)}, u32[]{:S(2)}) collective-permute-start(bf16[128,2048]{1,0:T(8,128)(2,1)} %bitcast.4.own), channel_id=1, source_target_pairs={{0,24},{4,28},{8,0},{12,4},{16,8},{20,12},{24,16},{28,20},{1,25},{... | collective-permute-start | bytes 1572872 | tf_op jit(solution)/shard_map/ppermute | solution.py:426
  62.2 13.9 %collective-permute-start.11 = (bf16[128,2048]{1,0:T(8,128)(2,1)}, bf16[128,2048]{1,0:T(8,128)(2,1)}, u32[]{:S(2)}, u32[]{:S(2)}) collective-permute-start(bf16[128,2048]{1,0:T(8,128)(2,1)} %bitcast.4.own), channel_id=1, source_target_pairs={{0,4},{4,0},{8,12},{12,8},{16,20},{20,16},{24,28},{28,24},{1,5},{5... | collective-permute-start | bytes 1572872 | tf_op jit(solution)/shard_map/ppermute | solution.py:430
  78.0 8.4 %collective-permute-start.13 = (bf16[128,1024]{1,0:T(8,128)(2,1)S(1)}, bf16[128,1024]{1,0:T(8,128)(2,1)S(1)}, u32[]{:S(2)}, u32[]{:S(2)}) collective-permute-start(bf16[128,1024]{1,0:T(8,128)(2,1)S(1)} %add_convert_fusion.10), channel_id=1, source_target_pairs={{0,2},{1,3},{2,0},{3,1},{4,6},{5,7},{6,4},{7,5},{8,10},{9,11},{10,... | collective-permute-start | bytes 786440 | tf_op jit(solution)/shard_map/ppermute | solution.py:413
  79.1 13.8 %collective-permute-start.17 = (bf16[128,2048]{1,0:T(8,128)(2,1)S(1)}, bf16[128,2048]{1,0:T(8,128)(2,1)S(1)}, u32[]{:S(2)}, u32[]{:S(2)}) collective-permute-start(bf16[128,2048]{1,0:T(8,128)(2,1)S(1)} %copy-done.14), channel_id=1, source_target_pairs={{0,4},{4,0},{8,12},{12,8},{16,20},{20,16},{24,28},{28,24},{1,5},{5... | collective-permute-start | bytes 1572872 | tf_op jit(solution)/shard_map/ppermute | solution.py:430
  80.1 15.9 %collective-permute-start.16 = (bf16[128,2048]{1,0:T(8,128)(2,1)S(1)}, bf16[128,2048]{1,0:T(8,128)(2,1)S(1)}, u32[]{:S(2)}, u32[]{:S(2)}) collective-permute-start(bf16[128,2048]{1,0:T(8,128)(2,1)S(1)} %copy-done.14), channel_id=1, source_target_pairs={{0,8},{4,12},{8,16},{12,20},{16,24},{20,28},{24,0},{28,4},{1,9},{5... | collective-permute-start | bytes 1572872 | tf_op jit(solution)/shard_map/ppermute | solution.py:422
  87.1 10.5 %collective-permute-start.14 = (bf16[128,1024]{1,0:T(8,128)(2,1)S(1)}, bf16[128,1024]{1,0:T(8,128)(2,1)S(1)}, u32[]{:S(2)}, u32[]{:S(2)}) collective-permute-start(bf16[128,1024]{1,0:T(8,128)(2,1)S(1)} %fusion.12.norm_own), channel_id=1, source_target_pairs={{0,2},{1,3},{2,0},{3,1},{4,6},{5,7},{6,4},{7,5},{8,10},{9,11},{10,... | collective-permute-start | bytes 786440 | tf_op jit(solution)/shard_map/ppermute | solution.py:413
  92.8 13.0 %collective-permute-start.18 = (bf16[128,2048]{1,0:T(8,128)(2,1)}, bf16[128,2048]{1,0:T(8,128)(2,1)S(1)}, u32[]{:S(2)}, u32[]{:S(2)}) collective-permute-start(bf16[128,2048]{1,0:T(8,128)(2,1)} %collective-permute-done.10.first), channel_id=1, source_target_pairs={{0,4},{4,0},{8,12},{12,8},{16,20},{20,16},{24,28},{28,24},{1,5},{5... | collective-permute-start | bytes 1572872 | tf_op jit(solution)/shard_map/ppermute | solution.py:430
  96.0 14.6 %collective-permute-start.19 = (bf16[128,2048]{1,0:T(8,128)(2,1)S(1)}, bf16[128,2048]{1,0:T(8,128)(2,1)S(1)}, u32[]{:S(2)}, u32[]{:S(2)}) collective-permute-start(bf16[128,2048]{1,0:T(8,128)(2,1)S(1)} %collective-permute-done.17.other_third), channel_id=1, source_target_pairs={{0,8},{4,12},{8,16},{12,20},{16,24},{20,28},{24,0},{28,4},{1,9},{5... | collective-permute-start | bytes 1572872 | tf_op jit(solution)/shard_map/ppermute | solution.py:422
  97.6 13.0 %collective-permute-start.15 = (bf16[256,1024]{1,0:T(8,128)(2,1)S(1)}, bf16[256,1024]{1,0:T(8,128)(2,1)S(1)}, u32[]{:S(2)}, u32[]{:S(2)}) collective-permute-start(bf16[256,1024]{1,0:T(8,128)(2,1)S(1)} %pad_maximum_fusion.5), channel_id=1, source_target_pairs={{0,1},{1,0},{2,3},{3,2},{4,5},{5,4},{6,7},{7,6},{8,9},{9,8},{10,11... | collective-permute-start | bytes 1572872 | tf_op jit(solution)/shard_map/ppermute | solution.py:413
  120.0 8.4 %collective-permute-start.21 = (bf16[128,1024]{1,0:T(8,128)(2,1)S(1)}, bf16[128,1024]{1,0:T(8,128)(2,1)S(1)}, u32[]{:S(2)}, u32[]{:S(2)}) collective-permute-start(bf16[128,1024]{1,0:T(8,128)(2,1)S(1)} %add_convert_fusion.9), channel_id=1, source_target_pairs={{0,2},{1,3},{2,0},{3,1},{4,6},{5,7},{6,4},{7,5},{8,10},{9,11},{10,... | collective-permute-start | bytes 786440 | tf_op jit(solution)/shard_map/ppermute | solution.py:413
  123.3 26.8 %collective-permute-start.24 = (bf16[256,2048]{1,0:T(8,128)(2,1)S(1)}, bf16[256,2048]{1,0:T(8,128)(2,1)S(1)}, u32[]{:S(2)}, u32[]{:S(2)}) collective-permute-start(bf16[256,2048]{1,0:T(8,128)(2,1)S(1)} %get-tuple-element.118), channel_id=1, source_target_pairs={{0,8},{4,12},{8,16},{12,20},{16,24},{20,28},{24,0},{28,4},{1,9},{5... | collective-permute-start | bytes 3145736 | tf_op jit(solution)/shard_map/ppermute | solution.py:422
  123.3 26.7 %collective-permute-start.25 = (bf16[256,2048]{1,0:T(8,128)(2,1)S(1)}, bf16[256,2048]{1,0:T(8,128)(2,1)S(1)}, u32[]{:S(2)}, u32[]{:S(2)}) collective-permute-start(bf16[256,2048]{1,0:T(8,128)(2,1)S(1)} %get-tuple-element.119), channel_id=1, source_target_pairs={{0,4},{4,0},{8,12},{12,8},{16,20},{20,16},{24,28},{28,24},{1,5},{5... | collective-permute-start | bytes 3145736 | tf_op jit(solution)/shard_map/ppermute | solution.py:430
  150.2 24.3 %collective-permute-start.27 = (bf16[128,2048]{1,0:T(8,128)(2,1)S(1)}, bf16[128,2048]{1,0:T(8,128)(2,1)S(1)}, u32[]{:S(2)}, u32[]{:S(2)}) collective-permute-start(bf16[128,2048]{1,0:T(8,128)(2,1)S(1)} %add_convert_fusion.3), channel_id=1, source_target_pairs={{0,24},{4,28},{8,0},{12,4},{16,8},{20,12},{24,16},{28,20},{1,25},{... | collective-permute-start | bytes 1572872 | tf_op jit(solution)/shard_map/ppermute | solution.py:426
  152.4 22.1 %collective-permute-start.26 = (bf16[128,2048]{1,0:T(8,128)(2,1)S(1)}, bf16[128,2048]{1,0:T(8,128)(2,1)S(1)}, u32[]{:S(2)}, u32[]{:S(2)}) collective-permute-start(bf16[128,2048]{1,0:T(8,128)(2,1)S(1)} %add_convert_fusion.4), channel_id=1, source_target_pairs={{0,4},{4,0},{8,12},{12,8},{16,20},{20,16},{24,28},{28,24},{1,5},{5... | collective-permute-start | bytes 1572872 | tf_op jit(solution)/shard_map/ppermute | solution.py:430
  153.7 20.8 %collective-permute-start.28 = (bf16[256,1024]{1,0:T(8,128)(2,1)S(1)}, bf16[256,1024]{1,0:T(8,128)(2,1)S(1)}, u32[]{:S(2)}, u32[]{:S(2)}) collective-permute-start(bf16[256,1024]{1,0:T(8,128)(2,1)S(1)} %get-tuple-element.123), channel_id=1, source_target_pairs={{0,8},{4,12},{8,16},{12,20},{16,24},{20,28},{24,0},{28,4},{1,9},{5... | collective-permute-start | bytes 1572872 | tf_op jit(solution)/shard_map/ppermute | solution.py:422
  154.0 21.9 %collective-permute-start.29 = (bf16[256,1024]{1,0:T(8,128)(2,1)S(1)}, bf16[256,1024]{1,0:T(8,128)(2,1)S(1)}, u32[]{:S(2)}, u32[]{:S(2)}) collective-permute-start(bf16[256,1024]{1,0:T(8,128)(2,1)S(1)} %get-tuple-element.124), channel_id=1, source_target_pairs={{0,4},{4,0},{8,12},{12,8},{16,20},{20,16},{24,28},{28,24},{1,5},{5... | collective-permute-start | bytes 1572872 | tf_op jit(solution)/shard_map/ppermute | solution.py:430
  180.8 16.9 %collective-permute-start.33 = (bf16[128,2048]{1,0:T(8,128)(2,1)S(1)}, bf16[128,2048]{1,0:T(8,128)(2,1)S(1)}, u32[]{:S(2)}, u32[]{:S(2)}) collective-permute-start(bf16[128,2048]{1,0:T(8,128)(2,1)S(1)} %add_convert_fusion.1), channel_id=1, source_target_pairs={{0,8},{4,12},{8,16},{12,20},{16,24},{20,28},{24,0},{28,4},{1,9},{5... | collective-permute-start | bytes 1572872 | tf_op jit(solution)/shard_map/ppermute | solution.py:422
  186.3 17.0 %collective-permute-start.34 = (bf16[128,1024]{1,0:T(8,128)(2,1)S(1)}, bf16[128,1024]{1,0:T(8,128)(2,1)S(1)}, u32[]{:S(2)}, u32[]{:S(2)}) collective-permute-start(bf16[128,1024]{1,0:T(8,128)(2,1)S(1)} %get-tuple-element.195), channel_id=1, source_target_pairs={{0,8},{4,12},{8,16},{12,20},{16,24},{20,28},{24,0},{28,4},{1,9},{5... | collective-permute-start | bytes 786440 | tf_op jit(solution)/shard_map/ppermute | solution.py:422
  186.9 20.3 %collective-permute-start.35 = (bf16[128,1024]{1,0:T(8,128)(2,1)S(1)}, bf16[128,1024]{1,0:T(8,128)(2,1)S(1)}, u32[]{:S(2)}, u32[]{:S(2)}) collective-permute-start(bf16[128,1024]{1,0:T(8,128)(2,1)S(1)} %get-tuple-element.194), channel_id=1, source_target_pairs={{0,24},{4,28},{8,0},{12,4},{16,8},{20,12},{24,16},{28,20},{1,25},{... | collective-permute-start | bytes 786440 | tf_op jit(solution)/shard_map/ppermute | solution.py:426
  190.1 22.8 %collective-permute-start.32 = (bf16[256,1024]{1,0:T(8,128)(2,1)}, bf16[256,1024]{1,0:T(8,128)(2,1)}, u32[]{:S(2)}, u32[]{:S(2)}) collective-permute-start(bf16[256,1024]{1,0:T(8,128)(2,1)} %add_convert_fusion.2), channel_id=1, source_target_pairs={{0,2},{1,3},{2,0},{3,1},{4,6},{5,7},{6,4},{7,5},{8,10},{9,11},{10,... | collective-permute-start | bytes 1572872 | tf_op jit(solution)/shard_map/ppermute | solution.py:413
  209.4 14.4 %all-to-all-start.2 = ((bf16[4,32,2816]{2,1,0:T(8,128)(2,1)}), bf16[4,32,2816]{2,1,0:T(8,128)(2,1)S(1)}, u32[]{:S(2)}, u32[]{:S(2)}) async-start(bf16[4,32,2816]{2,1,0:T(8,128)(2,1)} %bitcast.9), calls=%async_computation.2 | async-start | bytes 1441792 | tf_op jit(solution)/shard_map/all_to_all | solution.py:418
  (45 other events, 290.3 us)
